TPU v7x, 32 devices: a whole 2x2x4 slice. The times are simulated.
32 devices in a mesh: depth: 4 (over y, x), lat: 8 (over z, core).
Axes of the slice: x: 2, y: 2, z: 4, core: 2. Of those that a mesh axis runs over, the one named last changes fastest.
Arguments:
- operator: float32 [4, 40, 9, 256, 128], P('depth', 'lat'), may hold values from -0.125 to 0.125
- band_shift: int32 [4, 40], P('depth', 'lat'), may hold values from -1 to 1, as said below
- reflectivity: float32 [4, 5120], P('depth', 'lat'), may hold values from -0.4 to 0.4
- up_stored: float32 [4, 5120, 128], P('depth', 'lat'), may hold values from -6 to 6
- down_stored: float32 [4, 5120, 128], P('depth', 'lat'), may hold values from -6 to 6
- sources: float32 [5120, 128], P('lat'), may hold values from -6 to 6
- assignment: int32 [64], replicated, may hold values from 0 to 63, each once
Outputs:
- down_fields: float32 [4, 5120, 128], P('depth', 'lat')
- up_fields: float32 [4, 5120, 128], P('depth', 'lat')
Inputs may be any that keep to these rules, and one draw needn't show every extreme that they name: `band_shift`: in every section some tile row has -1 and some has +1.
All inputs are finite; a program needn't handle non-finite values.
Results may differ from a plain program's by a relative error of at most 0.00013.
Values sent between devices are 32-bit elements; how exact they have to be, the bound alone decides.
No kernel may reach another device: no remote copies, remote signals or barrier semaphores. Data moves between devices by JAX's collectives and lax.ppermute only.
A program may use at most 64 MiB of HBM per device.

v0:
```python
import jax
import jax.numpy as jnp
from jax import lax
from jax.sharding import PartitionSpec as P

TILE = 128
SHOTS = 32


def extended(block, sides, width):
    for axis, dim in sides:
        count = lax.axis_size(axis)
        forward = [(i, i + 1) for i in range(count - 1)]
        backward = [(target, source) for source, target in forward]
        low = lax.ppermute(
            lax.slice_in_dim(block, block.shape[dim] - width, None, axis=dim), axis, forward
        )
        high = lax.ppermute(lax.slice_in_dim(block, 0, width, axis=dim), axis, backward)
        block = jnp.concatenate([low, block, high], axis=dim)
    return block


def from_behind(shard, axis, by):
    devices = lax.axis_size(axis)
    pairs = [(i, i + by) for i in range(devices) if 0 <= i + by < devices]
    return lax.ppermute(shard, axis, pairs)


def combine_parts(real_rows, imag_rows):
    col_count = real_rows.shape[-1]
    shape_in = real_rows.shape[:-1] + (col_count // (2 * SHOTS), 2, SHOTS)
    real_terms = real_rows.reshape(shape_in)
    imag_terms = imag_rows.reshape(shape_in)
    real_part = real_terms[..., 0, :] - imag_terms[..., 1, :]
    imag_part = real_terms[..., 1, :] + imag_terms[..., 0, :]
    return jnp.stack([real_part, imag_part], axis=-2).reshape(real_rows.shape)


def arrange(extrapolator):
    tile_count = extrapolator.shape[0]
    return jnp.transpose(extrapolator, (0, 2, 1, 3)).reshape(tile_count, 2 * TILE, 9 * TILE)


def propagate(arranged, offsets, wavefield):
    tile_count = arranged.shape[0]
    col_count = wavefield.shape[1]
    padded = extended(wavefield, (("lat", 0),), 5 * TILE)
    rows_out = []
    for tile_no in range(tile_count):
        start = (tile_no + 1 + offsets[tile_no]) * TILE
        window = lax.dynamic_slice_in_dim(padded, start, 9 * TILE, 0)
        rows_out.append(
            jnp.dot(
                arranged[tile_no],
                window,
                precision=lax.Precision.HIGHEST,
                preferred_element_type=jnp.float32,
            )
        )
    product = jnp.stack(rows_out)
    real_rows = product[:, :TILE].reshape(tile_count * TILE, col_count)
    imag_rows = product[:, TILE:].reshape(tile_count * TILE, col_count)
    return combine_parts(real_rows, imag_rows)


def pass_down(wavefield):
    return from_behind(wavefield, "depth", 1)


def pass_up(wavefield):
    return from_behind(wavefield, "depth", -1)


def shards(operator, band_shift, reflectivity, up_stored, down_stored, sources, assignment):
    extrapolator = arrange(operator[0])
    offsets = band_shift[0]
    reflect_col = reflectivity[0][:, None]
    stored_up = up_stored[0]
    stored_down = down_stored[0]
    sections = lax.axis_size("depth")
    position = lax.axis_index("depth")
    lateral = sources.shape[0]
    columns = 4 * SHOTS
    real_src = jnp.take(sources[:, : 2 * SHOTS], assignment, axis=1)
    imag_src = jnp.take(sources[:, 2 * SHOTS :], assignment, axis=1)
    entering = jnp.stack(
        [real_src.reshape(lateral, 2, SHOTS), imag_src.reshape(lateral, 2, SHOTS)], axis=2
    ).reshape(lateral, columns)
    result_down = jnp.zeros((lateral, columns), jnp.float32)
    result_up = jnp.zeros((lateral, columns), jnp.float32)
    falling = entering
    rising = jnp.zeros((lateral, columns), jnp.float32)
    for segment_no in range(sections):
        joined = jnp.concatenate(
            [
                (1.0 + reflect_col) * falling - reflect_col * stored_up,
                (1.0 - reflect_col) * rising + reflect_col * stored_down,
            ],
            axis=1,
        )
        advanced = propagate(extrapolator, offsets, joined)
        leaving_down = advanced[:, :columns]
        leaving_up = advanced[:, columns:]
        result_down = jnp.where(position == segment_no, leaving_down, result_down)
        result_up = jnp.where(position == sections - 1 - segment_no, leaving_up, result_up)
        falling = pass_down(leaving_down)
        rising = pass_up(leaving_up)
    return (result_down[None], result_up[None])


def solution(mesh):
    return jax.shard_map(
        shards,
        mesh=mesh,
        in_specs=(
            P("depth", "lat", None, None, None),
            P("depth", "lat"),
            P("depth", "lat"),
            P("depth", "lat", None),
            P("depth", "lat", None),
            P("lat", None),
            P(),
        ),
        out_specs=(P("depth", "lat", None), P("depth", "lat", None)),
        check_vma=False,
    )
```

profile of v0, /device:TPU:1, one launch (start us, length us, event | category | flops | bytes accessed | tf_op | source)
XLA Modules:
  0.0 193.6 jit_solution(5108762489139152355)
XLA Ops:
  9.3 4.6 %collective-permute-start = (f32[640,256]{0,1:T(8,128)}, f32[640,256]{0,1:T(8,128)}, u32[]{:S(2)}, u32[]{:S(2)}) collective-permute-start(f32[640,256]{0,1:T(8,128)} %pad_maximum_fusion.4), channel_id=1, source_target_pairs={{0,1},{1,2},{2,3},{3,4},{4,5},{5,6},{6,7},{8,9},{9,10},{10,11},{11... | collective-permute-start | bytes 1966088 | tf_op jit(solution)/shard_map/ppermute | solution.py:15
  17.6 7.7 %copy.18 = f32[1,5,9,256,128]{3,4,2,1,0:T(8,128)} copy(f32[1,5,9,256,128]{4,3,2,1,0:T(8,128)} %param.9) | data formatting | bytes 11796480 | tf_op args[0]
  25.3 3.4 %fusion.184 = (f32[1,256,9,128]{1,3,2,0:T(8,128)S(1)}, f32[1,256,9,128]{1,3,2,0:T(8,128)S(1)}, f32[1,256,9,128]{1,3,2,0:T(8,128)S(1)}, f32[1,256,9,128]{1,3,2,0:T(8,128)S(1)}, f32[1,256,9,128]{1,3,2,0:T(8,128)S(1)}) fusion(f32[5,256,9,128]{1,3,2,0:T(8,128)} %bitcast.231), kind=kLoop, calls=%fused_computation.146 | loop fusion | bytes 11796480 | tf_op jit(solution)/shard_map/slice | solution.py:54
  41.9 2.5 %copy.19 = f32[5,128,256]{1,0,2:T(8,128)} copy(f32[5,128,256]{1,2,0:T(8,128)} %get-tuple-element.26) | data formatting | bytes 1310720 | tf_op jit(solution)/shard_map/slice | solution.py:61
  44.4 2.3 %reshape_reshape.24 = f32[640,4,2,32]{0,3,2,1:T(8,128)} reshape(f32[5,128,256]{1,0,2:T(8,128)} %copy.19) | data formatting | bytes 1310720 | tf_op jit(solution)/shard_map/reshape;reshape | solution.py:32
  49.0 3.1 %collective-permute-start.2 = (f32[640,128]{0,1:T(8,128)S(1)}, f32[640,128]{0,1:T(8,128)S(1)}, u32[]{:S(2)}, u32[]{:S(2)}) collective-permute-start(f32[640,128]{0,1:T(8,128)S(1)} %get-tuple-element.32), channel_id=1, source_target_pairs={{0,8},{8,16},{16,24},{1,9},{9,17},{17,25},{2,10},{10,18},{18,26},{... | collective-permute-start | bytes 983048 | tf_op jit(solution)/shard_map/ppermute | solution.py:26
  53.4 5.5 %collective-permute-done.2 = f32[640,128]{0,1:T(8,128)S(1)} collective-permute-done((f32[640,128]{0,1:T(8,128)S(1)}, f32[640,128]{0,1:T(8,128)S(1)}, u32[]{:S(2)}, u32[]{:S(2)}) %collective-permute-start.2) | collective-permute-done | bytes 327712 | tf_op jit(solution)/shard_map/ppermute | solution.py:26
  58.9 9.0 %collective-permute-done.3 = f32[640,128]{0,1:T(8,128)S(1)} collective-permute-done((f32[640,128]{0,1:T(8,128)S(1)}, f32[640,128]{0,1:T(8,128)S(1)}, u32[]{:S(2)}, u32[]{:S(2)}) %collective-permute-start.3) | collective-permute-done | bytes 327712 | tf_op jit(solution)/shard_map/ppermute | solution.py:26
  68.1 3.1 %collective-permute-start.5 = (f32[640,256]{0,1:T(8,128)S(1)}, f32[640,256]{0,1:T(8,128)S(1)}, u32[]{:S(2)}, u32[]{:S(2)}) collective-permute-start(f32[640,256]{0,1:T(8,128)S(1)} %pad_maximum_fusion.6), channel_id=1, source_target_pairs={{1,0},{2,1},{3,2},{4,3},{5,4},{6,5},{7,6},{9,8},{10,9},{11,10},{12... | collective-permute-start | bytes 1966088 | tf_op jit(solution)/shard_map/ppermute | solution.py:18
  71.2 2.8 %collective-permute-start.4 = (f32[640,256]{0,1:T(8,128)S(1)}, f32[640,256]{0,1:T(8,128)S(1)}, u32[]{:S(2)}, u32[]{:S(2)}) collective-permute-start(f32[640,256]{0,1:T(8,128)S(1)} %pad_maximum_fusion.6), channel_id=1, source_target_pairs={{0,1},{1,2},{2,3},{3,4},{4,5},{5,6},{6,7},{8,9},{9,10},{10,11},{11... | collective-permute-start | bytes 1966088 | tf_op jit(solution)/shard_map/ppermute | solution.py:15
  74.0 6.1 %collective-permute-done.5 = f32[640,256]{0,1:T(8,128)S(1)} collective-permute-done((f32[640,256]{0,1:T(8,128)S(1)}, f32[640,256]{0,1:T(8,128)S(1)}, u32[]{:S(2)}, u32[]{:S(2)}) %collective-permute-start.5) | collective-permute-done | bytes 655392 | tf_op jit(solution)/shard_map/ppermute | solution.py:18
  92.3 2.5 %copy.21 = f32[5,128,256]{1,0,2:T(8,128)} copy(f32[5,128,256]{1,2,0:T(8,128)} %get-tuple-element.22) | data formatting | bytes 1310720 | tf_op jit(solution)/shard_map/slice | solution.py:61
  94.8 2.3 %reshape_reshape.26 = f32[640,4,2,32]{0,3,2,1:T(8,128)} reshape(f32[5,128,256]{1,0,2:T(8,128)} %copy.21) | data formatting | bytes 1310720 | tf_op jit(solution)/shard_map/reshape;reshape | solution.py:32
  99.4 3.2 %collective-permute-start.6 = (f32[640,128]{0,1:T(8,128)S(1)}, f32[640,128]{0,1:T(8,128)S(1)}, u32[]{:S(2)}, u32[]{:S(2)}) collective-permute-start(f32[640,128]{0,1:T(8,128)S(1)} %get-tuple-element.30), channel_id=1, source_target_pairs={{0,8},{8,16},{16,24},{1,9},{9,17},{17,25},{2,10},{10,18},{18,26},{... | collective-permute-start | bytes 983048 | tf_op jit(solution)/shard_map/ppermute | solution.py:26
  103.9 2.7 %collective-permute-done.6 = f32[640,128]{0,1:T(8,128)S(1)} collective-permute-done((f32[640,128]{0,1:T(8,128)S(1)}, f32[640,128]{0,1:T(8,128)S(1)}, u32[]{:S(2)}, u32[]{:S(2)}) %collective-permute-start.6) | collective-permute-done | bytes 327712 | tf_op jit(solution)/shard_map/ppermute | solution.py:26
  106.6 5.6 %collective-permute-done.7 = f32[640,128]{0,1:T(8,128)S(1)} collective-permute-done((f32[640,128]{0,1:T(8,128)S(1)}, f32[640,128]{0,1:T(8,128)S(1)}, u32[]{:S(2)}, u32[]{:S(2)}) %collective-permute-start.7) | collective-permute-done | bytes 327712 | tf_op jit(solution)/shard_map/ppermute | solution.py:26
  114.4 9.6 %collective-permute-start.8 = (f32[640,256]{0,1:T(8,128)S(1)}, f32[640,256]{0,1:T(8,128)S(1)}, u32[]{:S(2)}, u32[]{:S(2)}) collective-permute-start(f32[640,256]{0,1:T(8,128)S(1)} %pad_maximum_fusion.8), channel_id=1, source_target_pairs={{0,1},{1,2},{2,3},{3,4},{4,5},{5,6},{6,7},{8,9},{9,10},{10,11},{11... | collective-permute-start | bytes 1966088 | tf_op jit(solution)/shard_map/ppermute | solution.py:15
  124.0 6.1 %collective-permute-done.9 = f32[640,256]{0,1:T(8,128)S(1)} collective-permute-done((f32[640,256]{0,1:T(8,128)S(1)}, f32[640,256]{0,1:T(8,128)S(1)}, u32[]{:S(2)}, u32[]{:S(2)}) %collective-permute-start.9) | collective-permute-done | bytes 655392 | tf_op jit(solution)/shard_map/ppermute | solution.py:18
  140.0 2.3 %reshape_reshape.29 = f32[640,4,2,32]{0,3,2,1:T(8,128)} reshape(f32[5,128,256]{1,0,2:T(8,128)} %copy.24) | data formatting | bytes 1310720 | tf_op jit(solution)/shard_map/reshape;reshape | solution.py:33
  142.3 2.5 %copy.23 = f32[5,128,256]{1,0,2:T(8,128)} copy(f32[5,128,256]{1,2,0:T(8,128)} %get-tuple-element.18) | data formatting | bytes 1310720 | tf_op jit(solution)/shard_map/slice | solution.py:61
  152.1 2.7 %collective-permute-done.10 = f32[640,128]{0,1:T(8,128)S(1)} collective-permute-done((f32[640,128]{0,1:T(8,128)S(1)}, f32[640,128]{0,1:T(8,128)S(1)}, u32[]{:S(2)}, u32[]{:S(2)}) %collective-permute-start.10) | collective-permute-done | bytes 327712 | tf_op jit(solution)/shard_map/ppermute | solution.py:26
  154.7 4.0 %collective-permute-done.11 = f32[640,128]{0,1:T(8,128)S(1)} collective-permute-done((f32[640,128]{0,1:T(8,128)S(1)}, f32[640,128]{0,1:T(8,128)S(1)}, u32[]{:S(2)}, u32[]{:S(2)}) %collective-permute-start.11) | collective-permute-done | bytes 327712 | tf_op jit(solution)/shard_map/ppermute | solution.py:26
  162.3 11.1 %collective-permute-start.12 = (f32[640,256]{0,1:T(8,128)}, f32[640,256]{0,1:T(8,128)}, u32[]{:S(2)}, u32[]{:S(2)}) collective-permute-start(f32[640,256]{0,1:T(8,128)} %pad_maximum_fusion.10), channel_id=1, source_target_pairs={{0,1},{1,2},{2,3},{3,4},{4,5},{5,6},{6,7},{8,9},{9,10},{10,11},{11... | collective-permute-start | bytes 1966088 | tf_op jit(solution)/shard_map/ppermute | solution.py:15
  173.5 6.4 %collective-permute-done.13 = f32[640,256]{0,1:T(8,128)} collective-permute-done((f32[640,256]{0,1:T(8,128)}, f32[640,256]{0,1:T(8,128)}, u32[]{:S(2)}, u32[]{:S(2)}) %collective-permute-start.13) | collective-permute-done | bytes 655392 | tf_op jit(solution)/shard_map/ppermute | solution.py:18
  (151 shorter events, 78.1 us)
Async XLA Ops:
  6.4 18.9 %copy-start.22 = (f32[640,128]{0,1:T(8,128)}, f32[640,128]{0,1:T(8,128)S(1)}, u32[]{:S(2)}) copy-start(f32[640,128]{0,1:T(8,128)S(1)} %get-tuple-element.45) | copy-start | bytes 983044
  6.4 18.9 %copy-start.24 = (f32[640,128]{0,1:T(8,128)}, f32[640,128]{0,1:T(8,128)S(1)}, u32[]{:S(2)}) copy-start(f32[640,128]{0,1:T(8,128)S(1)} %get-tuple-element.46) | copy-start | bytes 983044
  7.3 21.4 %collective-permute-start.1 = (f32[640,256]{0,1:T(8,128)}, f32[640,256]{0,1:T(8,128)}, u32[]{:S(2)}, u32[]{:S(2)}) collective-permute-start(f32[640,256]{0,1:T(8,128)} %pad_maximum_fusion.4), channel_id=1, source_target_pairs={{1,0},{2,1},{3,2},{4,3},{5,4},{6,5},{7,6},{9,8},{10,9},{11,10},{12... | collective-permute-start | bytes 1966088 | tf_op jit(solution)/shard_map/ppermute | solution.py:18
  9.3 19.5 %collective-permute-start = (f32[640,256]{0,1:T(8,128)}, f32[640,256]{0,1:T(8,128)}, u32[]{:S(2)}, u32[]{:S(2)}) collective-permute-start(f32[640,256]{0,1:T(8,128)} %pad_maximum_fusion.4), channel_id=1, source_target_pairs={{0,1},{1,2},{2,3},{3,4},{4,5},{5,6},{6,7},{8,9},{9,10},{10,11},{11... | collective-permute-start | bytes 1966088 | tf_op jit(solution)/shard_map/ppermute | solution.py:15
  48.0 19.9 %copy-start.9 = (f32[1,640,128]{1,2,0:T(8,128)S(1)}, f32[1,640,128]{1,2,0:T(8,128)}, u32[]{:S(2)}) copy-start(f32[1,640,128]{1,2,0:T(8,128)} %copy-done.8) | copy-start | bytes 983044
  48.0 19.9 %copy-start.13 = (f32[1,640,128]{1,2,0:T(8,128)S(1)}, f32[1,640,128]{1,2,0:T(8,128)}, u32[]{:S(2)}) copy-start(f32[1,640,128]{1,2,0:T(8,128)} %copy-done.12) | copy-start | bytes 983044
  49.0 9.9 %collective-permute-start.2 = (f32[640,128]{0,1:T(8,128)S(1)}, f32[640,128]{0,1:T(8,128)S(1)}, u32[]{:S(2)}, u32[]{:S(2)}) collective-permute-start(f32[640,128]{0,1:T(8,128)S(1)} %get-tuple-element.32), channel_id=1, source_target_pairs={{0,8},{8,16},{16,24},{1,9},{9,17},{17,25},{2,10},{10,18},{18,26},{... | collective-permute-start | bytes 983048 | tf_op jit(solution)/shard_map/ppermute | solution.py:26
  52.1 15.8 %collective-permute-start.3 = (f32[640,128]{0,1:T(8,128)S(1)}, f32[640,128]{0,1:T(8,128)S(1)}, u32[]{:S(2)}, u32[]{:S(2)}) collective-permute-start(f32[640,128]{0,1:T(8,128)S(1)} %get-tuple-element.33), channel_id=1, source_target_pairs={{8,0},{16,8},{24,16},{9,1},{17,9},{25,17},{10,2},{18,10},{26,18},{... | collective-permute-start | bytes 983048 | tf_op jit(solution)/shard_map/ppermute | solution.py:26
  68.0 13.4 %copy-start.5 = (f32[1,256,9,128]{1,3,2,0:T(8,128)S(1)}, f32[1,256,9,128]{1,3,2,0:T(8,128)}, u32[]{:S(2)}) copy-start(f32[1,256,9,128]{1,3,2,0:T(8,128)} %copy-done.4) | copy-start | bytes 3538948
  68.1 12.1 %collective-permute-start.5 = (f32[640,256]{0,1:T(8,128)S(1)}, f32[640,256]{0,1:T(8,128)S(1)}, u32[]{:S(2)}, u32[]{:S(2)}) collective-permute-start(f32[640,256]{0,1:T(8,128)S(1)} %pad_maximum_fusion.6), channel_id=1, source_target_pairs={{1,0},{2,1},{3,2},{4,3},{5,4},{6,5},{7,6},{9,8},{10,9},{11,10},{12... | collective-permute-start | bytes 1966088 | tf_op jit(solution)/shard_map/ppermute | solution.py:18
  71.2 10.1 %collective-permute-start.4 = (f32[640,256]{0,1:T(8,128)S(1)}, f32[640,256]{0,1:T(8,128)S(1)}, u32[]{:S(2)}, u32[]{:S(2)}) collective-permute-start(f32[640,256]{0,1:T(8,128)S(1)} %pad_maximum_fusion.6), channel_id=1, source_target_pairs={{0,1},{1,2},{2,3},{3,4},{4,5},{5,6},{6,7},{8,9},{9,10},{10,11},{11... | collective-permute-start | bytes 1966088 | tf_op jit(solution)/shard_map/ppermute | solution.py:15
  98.4 13.7 %copy-start.10 = (f32[1,640,128]{1,2,0:T(8,128)S(1)}, f32[1,640,128]{1,2,0:T(8,128)}, u32[]{:S(2)}) copy-start(f32[1,640,128]{1,2,0:T(8,128)} %copy-done.8) | copy-start | bytes 983044
  98.4 13.7 %copy-start.14 = (f32[1,640,128]{1,2,0:T(8,128)S(1)}, f32[1,640,128]{1,2,0:T(8,128)}, u32[]{:S(2)}) copy-start(f32[1,640,128]{1,2,0:T(8,128)} %copy-done.12) | copy-start | bytes 983044
  99.4 7.2 %collective-permute-start.6 = (f32[640,128]{0,1:T(8,128)S(1)}, f32[640,128]{0,1:T(8,128)S(1)}, u32[]{:S(2)}, u32[]{:S(2)}) collective-permute-start(f32[640,128]{0,1:T(8,128)S(1)} %get-tuple-element.30), channel_id=1, source_target_pairs={{0,8},{8,16},{16,24},{1,9},{9,17},{17,25},{2,10},{10,18},{18,26},{... | collective-permute-start | bytes 983048 | tf_op jit(solution)/shard_map/ppermute | solution.py:26
  102.6 9.6 %collective-permute-start.7 = (f32[640,128]{0,1:T(8,128)S(1)}, f32[640,128]{0,1:T(8,128)S(1)}, u32[]{:S(2)}, u32[]{:S(2)}) collective-permute-start(f32[640,128]{0,1:T(8,128)S(1)} %get-tuple-element.31), channel_id=1, source_target_pairs={{8,0},{16,8},{24,16},{9,1},{17,9},{25,17},{10,2},{18,10},{26,18},{... | collective-permute-start | bytes 983048 | tf_op jit(solution)/shard_map/ppermute | solution.py:26
  112.3 19.1 %copy-start.6 = (f32[1,256,9,128]{1,3,2,0:T(8,128)S(1)}, f32[1,256,9,128]{1,3,2,0:T(8,128)}, u32[]{:S(2)}) copy-start(f32[1,256,9,128]{1,3,2,0:T(8,128)} %copy-done.4) | copy-start | bytes 3538948
  112.3 17.8 %collective-permute-start.9 = (f32[640,256]{0,1:T(8,128)S(1)}, f32[640,256]{0,1:T(8,128)S(1)}, u32[]{:S(2)}, u32[]{:S(2)}) collective-permute-start(f32[640,256]{0,1:T(8,128)S(1)} %pad_maximum_fusion.8), channel_id=1, source_target_pairs={{1,0},{2,1},{3,2},{4,3},{5,4},{6,5},{7,6},{9,8},{10,9},{11,10},{12... | collective-permute-start | bytes 1966088 | tf_op jit(solution)/shard_map/ppermute | solution.py:18
  114.4 16.9 %collective-permute-start.8 = (f32[640,256]{0,1:T(8,128)S(1)}, f32[640,256]{0,1:T(8,128)S(1)}, u32[]{:S(2)}, u32[]{:S(2)}) collective-permute-start(f32[640,256]{0,1:T(8,128)S(1)} %pad_maximum_fusion.8), channel_id=1, source_target_pairs={{0,1},{1,2},{2,3},{3,4},{4,5},{5,6},{6,7},{8,9},{9,10},{10,11},{11... | collective-permute-start | bytes 1966088 | tf_op jit(solution)/shard_map/ppermute | solution.py:15
  148.4 10.3 %copy-start.11 = (f32[1,640,128]{1,2,0:T(8,128)S(1)}, f32[1,640,128]{1,2,0:T(8,128)}, u32[]{:S(2)}) copy-start(f32[1,640,128]{1,2,0:T(8,128)} %copy-done.8) | copy-start | bytes 983044
  148.4 10.3 %copy-start.15 = (f32[1,640,128]{1,2,0:T(8,128)S(1)}, f32[1,640,128]{1,2,0:T(8,128)}, u32[]{:S(2)}) copy-start(f32[1,640,128]{1,2,0:T(8,128)} %copy-done.12) | copy-start | bytes 983044
  149.4 5.4 %collective-permute-start.10 = (f32[640,128]{0,1:T(8,128)S(1)}, f32[640,128]{0,1:T(8,128)S(1)}, u32[]{:S(2)}, u32[]{:S(2)}) collective-permute-start(f32[640,128]{0,1:T(8,128)S(1)} %get-tuple-element.28), channel_id=1, source_target_pairs={{0,8},{8,16},{16,24},{1,9},{9,17},{17,25},{2,10},{10,18},{18,26},{... | collective-permute-start | bytes 983048 | tf_op jit(solution)/shard_map/ppermute | solution.py:26
  150.8 7.9 %collective-permute-start.11 = (f32[640,128]{0,1:T(8,128)S(1)}, f32[640,128]{0,1:T(8,128)S(1)}, u32[]{:S(2)}, u32[]{:S(2)}) collective-permute-start(f32[640,128]{0,1:T(8,128)S(1)} %get-tuple-element.29), channel_id=1, source_target_pairs={{8,0},{16,8},{24,16},{9,1},{17,9},{25,17},{10,2},{18,10},{26,18},{... | collective-permute-start | bytes 983048 | tf_op jit(solution)/shard_map/ppermute | solution.py:26
  160.4 19.4 %collective-permute-start.13 = (f32[640,256]{0,1:T(8,128)}, f32[640,256]{0,1:T(8,128)}, u32[]{:S(2)}, u32[]{:S(2)}) collective-permute-start(f32[640,256]{0,1:T(8,128)} %pad_maximum_fusion.10), channel_id=1, source_target_pairs={{1,0},{2,1},{3,2},{4,3},{5,4},{6,5},{7,6},{9,8},{10,9},{11,10},{12... | collective-permute-start | bytes 1966088 | tf_op jit(solution)/shard_map/ppermute | solution.py:18
  162.3 18.7 %collective-permute-start.12 = (f32[640,256]{0,1:T(8,128)}, f32[640,256]{0,1:T(8,128)}, u32[]{:S(2)}, u32[]{:S(2)}) collective-permute-start(f32[640,256]{0,1:T(8,128)} %pad_maximum_fusion.10), channel_id=1, source_target_pairs={{0,1},{1,2},{2,3},{3,4},{4,5},{5,6},{6,7},{8,9},{9,10},{10,11},{11... | collective-permute-start | bytes 1966088 | tf_op jit(solution)/shard_map/ppermute | solution.py:15
  (22 other events, 47.4 us)
where the time goes:
time: 195 us; the launch traced here: 194 us
  local copies, waits for them, and re-layouts  51.9 us (27%)
  waiting for transfers between devices  51.6 us (26%)
  starting transfers between devices  48.7 us (25%)
  matrix products  24.7 us (13%)
  other arithmetic  12.2 us (6%)
  between operations  4.58 us (2%)
    ppermute x6, waiting for transfers between devices, from_behind(): return lax.ppermute(shard, axis, pairs)  29.4 us
    ppermute x4, starting transfers between devices, extended(): lax.ppermute(lax.slice_in_dim(block, block.shape[dim] - width, None, axis...  28.1 us
    dot_general x20, matrix products, propagate(): jnp.dot(arranged[tile_no], window, precision=lax.Precision.HIGHEST, prefe...  24.7 us
    ppermute x4, waiting for transfers between devices, extended(): lax.ppermute(lax.slice_in_dim(block, 0, width, axis=dim), axis, backward)  18.6 us
    unnamed x71, local copies, waits for them, and re-layouts  15.5 us
    ppermute x6, starting transfers between devices, from_behind(): return lax.ppermute(shard, axis, pairs)  11.6 us
    slice x8, local copies, waits for them, and re-layouts, propagate(): real_rows = product[:, :TILE].reshape(tile_count * TILE, col_count)  10.9 us
    ppermute x4, starting transfers between devices, extended(): lax.ppermute(lax.slice_in_dim(block, 0, width, axis=dim), axis, backward)  8.99 us
  transfers between devices with their start and end apart: 14, of which 12 were waited for; matrix products, arithmetic and copies ran while one was open for 6% of the time, Pallas kernels for 0%

commit v1 on v0

v1 whole, which is shorter than its diff:
```python
import functools

import jax
import jax.numpy as jnp
from jax import lax
from jax.experimental import pallas as pl
from jax.experimental.pallas import tpu as pltpu
from jax.sharding import PartitionSpec as P

TILE = 128
CHUNKS = (5,)
VMEM = pltpu.VMEM
LIMIT = 24 * 1024 * 1024


def spec(space):
    return pl.BlockSpec(memory_space=space)


def spans():
    out, at = [], 0
    for count in CHUNKS:
        out.append((at, count))
        at += count
    return out


def f32(*shape):
    return jax.ShapeDtypeStruct(shape, jnp.float32)


def params():
    return pltpu.CompilerParams(vmem_limit_bytes=LIMIT)


def cost(flops, read):
    return pl.CostEstimate(flops=flops, bytes_accessed=read, transcendentals=0)


def down_column(row):
    return jnp.transpose(jnp.broadcast_to(row, (TILE, TILE)))


def split(value):
    high = value.astype(jnp.bfloat16)
    low = (value - high.astype(jnp.float32)).astype(jnp.bfloat16)
    return high, low


def prep_kernel(tiles, shots, sections, assign, refl, up, down, src, *outs):
    info_a, info_b = outs[-2:]
    firsts = outs[:-2]
    depth = lax.axis_index("depth")
    rows = tiles * TILE

    def rows_of(j):
        return pl.ds(j * TILE, TILE)

    @pl.when(depth == 0)
    def _():
        lane = lax.broadcasted_iota(jnp.int32, (8, TILE), 1)
        wanted = jnp.zeros((8, TILE), jnp.int32)
        for b in range(TILE // (2 * shots)):
            for i in range(shots):
                shot = assign[b * shots + i]
                at = b * 2 * shots + i
                wanted = jnp.where(lane == at, shot, wanted)
                wanted = jnp.where(lane == at + shots, shot + TILE // 2, wanted)
        source = lax.broadcasted_iota(jnp.int32, (TILE, TILE), 0)
        pick = (source == jnp.broadcast_to(wanted[0:1], (TILE, TILE))).astype(jnp.float32).astype(jnp.bfloat16)
        for (at, count), first in zip(spans(), firsts):
            for j in range(at, at + count):
                x = src[rows_of(j)]
                high = x.astype(jnp.bfloat16)
                rest = x - high.astype(jnp.float32)
                mid, low = split(rest)
                entering = jnp.dot(low, pick, preferred_element_type=jnp.float32)
                entering += jnp.dot(mid, pick, preferred_element_type=jnp.float32)
                entering += jnp.dot(high, pick, preferred_element_type=jnp.float32)
                r = down_column(refl[0:1, j * TILE : (j + 1) * TILE])
                first[(j - at) * TILE : (j - at + 1) * TILE] = (1.0 + r) * entering - r * up[0, rows_of(j)]

    @pl.when(depth == sections - 1)
    def _():
        for (at, count), first in zip(spans(), firsts):
            for j in range(at, at + count):
                r = down_column(refl[0:1, j * TILE : (j + 1) * TILE])
                first[(j - at) * TILE : (j - at + 1) * TILE] = r * down[0, rows_of(j)]

    def tell(upward, downward):
        for j in range(tiles):
            row = refl[0:1, j * TILE : (j + 1) * TILE]
            r = down_column(row)
            upward[rows_of(j)] = -r * down[0, rows_of(j)]
            downward[rows_of(j)] = r * up[0, rows_of(j)]
            upward[rows + j : rows + j + 1] = -row
            downward[rows + j : rows + j + 1] = row

    @pl.when(lax.rem(depth, 2) == 0)
    def _():
        tell(info_a, info_b)

    @pl.when(lax.rem(depth, 2) == 1)
    def _():
        tell(info_b, info_a)


def pack_kernel(band, shift, tile_in, out):
    j = pl.program_id(0)
    move = shift[0, j]
    for k in range(band):
        high, low = split(tile_in[0, 0, k])
        slot = k + 1 + move
        out[0, slot, :, :TILE] = high
        out[0, slot, :, TILE:] = low
    zero = jnp.zeros(out.shape[2:], jnp.bfloat16)
    out[0, jnp.where(move >= 0, 0, band)] = zero
    out[0, jnp.where(move <= 0, band + 1, 1)] = zero


def doubled(tile):
    high, low = split(tile)
    line = jnp.concatenate([high, low], axis=1)
    return jnp.concatenate([line, line], axis=0)


def folded(product):
    return product[:, :TILE] + product[:, TILE:]


def is_active(step, sections):
    depth = lax.axis_index("depth")
    return (depth == step) | (depth == sections - 1 - step)


def tile_of(chunks, t):
    for (at, count), chunk in zip(spans(), chunks):
        if at <= t < at + count:
            return chunk[(t - at) * TILE : (t - at + 1) * TILE]


def spread(chunks, tiles, mirrored, held):
    for t in range(tiles):
        slot = jnp.where(mirrored, tiles - 1 - t, t)
        held[slot] = doubled(tile_of(chunks, t))


def side_product(packed, held, tiles, band, low_side, jj):
    j = jnp.where(low_side, tiles - 1 - jj, jj)
    lhs, rhs = [], []
    for tt in range(jj + 1):
        slot = jnp.where(low_side, jj - tt, band + 1 + tt - jj)
        lhs.append(packed[j, slot])
        rhs.append(held[tt])
    return j, folded(
        jnp.dot(
            jnp.concatenate(lhs, axis=1),
            jnp.concatenate(rhs, axis=0),
            preferred_element_type=jnp.float32,
        )
    )


def inner_kernel(step, sections, tiles, band, packed, *refs):
    n = len(CHUNKS)
    own, near, total, held_own, held_near = refs[:n], refs[n : 2 * n], *refs[2 * n :]

    @pl.when(is_active(step, sections))
    def _():
        for t in range(tiles):
            held_own[t * 2 * TILE : (t + 1) * 2 * TILE] = doubled(tile_of(own, t))
        low_side = lax.rem(lax.axis_index("lat"), 2) == 1
        spread(near, tiles, low_side, held_near)
        for j in range(tiles):
            lhs = jnp.concatenate([packed[j, tiles - j + t] for t in range(tiles)], axis=1)
            total[j] = folded(jnp.dot(lhs, held_own[...], preferred_element_type=jnp.float32))
        for jj in range(tiles):
            j, more = side_product(packed, held_near, tiles, band, low_side, jj)
            total[j] = total[j] + more


def outer_kernel(step, sections, lats, tiles, band, shots, last, chained, packed, total, info, *refs):
    n = len(CHUNKS)
    far, refs = refs[:n], refs[n:]
    if chained:
        refs = refs[2:]
    result_down, result_up, refs = refs[0], refs[1], refs[2:]
    nexts, refs = ((), refs) if last else (refs[:n], refs[n:])
    held, leaving, sems = refs
    rows = tiles * TILE
    lat = lax.axis_index("lat")
    depth = lax.axis_index("depth")
    low_side = lax.rem(lat, 2) == 0

    @pl.when(is_active(step, sections))
    def _():
        lane = lax.broadcasted_iota(jnp.int32, (TILE, TILE), 1)
        real_lane = lax.rem(lane, 2 * shots) < shots

        def finish(j, product):
            by_imag = product[TILE:]
            ahead = pltpu.roll(by_imag, TILE - shots, 1)
            behind = pltpu.roll(by_imag, shots, 1)
            leaving[j] = product[:TILE] + jnp.where(real_lane, -ahead, behind)

        has_far = (lat > 0) & (lat < lats - 1)

        @pl.when(has_far)
        def _():
            spread(far, tiles, low_side, held)
            for jj in range(tiles):
                j, more = side_product(packed, held, tiles, band, low_side, jj)
                finish(j, total[j] + more)

        @pl.when(jnp.logical_not(has_far))
        def _():
            for j in range(tiles):
                finish(j, total[j])

        def leave(result):
            copy = pltpu.make_async_copy(leaving, result.at[0], sems)
            copy.start()
            for (at, count), nxt in zip(spans(), nexts):
                for j in range(at, at + count):
                    rho = down_column(info[rows + j : rows + j + 1])
                    nxt[(j - at) * TILE : (j - at + 1) * TILE] = (1.0 + rho) * leaving[j] - info[
                        j * TILE : (j + 1) * TILE
                    ]
            copy.wait()

        @pl.when(depth == step)
        def _():
            leave(result_down)

        @pl.when(depth != step)
        def _():
            leave(result_up)


def shards(sections, lats, operator, band_shift, reflectivity, up_stored, down_stored, sources, assignment):
    tiles, band = operator.shape[1], operator.shape[2]
    lateral, columns = sources.shape
    shots = columns // 4
    rows = tiles * TILE
    info_rows = rows + 8
    if sections % 2 or lats % 2 or tiles != band // 2 + 1 or tiles != sum(CHUNKS):
        raise ValueError("unsupported sizes")

    def pairs(partner):
        out = []
        for d in range(sections):
            for l in range(lats):
                e, m = partner(d, l)
                out.append((d * lats + l, e * lats + m))
        return out

    def near_of(d, l):
        return d, l ^ 1

    def far_of(d, l):
        m = l + 1 if l % 2 else l - 1
        return (d, m) if 0 <= m < lats else (d ^ 1, l)

    def across(lower):
        def partner(d, l):
            for low in lower:
                if d == low:
                    return low + 1, l
                if d == low + 1:
                    return low, l
            return near_of(d, l)

        return partner

    def move(x, partner):
        return lax.ppermute(x, ("depth", "lat"), pairs(partner))

    chunk_rows = [count * TILE for count in CHUNKS]
    prep = pl.pallas_call(
        functools.partial(prep_kernel, tiles, shots, sections),
        out_shape=[f32(c, columns) for c in chunk_rows] + [f32(info_rows, columns)] * 2,
        in_specs=[spec(pltpu.SMEM)] + [spec(VMEM)] * 4,
        out_specs=[spec(VMEM)] * (len(CHUNKS) + 2),
        compiler_params=params(),
        cost_estimate=cost(10**7, 5 * rows * columns * 4),
        name="prep",
    )
    *field, info_a, info_b = prep(assignment, reflectivity, up_stored, down_stored, sources)

    def halo(field):
        far = [move(f, far_of) for f in field]
        near = [move(f, near_of) for f in field]
        return near, far

    near, far = halo(field)
    info_a = move(info_a, across(range(0, sections, 2)))
    packed = pl.pallas_call(
        functools.partial(pack_kernel, band),
        out_shape=jax.ShapeDtypeStruct((tiles, band + 2, 2 * TILE, 2 * TILE), jnp.bfloat16),
        grid=(tiles,),
        in_specs=[
            spec(pltpu.SMEM),
            pl.BlockSpec((1, 1, band, 2 * TILE, TILE), lambda j: (0, j, 0, 0, 0)),
        ],
        out_specs=pl.BlockSpec((1, band + 2, 2 * TILE, 2 * TILE), lambda j: (j, 0, 0, 0)),
        compiler_params=params(),
        cost_estimate=cost(10**7, 2 * operator.size * 4),
        name="pack",
    )(band_shift, operator)
    info_b = move(info_b, across(range(1, sections - 1, 2)))

    results = None
    for step in range(sections):
        last = step == sections - 1
        total = pl.pallas_call(
            functools.partial(inner_kernel, step, sections, tiles, band),
            out_shape=f32(tiles, 2 * TILE, columns),
            in_specs=[spec(VMEM)] * (1 + 2 * len(CHUNKS)),
            out_specs=spec(VMEM),
            scratch_shapes=[
                VMEM((tiles * 2 * TILE, 2 * TILE), jnp.bfloat16),
                VMEM((tiles, 2 * TILE, 2 * TILE), jnp.bfloat16),
            ],
            compiler_params=params(),
            cost_estimate=cost(2 * 40 * 256**3, 8 * 2**20),
            name=f"inner_{step}",
        )(packed, *field, *near)
        n = len(CHUNKS)
        chained = results is not None
        result_shape = f32(1, tiles, TILE, columns)
        outs = pl.pallas_call(
            functools.partial(outer_kernel, step, sections, lats, tiles, band, shots, last, chained),
            out_shape=[result_shape] * 2 + ([] if last else [f32(c, columns) for c in chunk_rows]),
            in_specs=[spec(VMEM)] * (3 + n) + [spec(pl.ANY)] * (2 if chained else 0),
            out_specs=[spec(pl.ANY)] * 2 + [spec(VMEM)] * (0 if last else n),
            scratch_shapes=[
                VMEM((tiles, 2 * TILE, 2 * TILE), jnp.bfloat16),
                VMEM((tiles, TILE, columns), jnp.float32),
                pltpu.SemaphoreType.DMA(()),
            ],
            input_output_aliases={3 + n: 0, 4 + n: 1} if chained else {},
            compiler_params=params(),
            cost_estimate=cost(2 * 15 * 256**3, 4 * 2**20),
            name=f"outer_{step}",
        )(packed, total, info_a if step % 2 == 0 else info_b, *far, *(results or ()))
        results = outs[:2]
        if not last:
            lower = sorted({step, sections - 2 - step})
            field = [move(f, across(lower)) for f in outs[2:]]
            near, far = halo(field)
    return tuple(r.reshape(1, lateral, columns) for r in results)


def solution(mesh):
    return jax.shard_map(
        functools.partial(shards, mesh.shape["depth"], mesh.shape["lat"]),
        mesh=mesh,
        in_specs=(
            P("depth", "lat", None, None, None),
            P("depth", "lat"),
            P("depth", "lat"),
            P("depth", "lat", None),
            P("depth", "lat", None),
            P("lat", None),
            P(),
        ),
        out_specs=(P("depth", "lat", None), P("depth", "lat", None)),
        check_vma=False,
    )
```

time: 195 us -> 78.5 us (0.40)
  local copies, waits for them, and re-layouts: 51.9 us -> 7.57 us
  matrix products: 24.7 us -> 0 us
  starting transfers between devices: 48.7 us -> 28.6 us
  waiting for transfers between devices: 51.6 us -> 31.9 us
  other arithmetic: 12.2 us -> 0 us
  Pallas kernels: 0 us -> 9.4 us
  between operations: 4.58 us -> 0.74 us
    dot_general x20 -> x0, matrix products: 24.7 us -> none  [propagate(): jnp.dot(arranged[tile_no], window, precision=lax.Precision.HIGHEST, prefe...]
    slice x18 -> x0, local copies, waits for them, and re-layouts: 21.1 us -> none  [the longest x8 10.9 us: propagate(): real_rows = product[:, :TILE].reshape(tile_count * TILE, col_count)]
    ppermute x14 -> x13, starting transfers between devices: 48.7 us -> 28.6 us  [move(): return lax.ppermute(x, ('depth', 'lat'), pairs(partner))]
    ppermute x14 -> x13, waiting for transfers between devices: 51.6 us -> 31.9 us  [move(): return lax.ppermute(x, ('depth', 'lat'), pairs(partner))]
    another operation x8 -> x0, local copies, waits for them, and re-layouts: 13.9 us -> none  [the longest x4 6.94 us: combine_parts(): real_terms = real_rows.reshape(shape_in)]
    pallas_call x0 -> x10, Pallas kernels: none -> 9.4 us  [the longest x4 3.33 us: shards(): pl.pallas_call(functools.partial(inner_kernel, step, sections, tiles, ban...]
    unnamed x71 -> x14, local copies, waits for them, and re-layouts: 15.5 us -> 7.57 us
    concatenate x8 -> x0, other arithmetic: 6.01 us -> none  [the longest x4 4.09 us: extended(): block = jnp.concatenate([low, block, high], axis=dim)]
  transfers between devices with their start and end apart: 14 -> 13, of which waited for: 12 -> 9; matrix products, arithmetic and copies ran while one was open for 6% -> 0% of each run, Pallas kernels for 0% -> 6%
where the time goes in v1:
time: 78.5 us; the launch traced here: 78.2 us
  waiting for transfers between devices  31.9 us (41%)
  starting transfers between devices  28.6 us (36%)
  Pallas kernels  9.4 us (12%)
  local copies, waits for them, and re-layouts  7.57 us (10%)
    ppermute x13, waiting for transfers between devices, move(): return lax.ppermute(x, ('depth', 'lat'), pairs(partner))  31.9 us
    ppermute x13, starting transfers between devices, move(): return lax.ppermute(x, ('depth', 'lat'), pairs(partner))  28.6 us
    unnamed x14, local copies, waits for them, and re-layouts  7.57 us
    pallas_call x4, Pallas kernels, shards(): pl.pallas_call(functools.partial(inner_kernel, step, sections, tiles, ban...  3.33 us
    pallas_call x4, Pallas kernels, shards(): pl.pallas_call(functools.partial(outer_kernel, step, sections, lats, tile...  3.27 us
    pallas_call x1, Pallas kernels, shards(): pl.pallas_call(functools.partial(pack_kernel, band), out_shape=jax.ShapeD...  1.71 us
  transfers between devices with their start and end apart: 13, of which 9 were waited for; matrix products, arithmetic and copies ran while one was open for 0% of the time, Pallas kernels for 6%

profile of v1, /device:TPU:1, one launch (start us, length us, event | category | flops | bytes accessed | tf_op | source)
XLA Modules:
  0.0 78.2 jit_solution(11769374080118383204)
XLA Ops:
  0.6 1.0 %copy-done.1 = f32[1,640,128]{2,1,0:T(8,128)S(1)} copy-done((f32[1,640,128]{2,1,0:T(8,128)S(1)}, f32[1,640,128]{2,1,0:T(8,128)}, u32[]{:S(2)}) %copy-start.1) | copy-done | bytes 327704
  1.6 1.0 %copy-done.2 = f32[1,640,128]{2,1,0:T(8,128)S(1)} copy-done((f32[1,640,128]{2,1,0:T(8,128)S(1)}, f32[1,640,128]{2,1,0:T(8,128)}, u32[]{:S(2)}) %copy-start.2) | copy-done | bytes 327704
  2.6 1.0 %copy-done.3 = f32[640,128]{1,0:T(8,128)S(1)} copy-done((f32[640,128]{1,0:T(8,128)S(1)}, f32[640,128]{1,0:T(8,128)}, u32[]{:S(2)}) %copy-start.3) | copy-done | bytes 327704
  4.9 1.1 %prep.1 = (f32[640,128]{1,0:T(8,128)S(1)}, f32[648,128]{1,0:T(8,128)S(1)}, f32[648,128]{1,0:T(8,128)S(1)}) custom-call(s32[64]{0:T(128)S(1)} %copy-done.5, f32[1,640]{1,0:T(1,128)S(1)} %copy-done.4, f32[1,640,128]{2,1,0:T(8,128)S(1)} %copy-done.1, f32[1,640,128]{2,1,0:T(8,128)S(1)} %copy-done.2, f32[640,128]{1,0:T(8,128)S(1)} %copy-done.3), custom_call_target="tpu_custom_call" | custom-call | flops 10000000 | bytes 1638400 | tf_op jit(solution)/shard_map/prep/pallas_call | solution.py:288
  6.1 2.3 %collective-permute-start.1 = (f32[648,128]{1,0:T(8,128)S(1)}, f32[648,128]{1,0:T(8,128)S(1)}, u32[]{:S(2)}, u32[]{:S(2)}) collective-permute-start(f32[648,128]{1,0:T(8,128)S(1)} %get-tuple-element.17), channel_id=1, source_target_pairs={{0,8},{1,9},{2,10},{3,11},{4,12},{5,13},{6,14},{7,15},{8,0},{9,1},... | collective-permute-start | bytes 995336 | tf_op jit(solution)/shard_map/ppermute | solution.py:276
  8.4 1.5 %collective-permute-start.2 = (f32[640,128]{1,0:T(8,128)S(1)}, f32[640,128]{1,0:T(8,128)S(1)}, u32[]{:S(2)}, u32[]{:S(2)}) collective-permute-start(f32[640,128]{1,0:T(8,128)S(1)} %get-tuple-element.16.refs_0_), channel_id=1, source_target_pairs={{0,8},{1,2},{2,1},{3,4},{4,3},{5,6},{6,5},{7,15},{8,0},{9,10},{10,... | collective-permute-start | bytes 983048 | tf_op jit(solution)/shard_map/ppermute | solution.py:276
  9.9 2.7 %copy-done = f32[1,5,9,256,128]{4,3,2,1,0:T(8,128)S(1)} copy-done((f32[1,5,9,256,128]{4,3,2,1,0:T(8,128)S(1)}, f32[1,5,9,256,128]{4,3,2,1,0:T(8,128)}, u32[]{:S(2)}) %copy-start) | copy-done | bytes 5898264
  13.3 1.7 %pack.1.packed = bf16[5,11,256,256]{3,2,1,0:T(8,128)(2,1)S(1)} custom-call(s32[1,5]{1,0:T(1,128)S(1)} %copy-done.6, f32[1,5,9,256,128]{4,3,2,1,0:T(8,128)S(1)} %copy-done), custom_call_target="tpu_custom_call" | custom-call | flops 10000000 | bytes 11796480 | tf_op jit(solution)/shard_map/pack/pallas_call | solution.py:297
  15.0 1.7 %inner_0.1.total = f32[5,256,128]{2,1,0:T(8,128)S(1)} custom-call(bf16[5,11,256,256]{3,2,1,0:T(8,128)(2,1)S(1)} %pack.1.packed, f32[640,128]{1,0:T(8,128)S(1)} %get-tuple-element.16.refs_0_, f32[640,128]{1,0:T(8,128)S(1)} %collective-permute-done.refs_1_), custom_call_target="tpu_custom_call" | custom-call | flops 1342177280 | bytes 8388608 | tf_op jit(solution)/shard_map/inner_0/pallas_call | solution.py:315
  16.7 1.6 %outer_0.1 = (f32[1,5,128,128]{3,2,1,0:T(8,128)}, f32[1,5,128,128]{3,2,1,0:T(8,128)}, f32[640,128]{1,0:T(8,128)S(1)}) custom-call(bf16[5,11,256,256]{3,2,1,0:T(8,128)(2,1)S(1)} %pack.1.packed, f32[5,256,128]{2,1,0:T(8,128)S(1)} %inner_0.1.total, f32[648,128]{1,0:T(8,128)S(1)} %collective-permute-done.1.info, f32[640,128]{1,0:T(8,128)S(1)} %collective-permute-done.2.refs_0_), custom_call_target="tpu_custom_call" | custom-call | flops 503316480 | bytes 4194304 | tf_op jit(solution)/shard_map/outer_0/pallas_call | solution.py:331
  18.4 5.9 %collective-permute-done.3.refs_0_ = f32[640,128]{1,0:T(8,128)S(1)} collective-permute-done((f32[640,128]{1,0:T(8,128)S(1)}, f32[640,128]{1,0:T(8,128)S(1)}, u32[]{:S(2)}, u32[]{:S(2)}) %collective-permute-start.3) | collective-permute-done | bytes 327712 | tf_op jit(solution)/shard_map/ppermute | solution.py:276
  24.3 4.5 %collective-permute-start.4 = (f32[640,128]{1,0:T(8,128)S(1)}, f32[640,128]{1,0:T(8,128)S(1)}, u32[]{:S(2)}, u32[]{:S(2)}) collective-permute-start(f32[640,128]{1,0:T(8,128)S(1)} %collective-permute-done.3.refs_0_), channel_id=1, source_target_pairs={{0,1},{1,0},{2,3},{3,2},{4,5},{5,4},{6,7},{7,6},{8,9},{9,8},{10,11... | collective-permute-start | bytes 983048 | tf_op jit(solution)/shard_map/ppermute | solution.py:276
  28.8 1.5 %collective-permute-start.6 = (f32[640,128]{1,0:T(8,128)S(1)}, f32[640,128]{1,0:T(8,128)S(1)}, u32[]{:S(2)}, u32[]{:S(2)}) collective-permute-start(f32[640,128]{1,0:T(8,128)S(1)} %collective-permute-done.3.refs_0_), channel_id=1, source_target_pairs={{0,8},{1,2},{2,1},{3,4},{4,3},{5,6},{6,5},{7,15},{8,0},{9,10},{10,... | collective-permute-start | bytes 983048 | tf_op jit(solution)/shard_map/ppermute | solution.py:276
  30.5 4.8 %collective-permute-done.6.refs_0_ = f32[640,128]{1,0:T(8,128)S(1)} collective-permute-done((f32[640,128]{1,0:T(8,128)S(1)}, f32[640,128]{1,0:T(8,128)S(1)}, u32[]{:S(2)}, u32[]{:S(2)}) %collective-permute-start.6) | collective-permute-done | bytes 327712 | tf_op jit(solution)/shard_map/ppermute | solution.py:276
  35.3 8.1 %collective-permute-start.7 = (f32[640,128]{1,0:T(8,128)S(1)}, f32[640,128]{1,0:T(8,128)S(1)}, u32[]{:S(2)}, u32[]{:S(2)}) collective-permute-start(f32[640,128]{1,0:T(8,128)S(1)} %get-tuple-element.22), channel_id=1, source_target_pairs={{0,1},{1,0},{2,3},{3,2},{4,5},{5,4},{6,7},{7,6},{8,16},{9,17},{10,... | collective-permute-start | bytes 983048 | tf_op jit(solution)/shard_map/ppermute | solution.py:276
  43.4 1.3 %collective-permute-done.7.refs_0_ = f32[640,128]{1,0:T(8,128)S(1)} collective-permute-done((f32[640,128]{1,0:T(8,128)S(1)}, f32[640,128]{1,0:T(8,128)S(1)}, u32[]{:S(2)}, u32[]{:S(2)}) %collective-permute-start.7) | collective-permute-done | bytes 327712 | tf_op jit(solution)/shard_map/ppermute | solution.py:276
  45.1 1.3 %collective-permute-done.8.refs_1_ = f32[640,128]{1,0:T(8,128)S(1)} collective-permute-done((f32[640,128]{1,0:T(8,128)S(1)}, f32[640,128]{1,0:T(8,128)S(1)}, u32[]{:S(2)}, u32[]{:S(2)}) %collective-permute-start.8) | collective-permute-done | bytes 327712 | tf_op jit(solution)/shard_map/ppermute | solution.py:276
  46.3 5.2 %collective-permute-done.9.refs_0_ = f32[640,128]{1,0:T(8,128)S(1)} collective-permute-done((f32[640,128]{1,0:T(8,128)S(1)}, f32[640,128]{1,0:T(8,128)S(1)}, u32[]{:S(2)}, u32[]{:S(2)}) %collective-permute-start.9) | collective-permute-done | bytes 327712 | tf_op jit(solution)/shard_map/ppermute | solution.py:276
  51.6 9.7 %collective-permute-start.10 = (f32[640,128]{1,0:T(8,128)S(1)}, f32[640,128]{1,0:T(8,128)S(1)}, u32[]{:S(2)}, u32[]{:S(2)}) collective-permute-start(f32[640,128]{1,0:T(8,128)S(1)} %get-tuple-element.25), channel_id=1, source_target_pairs={{0,8},{1,9},{2,10},{3,11},{4,12},{5,13},{6,14},{7,15},{8,0},{9,1},... | collective-permute-start | bytes 983048 | tf_op jit(solution)/shard_map/ppermute | solution.py:276
  61.2 8.1 %collective-permute-done.10.refs_0_ = f32[640,128]{1,0:T(8,128)S(1)} collective-permute-done((f32[640,128]{1,0:T(8,128)S(1)}, f32[640,128]{1,0:T(8,128)S(1)}, u32[]{:S(2)}, u32[]{:S(2)}) %collective-permute-start.10) | collective-permute-done | bytes 327712 | tf_op jit(solution)/shard_map/ppermute | solution.py:276
  69.8 1.3 %collective-permute-done.11.refs_1_ = f32[640,128]{1,0:T(8,128)S(1)} collective-permute-done((f32[640,128]{1,0:T(8,128)S(1)}, f32[640,128]{1,0:T(8,128)S(1)}, u32[]{:S(2)}, u32[]{:S(2)}) %collective-permute-start.11) | collective-permute-done | bytes 327712 | tf_op jit(solution)/shard_map/ppermute | solution.py:276
  71.0 1.7 %inner_3.1.total = f32[5,256,128]{2,1,0:T(8,128)S(1)} custom-call(bf16[5,11,256,256]{3,2,1,0:T(8,128)(2,1)S(1)} %pack.1.packed, f32[640,128]{1,0:T(8,128)S(1)} %collective-permute-done.10.refs_0_, f32[640,128]{1,0:T(8,128)S(1)} %collective-permute-done.11.refs_1_), custom_call_target="tpu_custom_call" | custom-call | flops 1342177280 | bytes 8388608 | tf_op jit(solution)/shard_map/inner_3/pallas_call | solution.py:315
  72.7 3.9 %collective-permute-done.12.refs_0_ = f32[640,128]{1,0:T(8,128)S(1)} collective-permute-done((f32[640,128]{1,0:T(8,128)S(1)}, f32[640,128]{1,0:T(8,128)S(1)}, u32[]{:S(2)}, u32[]{:S(2)}) %collective-permute-start.12) | collective-permute-done | bytes 327712 | tf_op jit(solution)/shard_map/ppermute | solution.py:276
  76.6 1.6 %outer_3.1 = (f32[1,5,128,128]{3,2,1,0:T(8,128)}, f32[1,5,128,128]{3,2,1,0:T(8,128)}) custom-call(bf16[5,11,256,256]{3,2,1,0:T(8,128)(2,1)S(1)} %pack.1.packed, f32[5,256,128]{2,1,0:T(8,128)S(1)} %inner_3.1.total, f32[648,128]{1,0:T(8,128)S(1)} %collective-permute-done.5.info, ...), custom_call_target="tpu_custom_call", output_to_operand_aliasing={{0}: (4, {}), {1}: (5, {})} | custom-call | flops 503316480 | bytes 4194304 | tf_op jit(solution)/shard_map/outer_3/pallas_call | solution.py:331
  (26 shorter events, 3.1 us)
Async XLA Ops:
  0.6 1.0 %copy-start.1 = (f32[1,640,128]{2,1,0:T(8,128)S(1)}, f32[1,640,128]{2,1,0:T(8,128)}, u32[]{:S(2)}) copy-start(f32[1,640,128]{2,1,0:T(8,128)} %up.1) | copy-start | bytes 983044
  1.6 1.0 %copy-start.2 = (f32[1,640,128]{2,1,0:T(8,128)S(1)}, f32[1,640,128]{2,1,0:T(8,128)}, u32[]{:S(2)}) copy-start(f32[1,640,128]{2,1,0:T(8,128)} %down.1) | copy-start | bytes 983044
  2.6 1.0 %copy-start.3 = (f32[640,128]{1,0:T(8,128)S(1)}, f32[640,128]{1,0:T(8,128)}, u32[]{:S(2)}) copy-start(f32[640,128]{1,0:T(8,128)} %src.1) | copy-start | bytes 983044
  3.6 0.7 copy-start.4
  4.2 0.7 copy-start.5
  6.0 9.0 %collective-permute-start = (f32[640,128]{1,0:T(8,128)S(1)}, f32[640,128]{1,0:T(8,128)S(1)}, u32[]{:S(2)}, u32[]{:S(2)}) collective-permute-start(f32[640,128]{1,0:T(8,128)S(1)} %get-tuple-element.16.refs_0_), channel_id=1, source_target_pairs={{0,1},{1,0},{2,3},{3,2},{4,5},{5,4},{6,7},{7,6},{8,9},{9,8},{10,11... | collective-permute-start | bytes 983048 | tf_op jit(solution)/shard_map/ppermute | solution.py:276
  6.1 10.6 %collective-permute-start.1 = (f32[648,128]{1,0:T(8,128)S(1)}, f32[648,128]{1,0:T(8,128)S(1)}, u32[]{:S(2)}, u32[]{:S(2)}) collective-permute-start(f32[648,128]{1,0:T(8,128)S(1)} %get-tuple-element.17), channel_id=1, source_target_pairs={{0,8},{1,9},{2,10},{3,11},{4,12},{5,13},{6,14},{7,15},{8,0},{9,1},... | collective-permute-start | bytes 995336 | tf_op jit(solution)/shard_map/ppermute | solution.py:276
  8.4 8.3 %collective-permute-start.2 = (f32[640,128]{1,0:T(8,128)S(1)}, f32[640,128]{1,0:T(8,128)S(1)}, u32[]{:S(2)}, u32[]{:S(2)}) collective-permute-start(f32[640,128]{1,0:T(8,128)S(1)} %get-tuple-element.16.refs_0_), channel_id=1, source_target_pairs={{0,8},{1,2},{2,1},{3,4},{4,3},{5,6},{6,5},{7,15},{8,0},{9,10},{10,... | collective-permute-start | bytes 983048 | tf_op jit(solution)/shard_map/ppermute | solution.py:276
  9.9 2.7 %copy-start = (f32[1,5,9,256,128]{4,3,2,1,0:T(8,128)S(1)}, f32[1,5,9,256,128]{4,3,2,1,0:T(8,128)}, u32[]{:S(2)}) copy-start(f32[1,5,9,256,128]{4,3,2,1,0:T(8,128)} %tile_in.1) | copy-start | bytes 17694724
  12.6 0.7 copy-start.6
  18.3 6.0 %collective-permute-start.3 = (f32[640,128]{1,0:T(8,128)S(1)}, f32[640,128]{1,0:T(8,128)S(1)}, u32[]{:S(2)}, u32[]{:S(2)}) collective-permute-start(f32[640,128]{1,0:T(8,128)S(1)} %get-tuple-element.18), channel_id=1, source_target_pairs={{0,8},{1,9},{2,10},{3,11},{4,12},{5,13},{6,14},{7,15},{8,0},{9,1},... | collective-permute-start | bytes 983048 | tf_op jit(solution)/shard_map/ppermute | solution.py:276
  24.3 6.0 %collective-permute-start.4 = (f32[640,128]{1,0:T(8,128)S(1)}, f32[640,128]{1,0:T(8,128)S(1)}, u32[]{:S(2)}, u32[]{:S(2)}) collective-permute-start(f32[640,128]{1,0:T(8,128)S(1)} %collective-permute-done.3.refs_0_), channel_id=1, source_target_pairs={{0,1},{1,0},{2,3},{3,2},{4,5},{5,4},{6,7},{7,6},{8,9},{9,8},{10,11... | collective-permute-start | bytes 983048 | tf_op jit(solution)/shard_map/ppermute | solution.py:276
  28.8 1.7 %collective-permute-start.5 = (f32[648,128]{1,0:T(8,128)S(1)}, f32[648,128]{1,0:T(8,128)S(1)}, u32[]{:S(2)}, u32[]{:S(2)}) collective-permute-start(f32[648,128]{1,0:T(8,128)S(1)} %get-tuple-element.19), channel_id=1, source_target_pairs={{0,1},{1,0},{2,3},{3,2},{4,5},{5,4},{6,7},{7,6},{8,16},{9,17},{10,... | collective-permute-start | bytes 995336 | tf_op jit(solution)/shard_map/ppermute | solution.py:276
  28.8 6.5 %collective-permute-start.6 = (f32[640,128]{1,0:T(8,128)S(1)}, f32[640,128]{1,0:T(8,128)S(1)}, u32[]{:S(2)}, u32[]{:S(2)}) collective-permute-start(f32[640,128]{1,0:T(8,128)S(1)} %collective-permute-done.3.refs_0_), channel_id=1, source_target_pairs={{0,8},{1,2},{2,1},{3,4},{4,3},{5,6},{6,5},{7,15},{8,0},{9,10},{10,... | collective-permute-start | bytes 983048 | tf_op jit(solution)/shard_map/ppermute | solution.py:276
  35.3 9.4 %collective-permute-start.7 = (f32[640,128]{1,0:T(8,128)S(1)}, f32[640,128]{1,0:T(8,128)S(1)}, u32[]{:S(2)}, u32[]{:S(2)}) collective-permute-start(f32[640,128]{1,0:T(8,128)S(1)} %get-tuple-element.22), channel_id=1, source_target_pairs={{0,1},{1,0},{2,3},{3,2},{4,5},{5,4},{6,7},{7,6},{8,16},{9,17},{10,... | collective-permute-start | bytes 983048 | tf_op jit(solution)/shard_map/ppermute | solution.py:276
  44.7 1.6 %collective-permute-start.8 = (f32[640,128]{1,0:T(8,128)S(1)}, f32[640,128]{1,0:T(8,128)S(1)}, u32[]{:S(2)}, u32[]{:S(2)}) collective-permute-start(f32[640,128]{1,0:T(8,128)S(1)} %collective-permute-done.7.refs_0_), channel_id=1, source_target_pairs={{0,1},{1,0},{2,3},{3,2},{4,5},{5,4},{6,7},{7,6},{8,9},{9,8},{10,11... | collective-permute-start | bytes 983048 | tf_op jit(solution)/shard_map/ppermute | solution.py:276
  45.1 6.5 %collective-permute-start.9 = (f32[640,128]{1,0:T(8,128)S(1)}, f32[640,128]{1,0:T(8,128)S(1)}, u32[]{:S(2)}, u32[]{:S(2)}) collective-permute-start(f32[640,128]{1,0:T(8,128)S(1)} %collective-permute-done.7.refs_0_), channel_id=1, source_target_pairs={{0,8},{1,2},{2,1},{3,4},{4,3},{5,6},{6,5},{7,15},{8,0},{9,10},{10,... | collective-permute-start | bytes 983048 | tf_op jit(solution)/shard_map/ppermute | solution.py:276
  51.6 17.8 %collective-permute-start.10 = (f32[640,128]{1,0:T(8,128)S(1)}, f32[640,128]{1,0:T(8,128)S(1)}, u32[]{:S(2)}, u32[]{:S(2)}) collective-permute-start(f32[640,128]{1,0:T(8,128)S(1)} %get-tuple-element.25), channel_id=1, source_target_pairs={{0,8},{1,9},{2,10},{3,11},{4,12},{5,13},{6,14},{7,15},{8,0},{9,1},... | collective-permute-start | bytes 983048 | tf_op jit(solution)/shard_map/ppermute | solution.py:276
  69.4 1.7 %collective-permute-start.11 = (f32[640,128]{1,0:T(8,128)S(1)}, f32[640,128]{1,0:T(8,128)S(1)}, u32[]{:S(2)}, u32[]{:S(2)}) collective-permute-start(f32[640,128]{1,0:T(8,128)S(1)} %collective-permute-done.10.refs_0_), channel_id=1, source_target_pairs={{0,1},{1,0},{2,3},{3,2},{4,5},{5,4},{6,7},{7,6},{8,9},{9,8},{10,11... | collective-permute-start | bytes 983048 | tf_op jit(solution)/shard_map/ppermute | solution.py:276
  69.8 6.8 %collective-permute-start.12 = (f32[640,128]{1,0:T(8,128)S(1)}, f32[640,128]{1,0:T(8,128)S(1)}, u32[]{:S(2)}, u32[]{:S(2)}) collective-permute-start(f32[640,128]{1,0:T(8,128)S(1)} %collective-permute-done.10.refs_0_), channel_id=1, source_target_pairs={{0,8},{1,2},{2,1},{3,4},{4,3},{5,6},{6,5},{7,15},{8,0},{9,10},{10,... | collective-permute-start | bytes 983048 | tf_op jit(solution)/shard_map/ppermute | solution.py:276

commit v2 on v1

v2 whole, which is shorter than its diff:
```python
import functools

import jax
import jax.numpy as jnp
from jax import lax
from jax.experimental import pallas as pl
from jax.experimental.pallas import tpu as pltpu
from jax.sharding import PartitionSpec as P

TILE = 128
VMEM = pltpu.VMEM
LIMIT = 16 * 2**20


def spec(space):
    return pl.BlockSpec(memory_space=space)


def f32(*shape):
    return jax.ShapeDtypeStruct(shape, jnp.float32)


def params(limit=LIMIT):
    return pltpu.CompilerParams(vmem_limit_bytes=limit)


def cost(flops, read):
    return pl.CostEstimate(flops=flops, bytes_accessed=read, transcendentals=0)


def rows_of(t):
    return slice(t * TILE, (t + 1) * TILE)


def down_column(row):
    return jnp.transpose(jnp.broadcast_to(row, (TILE, TILE)))


def split(value):
    high = value.astype(jnp.bfloat16)
    low = (value - high.astype(jnp.float32)).astype(jnp.bfloat16)
    return high, low


def prep_kernel(tiles, shots, sections, assign_at, refl_at, up_at, down_at, src_at, first, second, assign, refl, up, down, src, sems):
    depth = lax.axis_index("depth")
    loads = [
        pltpu.make_async_copy(assign_at, assign, sems.at[0]),
        pltpu.make_async_copy(refl_at, refl, sems.at[1]),
        pltpu.make_async_copy(up_at, up, sems.at[2]),
        pltpu.make_async_copy(down_at, down, sems.at[3]),
        pltpu.make_async_copy(src_at, src, sems.at[4]),
    ]
    for load in loads:
        load.start()
    for load in loads:
        load.wait()
    descends = depth < sections // 2

    def write(of_up, of_down):
        for j in range(tiles):
            row = refl[0:1, rows_of(j)]
            r = down_column(row)
            of_up[rows_of(j)] = -(r * up[0, rows_of(j)])
            of_down[rows_of(j)] = r * down[0, rows_of(j)]
            first[tiles * TILE + j : tiles * TILE + j + 1] = row

    @pl.when(descends)
    def _():
        write(first, second)

    @pl.when(jnp.logical_not(descends))
    def _():
        write(second, first)

    @pl.when(depth == 0)
    def _():
        lane = lax.broadcasted_iota(jnp.int32, (8, TILE), 1)
        wanted = jnp.zeros((8, TILE), jnp.int32)
        for b in range(TILE // (2 * shots)):
            for i in range(shots):
                shot = assign[b * shots + i]
                at = b * 2 * shots + i
                wanted = jnp.where(lane == at, shot, wanted)
                wanted = jnp.where(lane == at + shots, shot + TILE // 2, wanted)
        source = lax.broadcasted_iota(jnp.int32, (TILE, TILE), 0)
        pick = (source == jnp.broadcast_to(wanted[0:1], (TILE, TILE))).astype(jnp.float32).astype(jnp.bfloat16)
        for j in range(tiles):
            x = src[rows_of(j)]
            high = x.astype(jnp.bfloat16)
            mid, low = split(x - high.astype(jnp.float32))
            entering = jnp.dot(low, pick, preferred_element_type=jnp.float32)
            entering += jnp.dot(mid, pick, preferred_element_type=jnp.float32)
            entering += jnp.dot(high, pick, preferred_element_type=jnp.float32)
            r = down_column(refl[0:1, rows_of(j)])
            first[rows_of(j)] = (1.0 + r) * entering + first[rows_of(j)]


def pack_kernel(tiles, band, shift_at, tiles_at, out, shift, held, sems):
    loads = [pltpu.make_async_copy(shift_at, shift, sems.at[tiles])]
    loads += [pltpu.make_async_copy(tiles_at.at[0, j], held.at[j], sems.at[j]) for j in range(tiles)]
    for load in loads:
        load.start()
    loads[0].wait()
    for j in range(tiles):
        loads[1 + j].wait()
        move = shift[0, j]
        for k in range(band):
            high, low = split(held[j, k])
            slot = k + 1 + move
            out[j, slot, :, :TILE] = high
            out[j, slot, :, TILE:] = low
        zero = jnp.zeros(out.shape[2:], jnp.bfloat16)
        out[j, jnp.where(move >= 0, 0, band)] = zero
        out[j, jnp.where(move <= 0, band + 1, 1)] = zero


def doubled(tile):
    high, low = split(tile)
    line = jnp.concatenate([high, low], axis=1)
    return jnp.concatenate([line, line], axis=0)


def folded(product):
    return product[:, :TILE] + product[:, TILE:]


def scaled(field, t, scale, sign):
    tile = field[rows_of(t)]
    return tile if scale is None else tile * (1.0 + sign * scale[t])


def spread(field, scale, sign, tiles, mirrored, held):
    for t in range(tiles):
        slot = jnp.where(mirrored, tiles - 1 - t, t)
        held[slot] = doubled(scaled(field, t, scale, sign))


def side_product(packed, held, tiles, band, low_side, jj):
    j = jnp.where(low_side, tiles - 1 - jj, jj)
    lhs, rhs = [], []
    for tt in range(jj + 1):
        slot = jnp.where(low_side, jj - tt, band + 1 + tt - jj)
        lhs.append(packed[j, slot])
        rhs.append(held[tt])
    return j, folded(
        jnp.dot(
            jnp.concatenate(lhs, axis=1),
            jnp.concatenate(rhs, axis=0),
            preferred_element_type=jnp.float32,
        )
    )


def when_active(step, sections, body):
    depth = lax.axis_index("depth")
    if step is None or step == 0:
        body()
    else:
        pl.when((depth == step) | (depth == sections - 1 - step))(body)


def inner_kernel(step, sections, tiles, band, packed, own, near, *refs):
    scales = [None, None]
    if step is None:
        own_rows, near_rows, total, own_scale, near_scale, held_own, held_near = refs
    elif step == 0:
        total, held_own, held_near = refs
    else:
        *scales, total, held_own, held_near = refs

    def body():
        sign = jnp.where(lax.axis_index("depth") == (step or 0), 1.0, -1.0)
        for t in range(tiles):
            held_own[t * 2 * TILE : (t + 1) * 2 * TILE] = doubled(scaled(own, t, scales[0], sign))
        low_side = lax.rem(lax.axis_index("lat"), 2) == 1
        spread(near, scales[1], sign, tiles, low_side, held_near)
        for j in range(tiles):
            lhs = jnp.concatenate([packed[j, tiles - j + t] for t in range(tiles)], axis=1)
            total[j] = folded(jnp.dot(lhs, held_own[...], preferred_element_type=jnp.float32))
        for jj in range(tiles):
            j, more = side_product(packed, held_near, tiles, band, low_side, jj)
            total[j] = total[j] + more
        if step is None:
            for t in range(tiles):
                at = tiles * TILE + t
                own_scale[t] = down_column(own_rows[at : at + 1])
                near_scale[t] = down_column(near_rows[at : at + 1])

    when_active(step, sections, body)


def outer_kernel(step, sections, lats, tiles, band, shots, packed, total, far, *refs):
    scale, base = None, None
    if step is None:
        far_rows, out, far_scale, held = refs
    elif step == 0:
        out, held = refs
    elif step < sections - 1:
        scale, base, out, held = refs
    else:
        scale, base, _, _, result_down, result_up, held, out, sem = refs
    lat = lax.axis_index("lat")
    depth = lax.axis_index("depth")
    low_side = lax.rem(lat, 2) == 0
    has_far = (lat > 0) & (lat < lats - 1)

    def body():
        sign = jnp.where(depth == (step or 0), 1.0, -1.0)
        lane = lax.broadcasted_iota(jnp.int32, (TILE, TILE), 1)
        real_lane = lax.rem(lane, 2 * shots) < shots

        def finish(j, product):
            by_imag = product[TILE:]
            ahead = pltpu.roll(by_imag, TILE - shots, 1)
            behind = pltpu.roll(by_imag, shots, 1)
            value = product[:TILE] + jnp.where(real_lane, -ahead, behind)
            at = pl.ds(pl.multiple_of(j * TILE, TILE), TILE)
            out[at] = value if base is None else value + base[at]

        @pl.when(has_far)
        def _():
            spread(far, scale, sign, tiles, low_side, held)
            for jj in range(tiles):
                j, more = side_product(packed, held, tiles, band, low_side, jj)
                finish(j, total[j] + more)

        @pl.when(jnp.logical_not(has_far))
        def _():
            for j in range(tiles):
                finish(j, total[j])

        if step is None:
            for t in range(tiles):
                at = tiles * TILE + t
                far_scale[t] = down_column(far_rows[at : at + 1])

        if step == sections - 1:

            def leave(result):
                copy = pltpu.make_async_copy(out, result.at[0], sem)
                copy.start()
                copy.wait()

            pl.when(depth == step)(lambda: leave(result_down))
            pl.when(depth != step)(lambda: leave(result_up))

    when_active(step, sections, body)


def keep_kernel(sections, *refs):
    fields, (result_down, result_up, sem) = refs[: sections - 1], refs[sections - 1 :]
    depth = lax.axis_index("depth")

    def put(field, result):
        copy = pltpu.make_async_copy(field, result.at[0], sem)
        copy.start()
        copy.wait()

    for step, field in enumerate(fields):
        pl.when(depth == step)(functools.partial(put, field, result_down))
        pl.when(depth == sections - 1 - step)(functools.partial(put, field, result_up))


def shards(sections, lats, operator, band_shift, reflectivity, up_stored, down_stored, sources, assignment):
    tiles, band = operator.shape[1], operator.shape[2]
    lateral, columns = sources.shape
    shots = columns // 4
    rows = tiles * TILE
    if sections % 2 or lats % 2 or tiles != band // 2 + 1:
        raise ValueError("unsupported sizes")

    def move(x, partner):
        pairs = []
        for d in range(sections):
            for l in range(lats):
                e, m = partner(d, l)
                pairs.append((d * lats + l, e * lats + m))
        return lax.ppermute(x, ("depth", "lat"), pairs)

    def near_of(d, l):
        return d, l ^ 1

    def far_of(spare, d, l):
        m = l + 1 if l % 2 else l - 1
        return (d, m) if 0 <= m < lats else (spare(d), l)

    def across(step, d, l):
        for low in (step, sections - 2 - step):
            if d == low:
                return low + 1, l
            if d == low + 1:
                return low, l
        return near_of(d, l)

    def halo(field, spare):
        return move(field, functools.partial(far_of, spare)), move(field, near_of)

    first, second = pl.pallas_call(
        functools.partial(prep_kernel, tiles, shots, sections),
        out_shape=[f32(rows + 8, columns), f32(rows, columns)],
        in_specs=[spec(pltpu.HBM)] * 5,
        out_specs=[spec(VMEM)] * 2,
        scratch_shapes=[
            pltpu.SMEM(assignment.shape, jnp.int32),
            VMEM(reflectivity.shape, jnp.float32),
            VMEM(up_stored.shape, jnp.float32),
            VMEM(down_stored.shape, jnp.float32),
            VMEM(sources.shape, jnp.float32),
            pltpu.SemaphoreType.DMA((5,)),
        ],
        compiler_params=params(),
        cost_estimate=cost(10**7, 5 * rows * columns * 4),
        name="prep",
    )(assignment, reflectivity, up_stored, down_stored, sources)

    packed = pl.pallas_call(
        functools.partial(pack_kernel, tiles, band),
        out_shape=jax.ShapeDtypeStruct((tiles, band + 2, 2 * TILE, 2 * TILE), jnp.bfloat16),
        in_specs=[spec(pltpu.HBM)] * 2,
        out_specs=spec(VMEM),
        scratch_shapes=[
            pltpu.SMEM(band_shift.shape, jnp.int32),
            VMEM(operator.shape[1:], jnp.float32),
            pltpu.SemaphoreType.DMA((tiles + 1,)),
        ],
        compiler_params=params(),
        cost_estimate=cost(10**7, 2 * operator.size * 4),
        name="pack",
    )(band_shift, operator)

    square = f32(tiles, TILE, columns)
    held = VMEM((tiles, 2 * TILE, 2 * TILE), jnp.bfloat16)

    def inner(step, own, near, more, extra):
        return pl.pallas_call(
            functools.partial(inner_kernel, step, sections, tiles, band),
            out_shape=[f32(tiles, 2 * TILE, columns)] + extra,
            in_specs=[spec(VMEM)] * (3 + len(more)),
            out_specs=[spec(VMEM)] * (1 + len(extra)),
            scratch_shapes=[VMEM((tiles * 2 * TILE, 2 * TILE), jnp.bfloat16), held],
            compiler_params=params(),
            cost_estimate=cost(2 * 40 * 256**3, 8 * 2**20),
            name=f"inner_{'base' if step is None else step}",
        )(packed, own, near, *more)

    def outer(step, total, far, more, extra):
        return pl.pallas_call(
            functools.partial(outer_kernel, step, sections, lats, tiles, band, shots),
            out_shape=[f32(rows, columns)] + extra,
            in_specs=[spec(VMEM)] * (3 + len(more)),
            out_specs=[spec(VMEM)] * (1 + len(extra)),
            scratch_shapes=[held],
            compiler_params=params(),
            cost_estimate=cost(2 * 15 * 256**3, 4 * 2**20),
            name=f"outer_{'base' if step is None else step}",
        )(packed, total, far, *more)

    first_far, first_near = halo(first, lambda d: d ^ 1)
    (total,) = inner(0, first, first_near, (), [])
    (field,) = outer(0, total, first_far, (), [])
    fields = [field]
    arrived = move(field, functools.partial(across, 0))

    second, _ = lax.optimization_barrier((second, field))
    far, near = halo(second, lambda d: (d + sections // 2) % sections)
    total, own_scale, near_scale = inner(None, second, near, (first, first_near), [square, square])
    second_base, far_scale = outer(None, total, far, (first_far,), [square])

    for step in range(1, sections):
        far, near = halo(arrived, lambda d: d ^ 1)
        (total,) = inner(step, arrived, near, (own_scale, near_scale), [])
        base = fields[0] if step < sections // 2 else second_base
        if step < sections - 1:
            (field,) = outer(step, total, far, (far_scale, base), [])
            fields.append(field)
            arrived = move(field, functools.partial(across, step))
            continue
        shape = f32(1, rows, columns)
        results = pl.pallas_call(
            functools.partial(keep_kernel, sections),
            out_shape=[shape] * 2,
            in_specs=[spec(VMEM)] * len(fields),
            out_specs=[spec(pl.ANY)] * 2,
            scratch_shapes=[pltpu.SemaphoreType.DMA(())],
            compiler_params=params(),
            cost_estimate=cost(0, 4 * rows * columns * 4),
            name="keep",
        )(*fields)
        results = pl.pallas_call(
            functools.partial(outer_kernel, step, sections, lats, tiles, band, shots),
            out_shape=[shape] * 2,
            in_specs=[spec(VMEM)] * 5 + [spec(pl.ANY)] * 2,
            out_specs=[spec(pl.ANY)] * 2,
            scratch_shapes=[held, VMEM((rows, columns), jnp.float32), pltpu.SemaphoreType.DMA(())],
            input_output_aliases={5: 0, 6: 1},
            compiler_params=params(),
            cost_estimate=cost(2 * 15 * 256**3, 4 * 2**20),
            name=f"outer_{step}",
        )(packed, total, far, far_scale, base, *results)
    return tuple(results)


def solution(mesh):
    return jax.shard_map(
        functools.partial(shards, mesh.shape["depth"], mesh.shape["lat"]),
        mesh=mesh,
        in_specs=(
            P("depth", "lat", None, None, None),
            P("depth", "lat"),
            P("depth", "lat"),
            P("depth", "lat", None),
            P("depth", "lat", None),
            P("lat", None),
            P(),
        ),
        out_specs=(P("depth", "lat", None), P("depth", "lat", None)),
        check_vma=False,
    )
```

time: 78.5 us -> 70.7 us (0.901)
  starting transfers between devices: 28.6 us -> 21.4 us
  waiting for transfers between devices: 31.9 us -> 27.7 us
  Pallas kernels: 9.4 us -> 12.8 us
    ppermute x13, starting transfers between devices: 28.6 us -> 21.4 us  [move(): return lax.ppermute(x, ('depth', 'lat'), pairs)]
    pallas_call x6 -> x12, Pallas kernels: 6.13 us -> 11.1 us  [the longest x5 5.05 us: inner(): pl.pallas_call(functools.partial(inner_kernel, step, sections, tiles, ban...]
    ppermute x13, waiting for transfers between devices: 31.9 us -> 27.7 us  [move(): return lax.ppermute(x, ('depth', 'lat'), pairs)]
    pallas_call x4 -> x1, Pallas kernels: 3.27 us -> 1.64 us  [shards(): pl.pallas_call(functools.partial(outer_kernel, step, sections, lats, tile...]
  transfers between devices with their start and end apart: 13 -> 13, of which waited for: 9 -> 7; matrix products, arithmetic and copies ran while one was open for 0% -> 0% of each run, Pallas kernels for 6% -> 13%
where the time goes in v2:
time: 70.7 us; the launch traced here: 70.4 us
  waiting for transfers between devices  27.7 us (39%)
  starting transfers between devices  21.4 us (30%)
  Pallas kernels  12.8 us (18%)
  local copies, waits for them, and re-layouts  7.57 us (11%)
  between operations  0.92 us (1%)
    ppermute x13, waiting for transfers between devices, move(): return lax.ppermute(x, ('depth', 'lat'), pairs)  27.7 us
    ppermute x13, starting transfers between devices, move(): return lax.ppermute(x, ('depth', 'lat'), pairs)  21.4 us
    unnamed x14, local copies, waits for them, and re-layouts  7.57 us
    pallas_call x5, Pallas kernels, inner(): pl.pallas_call(functools.partial(inner_kernel, step, sections, tiles, ban...  5.05 us
    pallas_call x1, Pallas kernels, shards(): pl.pallas_call(functools.partial(pack_kernel, tiles, band), out_shape=jax...  2.31 us
    pallas_call x4, Pallas kernels, outer(): pl.pallas_call(functools.partial(outer_kernel, step, sections, lats, tile...  1.93 us
    pallas_call x1, Pallas kernels, shards(): pl.pallas_call(functools.partial(outer_kernel, step, sections, lats, tile...  1.64 us
  transfers between devices with their start and end apart: 13, of which 7 were waited for; matrix products, arithmetic and copies ran while one was open for 0% of the time, Pallas kernels for 13%

profile of v2, /device:TPU:1, one launch (start us, length us, event | category | flops | bytes accessed | tf_op | source)
XLA Modules:
  0.0 70.4 jit_solution(472487334476553518)
XLA Ops:
  0.6 1.0 %copy-done.1 = f32[1,640,128]{2,1,0:T(8,128)S(1)} copy-done((f32[1,640,128]{2,1,0:T(8,128)S(1)}, f32[1,640,128]{2,1,0:T(8,128)}, u32[]{:S(2)}) %copy-start.1) | copy-done | bytes 327704
  1.6 1.0 %copy-done.2 = f32[1,640,128]{2,1,0:T(8,128)S(1)} copy-done((f32[1,640,128]{2,1,0:T(8,128)S(1)}, f32[1,640,128]{2,1,0:T(8,128)}, u32[]{:S(2)}) %copy-start.2) | copy-done | bytes 327704
  2.6 1.0 %copy-done.3 = f32[640,128]{1,0:T(8,128)S(1)} copy-done((f32[640,128]{1,0:T(8,128)S(1)}, f32[640,128]{1,0:T(8,128)}, u32[]{:S(2)}) %copy-start.3) | copy-done | bytes 327704
  4.9 1.1 %prep.1 = (f32[648,128]{1,0:T(8,128)S(1)}, f32[640,128]{1,0:T(8,128)S(1)}) custom-call(s32[64]{0:T(128)S(1)} %copy-done.5, f32[1,640]{1,0:T(1,128)S(1)} %copy-done.4, f32[1,640,128]{2,1,0:T(8,128)S(1)} %copy-done.1, f32[1,640,128]{2,1,0:T(8,128)S(1)} %copy-done.2, f32[640,128]{1,0:T(8,128)S(1)} %copy-done.3), custom_call_target="tpu_custom_call" | custom-call | flops 10000000 | bytes 1638400 | tf_op jit(solution)/shard_map/prep/pallas_call | solution.py:299
  6.1 2.7 %collective-permute-start.1 = (f32[648,128]{1,0:T(8,128)S(1)}, f32[648,128]{1,0:T(8,128)S(1)}, u32[]{:S(2)}, u32[]{:S(2)}) collective-permute-start(f32[648,128]{1,0:T(8,128)S(1)} %get-tuple-element.12.own.refs_0_), channel_id=1, source_target_pairs={{0,8},{1,2},{2,1},{3,4},{4,3},{5,6},{6,5},{7,15},{8,0},{9,10},{10,... | collective-permute-start | bytes 995336 | tf_op jit(solution)/shard_map/ppermute | solution.py:279
  8.8 2.7 %copy-done = f32[1,5,9,256,128]{4,3,2,1,0:T(8,128)S(1)} copy-done((f32[1,5,9,256,128]{4,3,2,1,0:T(8,128)S(1)}, f32[1,5,9,256,128]{4,3,2,1,0:T(8,128)}, u32[]{:S(2)}) %copy-start) | copy-done | bytes 5898264
  12.2 2.3 %pack.1.packed = bf16[5,11,256,256]{3,2,1,0:T(8,128)(2,1)S(1)} custom-call(s32[1,5]{1,0:T(1,128)S(1)} %copy-done.6, f32[1,5,9,256,128]{4,3,2,1,0:T(8,128)S(1)} %copy-done), custom_call_target="tpu_custom_call" | custom-call | flops 10000000 | bytes 11796480 | tf_op jit(solution)/shard_map/pack/pallas_call | solution.py:317
  14.5 1.7 %inner_0.1.total = f32[5,256,128]{2,1,0:T(8,128)S(1)} custom-call(bf16[5,11,256,256]{3,2,1,0:T(8,128)(2,1)S(1)} %pack.1.packed, f32[648,128]{1,0:T(8,128)S(1)} %get-tuple-element.12.own.refs_0_, f32[648,128]{1,0:T(8,128)S(1)} %collective-permute-done.near.refs_1_), custom_call_target="tpu_custom_call" | custom-call | flops 1342177280 | bytes 8388608 | tf_op jit(solution)/shard_map/inner_0/pallas_call | solution.py:336
  16.2 0.9 %outer_0.1.refs_1_.refs_0_ = f32[640,128]{1,0:T(8,128)S(1)} custom-call(bf16[5,11,256,256]{3,2,1,0:T(8,128)(2,1)S(1)} %pack.1.packed, f32[5,256,128]{2,1,0:T(8,128)S(1)} %inner_0.1.total, f32[648,128]{1,0:T(8,128)S(1)} %collective-permute-done.1.far.refs_0_), custom_call_target="tpu_custom_call" | custom-call | flops 503316480 | bytes 4194304 | tf_op jit(solution)/shard_map/outer_0/pallas_call | solution.py:348
  17.1 0.9 %collective-permute-start.2 = (f32[640,128]{1,0:T(8,128)S(1)}, f32[640,128]{1,0:T(8,128)S(1)}, u32[]{:S(2)}, u32[]{:S(2)}) collective-permute-start(f32[640,128]{1,0:T(8,128)S(1)} %outer_0.1.refs_1_.refs_0_), channel_id=1, source_target_pairs={{0,8},{1,9},{2,10},{3,11},{4,12},{5,13},{6,14},{7,15},{8,0},{9,1},... | collective-permute-start | bytes 983048 | tf_op jit(solution)/shard_map/ppermute | solution.py:279
  18.0 1.7 %collective-permute-start.6 = (f32[640,128]{1,0:T(8,128)S(1)}, f32[640,128]{1,0:T(8,128)S(1)}, u32[]{:S(2)}, u32[]{:S(2)}) collective-permute-start(f32[640,128]{1,0:T(8,128)S(1)} %get-tuple-element.14.own), channel_id=1, source_target_pairs={{0,16},{1,2},{2,1},{3,4},{4,3},{5,6},{6,5},{7,23},{8,24},{9,10},{1... | collective-permute-start | bytes 983048 | tf_op jit(solution)/shard_map/ppermute | solution.py:279
  19.7 6.7 %collective-permute-done.2.own = f32[640,128]{1,0:T(8,128)S(1)} collective-permute-done((f32[640,128]{1,0:T(8,128)S(1)}, f32[640,128]{1,0:T(8,128)S(1)}, u32[]{:S(2)}, u32[]{:S(2)}) %collective-permute-start.2) | collective-permute-done | bytes 327712 | tf_op jit(solution)/shard_map/ppermute | solution.py:279
  26.8 0.8 %collective-permute-start.5 = (f32[640,128]{1,0:T(8,128)S(1)}, f32[640,128]{1,0:T(8,128)S(1)}, u32[]{:S(2)}, u32[]{:S(2)}) collective-permute-start(f32[640,128]{1,0:T(8,128)S(1)} %collective-permute-done.2.own), channel_id=1, source_target_pairs={{0,8},{1,2},{2,1},{3,4},{4,3},{5,6},{6,5},{7,15},{8,0},{9,10},{10,... | collective-permute-start | bytes 983048 | tf_op jit(solution)/shard_map/ppermute | solution.py:279
  27.6 1.7 %inner_base.1 = (f32[5,256,128]{2,1,0:T(8,128)S(1)}, f32[5,128,128]{2,1,0:T(8,128)S(1)}, f32[5,128,128]{2,1,0:T(8,128)S(1)}) custom-call(bf16[5,11,256,256]{3,2,1,0:T(8,128)(2,1)S(1)} %pack.1.packed, f32[640,128]{1,0:T(8,128)S(1)} %get-tuple-element.14.own, f32[640,128]{1,0:T(8,128)S(1)} %collective-permute-done.4.near, ...), custom_call_target="tpu_custom_call" | custom-call | flops 1342177280 | bytes 8388608 | tf_op jit(solution)/shard_map/inner_base/pallas_call | solution.py:336
  29.2 1.0 %outer_base.1 = (f32[640,128]{1,0:T(8,128)S(1)}, f32[5,128,128]{2,1,0:T(8,128)S(1)}) custom-call(bf16[5,11,256,256]{3,2,1,0:T(8,128)(2,1)S(1)} %pack.1.packed, f32[5,256,128]{2,1,0:T(8,128)S(1)} %get-tuple-element.17.total, f32[640,128]{1,0:T(8,128)S(1)} %collective-permute-done.6.far, f32[648,128]{1,0:T(8,128)S(1)} %collective-permute-done.1.far.refs_0_), custom_call_target="tpu_custom_call" | custom-call | flops 503316480 | bytes 4194304 | tf_op jit(solution)/shard_map/outer_base/pallas_call | solution.py:348
  30.3 3.2 %collective-permute-done.5.far = f32[640,128]{1,0:T(8,128)S(1)} collective-permute-done((f32[640,128]{1,0:T(8,128)S(1)}, f32[640,128]{1,0:T(8,128)S(1)}, u32[]{:S(2)}, u32[]{:S(2)}) %collective-permute-start.5) | collective-permute-done | bytes 327712 | tf_op jit(solution)/shard_map/ppermute | solution.py:279
  34.0 1.3 %collective-permute-done.7.own = f32[640,128]{1,0:T(8,128)S(1)} collective-permute-done((f32[640,128]{1,0:T(8,128)S(1)}, f32[640,128]{1,0:T(8,128)S(1)}, u32[]{:S(2)}, u32[]{:S(2)}) %collective-permute-start.7) | collective-permute-done | bytes 327712 | tf_op jit(solution)/shard_map/ppermute | solution.py:279
  36.9 5.2 %collective-permute-done.9.far = f32[640,128]{1,0:T(8,128)S(1)} collective-permute-done((f32[640,128]{1,0:T(8,128)S(1)}, f32[640,128]{1,0:T(8,128)S(1)}, u32[]{:S(2)}, u32[]{:S(2)}) %collective-permute-start.9) | collective-permute-done | bytes 327712 | tf_op jit(solution)/shard_map/ppermute | solution.py:279
  42.1 11.3 %collective-permute-start.10 = (f32[640,128]{1,0:T(8,128)S(1)}, f32[640,128]{1,0:T(8,128)S(1)}, u32[]{:S(2)}, u32[]{:S(2)}) collective-permute-start(f32[640,128]{1,0:T(8,128)S(1)} %outer_2.1.refs_2_), channel_id=1, source_target_pairs={{0,8},{1,9},{2,10},{3,11},{4,12},{5,13},{6,14},{7,15},{8,0},{9,1},... | collective-permute-start | bytes 983048 | tf_op jit(solution)/shard_map/ppermute | solution.py:279
  53.4 8.1 %collective-permute-done.10.own = f32[640,128]{1,0:T(8,128)S(1)} collective-permute-done((f32[640,128]{1,0:T(8,128)S(1)}, f32[640,128]{1,0:T(8,128)S(1)}, u32[]{:S(2)}, u32[]{:S(2)}) %collective-permute-start.10) | collective-permute-done | bytes 327712 | tf_op jit(solution)/shard_map/ppermute | solution.py:279
  61.8 1.8 %collective-permute-start.12 = (f32[640,128]{1,0:T(8,128)S(1)}, f32[640,128]{1,0:T(8,128)S(1)}, u32[]{:S(2)}, u32[]{:S(2)}) collective-permute-start(f32[640,128]{1,0:T(8,128)S(1)} %collective-permute-done.10.own), channel_id=1, source_target_pairs={{0,8},{1,2},{2,1},{3,4},{4,3},{5,6},{6,5},{7,15},{8,0},{9,10},{10,... | collective-permute-start | bytes 983048 | tf_op jit(solution)/shard_map/ppermute | solution.py:279
  64.4 1.7 %inner_3.1.total = f32[5,256,128]{2,1,0:T(8,128)S(1)} custom-call(bf16[5,11,256,256]{3,2,1,0:T(8,128)(2,1)S(1)} %pack.1.packed, f32[640,128]{1,0:T(8,128)S(1)} %collective-permute-done.10.own, f32[640,128]{1,0:T(8,128)S(1)} %collective-permute-done.11.near, f32[5,128,128]{2,1,0:T(8,128)S(1)} %get-tuple-element.15.refs_0_, ...), custom_call_target="tpu_custom_call" | custom-call | flops 1342177280 | bytes 8388608 | tf_op jit(solution)/shard_map/inner_3/pallas_call | solution.py:336
  66.1 2.5 %collective-permute-done.12.far = f32[640,128]{1,0:T(8,128)S(1)} collective-permute-done((f32[640,128]{1,0:T(8,128)S(1)}, f32[640,128]{1,0:T(8,128)S(1)}, u32[]{:S(2)}, u32[]{:S(2)}) %collective-permute-start.12) | collective-permute-done | bytes 327712 | tf_op jit(solution)/shard_map/ppermute | solution.py:279
  68.6 1.6 %outer_3.1 = (f32[1,640,128]{2,1,0:T(8,128)}, f32[1,640,128]{2,1,0:T(8,128)}) custom-call(bf16[5,11,256,256]{3,2,1,0:T(8,128)(2,1)S(1)} %pack.1.packed, f32[5,256,128]{2,1,0:T(8,128)S(1)} %inner_3.1.total, f32[640,128]{1,0:T(8,128)S(1)} %collective-permute-done.12.far, ...), custom_call_target="tpu_custom_call", output_to_operand_aliasing={{0}: (5, {}), {1}: (6, {})} | custom-call | flops 503316480 | bytes 4194304 | tf_op jit(solution)/shard_map/outer_3/pallas_call | solution.py:390
  (29 shorter events, 5.7 us)
Async XLA Ops:
  0.6 1.0 %copy-start.1 = (f32[1,640,128]{2,1,0:T(8,128)S(1)}, f32[1,640,128]{2,1,0:T(8,128)}, u32[]{:S(2)}) copy-start(f32[1,640,128]{2,1,0:T(8,128)} %up_at.1) | copy-start | bytes 983044
  1.6 1.0 %copy-start.2 = (f32[1,640,128]{2,1,0:T(8,128)S(1)}, f32[1,640,128]{2,1,0:T(8,128)}, u32[]{:S(2)}) copy-start(f32[1,640,128]{2,1,0:T(8,128)} %down_at.1) | copy-start | bytes 983044
  2.6 1.0 %copy-start.3 = (f32[640,128]{1,0:T(8,128)S(1)}, f32[640,128]{1,0:T(8,128)}, u32[]{:S(2)}) copy-start(f32[640,128]{1,0:T(8,128)} %src_at.1) | copy-start | bytes 983044
  3.6 0.7 copy-start.4
  4.2 0.7 copy-start.5
  6.0 8.5 %collective-permute-start = (f32[648,128]{1,0:T(8,128)S(1)}, f32[648,128]{1,0:T(8,128)S(1)}, u32[]{:S(2)}, u32[]{:S(2)}) collective-permute-start(f32[648,128]{1,0:T(8,128)S(1)} %get-tuple-element.12.own.refs_0_), channel_id=1, source_target_pairs={{0,1},{1,0},{2,3},{3,2},{4,5},{5,4},{6,7},{7,6},{8,9},{9,8},{10,11... | collective-permute-start | bytes 995336 | tf_op jit(solution)/shard_map/ppermute | solution.py:279
  6.1 10.1 %collective-permute-start.1 = (f32[648,128]{1,0:T(8,128)S(1)}, f32[648,128]{1,0:T(8,128)S(1)}, u32[]{:S(2)}, u32[]{:S(2)}) collective-permute-start(f32[648,128]{1,0:T(8,128)S(1)} %get-tuple-element.12.own.refs_0_), channel_id=1, source_target_pairs={{0,8},{1,2},{2,1},{3,4},{4,3},{5,6},{6,5},{7,15},{8,0},{9,10},{10,... | collective-permute-start | bytes 995336 | tf_op jit(solution)/shard_map/ppermute | solution.py:279
  8.8 2.7 %copy-start = (f32[1,5,9,256,128]{4,3,2,1,0:T(8,128)S(1)}, f32[1,5,9,256,128]{4,3,2,1,0:T(8,128)}, u32[]{:S(2)}) copy-start(f32[1,5,9,256,128]{4,3,2,1,0:T(8,128)} %tiles_at.1) | copy-start | bytes 17694724
  11.5 0.7 copy-start.6
  17.1 9.3 %collective-permute-start.2 = (f32[640,128]{1,0:T(8,128)S(1)}, f32[640,128]{1,0:T(8,128)S(1)}, u32[]{:S(2)}, u32[]{:S(2)}) collective-permute-start(f32[640,128]{1,0:T(8,128)S(1)} %outer_0.1.refs_1_.refs_0_), channel_id=1, source_target_pairs={{0,8},{1,9},{2,10},{3,11},{4,12},{5,13},{6,14},{7,15},{8,0},{9,1},... | collective-permute-start | bytes 983048 | tf_op jit(solution)/shard_map/ppermute | solution.py:279
  18.0 9.6 %collective-permute-start.4 = (f32[640,128]{1,0:T(8,128)S(1)}, f32[640,128]{1,0:T(8,128)S(1)}, u32[]{:S(2)}, u32[]{:S(2)}) collective-permute-start(f32[640,128]{1,0:T(8,128)S(1)} %get-tuple-element.14.own), channel_id=1, source_target_pairs={{0,1},{1,0},{2,3},{3,2},{4,5},{5,4},{6,7},{7,6},{8,9},{9,8},{10,11... | collective-permute-start | bytes 983048 | tf_op jit(solution)/shard_map/ppermute | solution.py:279
  18.0 11.2 %collective-permute-start.6 = (f32[640,128]{1,0:T(8,128)S(1)}, f32[640,128]{1,0:T(8,128)S(1)}, u32[]{:S(2)}, u32[]{:S(2)}) collective-permute-start(f32[640,128]{1,0:T(8,128)S(1)} %get-tuple-element.14.own), channel_id=1, source_target_pairs={{0,16},{1,2},{2,1},{3,4},{4,3},{5,6},{6,5},{7,23},{8,24},{9,10},{1... | collective-permute-start | bytes 983048 | tf_op jit(solution)/shard_map/ppermute | solution.py:279
  26.4 3.9 %collective-permute-start.3 = (f32[640,128]{1,0:T(8,128)S(1)}, f32[640,128]{1,0:T(8,128)S(1)}, u32[]{:S(2)}, u32[]{:S(2)}) collective-permute-start(f32[640,128]{1,0:T(8,128)S(1)} %collective-permute-done.2.own), channel_id=1, source_target_pairs={{0,1},{1,0},{2,3},{3,2},{4,5},{5,4},{6,7},{7,6},{8,9},{9,8},{10,11... | collective-permute-start | bytes 983048 | tf_op jit(solution)/shard_map/ppermute | solution.py:279
  26.8 6.8 %collective-permute-start.5 = (f32[640,128]{1,0:T(8,128)S(1)}, f32[640,128]{1,0:T(8,128)S(1)}, u32[]{:S(2)}, u32[]{:S(2)}) collective-permute-start(f32[640,128]{1,0:T(8,128)S(1)} %collective-permute-done.2.own), channel_id=1, source_target_pairs={{0,8},{1,2},{2,1},{3,4},{4,3},{5,6},{6,5},{7,15},{8,0},{9,10},{10,... | collective-permute-start | bytes 983048 | tf_op jit(solution)/shard_map/ppermute | solution.py:279
  33.6 1.7 %collective-permute-start.7 = (f32[640,128]{1,0:T(8,128)S(1)}, f32[640,128]{1,0:T(8,128)S(1)}, u32[]{:S(2)}, u32[]{:S(2)}) collective-permute-start(f32[640,128]{1,0:T(8,128)S(1)} %outer_1.1.refs_1_), channel_id=1, source_target_pairs={{0,1},{1,0},{2,3},{3,2},{4,5},{5,4},{6,7},{7,6},{8,16},{9,17},{10,... | collective-permute-start | bytes 983048 | tf_op jit(solution)/shard_map/ppermute | solution.py:279
  35.2 1.6 %collective-permute-start.8 = (f32[640,128]{1,0:T(8,128)S(1)}, f32[640,128]{1,0:T(8,128)S(1)}, u32[]{:S(2)}, u32[]{:S(2)}) collective-permute-start(f32[640,128]{1,0:T(8,128)S(1)} %collective-permute-done.7.own), channel_id=1, source_target_pairs={{0,1},{1,0},{2,3},{3,2},{4,5},{5,4},{6,7},{7,6},{8,9},{9,8},{10,11... | collective-permute-start | bytes 983048 | tf_op jit(solution)/shard_map/ppermute | solution.py:279
  35.6 6.5 %collective-permute-start.9 = (f32[640,128]{1,0:T(8,128)S(1)}, f32[640,128]{1,0:T(8,128)S(1)}, u32[]{:S(2)}, u32[]{:S(2)}) collective-permute-start(f32[640,128]{1,0:T(8,128)S(1)} %collective-permute-done.7.own), channel_id=1, source_target_pairs={{0,8},{1,2},{2,1},{3,4},{4,3},{5,6},{6,5},{7,15},{8,0},{9,10},{10,... | collective-permute-start | bytes 983048 | tf_op jit(solution)/shard_map/ppermute | solution.py:279
  42.1 19.3 %collective-permute-start.10 = (f32[640,128]{1,0:T(8,128)S(1)}, f32[640,128]{1,0:T(8,128)S(1)}, u32[]{:S(2)}, u32[]{:S(2)}) collective-permute-start(f32[640,128]{1,0:T(8,128)S(1)} %outer_2.1.refs_2_), channel_id=1, source_target_pairs={{0,8},{1,9},{2,10},{3,11},{4,12},{5,13},{6,14},{7,15},{8,0},{9,1},... | collective-permute-start | bytes 983048 | tf_op jit(solution)/shard_map/ppermute | solution.py:279
  61.4 3.0 %collective-permute-start.11 = (f32[640,128]{1,0:T(8,128)S(1)}, f32[640,128]{1,0:T(8,128)S(1)}, u32[]{:S(2)}, u32[]{:S(2)}) collective-permute-start(f32[640,128]{1,0:T(8,128)S(1)} %collective-permute-done.10.own), channel_id=1, source_target_pairs={{0,1},{1,0},{2,3},{3,2},{4,5},{5,4},{6,7},{7,6},{8,9},{9,8},{10,11... | collective-permute-start | bytes 983048 | tf_op jit(solution)/shard_map/ppermute | solution.py:279
  61.8 6.8 %collective-permute-start.12 = (f32[640,128]{1,0:T(8,128)S(1)}, f32[640,128]{1,0:T(8,128)S(1)}, u32[]{:S(2)}, u32[]{:S(2)}) collective-permute-start(f32[640,128]{1,0:T(8,128)S(1)} %collective-permute-done.10.own), channel_id=1, source_target_pairs={{0,8},{1,2},{2,1},{3,4},{4,3},{5,6},{6,5},{7,15},{8,0},{9,10},{10,... | collective-permute-start | bytes 983048 | tf_op jit(solution)/shard_map/ppermute | solution.py:279

commit v3 on v2

v3 whole, which is shorter than its diff:
```python
import functools

import jax
import jax.numpy as jnp
from jax import lax
from jax.experimental import pallas as pl
from jax.experimental.pallas import tpu as pltpu
from jax.sharding import PartitionSpec as P

TILE = 128
VMEM = pltpu.VMEM
LIMIT = 16 * 2**20
CHUNKS = (3, 2)


def spec(space):
    return pl.BlockSpec(memory_space=space)


def f32(*shape):
    return jax.ShapeDtypeStruct(shape, jnp.float32)


def params(limit=LIMIT):
    return pltpu.CompilerParams(vmem_limit_bytes=limit)


def cost(flops, read):
    return pl.CostEstimate(flops=flops, bytes_accessed=read, transcendentals=0)


def in_hbm(x):
    return pltpu.with_memory_space_constraint(x, pltpu.HBM)


def rows_of(t):
    return slice(t * TILE, (t + 1) * TILE)


def down_column(row):
    return jnp.transpose(jnp.broadcast_to(row, (TILE, TILE)))


def split(value):
    high = value.astype(jnp.bfloat16)
    low = (value - high.astype(jnp.float32)).astype(jnp.bfloat16)
    return high, low


def prep_kernel(tiles, shots, sections, assign_at, refl_at, up_at, down_at, src_at, first, second, assign, refl, up, down, src, sems):
    depth = lax.axis_index("depth")
    loads = [
        pltpu.make_async_copy(assign_at, assign, sems.at[0]),
        pltpu.make_async_copy(refl_at, refl, sems.at[1]),
        pltpu.make_async_copy(up_at, up, sems.at[2]),
        pltpu.make_async_copy(down_at, down, sems.at[3]),
        pltpu.make_async_copy(src_at, src, sems.at[4]),
    ]
    for load in loads:
        load.start()
    for load in loads:
        load.wait()
    descends = depth < sections // 2

    def write(of_up, of_down):
        for j in range(tiles):
            row = refl[0:1, rows_of(j)]
            r = down_column(row)
            of_up[rows_of(j)] = -(r * up[0, rows_of(j)])
            of_down[rows_of(j)] = r * down[0, rows_of(j)]
            first[tiles * TILE + j : tiles * TILE + j + 1] = row

    @pl.when(descends)
    def _():
        write(first, second)

    @pl.when(jnp.logical_not(descends))
    def _():
        write(second, first)

    @pl.when(depth == 0)
    def _():
        lane = lax.broadcasted_iota(jnp.int32, (8, TILE), 1)
        wanted = jnp.zeros((8, TILE), jnp.int32)
        for b in range(TILE // (2 * shots)):
            for i in range(shots):
                shot = assign[b * shots + i]
                at = b * 2 * shots + i
                wanted = jnp.where(lane == at, shot, wanted)
                wanted = jnp.where(lane == at + shots, shot + TILE // 2, wanted)
        source = lax.broadcasted_iota(jnp.int32, (TILE, TILE), 0)
        pick = (source == jnp.broadcast_to(wanted[0:1], (TILE, TILE))).astype(jnp.float32).astype(jnp.bfloat16)
        for j in range(tiles):
            x = src[rows_of(j)]
            high = x.astype(jnp.bfloat16)
            mid, low = split(x - high.astype(jnp.float32))
            entering = jnp.dot(low, pick, preferred_element_type=jnp.float32)
            entering += jnp.dot(mid, pick, preferred_element_type=jnp.float32)
            entering += jnp.dot(high, pick, preferred_element_type=jnp.float32)
            r = down_column(refl[0:1, rows_of(j)])
            first[rows_of(j)] = (1.0 + r) * entering + first[rows_of(j)]


def pack_kernel(tiles, band, shift_at, tiles_at, out, shift, held, sems):
    loads = [pltpu.make_async_copy(shift_at, shift, sems.at[tiles])]
    loads += [pltpu.make_async_copy(tiles_at.at[0, j], held.at[j], sems.at[j]) for j in range(tiles)]
    for load in loads:
        load.start()
    loads[0].wait()
    for j in range(tiles):
        loads[1 + j].wait()
        move = shift[0, j]
        for k in range(band):
            high, low = split(held[j, k])
            slot = k + 1 + move
            out[j, slot, :, :TILE] = high
            out[j, slot, :, TILE:] = low
        zero = jnp.zeros(out.shape[2:], jnp.bfloat16)
        out[j, jnp.where(move >= 0, 0, band)] = zero
        out[j, jnp.where(move <= 0, band + 1, 1)] = zero


def doubled(tile):
    high, low = split(tile)
    line = jnp.concatenate([high, low], axis=1)
    return jnp.concatenate([line, line], axis=0)


def folded(product):
    return product[:, :TILE] + product[:, TILE:]


def tile_of(chunks, t):
    for chunk in chunks:
        count = chunk.shape[0] // TILE
        if t < count:
            return chunk, rows_of(t)
        t -= count


def read(chunks, t):
    chunk, at = tile_of(chunks, t)
    return chunk[at]


def spread(field, scale, sign, tiles, held):
    for t in range(tiles):
        tile = read(field, t)
        held[2 * t * TILE : 2 * (t + 1) * TILE] = doubled(tile if scale is None else tile * (1.0 + sign * scale[t]))


def product(packed, held, tiles, j, side):
    if side == "low":
        slots, first, last = range(tiles - j), j, tiles
    elif side == "own":
        slots, first, last = range(tiles - j, 2 * tiles - j), 0, tiles
    else:
        slots, first, last = range(2 * tiles - j, 2 * tiles + 1), 0, j + 1
    return folded(
        jnp.dot(
            jnp.concatenate([packed[j, slot] for slot in slots], axis=1),
            held[2 * first * TILE : 2 * last * TILE],
            preferred_element_type=jnp.float32,
        )
    )


def when_active(step, sections, body):
    depth = lax.axis_index("depth")
    if step is None or step == 0:
        body()
    else:
        pl.when((depth == step) | (depth == sections - 1 - step))(body)


def inner_kernel(step, sections, tiles, n, packed, *refs):
    own, near, refs = refs[:n], refs[n : 2 * n], refs[2 * n :]
    scales = [None, None]
    if step is None:
        rows_at, (total, *scales_out, held_own, held_near) = refs[:3], refs[3:]
    elif step == 0:
        total, held_own, held_near = refs
    else:
        *scales, total, held_own, held_near = refs

    def body():
        sign = jnp.where(lax.axis_index("depth") == (step or 0), 1.0, -1.0)
        spread(own, scales[0], sign, tiles, held_own)
        spread(near, scales[1], sign, tiles, held_near)
        for j in range(tiles):
            total[j] = product(packed, held_own, tiles, j, "own")
        low_side = lax.rem(lax.axis_index("lat"), 2) == 1

        def add(side):
            for j in range(tiles):
                total[j] = total[j] + product(packed, held_near, tiles, j, side)

        pl.when(low_side)(lambda: add("low"))
        pl.when(jnp.logical_not(low_side))(lambda: add("high"))
        if step is None:
            for source, out in zip(rows_at, scales_out):
                for t in range(tiles):
                    at = tiles * TILE + t
                    out[t] = down_column(source[at : at + 1])

    when_active(step, sections, body)


def outer_kernel(step, sections, lats, tiles, shots, n, bases, packed, total, *refs):
    far, refs = refs[:n], refs[n:]
    scale, base, sems = None, None, None
    if step:
        scale, refs = refs[0], refs[1:]
        base, refs = refs[:bases], refs[bases:]
    if step == sections - 1:
        _, _, result_down, result_up, held, leaving, sems = refs
        outs = (leaving,)
    else:
        outs, held = refs[:-1], refs[-1]
    lat = lax.axis_index("lat")
    depth = lax.axis_index("depth")
    low_side = lax.rem(lat, 2) == 0
    has_far = (lat > 0) & (lat < lats - 1)

    def body():
        sign = jnp.where(depth == (step or 0), 1.0, -1.0)
        lane = lax.broadcasted_iota(jnp.int32, (TILE, TILE), 1)
        real_lane = lax.rem(lane, 2 * shots) < shots

        def finish(j, value):
            by_imag = value[TILE:]
            ahead = pltpu.roll(by_imag, TILE - shots, 1)
            behind = pltpu.roll(by_imag, shots, 1)
            value = value[:TILE] + jnp.where(real_lane, -ahead, behind)
            out, at = tile_of(outs, j)
            out[at] = value if base is None else value + read(base, j)

        def with_far(side):
            spread(far, scale, sign, tiles, held)
            for j in range(tiles):
                finish(j, total[j] + product(packed, held, tiles, j, side))

        pl.when(has_far & low_side)(lambda: with_far("low"))
        pl.when(has_far & jnp.logical_not(low_side))(lambda: with_far("high"))

        @pl.when(jnp.logical_not(has_far))
        def _():
            for j in range(tiles):
                finish(j, total[j])

        if sems is not None:

            def leave(result):
                copy = pltpu.make_async_copy(leaving, result.at[0], sems)
                copy.start()
                copy.wait()

            pl.when(depth == step)(lambda: leave(result_down))
            pl.when(depth != step)(lambda: leave(result_up))

    when_active(step, sections, body)


def keep_kernel(sections, counts, *refs):
    result_down, result_up, sems = refs[-3:]
    depth = lax.axis_index("depth")

    def put(field, result):
        copies, at = [], 0
        for i, chunk in enumerate(field):
            span = pl.ds(at, chunk.shape[0])
            copies.append(pltpu.make_async_copy(chunk, result.at[0, span], sems.at[i]))
            at += chunk.shape[0]
        for copy in copies:
            copy.start()
        for copy in copies:
            copy.wait()

    at = 0
    for step, count in enumerate(counts):
        field = refs[at : at + count]
        at += count
        pl.when(depth == step)(functools.partial(put, field, result_down))
        pl.when(depth == sections - 1 - step)(functools.partial(put, field, result_up))


def shards(sections, lats, operator, band_shift, reflectivity, up_stored, down_stored, sources, assignment):
    tiles, band = operator.shape[1], operator.shape[2]
    lateral, columns = sources.shape
    shots = columns // 4
    rows = tiles * TILE
    if sections % 2 or lats % 2 or tiles != band // 2 + 1 or tiles != sum(CHUNKS):
        raise ValueError("unsupported sizes")

    def move(x, partner):
        pairs = []
        for d in range(sections):
            for l in range(lats):
                e, m = partner(d, l)
                pairs.append((d * lats + l, e * lats + m))
        return lax.ppermute(x, ("depth", "lat"), pairs)

    def near_of(d, l):
        return d, l ^ 1

    def far_of(spare, d, l):
        m = l + 1 if l % 2 else l - 1
        return (d, m) if 0 <= m < lats else (spare(d), l)

    def across(step, d, l):
        for low in (step, sections - 2 - step):
            if d == low:
                return low + 1, l
            if d == low + 1:
                return low, l
        return near_of(d, l)

    def halo(field, spare):
        far, near = [], []
        for chunk in field:
            far.append(move(chunk, functools.partial(far_of, spare)))
            near.append(move(chunk, near_of))
        return far, near

    first, second = pl.pallas_call(
        functools.partial(prep_kernel, tiles, shots, sections),
        out_shape=[f32(rows + 8, columns), f32(rows, columns)],
        in_specs=[spec(pltpu.HBM)] * 5,
        out_specs=[spec(VMEM)] * 2,
        scratch_shapes=[
            pltpu.SMEM(assignment.shape, jnp.int32),
            VMEM(reflectivity.shape, jnp.float32),
            VMEM(up_stored.shape, jnp.float32),
            VMEM(down_stored.shape, jnp.float32),
            VMEM(sources.shape, jnp.float32),
            pltpu.SemaphoreType.DMA((5,)),
        ],
        compiler_params=params(),
        cost_estimate=cost(10**7, 5 * rows * columns * 4),
        name="prep",
    )(*map(in_hbm, (assignment, reflectivity, up_stored, down_stored, sources)))

    packed = pl.pallas_call(
        functools.partial(pack_kernel, tiles, band),
        out_shape=jax.ShapeDtypeStruct((tiles, band + 2, 2 * TILE, 2 * TILE), jnp.bfloat16),
        in_specs=[spec(pltpu.HBM)] * 2,
        out_specs=spec(VMEM),
        scratch_shapes=[
            pltpu.SMEM(band_shift.shape, jnp.int32),
            VMEM(operator.shape[1:], jnp.float32),
            pltpu.SemaphoreType.DMA((tiles + 1,)),
        ],
        compiler_params=params(),
        cost_estimate=cost(10**7, 2 * operator.size * 4),
        name="pack",
    )(in_hbm(band_shift), in_hbm(operator))

    square = f32(tiles, TILE, columns)
    held = VMEM((tiles * 2 * TILE, 2 * TILE), jnp.bfloat16)
    chunked = [f32(count * TILE, columns) for count in CHUNKS]
    whole = [f32(rows, columns)]

    def inner(step, own, near, more, extra):
        return pl.pallas_call(
            functools.partial(inner_kernel, step, sections, tiles, len(own)),
            out_shape=[f32(tiles, 2 * TILE, columns)] + extra,
            in_specs=[spec(VMEM)] * (1 + 2 * len(own) + len(more)),
            out_specs=[spec(VMEM)] * (1 + len(extra)),
            scratch_shapes=[held, held],
            compiler_params=params(),
            cost_estimate=cost(2 * 40 * 256**3, 8 * 2**20),
            name=f"inner_{'base' if step is None else step}",
        )(packed, *own, *near, *more)

    def outer(step, total, far, scale, base, shapes):
        last = step == sections - 1
        args = [packed, total, *far, *scale, *base]
        specs = [spec(VMEM)] * len(args)
        scratch, out_specs, aliases = [held], [spec(VMEM)] * len(shapes), {}
        if last:
            aliases = {len(args): 0, len(args) + 1: 1}
            args += keep()
            specs += [spec(pl.ANY)] * 2
            out_specs = [spec(pl.ANY)] * 2
            scratch += [VMEM((rows, columns), jnp.float32), pltpu.SemaphoreType.DMA(())]
        return pl.pallas_call(
            functools.partial(outer_kernel, step, sections, lats, tiles, shots, len(far), len(base)),
            out_shape=shapes,
            in_specs=specs,
            out_specs=out_specs,
            scratch_shapes=scratch,
            input_output_aliases=aliases,
            compiler_params=params(),
            cost_estimate=cost(2 * 15 * 256**3, 4 * 2**20),
            name=f"outer_{'base' if step is None else step}",
        )(*args)

    def keep():
        return pl.pallas_call(
            functools.partial(keep_kernel, sections, [len(field) for field in fields]),
            out_shape=result,
            in_specs=[spec(VMEM)] * sum(len(field) for field in fields),
            out_specs=[spec(pl.ANY)] * 2,
            scratch_shapes=[pltpu.SemaphoreType.DMA((len(CHUNKS),))],
            compiler_params=params(),
            cost_estimate=cost(0, 4 * rows * columns * 4),
            name="keep",
        )(*[chunk for field in fields for chunk in field])

    def cross(step, field):
        return [move(chunk, functools.partial(across, step)) for chunk in field]

    result = [f32(1, rows, columns)] * 2
    first_far, first_near = halo([first], lambda d: d ^ 1)
    (total,) = inner(0, [first], first_near, (), [])
    fields = [outer(0, total, first_far, (), (), chunked)]
    arrived = cross(0, fields[0])

    second, *_ = lax.optimization_barrier((second, *fields[0]))
    far, near = halo([second], lambda d: (d + sections // 2) % sections)
    total, own_scale, near_scale, far_scale = inner(None, [second], near, (first, *first_near, *first_far), [square] * 3)
    second_base = outer(None, total, far, (), (), whole)

    for step in range(1, sections):
        far, near = halo(arrived, lambda d: d ^ 1)
        (total,) = inner(step, arrived, near, (own_scale, near_scale), [])
        base = fields[0] if step < sections // 2 else second_base
        shapes = result if step == sections - 1 else chunked
        fields.append(outer(step, total, far, (far_scale,), base, shapes))
        if step < sections - 1:
            arrived = cross(step, fields[step])
    return tuple(fields[-1])


def solution(mesh):
    return jax.shard_map(
        functools.partial(shards, mesh.shape["depth"], mesh.shape["lat"]),
        mesh=mesh,
        in_specs=(
            P("depth", "lat", None, None, None),
            P("depth", "lat"),
            P("depth", "lat"),
            P("depth", "lat", None),
            P("depth", "lat", None),
            P("lat", None),
            P(),
        ),
        out_specs=(P("depth", "lat", None), P("depth", "lat", None)),
        check_vma=False,
    )
```

time: 70.7 us -> 66.3 us (0.938)
  local copies, waits for them, and re-layouts: 7.57 us -> 0 us
  starting transfers between devices: 21.4 us -> 27.1 us
  waiting for transfers between devices: 27.7 us -> 23.8 us
  Pallas kernels: 12.8 us -> 14.3 us
    unnamed x14 -> x0, local copies, waits for them, and re-layouts: 7.57 us -> none
    ppermute x13 -> x22, starting transfers between devices: 21.4 us -> 27.1 us  [move(): return lax.ppermute(x, ('depth', 'lat'), pairs)]
    ppermute x13 -> x22, waiting for transfers between devices: 27.7 us -> 23.8 us  [move(): return lax.ppermute(x, ('depth', 'lat'), pairs)]
    pallas_call x4 -> x5, Pallas kernels: 1.93 us -> 3.22 us  [outer(): pl.pallas_call(functools.partial(outer_kernel, step, sections, lats, tile...]
    pallas_call x7 -> x6, Pallas kernels: 7.42 us -> 6.39 us  [the longest x5 5.66 us: inner(): pl.pallas_call(functools.partial(inner_kernel, step, sections, tiles, len...]
  transfers between devices with their start and end apart: 13 -> 22, of which waited for: 7 -> 11; matrix products, arithmetic and copies ran while one was open for 0% -> 0% of each run, Pallas kernels for 13% -> 15%
where the time goes in v3:
time: 66.3 us; the launch traced here: 66.2 us
  starting transfers between devices  27.1 us (41%)
  waiting for transfers between devices  23.8 us (36%)
  Pallas kernels  14.3 us (22%)
  between operations  0.95 us (1%)
    ppermute x22, starting transfers between devices, move(): return lax.ppermute(x, ('depth', 'lat'), pairs)  27.1 us
    ppermute x22, waiting for transfers between devices, move(): return lax.ppermute(x, ('depth', 'lat'), pairs)  23.8 us
    pallas_call x5, Pallas kernels, inner(): pl.pallas_call(functools.partial(inner_kernel, step, sections, tiles, len...  5.66 us
    pallas_call x5, Pallas kernels, outer(): pl.pallas_call(functools.partial(outer_kernel, step, sections, lats, tile...  3.22 us
    pallas_call x1, Pallas kernels, shards(): pl.pallas_call(functools.partial(pack_kernel, tiles, band), out_shape=jax...  2.95 us
    pallas_call x1, Pallas kernels, shards(): pl.pallas_call(functools.partial(prep_kernel, tiles, shots, sections), ou...  1.76 us
  transfers between devices with their start and end apart: 22, of which 11 were waited for; matrix products, arithmetic and copies ran while one was open for 0% of the time, Pallas kernels for 15%

profile of v3, /device:TPU:1, one launch (start us, length us, event | category | flops | bytes accessed | tf_op | source)
XLA Modules:
  0.0 66.2 jit_solution(6764411828023291268)
XLA Ops:
  0.6 1.8 %prep.1 = (f32[648,128]{1,0:T(8,128)S(1)}, f32[640,128]{1,0:T(8,128)S(1)}) custom-call(s32[64]{0:T(128)} %assign_at.1, f32[1,640]{1,0:T(1,128)} %refl_at.1, f32[1,640,128]{2,1,0:T(8,128)} %up_at.1, f32[1,640,128]{2,1,0:T(8,128)} %down_at.1, f32[640,128]{1,0:T(8,128)} %src_at.1), custom_call_target="tpu_custom_call" | custom-call | flops 10000000 | bytes 1638400 | tf_op jit(solution)/shard_map/prep/pallas_call | solution.py:325
  2.5 2.7 %collective-permute-start.1 = (f32[648,128]{1,0:T(8,128)S(1)}, f32[648,128]{1,0:T(8,128)S(1)}, u32[]{:S(2)}, u32[]{:S(2)}) collective-permute-start(f32[648,128]{1,0:T(8,128)S(1)} %get-tuple-element.17.refs_0_.refs_2_), channel_id=1, source_target_pairs={{0,8},{1,2},{2,1},{3,4},{4,3},{5,6},{6,5},{7,15},{8,0},{9,10},{10,... | collective-permute-start | bytes 995336 | tf_op jit(solution)/shard_map/ppermute | solution.py:301
  5.2 3.0 %pack.1.packed = bf16[5,11,256,256]{3,2,1,0:T(8,128)(2,1)S(1)} custom-call(s32[1,5]{1,0:T(1,128)} %shift_at.1, f32[1,5,9,256,128]{4,3,2,1,0:T(8,128)} %tiles_at.1), custom_call_target="tpu_custom_call" | custom-call | flops 10000000 | bytes 11796480 | tf_op jit(solution)/shard_map/pack/pallas_call | solution.py:343
  8.2 1.8 %inner_0.1.total = f32[5,256,128]{2,1,0:T(8,128)S(1)} custom-call(bf16[5,11,256,256]{3,2,1,0:T(8,128)(2,1)S(1)} %pack.1.packed, f32[648,128]{1,0:T(8,128)S(1)} %get-tuple-element.17.refs_0_.refs_2_, f32[648,128]{1,0:T(8,128)S(1)} %collective-permute-done.refs_1_.refs_3_), custom_call_target="tpu_custom_call" | custom-call | flops 1342177280 | bytes 8388608 | tf_op jit(solution)/shard_map/inner_0/pallas_call | solution.py:364
  11.0 1.6 %collective-permute-start.2 = (f32[384,128]{1,0:T(8,128)S(1)}, f32[384,128]{1,0:T(8,128)S(1)}, u32[]{:S(2)}, u32[]{:S(2)}) collective-permute-start(f32[384,128]{1,0:T(8,128)S(1)} %get-tuple-element.18.refs_3_.refs_0_), channel_id=1, source_target_pairs={{0,8},{1,9},{2,10},{3,11},{4,12},{5,13},{6,14},{7,15},{8,0},{9,1},... | collective-permute-start | bytes 589832 | tf_op jit(solution)/shard_map/ppermute | solution.py:301
  12.7 4.6 %collective-permute-done.2.refs_0_ = f32[384,128]{1,0:T(8,128)S(1)} collective-permute-done((f32[384,128]{1,0:T(8,128)S(1)}, f32[384,128]{1,0:T(8,128)S(1)}, u32[]{:S(2)}, u32[]{:S(2)}) %collective-permute-start.2) | collective-permute-done | bytes 196640 | tf_op jit(solution)/shard_map/ppermute | solution.py:301
  17.3 1.9 %collective-permute-start.4 = (f32[384,128]{1,0:T(8,128)S(1)}, f32[384,128]{1,0:T(8,128)S(1)}, u32[]{:S(2)}, u32[]{:S(2)}) collective-permute-start(f32[384,128]{1,0:T(8,128)S(1)} %collective-permute-done.2.refs_0_), channel_id=1, source_target_pairs={{0,1},{1,0},{2,3},{3,2},{4,5},{5,4},{6,7},{7,6},{8,9},{9,8},{10,11... | collective-permute-start | bytes 589832 | tf_op jit(solution)/shard_map/ppermute | solution.py:301
  19.2 0.9 %collective-permute-done.3.refs_1_ = f32[256,128]{1,0:T(8,128)S(1)} collective-permute-done((f32[256,128]{1,0:T(8,128)S(1)}, f32[256,128]{1,0:T(8,128)S(1)}, u32[]{:S(2)}, u32[]{:S(2)}) %collective-permute-start.3) | collective-permute-done | bytes 131104 | tf_op jit(solution)/shard_map/ppermute | solution.py:301
  20.1 1.2 %collective-permute-start.5 = (f32[256,128]{1,0:T(8,128)S(1)}, f32[256,128]{1,0:T(8,128)S(1)}, u32[]{:S(2)}, u32[]{:S(2)}) collective-permute-start(f32[256,128]{1,0:T(8,128)S(1)} %collective-permute-done.3.refs_1_), channel_id=1, source_target_pairs={{0,1},{1,0},{2,3},{3,2},{4,5},{5,4},{6,7},{7,6},{8,9},{9,8},{10,11... | collective-permute-start | bytes 393224 | tf_op jit(solution)/shard_map/ppermute | solution.py:301
  21.3 1.5 %collective-permute-start.8 = (f32[256,128]{1,0:T(8,128)S(1)}, f32[256,128]{1,0:T(8,128)S(1)}, u32[]{:S(2)}, u32[]{:S(2)}) collective-permute-start(f32[256,128]{1,0:T(8,128)S(1)} %collective-permute-done.3.refs_1_), channel_id=1, source_target_pairs={{0,8},{1,2},{2,1},{3,4},{4,3},{5,6},{6,5},{7,15},{8,0},{9,10},{10,... | collective-permute-start | bytes 393224 | tf_op jit(solution)/shard_map/ppermute | solution.py:301
  23.0 2.1 %inner_base.1 = (f32[5,256,128]{2,1,0:T(8,128)S(1)}, f32[5,128,128]{2,1,0:T(8,128)S(1)}, f32[5,128,128]{2,1,0:T(8,128)S(1)}, f32[5,128,128]{2,1,0:T(8,128)S(1)}) custom-call(bf16[5,11,256,256]{3,2,1,0:T(8,128)(2,1)S(1)} %pack.1.packed, f32[640,128]{1,0:T(8,128)S(1)} %get-tuple-element.21.refs_0_, f32[640,128]{1,0:T(8,128)S(1)} %collective-permute-done.6.refs_1_, ...), custom_call_target="tpu_custom_call" | custom-call | flops 1342177280 | bytes 8388608 | tf_op jit(solution)/shard_map/inner_base/pallas_call | solution.py:364
  25.8 2.4 %collective-permute-done.7.refs_0_ = f32[384,128]{1,0:T(8,128)S(1)} collective-permute-done((f32[384,128]{1,0:T(8,128)S(1)}, f32[384,128]{1,0:T(8,128)S(1)}, u32[]{:S(2)}, u32[]{:S(2)}) %collective-permute-start.7) | collective-permute-done | bytes 196640 | tf_op jit(solution)/shard_map/ppermute | solution.py:301
  28.7 1.1 %collective-permute-start.15 = (f32[640,128]{1,0:T(8,128)S(1)}, f32[640,128]{1,0:T(8,128)S(1)}, u32[]{:S(2)}, u32[]{:S(2)}) collective-permute-start(f32[640,128]{1,0:T(8,128)S(1)} %get-tuple-element.21.refs_0_), channel_id=1, source_target_pairs={{0,16},{1,2},{2,1},{3,4},{4,3},{5,6},{6,5},{7,23},{8,24},{9,10},{1... | collective-permute-start | bytes 983048 | tf_op jit(solution)/shard_map/ppermute | solution.py:301
  29.8 2.0 %collective-permute-start.10 = (f32[256,128]{1,0:T(8,128)S(1)}, f32[256,128]{1,0:T(8,128)S(1)}, u32[]{:S(2)}, u32[]{:S(2)}) collective-permute-start(f32[256,128]{1,0:T(8,128)S(1)} %get-tuple-element.26.refs_3_), channel_id=1, source_target_pairs={{0,1},{1,0},{2,3},{3,2},{4,5},{5,4},{6,7},{7,6},{8,16},{9,17},{10,... | collective-permute-start | bytes 393224 | tf_op jit(solution)/shard_map/ppermute | solution.py:301
  31.9 1.0 %collective-permute-done.10.refs_1_ = f32[256,128]{1,0:T(8,128)S(1)} collective-permute-done((f32[256,128]{1,0:T(8,128)S(1)}, f32[256,128]{1,0:T(8,128)S(1)}, u32[]{:S(2)}, u32[]{:S(2)}) %collective-permute-start.10) | collective-permute-done | bytes 131104 | tf_op jit(solution)/shard_map/ppermute | solution.py:301
  33.2 1.7 %collective-permute-start.14 = (f32[256,128]{1,0:T(8,128)S(1)}, f32[256,128]{1,0:T(8,128)S(1)}, u32[]{:S(2)}, u32[]{:S(2)}) collective-permute-start(f32[256,128]{1,0:T(8,128)S(1)} %collective-permute-done.10.refs_1_), channel_id=1, source_target_pairs={{0,8},{1,2},{2,1},{3,4},{4,3},{5,6},{6,5},{7,15},{8,0},{9,10},{10,... | collective-permute-start | bytes 393224 | tf_op jit(solution)/shard_map/ppermute | solution.py:301
  36.3 3.4 %collective-permute-done.14.refs_1_ = f32[256,128]{1,0:T(8,128)S(1)} collective-permute-done((f32[256,128]{1,0:T(8,128)S(1)}, f32[256,128]{1,0:T(8,128)S(1)}, u32[]{:S(2)}, u32[]{:S(2)}) %collective-permute-start.14) | collective-permute-done | bytes 131104 | tf_op jit(solution)/shard_map/ppermute | solution.py:301
  39.7 9.3 %collective-permute-start.16 = (f32[384,128]{1,0:T(8,128)S(1)}, f32[384,128]{1,0:T(8,128)S(1)}, u32[]{:S(2)}, u32[]{:S(2)}) collective-permute-start(f32[384,128]{1,0:T(8,128)S(1)} %get-tuple-element.28.refs_4_), channel_id=1, source_target_pairs={{0,8},{1,9},{2,10},{3,11},{4,12},{5,13},{6,14},{7,15},{8,0},{9,1},... | collective-permute-start | bytes 589832 | tf_op jit(solution)/shard_map/ppermute | solution.py:301
  49.1 5.4 %collective-permute-done.16.refs_0_ = f32[384,128]{1,0:T(8,128)S(1)} collective-permute-done((f32[384,128]{1,0:T(8,128)S(1)}, f32[384,128]{1,0:T(8,128)S(1)}, u32[]{:S(2)}, u32[]{:S(2)}) %collective-permute-start.16) | collective-permute-done | bytes 196640 | tf_op jit(solution)/shard_map/ppermute | solution.py:301
  54.8 2.4 %collective-permute-done.17.refs_1_ = f32[256,128]{1,0:T(8,128)S(1)} collective-permute-done((f32[256,128]{1,0:T(8,128)S(1)}, f32[256,128]{1,0:T(8,128)S(1)}, u32[]{:S(2)}, u32[]{:S(2)}) %collective-permute-start.17) | collective-permute-done | bytes 131104 | tf_op jit(solution)/shard_map/ppermute | solution.py:301
  58.2 1.2 %collective-permute-start.21 = (f32[256,128]{1,0:T(8,128)S(1)}, f32[256,128]{1,0:T(8,128)S(1)}, u32[]{:S(2)}, u32[]{:S(2)}) collective-permute-start(f32[256,128]{1,0:T(8,128)S(1)} %collective-permute-done.17.refs_1_), channel_id=1, source_target_pairs={{0,8},{1,2},{2,1},{3,4},{4,3},{5,6},{6,5},{7,15},{8,0},{9,10},{10,... | collective-permute-start | bytes 393224 | tf_op jit(solution)/shard_map/ppermute | solution.py:301
  60.2 1.8 %inner_3.1.total = f32[5,256,128]{2,1,0:T(8,128)S(1)} custom-call(bf16[5,11,256,256]{3,2,1,0:T(8,128)(2,1)S(1)} %pack.1.packed, f32[384,128]{1,0:T(8,128)S(1)} %collective-permute-done.16.refs_0_, f32[256,128]{1,0:T(8,128)S(1)} %collective-permute-done.17.refs_1_, f32[384,128]{1,0:T(8,128)S(1)} %collective-permute-done.18.refs_2_, ...), custom_call_target="tpu_custom_call" | custom-call | flops 1342177280 | bytes 8388608 | tf_op jit(solution)/shard_map/inner_3/pallas_call | solution.py:364
  62.0 2.5 %collective-permute-done.21.refs_1_ = f32[256,128]{1,0:T(8,128)S(1)} collective-permute-done((f32[256,128]{1,0:T(8,128)S(1)}, f32[256,128]{1,0:T(8,128)S(1)}, u32[]{:S(2)}, u32[]{:S(2)}) %collective-permute-start.21) | collective-permute-done | bytes 131104 | tf_op jit(solution)/shard_map/ppermute | solution.py:301
  64.4 1.6 %outer_3.1 = (f32[1,640,128]{2,1,0:T(8,128)}, f32[1,640,128]{2,1,0:T(8,128)}) custom-call(bf16[5,11,256,256]{3,2,1,0:T(8,128)(2,1)S(1)} %pack.1.packed, f32[5,256,128]{2,1,0:T(8,128)S(1)} %inner_3.1.total, f32[384,128]{1,0:T(8,128)S(1)} %collective-permute-done.20.refs_0_, ...), custom_call_target="tpu_custom_call", output_to_operand_aliasing={{0}: (6, {}), {1}: (7, {})} | custom-call | flops 503316480 | bytes 4194304 | tf_op jit(solution)/shard_map/outer_3/pallas_call | solution.py:386
  (33 shorter events, 6.4 us)
Async XLA Ops:
  2.4 5.8 %collective-permute-start = (f32[648,128]{1,0:T(8,128)S(1)}, f32[648,128]{1,0:T(8,128)S(1)}, u32[]{:S(2)}, u32[]{:S(2)}) collective-permute-start(f32[648,128]{1,0:T(8,128)S(1)} %get-tuple-element.17.refs_0_.refs_2_), channel_id=1, source_target_pairs={{0,1},{1,0},{2,3},{3,2},{4,5},{5,4},{6,7},{7,6},{8,9},{9,8},{10,11... | collective-permute-start | bytes 995336 | tf_op jit(solution)/shard_map/ppermute | solution.py:301
  2.5 7.5 %collective-permute-start.1 = (f32[648,128]{1,0:T(8,128)S(1)}, f32[648,128]{1,0:T(8,128)S(1)}, u32[]{:S(2)}, u32[]{:S(2)}) collective-permute-start(f32[648,128]{1,0:T(8,128)S(1)} %get-tuple-element.17.refs_0_.refs_2_), channel_id=1, source_target_pairs={{0,8},{1,2},{2,1},{3,4},{4,3},{5,6},{6,5},{7,15},{8,0},{9,10},{10,... | collective-permute-start | bytes 995336 | tf_op jit(solution)/shard_map/ppermute | solution.py:301
  10.9 12.1 %collective-permute-start.6 = (f32[640,128]{1,0:T(8,128)S(1)}, f32[640,128]{1,0:T(8,128)S(1)}, u32[]{:S(2)}, u32[]{:S(2)}) collective-permute-start(f32[640,128]{1,0:T(8,128)S(1)} %get-tuple-element.21.refs_0_), channel_id=1, source_target_pairs={{0,1},{1,0},{2,3},{3,2},{4,5},{5,4},{6,7},{7,6},{8,9},{9,8},{10,11... | collective-permute-start | bytes 983048 | tf_op jit(solution)/shard_map/ppermute | solution.py:301
  11.0 6.3 %collective-permute-start.2 = (f32[384,128]{1,0:T(8,128)S(1)}, f32[384,128]{1,0:T(8,128)S(1)}, u32[]{:S(2)}, u32[]{:S(2)}) collective-permute-start(f32[384,128]{1,0:T(8,128)S(1)} %get-tuple-element.18.refs_3_.refs_0_), channel_id=1, source_target_pairs={{0,8},{1,9},{2,10},{3,11},{4,12},{5,13},{6,14},{7,15},{8,0},{9,1},... | collective-permute-start | bytes 589832 | tf_op jit(solution)/shard_map/ppermute | solution.py:301
  12.6 7.5 %collective-permute-start.3 = (f32[256,128]{1,0:T(8,128)S(1)}, f32[256,128]{1,0:T(8,128)S(1)}, u32[]{:S(2)}, u32[]{:S(2)}) collective-permute-start(f32[256,128]{1,0:T(8,128)S(1)} %get-tuple-element.19.refs_4_.refs_1_), channel_id=1, source_target_pairs={{0,8},{1,9},{2,10},{3,11},{4,12},{5,13},{6,14},{7,15},{8,0},{9,1},... | collective-permute-start | bytes 393224 | tf_op jit(solution)/shard_map/ppermute | solution.py:301
  17.3 7.8 %collective-permute-start.4 = (f32[384,128]{1,0:T(8,128)S(1)}, f32[384,128]{1,0:T(8,128)S(1)}, u32[]{:S(2)}, u32[]{:S(2)}) collective-permute-start(f32[384,128]{1,0:T(8,128)S(1)} %collective-permute-done.2.refs_0_), channel_id=1, source_target_pairs={{0,1},{1,0},{2,3},{3,2},{4,5},{5,4},{6,7},{7,6},{8,9},{9,8},{10,11... | collective-permute-start | bytes 589832 | tf_op jit(solution)/shard_map/ppermute | solution.py:301
  20.1 5.0 %collective-permute-start.5 = (f32[256,128]{1,0:T(8,128)S(1)}, f32[256,128]{1,0:T(8,128)S(1)}, u32[]{:S(2)}, u32[]{:S(2)}) collective-permute-start(f32[256,128]{1,0:T(8,128)S(1)} %collective-permute-done.3.refs_1_), channel_id=1, source_target_pairs={{0,1},{1,0},{2,3},{3,2},{4,5},{5,4},{6,7},{7,6},{8,9},{9,8},{10,11... | collective-permute-start | bytes 393224 | tf_op jit(solution)/shard_map/ppermute | solution.py:301
  21.3 4.6 %collective-permute-start.8 = (f32[256,128]{1,0:T(8,128)S(1)}, f32[256,128]{1,0:T(8,128)S(1)}, u32[]{:S(2)}, u32[]{:S(2)}) collective-permute-start(f32[256,128]{1,0:T(8,128)S(1)} %collective-permute-done.3.refs_1_), channel_id=1, source_target_pairs={{0,8},{1,2},{2,1},{3,4},{4,3},{5,6},{6,5},{7,15},{8,0},{9,10},{10,... | collective-permute-start | bytes 393224 | tf_op jit(solution)/shard_map/ppermute | solution.py:301
  22.8 5.4 %collective-permute-start.7 = (f32[384,128]{1,0:T(8,128)S(1)}, f32[384,128]{1,0:T(8,128)S(1)}, u32[]{:S(2)}, u32[]{:S(2)}) collective-permute-start(f32[384,128]{1,0:T(8,128)S(1)} %collective-permute-done.2.refs_0_), channel_id=1, source_target_pairs={{0,8},{1,2},{2,1},{3,4},{4,3},{5,6},{6,5},{7,15},{8,0},{9,10},{10,... | collective-permute-start | bytes 589832 | tf_op jit(solution)/shard_map/ppermute | solution.py:301
  28.2 3.7 %collective-permute-start.9 = (f32[384,128]{1,0:T(8,128)S(1)}, f32[384,128]{1,0:T(8,128)S(1)}, u32[]{:S(2)}, u32[]{:S(2)}) collective-permute-start(f32[384,128]{1,0:T(8,128)S(1)} %get-tuple-element.25.refs_2_), channel_id=1, source_target_pairs={{0,1},{1,0},{2,3},{3,2},{4,5},{5,4},{6,7},{7,6},{8,16},{9,17},{10,... | collective-permute-start | bytes 589832 | tf_op jit(solution)/shard_map/ppermute | solution.py:301
  28.7 6.8 %collective-permute-start.15 = (f32[640,128]{1,0:T(8,128)S(1)}, f32[640,128]{1,0:T(8,128)S(1)}, u32[]{:S(2)}, u32[]{:S(2)}) collective-permute-start(f32[640,128]{1,0:T(8,128)S(1)} %get-tuple-element.21.refs_0_), channel_id=1, source_target_pairs={{0,16},{1,2},{2,1},{3,4},{4,3},{5,6},{6,5},{7,23},{8,24},{9,10},{1... | collective-permute-start | bytes 983048 | tf_op jit(solution)/shard_map/ppermute | solution.py:301
  29.8 3.0 %collective-permute-start.10 = (f32[256,128]{1,0:T(8,128)S(1)}, f32[256,128]{1,0:T(8,128)S(1)}, u32[]{:S(2)}, u32[]{:S(2)}) collective-permute-start(f32[256,128]{1,0:T(8,128)S(1)} %get-tuple-element.26.refs_3_), channel_id=1, source_target_pairs={{0,1},{1,0},{2,3},{3,2},{4,5},{5,4},{6,7},{7,6},{8,16},{9,17},{10,... | collective-permute-start | bytes 393224 | tf_op jit(solution)/shard_map/ppermute | solution.py:301
  31.9 4.4 %collective-permute-start.11 = (f32[384,128]{1,0:T(8,128)S(1)}, f32[384,128]{1,0:T(8,128)S(1)}, u32[]{:S(2)}, u32[]{:S(2)}) collective-permute-start(f32[384,128]{1,0:T(8,128)S(1)} %collective-permute-done.9.refs_0_), channel_id=1, source_target_pairs={{0,1},{1,0},{2,3},{3,2},{4,5},{5,4},{6,7},{7,6},{8,9},{9,8},{10,11... | collective-permute-start | bytes 589832 | tf_op jit(solution)/shard_map/ppermute | solution.py:301
  32.8 3.5 %collective-permute-start.12 = (f32[256,128]{1,0:T(8,128)S(1)}, f32[256,128]{1,0:T(8,128)S(1)}, u32[]{:S(2)}, u32[]{:S(2)}) collective-permute-start(f32[256,128]{1,0:T(8,128)S(1)} %collective-permute-done.10.refs_1_), channel_id=1, source_target_pairs={{0,1},{1,0},{2,3},{3,2},{4,5},{5,4},{6,7},{7,6},{8,9},{9,8},{10,11... | collective-permute-start | bytes 393224 | tf_op jit(solution)/shard_map/ppermute | solution.py:301
  33.2 6.5 %collective-permute-start.13 = (f32[384,128]{1,0:T(8,128)S(1)}, f32[384,128]{1,0:T(8,128)S(1)}, u32[]{:S(2)}, u32[]{:S(2)}) collective-permute-start(f32[384,128]{1,0:T(8,128)S(1)} %collective-permute-done.9.refs_0_), channel_id=1, source_target_pairs={{0,8},{1,2},{2,1},{3,4},{4,3},{5,6},{6,5},{7,15},{8,0},{9,10},{10,... | collective-permute-start | bytes 589832 | tf_op jit(solution)/shard_map/ppermute | solution.py:301
  33.2 6.5 %collective-permute-start.14 = (f32[256,128]{1,0:T(8,128)S(1)}, f32[256,128]{1,0:T(8,128)S(1)}, u32[]{:S(2)}, u32[]{:S(2)}) collective-permute-start(f32[256,128]{1,0:T(8,128)S(1)} %collective-permute-done.10.refs_1_), channel_id=1, source_target_pairs={{0,8},{1,2},{2,1},{3,4},{4,3},{5,6},{6,5},{7,15},{8,0},{9,10},{10,... | collective-permute-start | bytes 393224 | tf_op jit(solution)/shard_map/ppermute | solution.py:301
  39.7 14.8 %collective-permute-start.16 = (f32[384,128]{1,0:T(8,128)S(1)}, f32[384,128]{1,0:T(8,128)S(1)}, u32[]{:S(2)}, u32[]{:S(2)}) collective-permute-start(f32[384,128]{1,0:T(8,128)S(1)} %get-tuple-element.28.refs_4_), channel_id=1, source_target_pairs={{0,8},{1,9},{2,10},{3,11},{4,12},{5,13},{6,14},{7,15},{8,0},{9,1},... | collective-permute-start | bytes 589832 | tf_op jit(solution)/shard_map/ppermute | solution.py:301
  49.0 8.2 %collective-permute-start.17 = (f32[256,128]{1,0:T(8,128)S(1)}, f32[256,128]{1,0:T(8,128)S(1)}, u32[]{:S(2)}, u32[]{:S(2)}) collective-permute-start(f32[256,128]{1,0:T(8,128)S(1)} %get-tuple-element.29.refs_5_), channel_id=1, source_target_pairs={{0,8},{1,9},{2,10},{3,11},{4,12},{5,13},{6,14},{7,15},{8,0},{9,1},... | collective-permute-start | bytes 393224 | tf_op jit(solution)/shard_map/ppermute | solution.py:301
  54.5 5.6 %collective-permute-start.18 = (f32[384,128]{1,0:T(8,128)S(1)}, f32[384,128]{1,0:T(8,128)S(1)}, u32[]{:S(2)}, u32[]{:S(2)}) collective-permute-start(f32[384,128]{1,0:T(8,128)S(1)} %collective-permute-done.16.refs_0_), channel_id=1, source_target_pairs={{0,1},{1,0},{2,3},{3,2},{4,5},{5,4},{6,7},{7,6},{8,9},{9,8},{10,11... | collective-permute-start | bytes 589832 | tf_op jit(solution)/shard_map/ppermute | solution.py:301
  57.3 2.9 %collective-permute-start.19 = (f32[256,128]{1,0:T(8,128)S(1)}, f32[256,128]{1,0:T(8,128)S(1)}, u32[]{:S(2)}, u32[]{:S(2)}) collective-permute-start(f32[256,128]{1,0:T(8,128)S(1)} %collective-permute-done.17.refs_1_), channel_id=1, source_target_pairs={{0,1},{1,0},{2,3},{3,2},{4,5},{5,4},{6,7},{7,6},{8,9},{9,8},{10,11... | collective-permute-start | bytes 393224 | tf_op jit(solution)/shard_map/ppermute | solution.py:301
  57.6 6.8 %collective-permute-start.20 = (f32[384,128]{1,0:T(8,128)S(1)}, f32[384,128]{1,0:T(8,128)S(1)}, u32[]{:S(2)}, u32[]{:S(2)}) collective-permute-start(f32[384,128]{1,0:T(8,128)S(1)} %collective-permute-done.16.refs_0_), channel_id=1, source_target_pairs={{0,8},{1,2},{2,1},{3,4},{4,3},{5,6},{6,5},{7,15},{8,0},{9,10},{10,... | collective-permute-start | bytes 589832 | tf_op jit(solution)/shard_map/ppermute | solution.py:301
  58.2 6.3 %collective-permute-start.21 = (f32[256,128]{1,0:T(8,128)S(1)}, f32[256,128]{1,0:T(8,128)S(1)}, u32[]{:S(2)}, u32[]{:S(2)}) collective-permute-start(f32[256,128]{1,0:T(8,128)S(1)} %collective-permute-done.17.refs_1_), channel_id=1, source_target_pairs={{0,8},{1,2},{2,1},{3,4},{4,3},{5,6},{6,5},{7,15},{8,0},{9,10},{10,... | collective-permute-start | bytes 393224 | tf_op jit(solution)/shard_map/ppermute | solution.py:301

commit v4 on v3

--- a/solution.py
+++ b/solution.py
@@ -7,6 +7,7 @@
 from jax.experimental.pallas import tpu as pltpu
 from jax.sharding import PartitionSpec as P
 
+
 TILE = 128
 VMEM = pltpu.VMEM
 LIMIT = 16 * 2**20
@@ -19,6 +20,10 @@
 
 def f32(*shape):
     return jax.ShapeDtypeStruct(shape, jnp.float32)
+
+
+def call(kernel, **kwargs):
+    return pl.pallas_call(kernel, **kwargs)
 
 
 def params(limit=LIMIT):
@@ -143,26 +148,26 @@
     return chunk[at]
 
 
-def spread(field, scale, sign, tiles, held):
-    for t in range(tiles):
-        tile = read(field, t)
+def spread(field, scale, sign, span, held):
+    for t in span:
+        tile = read(field, t - span.start)
         held[2 * t * TILE : 2 * (t + 1) * TILE] = doubled(tile if scale is None else tile * (1.0 + sign * scale[t]))
 
 
-def product(packed, held, tiles, j, side):
-    if side == "low":
-        slots, first, last = range(tiles - j), j, tiles
-    elif side == "own":
-        slots, first, last = range(tiles - j, 2 * tiles - j), 0, tiles
-    else:
-        slots, first, last = range(2 * tiles - j, 2 * tiles + 1), 0, j + 1
+def product(packed, held, j, slots, at):
     return folded(
         jnp.dot(
             jnp.concatenate([packed[j, slot] for slot in slots], axis=1),
-            held[2 * first * TILE : 2 * last * TILE],
+            held[2 * at * TILE : 2 * (at + len(slots)) * TILE],
             preferred_element_type=jnp.float32,
         )
     )
+
+
+def side_product(packed, held, tiles, j, low_side):
+    if low_side:
+        return product(packed, held, j, range(tiles - j), j)
+    return product(packed, held, j, range(2 * tiles - j, 2 * tiles + 1), 0)
 
 
 def when_active(step, sections, body):
@@ -173,35 +178,40 @@
         pl.when((depth == step) | (depth == sections - 1 - step))(body)
 
 
-def inner_kernel(step, sections, tiles, n, packed, *refs):
-    own, near, refs = refs[:n], refs[n : 2 * n], refs[2 * n :]
-    scales = [None, None]
-    if step is None:
-        rows_at, (total, *scales_out, held_own, held_near) = refs[:3], refs[3:]
-    elif step == 0:
-        total, held_own, held_near = refs
-    else:
-        *scales, total, held_own, held_near = refs
+def scale_kernel(tiles, *refs):
+    for source, out in zip(refs[:3], refs[3:]):
+        for t in range(tiles):
+            at = tiles * TILE + t
+            out[t] = down_column(source[at : at + 1])
+
+
+def inner_kernel(step, sections, tiles, span, n_own, n_near, packed, *refs):
+    own, near, refs = refs[:n_own], refs[n_own : n_own + n_near], refs[n_own + n_near :]
+    scale, near_scale, before = None, None, None
+    if step:
+        scale, refs = refs[0], refs[1:]
+        if near:
+            near_scale, refs = refs[0], refs[1:]
+    if span.start:
+        before, refs = refs[0], refs[1:]
+    total, held_own, held_near = refs
 
     def body():
         sign = jnp.where(lax.axis_index("depth") == (step or 0), 1.0, -1.0)
-        spread(own, scales[0], sign, tiles, held_own)
-        spread(near, scales[1], sign, tiles, held_near)
+        spread(own, scale, sign, span, held_own)
         for j in range(tiles):
-            total[j] = product(packed, held_own, tiles, j, "own")
-        low_side = lax.rem(lax.axis_index("lat"), 2) == 1
-
-        def add(side):
-            for j in range(tiles):
-                total[j] = total[j] + product(packed, held_near, tiles, j, side)
-
-        pl.when(low_side)(lambda: add("low"))
-        pl.when(jnp.logical_not(low_side))(lambda: add("high"))
-        if step is None:
-            for source, out in zip(rows_at, scales_out):
-                for t in range(tiles):
-                    at = tiles * TILE + t
-                    out[t] = down_column(source[at : at + 1])
+            value = product(packed, held_own, j, range(tiles - j + span.start, tiles - j + span.stop), span.start)
+            total[j] = value if before is None else before[j] + value
+        if near:
+            spread(near, near_scale, sign, range(tiles), held_near)
+            low_side = lax.rem(lax.axis_index("lat"), 2) == 1
+
+            def add(low):
+                for j in range(tiles):
+                    total[j] = total[j] + side_product(packed, held_near, tiles, j, low)
+
+            pl.when(low_side)(lambda: add(True))
+            pl.when(jnp.logical_not(low_side))(lambda: add(False))
 
     when_active(step, sections, body)
 
@@ -236,12 +246,12 @@
             out[at] = value if base is None else value + read(base, j)
 
         def with_far(side):
-            spread(far, scale, sign, tiles, held)
+            spread(far, scale, sign, range(tiles), held)
             for j in range(tiles):
-                finish(j, total[j] + product(packed, held, tiles, j, side))
-
-        pl.when(has_far & low_side)(lambda: with_far("low"))
-        pl.when(has_far & jnp.logical_not(low_side))(lambda: with_far("high"))
+                finish(j, total[j] + side_product(packed, held, tiles, j, side))
+
+        pl.when(has_far & low_side)(lambda: with_far(True))
+        pl.when(has_far & jnp.logical_not(low_side))(lambda: with_far(False))
 
         @pl.when(jnp.logical_not(has_far))
         def _():
@@ -286,7 +296,7 @@
 
 def shards(sections, lats, operator, band_shift, reflectivity, up_stored, down_stored, sources, assignment):
     tiles, band = operator.shape[1], operator.shape[2]
-    lateral, columns = sources.shape
+    _, columns = sources.shape
     shots = columns // 4
     rows = tiles * TILE
     if sections % 2 or lats % 2 or tiles != band // 2 + 1 or tiles != sum(CHUNKS):
@@ -322,7 +332,7 @@
             near.append(move(chunk, near_of))
         return far, near
 
-    first, second = pl.pallas_call(
+    first, second = call(
         functools.partial(prep_kernel, tiles, shots, sections),
         out_shape=[f32(rows + 8, columns), f32(rows, columns)],
         in_specs=[spec(pltpu.HBM)] * 5,
@@ -337,10 +347,9 @@
         ],
         compiler_params=params(),
         cost_estimate=cost(10**7, 5 * rows * columns * 4),
-        name="prep",
     )(*map(in_hbm, (assignment, reflectivity, up_stored, down_stored, sources)))
 
-    packed = pl.pallas_call(
+    packed = call(
         functools.partial(pack_kernel, tiles, band),
         out_shape=jax.ShapeDtypeStruct((tiles, band + 2, 2 * TILE, 2 * TILE), jnp.bfloat16),
         in_specs=[spec(pltpu.HBM)] * 2,
@@ -352,7 +361,6 @@
         ],
         compiler_params=params(),
         cost_estimate=cost(10**7, 2 * operator.size * 4),
-        name="pack",
     )(in_hbm(band_shift), in_hbm(operator))
 
     square = f32(tiles, TILE, columns)
@@ -360,17 +368,20 @@
     chunked = [f32(count * TILE, columns) for count in CHUNKS]
     whole = [f32(rows, columns)]
 
-    def inner(step, own, near, more, extra):
-        return pl.pallas_call(
-            functools.partial(inner_kernel, step, sections, tiles, len(own)),
-            out_shape=[f32(tiles, 2 * TILE, columns)] + extra,
-            in_specs=[spec(VMEM)] * (1 + 2 * len(own) + len(more)),
-            out_specs=[spec(VMEM)] * (1 + len(extra)),
+    def inner(step, own, near, more, at=0):
+        count = sum(chunk.shape[0] for chunk in own) // TILE
+        args = [packed, *own, *near, *more]
+        return call(
+            functools.partial(
+                inner_kernel, step, sections, tiles, range(at, at + count), len(own), len(near)
+            ),
+            out_shape=f32(tiles, 2 * TILE, columns),
+            in_specs=[spec(VMEM)] * len(args),
+            out_specs=spec(VMEM),
             scratch_shapes=[held, held],
             compiler_params=params(),
             cost_estimate=cost(2 * 40 * 256**3, 8 * 2**20),
-            name=f"inner_{'base' if step is None else step}",
-        )(packed, *own, *near, *more)
+        )(*args)
 
     def outer(step, total, far, scale, base, shapes):
         last = step == sections - 1
@@ -383,7 +394,7 @@
             specs += [spec(pl.ANY)] * 2
             out_specs = [spec(pl.ANY)] * 2
             scratch += [VMEM((rows, columns), jnp.float32), pltpu.SemaphoreType.DMA(())]
-        return pl.pallas_call(
+        return call(
             functools.partial(outer_kernel, step, sections, lats, tiles, shots, len(far), len(base)),
             out_shape=shapes,
             in_specs=specs,
@@ -392,11 +403,10 @@
             input_output_aliases=aliases,
             compiler_params=params(),
             cost_estimate=cost(2 * 15 * 256**3, 4 * 2**20),
-            name=f"outer_{'base' if step is None else step}",
         )(*args)
 
     def keep():
-        return pl.pallas_call(
+        return call(
             functools.partial(keep_kernel, sections, [len(field) for field in fields]),
             out_shape=result,
             in_specs=[spec(VMEM)] * sum(len(field) for field in fields),
@@ -404,7 +414,6 @@
             scratch_shapes=[pltpu.SemaphoreType.DMA((len(CHUNKS),))],
             compiler_params=params(),
             cost_estimate=cost(0, 4 * rows * columns * 4),
-            name="keep",
         )(*[chunk for field in fields for chunk in field])
 
     def cross(step, field):
@@ -412,18 +421,32 @@
 
     result = [f32(1, rows, columns)] * 2
     first_far, first_near = halo([first], lambda d: d ^ 1)
-    (total,) = inner(0, [first], first_near, (), [])
+    total = inner(0, [first], first_near, ())
     fields = [outer(0, total, first_far, (), (), chunked)]
     arrived = cross(0, fields[0])
 
     second, *_ = lax.optimization_barrier((second, *fields[0]))
     far, near = halo([second], lambda d: (d + sections // 2) % sections)
-    total, own_scale, near_scale, far_scale = inner(None, [second], near, (first, *first_near, *first_far), [square] * 3)
+    own_scale, near_scale, far_scale = call(
+        functools.partial(scale_kernel, tiles),
+        out_shape=[square] * 3,
+        in_specs=[spec(VMEM)] * 3,
+        out_specs=[spec(VMEM)] * 3,
+        compiler_params=params(),
+        cost_estimate=cost(10**6, 4 * rows * columns * 4),
+    )(first, *first_near, *first_far)
+    total = inner(None, [second], near, ())
     second_base = outer(None, total, far, (), (), whole)
 
     for step in range(1, sections):
         far, near = halo(arrived, lambda d: d ^ 1)
-        (total,) = inner(step, arrived, near, (own_scale, near_scale), [])
+        total, at = None, 0
+        for chunk in arrived[:-1]:
+            before = () if total is None else (total,)
+            total = inner(step, [chunk], [], (own_scale, *before), at)
+            at += chunk.shape[0] // TILE
+        before = () if total is None else (total,)
+        total = inner(step, arrived[-1:], near, (own_scale, near_scale, *before), at=at)
         base = fields[0] if step < sections // 2 else second_base
         shapes = result if step == sections - 1 else chunked
         fields.append(outer(step, total, far, (far_scale,), base, shapes))

time: 66.3 us -> 68.9 us (1.039); the launches traced: 66.2 us -> 68 us
  waiting for transfers between devices: 23.8 us -> 27.9 us
  starting transfers between devices: 27.1 us -> 24.9 us
    ppermute x22, waiting for transfers between devices: 23.8 us -> 27.9 us  [move(): return lax.ppermute(x, ('depth', 'lat'), pairs)]
    ppermute x22, starting transfers between devices: 27.1 us -> 24.9 us  [move(): return lax.ppermute(x, ('depth', 'lat'), pairs)]
    pallas_call x13 -> x17, Pallas kernels: 14.3 us -> 14.3 us  [the longest x8 5.34 us: inner(): call(functools.partial(inner_kernel, step, sections, tiles, range(at, at...]
  transfers between devices with their start and end apart: 22 -> 22, of which waited for: 11 -> 12; matrix products, arithmetic and copies ran while one was open for 0% -> 0% of each run, Pallas kernels for 15% -> 15%
where the time goes in v4:
time: 68.9 us; the launch traced here: 68 us
  waiting for transfers between devices  27.9 us (40%)
  starting transfers between devices  24.9 us (36%)
  Pallas kernels  14.3 us (21%)
  between operations  0.93 us (1%)
    ppermute x22, waiting for transfers between devices, move(): return lax.ppermute(x, ('depth', 'lat'), pairs)  27.9 us
    ppermute x22, starting transfers between devices, move(): return lax.ppermute(x, ('depth', 'lat'), pairs)  24.9 us
    pallas_call x8, Pallas kernels, inner(): call(functools.partial(inner_kernel, step, sections, tiles, range(at, at...  5.34 us
    pallas_call x5, Pallas kernels, outer(): call(functools.partial(outer_kernel, step, sections, lats, tiles, shots,...  3.22 us
    pallas_call x1, Pallas kernels, shards(): call(functools.partial(pack_kernel, tiles, band), out_shape=jax.ShapeDtyp...  2.95 us
    pallas_call x1, Pallas kernels, shards(): call(functools.partial(prep_kernel, tiles, shots, sections), out_shape=[f...  1.76 us
  transfers between devices with their start and end apart: 22, of which 12 were waited for; matrix products, arithmetic and copies ran while one was open for 0% of the time, Pallas kernels for 15%

profile of v4, /device:TPU:1, one launch (start us, length us, event | category | flops | bytes accessed | tf_op | source)
XLA Modules:
  0.0 68.0 jit_solution(7706331424255503583)
XLA Ops:
  0.6 1.8 %shard_map.87 = (f32[648,128]{1,0:T(8,128)S(1)}, f32[640,128]{1,0:T(8,128)S(1)}) custom-call(s32[64]{0:T(128)} %assign_at.1, f32[1,640]{1,0:T(1,128)} %refl_at.1, f32[1,640,128]{2,1,0:T(8,128)} %up_at.1, f32[1,640,128]{2,1,0:T(8,128)} %down_at.1, f32[640,128]{1,0:T(8,128)} %src_at.1), custom_call_target="tpu_custom_call" | custom-call | flops 10000000 | bytes 1638400 | tf_op jit(solution)/shard_map/pallas_call | solution.py:335
  2.5 2.7 %collective-permute-start.1 = (f32[648,128]{1,0:T(8,128)S(1)}, f32[648,128]{1,0:T(8,128)S(1)}, u32[]{:S(2)}, u32[]{:S(2)}) collective-permute-start(f32[648,128]{1,0:T(8,128)S(1)} %get-tuple-element.16.refs_0_), channel_id=1, source_target_pairs={{0,8},{1,2},{2,1},{3,4},{4,3},{5,6},{6,5},{7,15},{8,0},{9,10},{10,... | collective-permute-start | bytes 995336 | tf_op jit(solution)/shard_map/ppermute | solution.py:311
  5.2 3.0 %shard_map.86.packed = bf16[5,11,256,256]{3,2,1,0:T(8,128)(2,1)S(1)} custom-call(s32[1,5]{1,0:T(1,128)} %shift_at.1, f32[1,5,9,256,128]{4,3,2,1,0:T(8,128)} %tiles_at.1), custom_call_target="tpu_custom_call" | custom-call | flops 10000000 | bytes 11796480 | tf_op jit(solution)/shard_map/pallas_call | solution.py:352
  8.2 1.7 %shard_map.88.total = f32[5,256,128]{2,1,0:T(8,128)S(1)} custom-call(bf16[5,11,256,256]{3,2,1,0:T(8,128)(2,1)S(1)} %shard_map.86.packed, f32[648,128]{1,0:T(8,128)S(1)} %get-tuple-element.16.refs_0_, f32[648,128]{1,0:T(8,128)S(1)} %collective-permute-done.refs_1_), custom_call_target="tpu_custom_call" | custom-call | flops 1342177280 | bytes 8388608 | tf_op jit(solution)/shard_map/pallas_call | solution.py:374
  10.9 1.6 %collective-permute-start.3 = (f32[384,128]{1,0:T(8,128)S(1)}, f32[384,128]{1,0:T(8,128)S(1)}, u32[]{:S(2)}, u32[]{:S(2)}) collective-permute-start(f32[384,128]{1,0:T(8,128)S(1)} %get-tuple-element.18.refs_3_.refs_0_), channel_id=1, source_target_pairs={{0,8},{1,9},{2,10},{3,11},{4,12},{5,13},{6,14},{7,15},{8,0},{9,1},... | collective-permute-start | bytes 589832 | tf_op jit(solution)/shard_map/ppermute | solution.py:311
  12.6 5.4 %collective-permute-done.3.refs_0_ = f32[384,128]{1,0:T(8,128)S(1)} collective-permute-done((f32[384,128]{1,0:T(8,128)S(1)}, f32[384,128]{1,0:T(8,128)S(1)}, u32[]{:S(2)}, u32[]{:S(2)}) %collective-permute-start.3) | collective-permute-done | bytes 196640 | tf_op jit(solution)/shard_map/ppermute | solution.py:311
  18.3 2.4 %collective-permute-done.2.refs_0_ = f32[256,128]{1,0:T(8,128)S(1)} collective-permute-done((f32[256,128]{1,0:T(8,128)S(1)}, f32[256,128]{1,0:T(8,128)S(1)}, u32[]{:S(2)}, u32[]{:S(2)}) %collective-permute-start.2) | collective-permute-done | bytes 131104 | tf_op jit(solution)/shard_map/ppermute | solution.py:311
  21.6 2.0 %collective-permute-start.7 = (f32[256,128]{1,0:T(8,128)S(1)}, f32[256,128]{1,0:T(8,128)S(1)}, u32[]{:S(2)}, u32[]{:S(2)}) collective-permute-start(f32[256,128]{1,0:T(8,128)S(1)} %collective-permute-done.2.refs_0_), channel_id=1, source_target_pairs={{0,8},{1,2},{2,1},{3,4},{4,3},{5,6},{6,5},{7,15},{8,0},{9,10},{10,... | collective-permute-start | bytes 393224 | tf_op jit(solution)/shard_map/ppermute | solution.py:311
  23.7 1.7 %collective-permute-start.15 = (f32[640,128]{1,0:T(8,128)S(1)}, f32[640,128]{1,0:T(8,128)S(1)}, u32[]{:S(2)}, u32[]{:S(2)}) collective-permute-start(f32[640,128]{1,0:T(8,128)S(1)} %get-tuple-element.25.refs_0_), channel_id=1, source_target_pairs={{0,16},{1,2},{2,1},{3,4},{4,3},{5,6},{6,5},{7,23},{8,24},{9,10},{1... | collective-permute-start | bytes 983048 | tf_op jit(solution)/shard_map/ppermute | solution.py:311
  25.4 1.2 %collective-permute-done.7.refs_1_ = f32[256,128]{1,0:T(8,128)S(1)} collective-permute-done((f32[256,128]{1,0:T(8,128)S(1)}, f32[256,128]{1,0:T(8,128)S(1)}, u32[]{:S(2)}, u32[]{:S(2)}) %collective-permute-start.7) | collective-permute-done | bytes 131104 | tf_op jit(solution)/shard_map/ppermute | solution.py:311
  26.6 2.4 %collective-permute-done.6.refs_0_ = f32[384,128]{1,0:T(8,128)S(1)} collective-permute-done((f32[384,128]{1,0:T(8,128)S(1)}, f32[384,128]{1,0:T(8,128)S(1)}, u32[]{:S(2)}, u32[]{:S(2)}) %collective-permute-start.6) | collective-permute-done | bytes 196640 | tf_op jit(solution)/shard_map/ppermute | solution.py:311
  29.5 1.0 %collective-permute-done.9.refs_0_ = f32[384,128]{1,0:T(8,128)S(1)} collective-permute-done((f32[384,128]{1,0:T(8,128)S(1)}, f32[384,128]{1,0:T(8,128)S(1)}, u32[]{:S(2)}, u32[]{:S(2)}) %collective-permute-start.9) | collective-permute-done | bytes 196640 | tf_op jit(solution)/shard_map/ppermute | solution.py:311
  30.9 1.7 %shard_map.96.total = f32[5,256,128]{2,1,0:T(8,128)S(1)} custom-call(bf16[5,11,256,256]{3,2,1,0:T(8,128)(2,1)S(1)} %shard_map.86.packed, f32[640,128]{1,0:T(8,128)S(1)} %get-tuple-element.25.refs_0_, f32[640,128]{1,0:T(8,128)S(1)} %collective-permute-done.14.refs_1_), custom_call_target="tpu_custom_call" | custom-call | flops 1342177280 | bytes 8388608 | tf_op jit(solution)/shard_map/pallas_call | solution.py:374
  33.7 1.4 %collective-permute-start.13 = (f32[256,128]{1,0:T(8,128)S(1)}, f32[256,128]{1,0:T(8,128)S(1)}, u32[]{:S(2)}, u32[]{:S(2)}) collective-permute-start(f32[256,128]{1,0:T(8,128)S(1)} %collective-permute-done.8.refs_0_), channel_id=1, source_target_pairs={{0,8},{1,2},{2,1},{3,4},{4,3},{5,6},{6,5},{7,15},{8,0},{9,10},{10,... | collective-permute-start | bytes 393224 | tf_op jit(solution)/shard_map/ppermute | solution.py:311
  35.5 2.6 %collective-permute-done.13.refs_1_ = f32[256,128]{1,0:T(8,128)S(1)} collective-permute-done((f32[256,128]{1,0:T(8,128)S(1)}, f32[256,128]{1,0:T(8,128)S(1)}, u32[]{:S(2)}, u32[]{:S(2)}) %collective-permute-start.13) | collective-permute-done | bytes 131104 | tf_op jit(solution)/shard_map/ppermute | solution.py:311
  38.2 2.1 %collective-permute-done.12.refs_0_ = f32[384,128]{1,0:T(8,128)S(1)} collective-permute-done((f32[384,128]{1,0:T(8,128)S(1)}, f32[384,128]{1,0:T(8,128)S(1)}, u32[]{:S(2)}, u32[]{:S(2)}) %collective-permute-start.12) | collective-permute-done | bytes 196640 | tf_op jit(solution)/shard_map/ppermute | solution.py:311
  40.3 9.7 %collective-permute-start.17 = (f32[384,128]{1,0:T(8,128)S(1)}, f32[384,128]{1,0:T(8,128)S(1)}, u32[]{:S(2)}, u32[]{:S(2)}) collective-permute-start(f32[384,128]{1,0:T(8,128)S(1)} %get-tuple-element.27.refs_4_), channel_id=1, source_target_pairs={{0,8},{1,9},{2,10},{3,11},{4,12},{5,13},{6,14},{7,15},{8,0},{9,1},... | collective-permute-start | bytes 589832 | tf_op jit(solution)/shard_map/ppermute | solution.py:311
  50.1 5.3 %collective-permute-done.17.refs_0_ = f32[384,128]{1,0:T(8,128)S(1)} collective-permute-done((f32[384,128]{1,0:T(8,128)S(1)}, f32[384,128]{1,0:T(8,128)S(1)}, u32[]{:S(2)}, u32[]{:S(2)}) %collective-permute-start.17) | collective-permute-done | bytes 196640 | tf_op jit(solution)/shard_map/ppermute | solution.py:311
  56.0 2.2 %collective-permute-done.16.refs_0_ = f32[256,128]{1,0:T(8,128)S(1)} collective-permute-done((f32[256,128]{1,0:T(8,128)S(1)}, f32[256,128]{1,0:T(8,128)S(1)}, u32[]{:S(2)}, u32[]{:S(2)}) %collective-permute-start.16) | collective-permute-done | bytes 131104 | tf_op jit(solution)/shard_map/ppermute | solution.py:311
  59.4 1.2 %collective-permute-start.21 = (f32[256,128]{1,0:T(8,128)S(1)}, f32[256,128]{1,0:T(8,128)S(1)}, u32[]{:S(2)}, u32[]{:S(2)}) collective-permute-start(f32[256,128]{1,0:T(8,128)S(1)} %collective-permute-done.16.refs_0_), channel_id=1, source_target_pairs={{0,8},{1,2},{2,1},{3,4},{4,3},{5,6},{6,5},{7,15},{8,0},{9,10},{10,... | collective-permute-start | bytes 393224 | tf_op jit(solution)/shard_map/ppermute | solution.py:311
  62.0 1.2 %shard_map.100.total = f32[5,256,128]{2,1,0:T(8,128)S(1)} custom-call(bf16[5,11,256,256]{3,2,1,0:T(8,128)(2,1)S(1)} %shard_map.86.packed, f32[256,128]{1,0:T(8,128)S(1)} %collective-permute-done.16.refs_0_, f32[384,128]{1,0:T(8,128)S(1)} %collective-permute-done.18.refs_1_, f32[256,128]{1,0:T(8,128)S(1)} %collective-permute-done.19.refs_2_, ...), custom_call_target="tpu_custom_call" | custom-call | flops 1342177280 | bytes 8388608 | tf_op jit(solution)/shard_map/pallas_call | solution.py:374
  63.2 1.0 %collective-permute-done.21.refs_1_ = f32[256,128]{1,0:T(8,128)S(1)} collective-permute-done((f32[256,128]{1,0:T(8,128)S(1)}, f32[256,128]{1,0:T(8,128)S(1)}, u32[]{:S(2)}, u32[]{:S(2)}) %collective-permute-start.21) | collective-permute-done | bytes 131104 | tf_op jit(solution)/shard_map/ppermute | solution.py:311
  64.2 2.1 %collective-permute-done.20.refs_0_ = f32[384,128]{1,0:T(8,128)S(1)} collective-permute-done((f32[384,128]{1,0:T(8,128)S(1)}, f32[384,128]{1,0:T(8,128)S(1)}, u32[]{:S(2)}, u32[]{:S(2)}) %collective-permute-start.20) | collective-permute-done | bytes 196640 | tf_op jit(solution)/shard_map/ppermute | solution.py:311
  66.3 1.6 %shard_map.102 = (f32[1,640,128]{2,1,0:T(8,128)}, f32[1,640,128]{2,1,0:T(8,128)}) custom-call(bf16[5,11,256,256]{3,2,1,0:T(8,128)(2,1)S(1)} %shard_map.86.packed, f32[5,256,128]{2,1,0:T(8,128)S(1)} %shard_map.100.total, f32[384,128]{1,0:T(8,128)S(1)} %collective-permute-done.20.refs_0_, ...), custom_call_target="tpu_custom_call", output_to_operand_aliasing={{0}: (6, {}), {1}: (7, {})} | custom-call | flops 503316480 | bytes 4194304 | tf_op jit(solution)/shard_map/pallas_call | solution.py:397
  (37 shorter events, 8.0 us)
Async XLA Ops:
  2.4 5.8 %collective-permute-start = (f32[648,128]{1,0:T(8,128)S(1)}, f32[648,128]{1,0:T(8,128)S(1)}, u32[]{:S(2)}, u32[]{:S(2)}) collective-permute-start(f32[648,128]{1,0:T(8,128)S(1)} %get-tuple-element.16.refs_0_), channel_id=1, source_target_pairs={{0,1},{1,0},{2,3},{3,2},{4,5},{5,4},{6,7},{7,6},{8,9},{9,8},{10,11... | collective-permute-start | bytes 995336 | tf_op jit(solution)/shard_map/ppermute | solution.py:311
  2.5 7.5 %collective-permute-start.1 = (f32[648,128]{1,0:T(8,128)S(1)}, f32[648,128]{1,0:T(8,128)S(1)}, u32[]{:S(2)}, u32[]{:S(2)}) collective-permute-start(f32[648,128]{1,0:T(8,128)S(1)} %get-tuple-element.16.refs_0_), channel_id=1, source_target_pairs={{0,8},{1,2},{2,1},{3,4},{4,3},{5,6},{6,5},{7,15},{8,0},{9,10},{10,... | collective-permute-start | bytes 995336 | tf_op jit(solution)/shard_map/ppermute | solution.py:311
  10.9 7.1 %collective-permute-start.3 = (f32[384,128]{1,0:T(8,128)S(1)}, f32[384,128]{1,0:T(8,128)S(1)}, u32[]{:S(2)}, u32[]{:S(2)}) collective-permute-start(f32[384,128]{1,0:T(8,128)S(1)} %get-tuple-element.18.refs_3_.refs_0_), channel_id=1, source_target_pairs={{0,8},{1,9},{2,10},{3,11},{4,12},{5,13},{6,14},{7,15},{8,0},{9,1},... | collective-permute-start | bytes 589832 | tf_op jit(solution)/shard_map/ppermute | solution.py:311
  12.5 8.3 %collective-permute-start.2 = (f32[256,128]{1,0:T(8,128)S(1)}, f32[256,128]{1,0:T(8,128)S(1)}, u32[]{:S(2)}, u32[]{:S(2)}) collective-permute-start(f32[256,128]{1,0:T(8,128)S(1)} %get-tuple-element.17.refs_4_.refs_1_), channel_id=1, source_target_pairs={{0,8},{1,9},{2,10},{3,11},{4,12},{5,13},{6,14},{7,15},{8,0},{9,1},... | collective-permute-start | bytes 393224 | tf_op jit(solution)/shard_map/ppermute | solution.py:311
  18.0 7.4 %collective-permute-start.4 = (f32[384,128]{1,0:T(8,128)S(1)}, f32[384,128]{1,0:T(8,128)S(1)}, u32[]{:S(2)}, u32[]{:S(2)}) collective-permute-start(f32[384,128]{1,0:T(8,128)S(1)} %collective-permute-done.3.refs_0_), channel_id=1, source_target_pairs={{0,1},{1,0},{2,3},{3,2},{4,5},{5,4},{6,7},{7,6},{8,9},{9,8},{10,11... | collective-permute-start | bytes 589832 | tf_op jit(solution)/shard_map/ppermute | solution.py:311
  20.8 2.9 %collective-permute-start.5 = (f32[256,128]{1,0:T(8,128)S(1)}, f32[256,128]{1,0:T(8,128)S(1)}, u32[]{:S(2)}, u32[]{:S(2)}) collective-permute-start(f32[256,128]{1,0:T(8,128)S(1)} %collective-permute-done.2.refs_0_), channel_id=1, source_target_pairs={{0,1},{1,0},{2,3},{3,2},{4,5},{5,4},{6,7},{7,6},{8,9},{9,8},{10,11... | collective-permute-start | bytes 393224 | tf_op jit(solution)/shard_map/ppermute | solution.py:311
  21.2 9.8 %collective-permute-start.14 = (f32[640,128]{1,0:T(8,128)S(1)}, f32[640,128]{1,0:T(8,128)S(1)}, u32[]{:S(2)}, u32[]{:S(2)}) collective-permute-start(f32[640,128]{1,0:T(8,128)S(1)} %get-tuple-element.25.refs_0_), channel_id=1, source_target_pairs={{0,1},{1,0},{2,3},{3,2},{4,5},{5,4},{6,7},{7,6},{8,9},{9,8},{10,11... | collective-permute-start | bytes 983048 | tf_op jit(solution)/shard_map/ppermute | solution.py:311
  21.6 5.0 %collective-permute-start.7 = (f32[256,128]{1,0:T(8,128)S(1)}, f32[256,128]{1,0:T(8,128)S(1)}, u32[]{:S(2)}, u32[]{:S(2)}) collective-permute-start(f32[256,128]{1,0:T(8,128)S(1)} %collective-permute-done.2.refs_0_), channel_id=1, source_target_pairs={{0,8},{1,2},{2,1},{3,4},{4,3},{5,6},{6,5},{7,15},{8,0},{9,10},{10,... | collective-permute-start | bytes 393224 | tf_op jit(solution)/shard_map/ppermute | solution.py:311
  23.6 5.4 %collective-permute-start.6 = (f32[384,128]{1,0:T(8,128)S(1)}, f32[384,128]{1,0:T(8,128)S(1)}, u32[]{:S(2)}, u32[]{:S(2)}) collective-permute-start(f32[384,128]{1,0:T(8,128)S(1)} %collective-permute-done.3.refs_0_), channel_id=1, source_target_pairs={{0,8},{1,2},{2,1},{3,4},{4,3},{5,6},{6,5},{7,15},{8,0},{9,10},{10,... | collective-permute-start | bytes 589832 | tf_op jit(solution)/shard_map/ppermute | solution.py:311
  23.7 9.2 %collective-permute-start.15 = (f32[640,128]{1,0:T(8,128)S(1)}, f32[640,128]{1,0:T(8,128)S(1)}, u32[]{:S(2)}, u32[]{:S(2)}) collective-permute-start(f32[640,128]{1,0:T(8,128)S(1)} %get-tuple-element.25.refs_0_), channel_id=1, source_target_pairs={{0,16},{1,2},{2,1},{3,4},{4,3},{5,6},{6,5},{7,23},{8,24},{9,10},{1... | collective-permute-start | bytes 983048 | tf_op jit(solution)/shard_map/ppermute | solution.py:311
  29.0 1.5 %collective-permute-start.9 = (f32[384,128]{1,0:T(8,128)S(1)}, f32[384,128]{1,0:T(8,128)S(1)}, u32[]{:S(2)}, u32[]{:S(2)}) collective-permute-start(f32[384,128]{1,0:T(8,128)S(1)} %get-tuple-element.23.refs_2_), channel_id=1, source_target_pairs={{0,1},{1,0},{2,3},{3,2},{4,5},{5,4},{6,7},{7,6},{8,16},{9,17},{10,... | collective-permute-start | bytes 589832 | tf_op jit(solution)/shard_map/ppermute | solution.py:311
  29.5 3.1 %collective-permute-start.8 = (f32[256,128]{1,0:T(8,128)S(1)}, f32[256,128]{1,0:T(8,128)S(1)}, u32[]{:S(2)}, u32[]{:S(2)}) collective-permute-start(f32[256,128]{1,0:T(8,128)S(1)} %get-tuple-element.22.refs_3_), channel_id=1, source_target_pairs={{0,1},{1,0},{2,3},{3,2},{4,5},{5,4},{6,7},{7,6},{8,16},{9,17},{10,... | collective-permute-start | bytes 393224 | tf_op jit(solution)/shard_map/ppermute | solution.py:311
  30.6 5.0 %collective-permute-start.10 = (f32[384,128]{1,0:T(8,128)S(1)}, f32[384,128]{1,0:T(8,128)S(1)}, u32[]{:S(2)}, u32[]{:S(2)}) collective-permute-start(f32[384,128]{1,0:T(8,128)S(1)} %collective-permute-done.9.refs_0_), channel_id=1, source_target_pairs={{0,1},{1,0},{2,3},{3,2},{4,5},{5,4},{6,7},{7,6},{8,9},{9,8},{10,11... | collective-permute-start | bytes 589832 | tf_op jit(solution)/shard_map/ppermute | solution.py:311
  32.6 2.9 %collective-permute-start.11 = (f32[256,128]{1,0:T(8,128)S(1)}, f32[256,128]{1,0:T(8,128)S(1)}, u32[]{:S(2)}, u32[]{:S(2)}) collective-permute-start(f32[256,128]{1,0:T(8,128)S(1)} %collective-permute-done.8.refs_0_), channel_id=1, source_target_pairs={{0,1},{1,0},{2,3},{3,2},{4,5},{5,4},{6,7},{7,6},{8,9},{9,8},{10,11... | collective-permute-start | bytes 393224 | tf_op jit(solution)/shard_map/ppermute | solution.py:311
  33.7 4.5 %collective-permute-start.13 = (f32[256,128]{1,0:T(8,128)S(1)}, f32[256,128]{1,0:T(8,128)S(1)}, u32[]{:S(2)}, u32[]{:S(2)}) collective-permute-start(f32[256,128]{1,0:T(8,128)S(1)} %collective-permute-done.8.refs_0_), channel_id=1, source_target_pairs={{0,8},{1,2},{2,1},{3,4},{4,3},{5,6},{6,5},{7,15},{8,0},{9,10},{10,... | collective-permute-start | bytes 393224 | tf_op jit(solution)/shard_map/ppermute | solution.py:311
  35.1 5.2 %collective-permute-start.12 = (f32[384,128]{1,0:T(8,128)S(1)}, f32[384,128]{1,0:T(8,128)S(1)}, u32[]{:S(2)}, u32[]{:S(2)}) collective-permute-start(f32[384,128]{1,0:T(8,128)S(1)} %collective-permute-done.9.refs_0_), channel_id=1, source_target_pairs={{0,8},{1,2},{2,1},{3,4},{4,3},{5,6},{6,5},{7,15},{8,0},{9,10},{10,... | collective-permute-start | bytes 589832 | tf_op jit(solution)/shard_map/ppermute | solution.py:311
  40.3 15.1 %collective-permute-start.17 = (f32[384,128]{1,0:T(8,128)S(1)}, f32[384,128]{1,0:T(8,128)S(1)}, u32[]{:S(2)}, u32[]{:S(2)}) collective-permute-start(f32[384,128]{1,0:T(8,128)S(1)} %get-tuple-element.27.refs_4_), channel_id=1, source_target_pairs={{0,8},{1,9},{2,10},{3,11},{4,12},{5,13},{6,14},{7,15},{8,0},{9,1},... | collective-permute-start | bytes 589832 | tf_op jit(solution)/shard_map/ppermute | solution.py:311
  50.0 8.2 %collective-permute-start.16 = (f32[256,128]{1,0:T(8,128)S(1)}, f32[256,128]{1,0:T(8,128)S(1)}, u32[]{:S(2)}, u32[]{:S(2)}) collective-permute-start(f32[256,128]{1,0:T(8,128)S(1)} %get-tuple-element.26.refs_5_), channel_id=1, source_target_pairs={{0,8},{1,9},{2,10},{3,11},{4,12},{5,13},{6,14},{7,15},{8,0},{9,1},... | collective-permute-start | bytes 393224 | tf_op jit(solution)/shard_map/ppermute | solution.py:311
  55.4 6.6 %collective-permute-start.18 = (f32[384,128]{1,0:T(8,128)S(1)}, f32[384,128]{1,0:T(8,128)S(1)}, u32[]{:S(2)}, u32[]{:S(2)}) collective-permute-start(f32[384,128]{1,0:T(8,128)S(1)} %collective-permute-done.17.refs_0_), channel_id=1, source_target_pairs={{0,1},{1,0},{2,3},{3,2},{4,5},{5,4},{6,7},{7,6},{8,9},{9,8},{10,11... | collective-permute-start | bytes 589832 | tf_op jit(solution)/shard_map/ppermute | solution.py:311
  58.2 3.8 %collective-permute-start.19 = (f32[256,128]{1,0:T(8,128)S(1)}, f32[256,128]{1,0:T(8,128)S(1)}, u32[]{:S(2)}, u32[]{:S(2)}) collective-permute-start(f32[256,128]{1,0:T(8,128)S(1)} %collective-permute-done.16.refs_0_), channel_id=1, source_target_pairs={{0,1},{1,0},{2,3},{3,2},{4,5},{5,4},{6,7},{7,6},{8,9},{9,8},{10,11... | collective-permute-start | bytes 393224 | tf_op jit(solution)/shard_map/ppermute | solution.py:311
  59.4 4.8 %collective-permute-start.21 = (f32[256,128]{1,0:T(8,128)S(1)}, f32[256,128]{1,0:T(8,128)S(1)}, u32[]{:S(2)}, u32[]{:S(2)}) collective-permute-start(f32[256,128]{1,0:T(8,128)S(1)} %collective-permute-done.16.refs_0_), channel_id=1, source_target_pairs={{0,8},{1,2},{2,1},{3,4},{4,3},{5,6},{6,5},{7,15},{8,0},{9,10},{10,... | collective-permute-start | bytes 393224 | tf_op jit(solution)/shard_map/ppermute | solution.py:311
  60.7 5.6 %collective-permute-start.20 = (f32[384,128]{1,0:T(8,128)S(1)}, f32[384,128]{1,0:T(8,128)S(1)}, u32[]{:S(2)}, u32[]{:S(2)}) collective-permute-start(f32[384,128]{1,0:T(8,128)S(1)} %collective-permute-done.17.refs_0_), channel_id=1, source_target_pairs={{0,8},{1,2},{2,1},{3,4},{4,3},{5,6},{6,5},{7,15},{8,0},{9,10},{10,... | collective-permute-start | bytes 589832 | tf_op jit(solution)/shard_map/ppermute | solution.py:311

commit v5 on v4

v5 whole, which is shorter than its diff:
```python
import functools

import jax
import jax.numpy as jnp
from jax import lax
from jax.experimental import pallas as pl
from jax.experimental.pallas import tpu as pltpu
from jax.sharding import PartitionSpec as P


TILE = 128
HALF = TILE // 2
VMEM = pltpu.VMEM
LIMIT = 16 * 2**20
STREAMS = 2


def spec(space):
    return pl.BlockSpec(memory_space=space)


def f32(*shape):
    return jax.ShapeDtypeStruct(shape, jnp.float32)


def call(kernel, **kwargs):
    return pl.pallas_call(kernel, **kwargs)


def params(limit=LIMIT):
    return pltpu.CompilerParams(vmem_limit_bytes=limit)


def cost(flops, read):
    return pl.CostEstimate(flops=flops, bytes_accessed=read, transcendentals=0)


def in_hbm(x):
    return pltpu.with_memory_space_constraint(x, pltpu.HBM)


def rows_of(t):
    return slice(t * TILE, (t + 1) * TILE)


def down_column(row):
    return jnp.transpose(jnp.broadcast_to(row, (TILE, TILE)))


def split(value):
    high = value.astype(jnp.bfloat16)
    low = (value - high.astype(jnp.float32)).astype(jnp.bfloat16)
    return high, low


def prep_kernel(tiles, shots, sections, assign_at, refl_at, up_at, down_at, src_at, first, second, assign, refl, up, down, src, sems):
    depth = lax.axis_index("depth")
    loads = [
        pltpu.make_async_copy(assign_at, assign, sems.at[0]),
        pltpu.make_async_copy(refl_at, refl, sems.at[1]),
        pltpu.make_async_copy(up_at, up, sems.at[2]),
        pltpu.make_async_copy(down_at, down, sems.at[3]),
        pltpu.make_async_copy(src_at, src, sems.at[4]),
    ]
    for load in loads:
        load.start()
    for load in loads:
        load.wait()
    descends = depth < sections // 2

    def write(of_up, of_down):
        for j in range(tiles):
            row = refl[0:1, rows_of(j)]
            r = down_column(row)
            of_up[rows_of(j)] = -(r * up[0, rows_of(j)])
            of_down[rows_of(j)] = r * down[0, rows_of(j)]
            first[tiles * TILE + j : tiles * TILE + j + 1] = row

    @pl.when(descends)
    def _():
        write(first, second)

    @pl.when(jnp.logical_not(descends))
    def _():
        write(second, first)

    @pl.when(depth == 0)
    def _():
        lane = lax.broadcasted_iota(jnp.int32, (8, TILE), 1)
        wanted = jnp.zeros((8, TILE), jnp.int32)
        for b in range(TILE // (2 * shots)):
            for i in range(shots):
                shot = assign[b * shots + i]
                at = b * 2 * shots + i
                wanted = jnp.where(lane == at, shot, wanted)
                wanted = jnp.where(lane == at + shots, shot + TILE // 2, wanted)
        source = lax.broadcasted_iota(jnp.int32, (TILE, TILE), 0)
        pick = (source == jnp.broadcast_to(wanted[0:1], (TILE, TILE))).astype(jnp.float32).astype(jnp.bfloat16)
        for j in range(tiles):
            x = src[rows_of(j)]
            high = x.astype(jnp.bfloat16)
            mid, low = split(x - high.astype(jnp.float32))
            entering = jnp.dot(low, pick, preferred_element_type=jnp.float32)
            entering += jnp.dot(mid, pick, preferred_element_type=jnp.float32)
            entering += jnp.dot(high, pick, preferred_element_type=jnp.float32)
            r = down_column(refl[0:1, rows_of(j)])
            first[rows_of(j)] = (1.0 + r) * entering + first[rows_of(j)]


def pack_kernel(tiles, band, shift_at, tiles_at, out, shift, held, sems):
    loads = [pltpu.make_async_copy(shift_at, shift, sems.at[tiles])]
    loads += [pltpu.make_async_copy(tiles_at.at[0, j], held.at[j], sems.at[j]) for j in range(tiles)]
    for load in loads:
        load.start()
    loads[0].wait()
    for j in range(tiles):
        loads[1 + j].wait()
        move = shift[0, j]
        for k in range(band):
            high, low = split(held[j, k])
            slot = k + 1 + move
            out[j, slot, :, :TILE] = high
            out[j, slot, :, TILE:] = low
        zero = jnp.zeros(out.shape[2:], jnp.bfloat16)
        out[j, jnp.where(move >= 0, 0, band)] = zero
        out[j, jnp.where(move <= 0, band + 1, 1)] = zero


def doubled(tile):
    high, low = split(tile)
    line = jnp.concatenate([high, low], axis=1)
    return jnp.concatenate([line, line], axis=0)


def folded(value):
    return value[:, :TILE] + value[:, TILE:]


def lanes(rows):
    return lax.broadcasted_iota(jnp.int32, (rows, TILE), 1)


def turned(value):
    return pltpu.roll(value, HALF, 1)


def left_half(rows):
    return lanes(rows) < HALF


def halves_of(t):
    return slice(t * HALF, (t + 1) * HALF)


def unpack_tile(chunk, t):
    part = chunk[halves_of(t)]
    return jnp.concatenate([part, turned(part)], axis=0)


def stream_line(tile):
    rest = tile - tile.astype(jnp.bfloat16).astype(jnp.float32)
    line = jnp.where(left_half(TILE), tile, turned(rest)).astype(jnp.bfloat16)
    return jnp.concatenate([line, line], axis=0)


def merged(first, second):
    left = left_half(HALF)
    upper = jnp.where(left, first, turned(second))
    lower = jnp.where(left, turned(first), second)
    return jnp.concatenate([upper, lower], axis=0)


def parted(value):
    upper, lower = value[:HALF], value[HALF:]
    left = left_half(HALF)
    return jnp.where(left, upper, turned(lower)), jnp.where(left, turned(upper), lower)


def spread(field, scale, sign, tiles, narrow, mirrored, held):
    for t in range(tiles):
        tile = unpack_tile(field, t) if narrow else field[rows_of(t)]
        if scale is not None:
            tile = tile * (1.0 + sign * scale[t])
        at = 2 * t * TILE
        if mirrored is not None:
            at = pl.multiple_of(jnp.where(mirrored, 2 * (tiles - 1 - t) * TILE, at), 2 * TILE)
        held[pl.ds(at, 2 * TILE)] = stream_line(tile) if narrow else doubled(tile)


def product(packed, held, j, slots, narrow):
    value = jnp.dot(
        jnp.concatenate([packed[j, slot] for slot in slots], axis=1),
        held[: 2 * len(slots) * TILE],
        preferred_element_type=jnp.float32,
    )
    return value if narrow else folded(value)


def side_product(packed, held, tiles, jj, low_side, narrow):
    j = jnp.where(low_side, tiles - 1 - jj, jj)
    slots = [jnp.where(low_side, jj - t, 2 * tiles + t - jj) for t in range(jj + 1)]
    return j, product(packed, held, j, slots, narrow)


def when_active(step, sections, body):
    depth = lax.axis_index("depth")
    if step:
        pl.when((depth == step) | (depth == sections - 1 - step))(body)
    else:
        body()


def combined(value, shots):
    by_imag = value[TILE:]
    ahead = pltpu.roll(by_imag, TILE - shots, 1)
    behind = pltpu.roll(by_imag, shots, 1)
    return value[:TILE] + jnp.where(lax.rem(lanes(TILE), 2 * shots) < shots, -ahead, behind)


def scale_kernel(tiles, *refs):
    for source, out in zip(refs[:3], refs[3:]):
        for t in range(tiles):
            at = tiles * TILE + t
            out[t] = down_column(source[at : at + 1])


def inner_kernel(step, sections, tiles, packed, own, near, *refs):
    narrow = bool(step)
    scale, near_scale = refs[:2] if narrow else (None, None)
    total, held_own, held_near = refs[-3:]

    def body():
        sign = jnp.where(lax.axis_index("depth") == (step or 0), 1.0, -1.0)
        low_side = lax.rem(lax.axis_index("lat"), 2) == 1
        spread(own, scale, sign, tiles, narrow, None, held_own)
        spread(near, near_scale, sign, tiles, narrow, low_side, held_near)
        for j in range(tiles):
            total[j] = product(packed, held_own, j, range(tiles - j, 2 * tiles - j), narrow)
        for jj in range(tiles):
            j, value = side_product(packed, held_near, tiles, jj, low_side, narrow)
            total[j] = total[j] + value

    when_active(step, sections, body)


def outer_kernel(step, sections, lats, tiles, shots, ends, packed, total, far, *refs):
    narrow = bool(step)
    scale, base, other = None, None, None
    if narrow:
        (scale, base), refs = refs[:2], refs[2:]
    if ends:
        other, _, _, result_down, result_up, held, leaving, sems = refs
    else:
        outs, held = refs[:-1], refs[-1]
    lat = lax.axis_index("lat")
    depth = lax.axis_index("depth")
    low_side = lax.rem(lat, 2) == 0
    has_far = (lat > 0) & (lat < lats - 1)

    def body():
        sign = jnp.where(depth == (step or 0), 1.0, -1.0)

        def finish(j, value):
            at = pl.ds(pl.multiple_of(j * HALF, HALF), HALF)
            if not narrow:
                for out, part in zip(outs, parted(combined(value, shots))):
                    out[at] = part
                return
            value = combined(value + turned(value), shots)
            part = jnp.where(left_half(HALF), value[:HALF], value[HALF:]) + base[at]
            if ends:
                leaving[pl.ds(pl.multiple_of(j * TILE, TILE), TILE)] = merged(other[at], part)
            else:
                outs[0][at] = part

        @pl.when(has_far)
        def _():
            spread(far, scale, sign, tiles, narrow, low_side, held)
            for jj in range(tiles):
                j, value = side_product(packed, held, tiles, jj, low_side, narrow)
                finish(j, total[j] + value)

        @pl.when(jnp.logical_not(has_far))
        def _():
            for j in range(tiles):
                finish(j, total[j])

        if ends:

            def leave(result):
                copy = pltpu.make_async_copy(leaving, result.at[0], sems)
                copy.start()
                copy.wait()

            pl.when(depth == step)(lambda: leave(result_down))
            pl.when(depth != step)(lambda: leave(result_up))

    when_active(step, sections, body)


def keep_kernel(sections, tiles, *refs):
    fields, (result_down, result_up, whole, sems) = refs[:-4], refs[-4:]
    depth = lax.axis_index("depth")

    def put(first, second, result):
        for j in range(tiles):
            whole[rows_of(j)] = merged(first[halves_of(j)], second[halves_of(j)])
        copy = pltpu.make_async_copy(whole, result.at[0], sems)
        copy.start()
        copy.wait()

    for step in range(sections - 1):
        first, second = fields[2 * step : 2 * step + 2]
        pl.when(depth == step)(functools.partial(put, first, second, result_down))
        pl.when(depth == sections - 1 - step)(functools.partial(put, first, second, result_up))


def shards(sections, lats, operator, band_shift, reflectivity, up_stored, down_stored, sources, assignment):
    tiles, band = operator.shape[1], operator.shape[2]
    _, columns = sources.shape
    shots = columns // 4
    rows = tiles * TILE
    if sections % 2 or lats % 2 or tiles != band // 2 + 1 or columns != TILE:
        raise ValueError("unsupported sizes")

    def move(x, partner):
        pairs = []
        for d in range(sections):
            for l in range(lats):
                e, m = partner(d, l)
                pairs.append((d * lats + l, e * lats + m))
        return lax.ppermute(x, ("depth", "lat"), pairs)

    def near_of(d, l):
        return d, l ^ 1

    def far_of(spare, d, l):
        m = l + 1 if l % 2 else l - 1
        return (d, m) if 0 <= m < lats else (spare(d), l)

    def across(step, d, l):
        for low in (step, sections - 2 - step):
            if d == low:
                return low + 1, l
            if d == low + 1:
                return low, l
        return near_of(d, l)

    def halo(field, spare):
        near = move(field, near_of)
        return near, move(field, functools.partial(far_of, spare))

    def next_door(d):
        return d ^ 1

    first, second = call(
        functools.partial(prep_kernel, tiles, shots, sections),
        out_shape=[f32(rows + 8, columns), f32(rows, columns)],
        in_specs=[spec(pltpu.HBM)] * 5,
        out_specs=[spec(VMEM)] * 2,
        scratch_shapes=[
            pltpu.SMEM(assignment.shape, jnp.int32),
            VMEM(reflectivity.shape, jnp.float32),
            VMEM(up_stored.shape, jnp.float32),
            VMEM(down_stored.shape, jnp.float32),
            VMEM(sources.shape, jnp.float32),
            pltpu.SemaphoreType.DMA((5,)),
        ],
        compiler_params=params(),
        cost_estimate=cost(10**7, 5 * rows * columns * 4),
    )(*map(in_hbm, (assignment, reflectivity, up_stored, down_stored, sources)))

    packed = call(
        functools.partial(pack_kernel, tiles, band),
        out_shape=jax.ShapeDtypeStruct((tiles, band + 2, 2 * TILE, 2 * TILE), jnp.bfloat16),
        in_specs=[spec(pltpu.HBM)] * 2,
        out_specs=spec(VMEM),
        scratch_shapes=[
            pltpu.SMEM(band_shift.shape, jnp.int32),
            VMEM(operator.shape[1:], jnp.float32),
            pltpu.SemaphoreType.DMA((tiles + 1,)),
        ],
        compiler_params=params(),
        cost_estimate=cost(10**7, 2 * operator.size * 4),
    )(in_hbm(band_shift), in_hbm(operator))

    square = f32(tiles, TILE, columns)
    half = f32(rows // STREAMS, columns)
    result = [f32(1, rows, columns)] * 2

    def held(step):
        return VMEM((tiles * 2 * TILE, TILE if step else 2 * TILE), jnp.bfloat16)

    def inner(step, own, near, *scales):
        args = [packed, own, near, *scales]
        return call(
            functools.partial(inner_kernel, step, sections, tiles),
            out_shape=f32(tiles, 2 * TILE, columns),
            in_specs=[spec(VMEM)] * len(args),
            out_specs=spec(VMEM),
            scratch_shapes=[held(step)] * 2,
            compiler_params=params(),
            cost_estimate=cost(2 * 40 * 256**3, 8 * 2**20),
        )(*args)

    def outer(step, *args, shapes, kept=()):
        count = len(args) + 1
        ends = bool(kept)
        scratch = [held(step)]
        if ends:
            scratch += [VMEM((rows, columns), jnp.float32), pltpu.SemaphoreType.DMA(())]
        return call(
            functools.partial(outer_kernel, step, sections, lats, tiles, shots, ends),
            out_shape=shapes,
            in_specs=[spec(VMEM)] * count + [spec(pl.ANY)] * len(kept),
            out_specs=[spec(pl.ANY if ends else VMEM)] * len(shapes),
            scratch_shapes=scratch,
            input_output_aliases={count: 0, count + 1: 1} if ends else {},
            compiler_params=params(),
            cost_estimate=cost(2 * 15 * 256**3, 4 * 2**20),
        )(packed, *args, *kept)

    def cross(step, field):
        return [move(part, functools.partial(across, step)) for part in field]

    first_near, first_far = halo(first, next_door)
    total = inner(0, first, first_near)
    fields = [outer(0, total, first_far, shapes=[half] * STREAMS)]
    arrived = cross(0, fields[0])

    second, *_ = lax.optimization_barrier((second, *fields[0]))
    near, far = halo(second, lambda d: (d + sections // 2) % sections)
    own_scale, near_scale, far_scale = call(
        functools.partial(scale_kernel, tiles),
        out_shape=[square] * 3,
        in_specs=[spec(VMEM)] * 3,
        out_specs=[spec(VMEM)] * 3,
        compiler_params=params(),
        cost_estimate=cost(10**6, 4 * rows * columns * 4),
    )(first, first_near, first_far)
    total = inner(None, second, near)
    second_base = outer(None, total, far, shapes=[half] * STREAMS)

    for step in range(1, sections):
        bases = fields[0] if step < sections // 2 else second_base
        field = []
        for q in range(STREAMS):
            near, far = halo(arrived[q], next_door)
            total = inner(step, arrived[q], near, own_scale, near_scale)
            if step == sections - 1 and q == STREAMS - 1:
                kept = call(
                    functools.partial(keep_kernel, sections, tiles),
                    out_shape=result,
                    in_specs=[spec(VMEM)] * (len(fields) * STREAMS),
                    out_specs=[spec(pl.ANY)] * 2,
                    scratch_shapes=[VMEM((rows, columns), jnp.float32), pltpu.SemaphoreType.DMA(())],
                    compiler_params=params(),
                    cost_estimate=cost(0, 4 * rows * columns * 4),
                )(*[part for field_ in fields for part in field_])
                ended = outer(
                    step, total, far, far_scale, bases[q], field[0], shapes=result, kept=kept
                )
                return tuple(ended)
            (part,) = outer(step, total, far, far_scale, bases[q], shapes=[half])
            field.append(part)
        fields.append(field)
        arrived = cross(step, field)


def solution(mesh):
    return jax.shard_map(
        functools.partial(shards, mesh.shape["depth"], mesh.shape["lat"]),
        mesh=mesh,
        in_specs=(
            P("depth", "lat", None, None, None),
            P("depth", "lat"),
            P("depth", "lat"),
            P("depth", "lat", None),
            P("depth", "lat", None),
            P("lat", None),
            P(),
        ),
        out_specs=(P("depth", "lat", None), P("depth", "lat", None)),
        check_vma=False,
    )
```

time: 68.9 us -> 60 us (0.87)
  waiting for transfers between devices: 27.9 us -> 11.6 us
  starting transfers between devices: 24.9 us -> 28.8 us
  Pallas kernels: 14.3 us -> 17.8 us
    ppermute x22, waiting for transfers between devices: 27.9 us -> 11.6 us  [move(): return lax.ppermute(x, ('depth', 'lat'), pairs)]
    ppermute x22, starting transfers between devices: 24.9 us -> 28.8 us  [move(): return lax.ppermute(x, ('depth', 'lat'), pairs)]
    pallas_call x9, Pallas kernels: 6.08 us -> 7.83 us  [the longest x8 6.95 us: inner(): call(functools.partial(inner_kernel, step, sections, tiles), out_shape=f3...]
    pallas_call x5 -> x8, Pallas kernels: 3.22 us -> 4.9 us  [outer(): call(functools.partial(outer_kernel, step, sections, lats, tiles, shots,...]
  transfers between devices with their start and end apart: 22 -> 22, of which waited for: 12 -> 5; matrix products, arithmetic and copies ran while one was open for 0% -> 0% of each run, Pallas kernels for 15% -> 22%
where the time goes in v5:
time: 60 us; the launch traced here: 59.2 us
  starting transfers between devices  28.8 us (48%)
  Pallas kernels  17.8 us (30%)
  waiting for transfers between devices  11.6 us (19%)
  between operations  1.01 us (2%)
    ppermute x22, starting transfers between devices, move(): return lax.ppermute(x, ('depth', 'lat'), pairs)  28.8 us
    ppermute x22, waiting for transfers between devices, move(): return lax.ppermute(x, ('depth', 'lat'), pairs)  11.6 us
    pallas_call x8, Pallas kernels, inner(): call(functools.partial(inner_kernel, step, sections, tiles), out_shape=f3...  6.95 us
    pallas_call x8, Pallas kernels, outer(): call(functools.partial(outer_kernel, step, sections, lats, tiles, shots,...  4.9 us
    pallas_call x1, Pallas kernels, shards(): call(functools.partial(pack_kernel, tiles, band), out_shape=jax.ShapeDtyp...  2.95 us
    pallas_call x1, Pallas kernels, shards(): call(functools.partial(prep_kernel, tiles, shots, sections), out_shape=[f...  1.76 us
  transfers between devices with their start and end apart: 22, of which 5 were waited for; matrix products, arithmetic and copies ran while one was open for 0% of the time, Pallas kernels for 22%

profile of v5, /device:TPU:1, one launch (start us, length us, event | category | flops | bytes accessed | tf_op | source)
XLA Modules:
  0.0 59.2 jit_solution(4139960655347076857)
XLA Ops:
  0.6 1.8 %shard_map.87 = (f32[648,128]{1,0:T(8,128)S(1)}, f32[640,128]{1,0:T(8,128)S(1)}) custom-call(s32[64]{0:T(128)} %assign_at.1, f32[1,640]{1,0:T(1,128)} %refl_at.1, f32[1,640,128]{2,1,0:T(8,128)} %up_at.1, f32[1,640,128]{2,1,0:T(8,128)} %down_at.1, f32[640,128]{1,0:T(8,128)} %src_at.1), custom_call_target="tpu_custom_call" | custom-call | flops 10000000 | bytes 1638400 | tf_op jit(solution)/shard_map/pallas_call | solution.py:356
  2.5 2.7 %collective-permute-start.1 = (f32[648,128]{1,0:T(8,128)S(1)}, f32[648,128]{1,0:T(8,128)S(1)}, u32[]{:S(2)}, u32[]{:S(2)}) collective-permute-start(f32[648,128]{1,0:T(8,128)S(1)} %get-tuple-element.14.own.refs_0_), channel_id=1, source_target_pairs={{0,8},{1,2},{2,1},{3,4},{4,3},{5,6},{6,5},{7,15},{8,0},{9,10},{10,... | collective-permute-start | bytes 995336 | tf_op jit(solution)/shard_map/ppermute | solution.py:332
  5.2 3.0 %shard_map.86.packed = bf16[5,11,256,256]{3,2,1,0:T(8,128)(2,1)S(1)} custom-call(s32[1,5]{1,0:T(1,128)} %shift_at.1, f32[1,5,9,256,128]{4,3,2,1,0:T(8,128)} %tiles_at.1), custom_call_target="tpu_custom_call" | custom-call | flops 10000000 | bytes 11796480 | tf_op jit(solution)/shard_map/pallas_call | solution.py:373
  8.2 1.6 %shard_map.88.total = f32[5,256,128]{2,1,0:T(8,128)S(1)} custom-call(bf16[5,11,256,256]{3,2,1,0:T(8,128)(2,1)S(1)} %shard_map.86.packed, f32[648,128]{1,0:T(8,128)S(1)} %get-tuple-element.14.own.refs_0_, f32[648,128]{1,0:T(8,128)S(1)} %collective-permute-done.near.refs_1_), custom_call_target="tpu_custom_call" | custom-call | flops 1342177280 | bytes 8388608 | tf_op jit(solution)/shard_map/pallas_call | solution.py:396
  10.0 0.9 %shard_map.89 = (f32[320,128]{1,0:T(8,128)S(1)}, f32[320,128]{1,0:T(8,128)S(1)}) custom-call(bf16[5,11,256,256]{3,2,1,0:T(8,128)(2,1)S(1)} %shard_map.86.packed, f32[5,256,128]{2,1,0:T(8,128)S(1)} %shard_map.88.total, f32[648,128]{1,0:T(8,128)S(1)} %collective-permute-done.1.far.refs_2_), custom_call_target="tpu_custom_call" | custom-call | flops 503316480 | bytes 4194304 | tf_op jit(solution)/shard_map/pallas_call | solution.py:412
  11.0 1.6 %collective-permute-start.13 = (f32[320,128]{1,0:T(8,128)S(1)}, f32[320,128]{1,0:T(8,128)S(1)}, u32[]{:S(2)}, u32[]{:S(2)}) collective-permute-start(f32[320,128]{1,0:T(8,128)S(1)} %get-tuple-element.20.refs_1_.refs_0_), channel_id=1, source_target_pairs={{0,8},{1,9},{2,10},{3,11},{4,12},{5,13},{6,14},{7,15},{8,0},{9,1},... | collective-permute-start | bytes 491528 | tf_op jit(solution)/shard_map/ppermute | solution.py:332
  12.7 4.5 %collective-permute-done.13.own = f32[320,128]{1,0:T(8,128)S(1)} collective-permute-done((f32[320,128]{1,0:T(8,128)S(1)}, f32[320,128]{1,0:T(8,128)S(1)}, u32[]{:S(2)}, u32[]{:S(2)}) %collective-permute-start.13) | collective-permute-done | bytes 163872 | tf_op jit(solution)/shard_map/ppermute | solution.py:332
  17.9 1.9 %collective-permute-start.15 = (f32[320,128]{1,0:T(8,128)S(1)}, f32[320,128]{1,0:T(8,128)S(1)}, u32[]{:S(2)}, u32[]{:S(2)}) collective-permute-start(f32[320,128]{1,0:T(8,128)S(1)} %collective-permute-done.13.own), channel_id=1, source_target_pairs={{0,8},{1,2},{2,1},{3,4},{4,3},{5,6},{6,5},{7,15},{8,0},{9,10},{10,... | collective-permute-start | bytes 491528 | tf_op jit(solution)/shard_map/ppermute | solution.py:332
  20.0 1.6 %collective-permute-start.9 = (f32[640,128]{1,0:T(8,128)S(1)}, f32[640,128]{1,0:T(8,128)S(1)}, u32[]{:S(2)}, u32[]{:S(2)}) collective-permute-start(f32[640,128]{1,0:T(8,128)S(1)} %get-tuple-element.21.own), channel_id=1, source_target_pairs={{0,16},{1,2},{2,1},{3,4},{4,3},{5,6},{6,5},{7,23},{8,24},{9,10},{1... | collective-permute-start | bytes 983048 | tf_op jit(solution)/shard_map/ppermute | solution.py:332
  22.0 1.7 %collective-permute-start.4 = (f32[320,128]{1,0:T(8,128)S(1)}, f32[320,128]{1,0:T(8,128)S(1)}, u32[]{:S(2)}, u32[]{:S(2)}) collective-permute-start(f32[320,128]{1,0:T(8,128)S(1)} %collective-permute-done.2.own), channel_id=1, source_target_pairs={{0,8},{1,2},{2,1},{3,4},{4,3},{5,6},{6,5},{7,15},{8,0},{9,10},{10,... | collective-permute-start | bytes 491528 | tf_op jit(solution)/shard_map/ppermute | solution.py:332
  23.7 4.5 %collective-permute-done.4.far = f32[320,128]{1,0:T(8,128)S(1)} collective-permute-done((f32[320,128]{1,0:T(8,128)S(1)}, f32[320,128]{1,0:T(8,128)S(1)}, u32[]{:S(2)}, u32[]{:S(2)}) %collective-permute-start.4) | collective-permute-done | bytes 163872 | tf_op jit(solution)/shard_map/ppermute | solution.py:332
  28.7 1.6 %shard_map.94.total = f32[5,256,128]{2,1,0:T(8,128)S(1)} custom-call(bf16[5,11,256,256]{3,2,1,0:T(8,128)(2,1)S(1)} %shard_map.86.packed, f32[640,128]{1,0:T(8,128)S(1)} %get-tuple-element.21.own, f32[640,128]{1,0:T(8,128)S(1)} %collective-permute-done.8.near), custom_call_target="tpu_custom_call" | custom-call | flops 1342177280 | bytes 8388608 | tf_op jit(solution)/shard_map/pallas_call | solution.py:396
  30.4 1.8 %collective-permute-start.18 = (f32[320,128]{1,0:T(8,128)S(1)}, f32[320,128]{1,0:T(8,128)S(1)}, u32[]{:S(2)}, u32[]{:S(2)}) collective-permute-start(f32[320,128]{1,0:T(8,128)S(1)} %collective-permute-done.16.own), channel_id=1, source_target_pairs={{0,8},{1,2},{2,1},{3,4},{4,3},{5,6},{6,5},{7,15},{8,0},{9,10},{10,... | collective-permute-start | bytes 491528 | tf_op jit(solution)/shard_map/ppermute | solution.py:332
  32.1 0.9 %shard_map.95 = (f32[320,128]{1,0:T(8,128)S(1)}, f32[320,128]{1,0:T(8,128)S(1)}) custom-call(bf16[5,11,256,256]{3,2,1,0:T(8,128)(2,1)S(1)} %shard_map.86.packed, f32[5,256,128]{2,1,0:T(8,128)S(1)} %shard_map.94.total, f32[640,128]{1,0:T(8,128)S(1)} %collective-permute-done.9.far), custom_call_target="tpu_custom_call" | custom-call | flops 503316480 | bytes 4194304 | tf_op jit(solution)/shard_map/pallas_call | solution.py:412
  33.1 4.2 %collective-permute-start.6 = (f32[320,128]{1,0:T(8,128)S(1)}, f32[320,128]{1,0:T(8,128)S(1)}, u32[]{:S(2)}, u32[]{:S(2)}) collective-permute-start(f32[320,128]{1,0:T(8,128)S(1)} %collective-permute-done.5.own), channel_id=1, source_target_pairs={{0,1},{1,0},{2,3},{3,2},{4,5},{5,4},{6,7},{7,6},{8,9},{9,8},{10,11... | collective-permute-start | bytes 491528 | tf_op jit(solution)/shard_map/ppermute | solution.py:332
  37.3 5.5 %collective-permute-start.19 = (f32[320,128]{1,0:T(8,128)S(1)}, f32[320,128]{1,0:T(8,128)S(1)}, u32[]{:S(2)}, u32[]{:S(2)}) collective-permute-start(f32[320,128]{1,0:T(8,128)S(1)} %shard_map.101.refs_4_), channel_id=1, source_target_pairs={{0,8},{1,9},{2,10},{3,11},{4,12},{5,13},{6,14},{7,15},{8,0},{9,1},... | collective-permute-start | bytes 491528 | tf_op jit(solution)/shard_map/ppermute | solution.py:332
  42.9 2.9 %collective-permute-start.10 = (f32[320,128]{1,0:T(8,128)S(1)}, f32[320,128]{1,0:T(8,128)S(1)}, u32[]{:S(2)}, u32[]{:S(2)}) collective-permute-start(f32[320,128]{1,0:T(8,128)S(1)} %shard_map.96.refs_5_), channel_id=1, source_target_pairs={{0,8},{1,9},{2,10},{3,11},{4,12},{5,13},{6,14},{7,15},{8,0},{9,1},... | collective-permute-start | bytes 491528 | tf_op jit(solution)/shard_map/ppermute | solution.py:332
  45.8 1.8 %collective-permute-done.19.own = f32[320,128]{1,0:T(8,128)S(1)} collective-permute-done((f32[320,128]{1,0:T(8,128)S(1)}, f32[320,128]{1,0:T(8,128)S(1)}, u32[]{:S(2)}, u32[]{:S(2)}) %collective-permute-start.19) | collective-permute-done | bytes 163872 | tf_op jit(solution)/shard_map/ppermute | solution.py:332
  47.6 1.6 %collective-permute-start.21 = (f32[320,128]{1,0:T(8,128)S(1)}, f32[320,128]{1,0:T(8,128)S(1)}, u32[]{:S(2)}, u32[]{:S(2)}) collective-permute-start(f32[320,128]{1,0:T(8,128)S(1)} %collective-permute-done.19.own), channel_id=1, source_target_pairs={{0,8},{1,2},{2,1},{3,4},{4,3},{5,6},{6,5},{7,15},{8,0},{9,10},{10,... | collective-permute-start | bytes 491528 | tf_op jit(solution)/shard_map/ppermute | solution.py:332
  51.0 1.2 %collective-permute-start.12 = (f32[320,128]{1,0:T(8,128)S(1)}, f32[320,128]{1,0:T(8,128)S(1)}, u32[]{:S(2)}, u32[]{:S(2)}) collective-permute-start(f32[320,128]{1,0:T(8,128)S(1)} %collective-permute-done.10.own), channel_id=1, source_target_pairs={{0,8},{1,2},{2,1},{3,4},{4,3},{5,6},{6,5},{7,15},{8,0},{9,10},{10,... | collective-permute-start | bytes 491528 | tf_op jit(solution)/shard_map/ppermute | solution.py:332
  52.2 1.8 %shard_map.102.total = f32[5,256,128]{2,1,0:T(8,128)S(1)} custom-call(bf16[5,11,256,256]{3,2,1,0:T(8,128)(2,1)S(1)} %shard_map.86.packed, f32[320,128]{1,0:T(8,128)S(1)} %collective-permute-done.19.own, f32[320,128]{1,0:T(8,128)S(1)} %collective-permute-done.20.near, f32[5,128,128]{2,1,0:T(8,128)S(1)} %get-tuple-element.16.refs_0_, ...), custom_call_target="tpu_custom_call" | custom-call | flops 1342177280 | bytes 8388608 | tf_op jit(solution)/shard_map/pallas_call | solution.py:396
  54.1 1.2 %shard_map.103.refs_2_ = f32[320,128]{1,0:T(8,128)S(1)} custom-call(bf16[5,11,256,256]{3,2,1,0:T(8,128)(2,1)S(1)} %shard_map.86.packed, f32[5,256,128]{2,1,0:T(8,128)S(1)} %shard_map.102.total, f32[320,128]{1,0:T(8,128)S(1)} %collective-permute-done.21.far, f32[5,128,128]{2,1,0:T(8,128)S(1)} %get-tuple-element.18.refs_0_, ...), custom_call_target="tpu_custom_call" | custom-call | flops 503316480 | bytes 4194304 | tf_op jit(solution)/shard_map/pallas_call | solution.py:412
  55.3 1.8 %shard_map.97.total = f32[5,256,128]{2,1,0:T(8,128)S(1)} custom-call(bf16[5,11,256,256]{3,2,1,0:T(8,128)(2,1)S(1)} %shard_map.86.packed, f32[320,128]{1,0:T(8,128)S(1)} %collective-permute-done.10.own, f32[320,128]{1,0:T(8,128)S(1)} %collective-permute-done.11.near, f32[5,128,128]{2,1,0:T(8,128)S(1)} %get-tuple-element.16.refs_0_, ...), custom_call_target="tpu_custom_call" | custom-call | flops 1342177280 | bytes 8388608 | tf_op jit(solution)/shard_map/pallas_call | solution.py:396
  57.2 1.8 %shard_map.105 = (f32[1,640,128]{2,1,0:T(8,128)}, f32[1,640,128]{2,1,0:T(8,128)}) custom-call(bf16[5,11,256,256]{3,2,1,0:T(8,128)(2,1)S(1)} %shard_map.86.packed, f32[5,256,128]{2,1,0:T(8,128)S(1)} %shard_map.97.total, f32[320,128]{1,0:T(8,128)S(1)} %collective-permute-done.12.far, ...), custom_call_target="tpu_custom_call", output_to_operand_aliasing={{0}: (6, {}), {1}: (7, {})} | custom-call | flops 503316480 | bytes 4194304 | tf_op jit(solution)/shard_map/pallas_call | solution.py:412
  (40 shorter events, 3.9 us)
Async XLA Ops:
  2.4 5.8 %collective-permute-start = (f32[648,128]{1,0:T(8,128)S(1)}, f32[648,128]{1,0:T(8,128)S(1)}, u32[]{:S(2)}, u32[]{:S(2)}) collective-permute-start(f32[648,128]{1,0:T(8,128)S(1)} %get-tuple-element.14.own.refs_0_), channel_id=1, source_target_pairs={{0,1},{1,0},{2,3},{3,2},{4,5},{5,4},{6,7},{7,6},{8,9},{9,8},{10,11... | collective-permute-start | bytes 995336 | tf_op jit(solution)/shard_map/ppermute | solution.py:332
  2.5 7.5 %collective-permute-start.1 = (f32[648,128]{1,0:T(8,128)S(1)}, f32[648,128]{1,0:T(8,128)S(1)}, u32[]{:S(2)}, u32[]{:S(2)}) collective-permute-start(f32[648,128]{1,0:T(8,128)S(1)} %get-tuple-element.14.own.refs_0_), channel_id=1, source_target_pairs={{0,8},{1,2},{2,1},{3,4},{4,3},{5,6},{6,5},{7,15},{8,0},{9,10},{10,... | collective-permute-start | bytes 995336 | tf_op jit(solution)/shard_map/ppermute | solution.py:332
  11.0 6.2 %collective-permute-start.13 = (f32[320,128]{1,0:T(8,128)S(1)}, f32[320,128]{1,0:T(8,128)S(1)}, u32[]{:S(2)}, u32[]{:S(2)}) collective-permute-start(f32[320,128]{1,0:T(8,128)S(1)} %get-tuple-element.20.refs_1_.refs_0_), channel_id=1, source_target_pairs={{0,8},{1,9},{2,10},{3,11},{4,12},{5,13},{6,14},{7,15},{8,0},{9,1},... | collective-permute-start | bytes 491528 | tf_op jit(solution)/shard_map/ppermute | solution.py:332
  12.6 9.3 %collective-permute-start.2 = (f32[320,128]{1,0:T(8,128)S(1)}, f32[320,128]{1,0:T(8,128)S(1)}, u32[]{:S(2)}, u32[]{:S(2)}) collective-permute-start(f32[320,128]{1,0:T(8,128)S(1)} %get-tuple-element.15.refs_1_), channel_id=1, source_target_pairs={{0,8},{1,9},{2,10},{3,11},{4,12},{5,13},{6,14},{7,15},{8,0},{9,1},... | collective-permute-start | bytes 491528 | tf_op jit(solution)/shard_map/ppermute | solution.py:332
  17.2 4.7 %collective-permute-start.14 = (f32[320,128]{1,0:T(8,128)S(1)}, f32[320,128]{1,0:T(8,128)S(1)}, u32[]{:S(2)}, u32[]{:S(2)}) collective-permute-start(f32[320,128]{1,0:T(8,128)S(1)} %collective-permute-done.13.own), channel_id=1, source_target_pairs={{0,1},{1,0},{2,3},{3,2},{4,5},{5,4},{6,7},{7,6},{8,9},{9,8},{10,11... | collective-permute-start | bytes 491528 | tf_op jit(solution)/shard_map/ppermute | solution.py:332
  17.9 5.7 %collective-permute-start.15 = (f32[320,128]{1,0:T(8,128)S(1)}, f32[320,128]{1,0:T(8,128)S(1)}, u32[]{:S(2)}, u32[]{:S(2)}) collective-permute-start(f32[320,128]{1,0:T(8,128)S(1)} %collective-permute-done.13.own), channel_id=1, source_target_pairs={{0,8},{1,2},{2,1},{3,4},{4,3},{5,6},{6,5},{7,15},{8,0},{9,10},{10,... | collective-permute-start | bytes 491528 | tf_op jit(solution)/shard_map/ppermute | solution.py:332
  19.9 8.9 %collective-permute-start.8 = (f32[640,128]{1,0:T(8,128)S(1)}, f32[640,128]{1,0:T(8,128)S(1)}, u32[]{:S(2)}, u32[]{:S(2)}) collective-permute-start(f32[640,128]{1,0:T(8,128)S(1)} %get-tuple-element.21.own), channel_id=1, source_target_pairs={{0,1},{1,0},{2,3},{3,2},{4,5},{5,4},{6,7},{7,6},{8,9},{9,8},{10,11... | collective-permute-start | bytes 983048 | tf_op jit(solution)/shard_map/ppermute | solution.py:332
  20.0 12.2 %collective-permute-start.9 = (f32[640,128]{1,0:T(8,128)S(1)}, f32[640,128]{1,0:T(8,128)S(1)}, u32[]{:S(2)}, u32[]{:S(2)}) collective-permute-start(f32[640,128]{1,0:T(8,128)S(1)} %get-tuple-element.21.own), channel_id=1, source_target_pairs={{0,16},{1,2},{2,1},{3,4},{4,3},{5,6},{6,5},{7,23},{8,24},{9,10},{1... | collective-permute-start | bytes 983048 | tf_op jit(solution)/shard_map/ppermute | solution.py:332
  21.9 1.8 %collective-permute-start.3 = (f32[320,128]{1,0:T(8,128)S(1)}, f32[320,128]{1,0:T(8,128)S(1)}, u32[]{:S(2)}, u32[]{:S(2)}) collective-permute-start(f32[320,128]{1,0:T(8,128)S(1)} %collective-permute-done.2.own), channel_id=1, source_target_pairs={{0,1},{1,0},{2,3},{3,2},{4,5},{5,4},{6,7},{7,6},{8,9},{9,8},{10,11... | collective-permute-start | bytes 491528 | tf_op jit(solution)/shard_map/ppermute | solution.py:332
  22.0 6.2 %collective-permute-start.4 = (f32[320,128]{1,0:T(8,128)S(1)}, f32[320,128]{1,0:T(8,128)S(1)}, u32[]{:S(2)}, u32[]{:S(2)}) collective-permute-start(f32[320,128]{1,0:T(8,128)S(1)} %collective-permute-done.2.own), channel_id=1, source_target_pairs={{0,8},{1,2},{2,1},{3,4},{4,3},{5,6},{6,5},{7,15},{8,0},{9,10},{10,... | collective-permute-start | bytes 491528 | tf_op jit(solution)/shard_map/ppermute | solution.py:332
  23.6 4.6 %collective-permute-start.16 = (f32[320,128]{1,0:T(8,128)S(1)}, f32[320,128]{1,0:T(8,128)S(1)}, u32[]{:S(2)}, u32[]{:S(2)}) collective-permute-start(f32[320,128]{1,0:T(8,128)S(1)} %shard_map.99.refs_2_), channel_id=1, source_target_pairs={{0,1},{1,0},{2,3},{3,2},{4,5},{5,4},{6,7},{7,6},{8,16},{9,17},{10,... | collective-permute-start | bytes 491528 | tf_op jit(solution)/shard_map/ppermute | solution.py:332
  28.2 4.9 %collective-permute-start.5 = (f32[320,128]{1,0:T(8,128)S(1)}, f32[320,128]{1,0:T(8,128)S(1)}, u32[]{:S(2)}, u32[]{:S(2)}) collective-permute-start(f32[320,128]{1,0:T(8,128)S(1)} %shard_map.92.refs_3_), channel_id=1, source_target_pairs={{0,1},{1,0},{2,3},{3,2},{4,5},{5,4},{6,7},{7,6},{8,16},{9,17},{10,... | collective-permute-start | bytes 491528 | tf_op jit(solution)/shard_map/ppermute | solution.py:332
  28.2 9.1 %collective-permute-start.17 = (f32[320,128]{1,0:T(8,128)S(1)}, f32[320,128]{1,0:T(8,128)S(1)}, u32[]{:S(2)}, u32[]{:S(2)}) collective-permute-start(f32[320,128]{1,0:T(8,128)S(1)} %collective-permute-done.16.own), channel_id=1, source_target_pairs={{0,1},{1,0},{2,3},{3,2},{4,5},{5,4},{6,7},{7,6},{8,9},{9,8},{10,11... | collective-permute-start | bytes 491528 | tf_op jit(solution)/shard_map/ppermute | solution.py:332
  30.4 6.9 %collective-permute-start.18 = (f32[320,128]{1,0:T(8,128)S(1)}, f32[320,128]{1,0:T(8,128)S(1)}, u32[]{:S(2)}, u32[]{:S(2)}) collective-permute-start(f32[320,128]{1,0:T(8,128)S(1)} %collective-permute-done.16.own), channel_id=1, source_target_pairs={{0,8},{1,2},{2,1},{3,4},{4,3},{5,6},{6,5},{7,15},{8,0},{9,10},{10,... | collective-permute-start | bytes 491528 | tf_op jit(solution)/shard_map/ppermute | solution.py:332
  33.1 9.8 %collective-permute-start.6 = (f32[320,128]{1,0:T(8,128)S(1)}, f32[320,128]{1,0:T(8,128)S(1)}, u32[]{:S(2)}, u32[]{:S(2)}) collective-permute-start(f32[320,128]{1,0:T(8,128)S(1)} %collective-permute-done.5.own), channel_id=1, source_target_pairs={{0,1},{1,0},{2,3},{3,2},{4,5},{5,4},{6,7},{7,6},{8,9},{9,8},{10,11... | collective-permute-start | bytes 491528 | tf_op jit(solution)/shard_map/ppermute | solution.py:332
  37.3 5.6 %collective-permute-start.7 = (f32[320,128]{1,0:T(8,128)S(1)}, f32[320,128]{1,0:T(8,128)S(1)}, u32[]{:S(2)}, u32[]{:S(2)}) collective-permute-start(f32[320,128]{1,0:T(8,128)S(1)} %collective-permute-done.5.own), channel_id=1, source_target_pairs={{0,8},{1,2},{2,1},{3,4},{4,3},{5,6},{6,5},{7,15},{8,0},{9,10},{10,... | collective-permute-start | bytes 491528 | tf_op jit(solution)/shard_map/ppermute | solution.py:332
  37.3 10.3 %collective-permute-start.19 = (f32[320,128]{1,0:T(8,128)S(1)}, f32[320,128]{1,0:T(8,128)S(1)}, u32[]{:S(2)}, u32[]{:S(2)}) collective-permute-start(f32[320,128]{1,0:T(8,128)S(1)} %shard_map.101.refs_4_), channel_id=1, source_target_pairs={{0,8},{1,9},{2,10},{3,11},{4,12},{5,13},{6,14},{7,15},{8,0},{9,1},... | collective-permute-start | bytes 491528 | tf_op jit(solution)/shard_map/ppermute | solution.py:332
  42.9 7.8 %collective-permute-start.10 = (f32[320,128]{1,0:T(8,128)S(1)}, f32[320,128]{1,0:T(8,128)S(1)}, u32[]{:S(2)}, u32[]{:S(2)}) collective-permute-start(f32[320,128]{1,0:T(8,128)S(1)} %shard_map.96.refs_5_), channel_id=1, source_target_pairs={{0,8},{1,9},{2,10},{3,11},{4,12},{5,13},{6,14},{7,15},{8,0},{9,1},... | collective-permute-start | bytes 491528 | tf_op jit(solution)/shard_map/ppermute | solution.py:332
  47.6 4.6 %collective-permute-start.20 = (f32[320,128]{1,0:T(8,128)S(1)}, f32[320,128]{1,0:T(8,128)S(1)}, u32[]{:S(2)}, u32[]{:S(2)}) collective-permute-start(f32[320,128]{1,0:T(8,128)S(1)} %collective-permute-done.19.own), channel_id=1, source_target_pairs={{0,1},{1,0},{2,3},{3,2},{4,5},{5,4},{6,7},{7,6},{8,9},{9,8},{10,11... | collective-permute-start | bytes 491528 | tf_op jit(solution)/shard_map/ppermute | solution.py:332
  47.6 6.4 %collective-permute-start.21 = (f32[320,128]{1,0:T(8,128)S(1)}, f32[320,128]{1,0:T(8,128)S(1)}, u32[]{:S(2)}, u32[]{:S(2)}) collective-permute-start(f32[320,128]{1,0:T(8,128)S(1)} %collective-permute-done.19.own), channel_id=1, source_target_pairs={{0,8},{1,2},{2,1},{3,4},{4,3},{5,6},{6,5},{7,15},{8,0},{9,10},{10,... | collective-permute-start | bytes 491528 | tf_op jit(solution)/shard_map/ppermute | solution.py:332
  50.6 4.7 %collective-permute-start.11 = (f32[320,128]{1,0:T(8,128)S(1)}, f32[320,128]{1,0:T(8,128)S(1)}, u32[]{:S(2)}, u32[]{:S(2)}) collective-permute-start(f32[320,128]{1,0:T(8,128)S(1)} %collective-permute-done.10.own), channel_id=1, source_target_pairs={{0,1},{1,0},{2,3},{3,2},{4,5},{5,4},{6,7},{7,6},{8,9},{9,8},{10,11... | collective-permute-start | bytes 491528 | tf_op jit(solution)/shard_map/ppermute | solution.py:332
  51.0 6.1 %collective-permute-start.12 = (f32[320,128]{1,0:T(8,128)S(1)}, f32[320,128]{1,0:T(8,128)S(1)}, u32[]{:S(2)}, u32[]{:S(2)}) collective-permute-start(f32[320,128]{1,0:T(8,128)S(1)} %collective-permute-done.10.own), channel_id=1, source_target_pairs={{0,8},{1,2},{2,1},{3,4},{4,3},{5,6},{6,5},{7,15},{8,0},{9,10},{10,... | collective-permute-start | bytes 491528 | tf_op jit(solution)/shard_map/ppermute | solution.py:332

commit v6 on v5

--- a/solution.py
+++ b/solution.py
@@ -204,10 +204,10 @@
 
 def when_active(step, sections, body):
     depth = lax.axis_index("depth")
-    if step:
+    if step is None:
+        body()
+    else:
         pl.when((depth == step) | (depth == sections - 1 - step))(body)
-    else:
-        body()
 
 
 def combined(value, shots):
@@ -240,10 +240,10 @@
             j, value = side_product(packed, held_near, tiles, jj, low_side, narrow)
             total[j] = total[j] + value
 
-    when_active(step, sections, body)
-
-
-def outer_kernel(step, sections, lats, tiles, shots, ends, packed, total, far, *refs):
+    when_active(step or None, sections, body)
+
+
+def outer_kernel(step, sections, lats, tiles, shots, ends, late, packed, total, far, *refs):
     narrow = bool(step)
     scale, base, other = None, None, None
     if narrow:
@@ -260,6 +260,10 @@
     def body():
         sign = jnp.where(depth == (step or 0), 1.0, -1.0)
 
+        def copy_of(j, result):
+            at = pl.ds(pl.multiple_of(j * TILE, TILE), TILE)
+            return pltpu.make_async_copy(leaving.at[at], result.at[0, at], sems.at[j])
+
         def finish(j, value):
             at = pl.ds(pl.multiple_of(j * HALF, HALF), HALF)
             if not narrow:
@@ -270,6 +274,8 @@
             part = jnp.where(left_half(HALF), value[:HALF], value[HALF:]) + base[at]
             if ends:
                 leaving[pl.ds(pl.multiple_of(j * TILE, TILE), TILE)] = merged(other[at], part)
+                pl.when(depth == step)(lambda: copy_of(j, result_down).start())
+                pl.when(depth != step)(lambda: copy_of(j, result_up).start())
             else:
                 outs[0][at] = part
 
@@ -287,15 +293,17 @@
 
         if ends:
 
-            def leave(result):
-                copy = pltpu.make_async_copy(leaving, result.at[0], sems)
-                copy.start()
-                copy.wait()
-
-            pl.when(depth == step)(lambda: leave(result_down))
-            pl.when(depth != step)(lambda: leave(result_up))
-
-    when_active(step, sections, body)
+            def wait_all(result):
+                for j in range(tiles):
+                    copy_of(j, result).wait()
+
+            pl.when(depth == step)(lambda: wait_all(result_down))
+            pl.when(depth != step)(lambda: wait_all(result_up))
+
+    if late:
+        pl.when((depth > 0) & (depth < sections - 1))(body)
+    else:
+        when_active(step, sections, body)
 
 
 def keep_kernel(sections, tiles, *refs):
@@ -403,14 +411,14 @@
             cost_estimate=cost(2 * 40 * 256**3, 8 * 2**20),
         )(*args)
 
-    def outer(step, *args, shapes, kept=()):
+    def outer(step, *args, shapes, kept=(), late=False):
         count = len(args) + 1
         ends = bool(kept)
         scratch = [held(step)]
         if ends:
-            scratch += [VMEM((rows, columns), jnp.float32), pltpu.SemaphoreType.DMA(())]
+            scratch += [VMEM((rows, columns), jnp.float32), pltpu.SemaphoreType.DMA((tiles,))]
         return call(
-            functools.partial(outer_kernel, step, sections, lats, tiles, shots, ends),
+            functools.partial(outer_kernel, step, sections, lats, tiles, shots, ends, late),
             out_shape=shapes,
             in_specs=[spec(VMEM)] * count + [spec(pl.ANY)] * len(kept),
             out_specs=[spec(pl.ANY if ends else VMEM)] * len(shapes),
@@ -426,6 +434,7 @@
     first_near, first_far = halo(first, next_door)
     total = inner(0, first, first_near)
     fields = [outer(0, total, first_far, shapes=[half] * STREAMS)]
+    first_base = outer(0, total, first_far, shapes=[half] * STREAMS, late=True)
     arrived = cross(0, fields[0])
 
     second, *_ = lax.optimization_barrier((second, *fields[0]))
@@ -442,7 +451,7 @@
     second_base = outer(None, total, far, shapes=[half] * STREAMS)
 
     for step in range(1, sections):
-        bases = fields[0] if step < sections // 2 else second_base
+        bases = first_base if step < sections // 2 else second_base
         field = []
         for q in range(STREAMS):
             near, far = halo(arrived[q], next_door)

time: 60 us -> 61.6 us (1.027)
  the two profiles are of different devices: /device:TPU:1 before, /device:TPU:0 now
where the time goes in v6:
time: 61.6 us; the launch traced here: 61.4 us
  starting transfers between devices  32.2 us (52%)
  Pallas kernels  16.4 us (27%)
  waiting for transfers between devices  11.8 us (19%)
  between operations  0.97 us (2%)
    ppermute x22, starting transfers between devices, move(): return lax.ppermute(x, ('depth', 'lat'), pairs)  32.2 us
    ppermute x22, waiting for transfers between devices, move(): return lax.ppermute(x, ('depth', 'lat'), pairs)  11.8 us
    pallas_call x8, Pallas kernels, inner(): call(functools.partial(inner_kernel, step, sections, tiles), out_shape=f3...  6.91 us
    pallas_call x9, Pallas kernels, outer(): call(functools.partial(outer_kernel, step, sections, lats, tiles, shots,...  3.55 us
    pallas_call x1, Pallas kernels, shards(): call(functools.partial(pack_kernel, tiles, band), out_shape=jax.ShapeDtyp...  2.95 us
    pallas_call x1, Pallas kernels, shards(): call(functools.partial(prep_kernel, tiles, shots, sections), out_shape=[f...  1.77 us
  transfers between devices with their start and end apart: 22, of which 7 were waited for; matrix products, arithmetic and copies ran while one was open for 0% of the time, Pallas kernels for 20%

profile of v6, /device:TPU:0, one launch (start us, length us, event | category | flops | bytes accessed | tf_op | source)
XLA Modules:
  0.0 61.4 jit_solution(12905321039026471699)
XLA Ops:
  0.6 1.8 %shard_map.87 = (f32[648,128]{1,0:T(8,128)S(1)}, f32[640,128]{1,0:T(8,128)S(1)}) custom-call(s32[64]{0:T(128)} %assign_at.1, f32[1,640]{1,0:T(1,128)} %refl_at.1, f32[1,640,128]{2,1,0:T(8,128)} %up_at.1, f32[1,640,128]{2,1,0:T(8,128)} %down_at.1, f32[640,128]{1,0:T(8,128)} %src_at.1), custom_call_target="tpu_custom_call" | custom-call | flops 10000000 | bytes 1638400 | tf_op jit(solution)/shard_map/pallas_call | solution.py:364
  3.0 2.2 %collective-permute-start.1 = (f32[648,128]{1,0:T(8,128)S(1)}, f32[648,128]{1,0:T(8,128)S(1)}, u32[]{:S(2)}, u32[]{:S(2)}) collective-permute-start(f32[648,128]{1,0:T(8,128)S(1)} %get-tuple-element.16.own.refs_0_), channel_id=1, source_target_pairs={{0,8},{1,2},{2,1},{3,4},{4,3},{5,6},{6,5},{7,15},{8,0},{9,10},{10,... | collective-permute-start | bytes 995336 | tf_op jit(solution)/shard_map/ppermute | solution.py:340
  5.2 3.0 %shard_map.86.packed = bf16[5,11,256,256]{3,2,1,0:T(8,128)(2,1)S(1)} custom-call(s32[1,5]{1,0:T(1,128)} %shift_at.1, f32[1,5,9,256,128]{4,3,2,1,0:T(8,128)} %tiles_at.1), custom_call_target="tpu_custom_call" | custom-call | flops 10000000 | bytes 11796480 | tf_op jit(solution)/shard_map/pallas_call | solution.py:381
  8.1 1.6 %shard_map.88.total = f32[5,256,128]{2,1,0:T(8,128)S(1)} custom-call(bf16[5,11,256,256]{3,2,1,0:T(8,128)(2,1)S(1)} %shard_map.86.packed, f32[648,128]{1,0:T(8,128)S(1)} %get-tuple-element.16.own.refs_0_, f32[648,128]{1,0:T(8,128)S(1)} %collective-permute-done.near.refs_1_), custom_call_target="tpu_custom_call" | custom-call | flops 1342177280 | bytes 8388608 | tf_op jit(solution)/shard_map/pallas_call | solution.py:404
  10.8 1.5 %collective-permute-start.13 = (f32[320,128]{1,0:T(8,128)S(1)}, f32[320,128]{1,0:T(8,128)S(1)}, u32[]{:S(2)}, u32[]{:S(2)}) collective-permute-start(f32[320,128]{1,0:T(8,128)S(1)} %get-tuple-element.23.refs_0_), channel_id=1, source_target_pairs={{0,8},{1,9},{2,10},{3,11},{4,12},{5,13},{6,14},{7,15},{8,0},{9,1},... | collective-permute-start | bytes 491528 | tf_op jit(solution)/shard_map/ppermute | solution.py:340
  12.9 5.0 %collective-permute-done.13.own = f32[320,128]{1,0:T(8,128)S(1)} collective-permute-done((f32[320,128]{1,0:T(8,128)S(1)}, f32[320,128]{1,0:T(8,128)S(1)}, u32[]{:S(2)}, u32[]{:S(2)}) %collective-permute-start.13) | collective-permute-done | bytes 163872 | tf_op jit(solution)/shard_map/ppermute | solution.py:340
  18.4 1.5 %collective-permute-start.9 = (f32[640,128]{1,0:T(8,128)S(1)}, f32[640,128]{1,0:T(8,128)S(1)}, u32[]{:S(2)}, u32[]{:S(2)}) collective-permute-start(f32[640,128]{1,0:T(8,128)S(1)} %get-tuple-element.24.own), channel_id=1, source_target_pairs={{0,16},{1,2},{2,1},{3,4},{4,3},{5,6},{6,5},{7,23},{8,24},{9,10},{1... | collective-permute-start | bytes 983048 | tf_op jit(solution)/shard_map/ppermute | solution.py:340
  20.3 2.1 %collective-permute-start.15 = (f32[320,128]{1,0:T(8,128)S(1)}, f32[320,128]{1,0:T(8,128)S(1)}, u32[]{:S(2)}, u32[]{:S(2)}) collective-permute-start(f32[320,128]{1,0:T(8,128)S(1)} %collective-permute-done.13.own), channel_id=1, source_target_pairs={{0,8},{1,2},{2,1},{3,4},{4,3},{5,6},{6,5},{7,15},{8,0},{9,10},{10,... | collective-permute-start | bytes 491528 | tf_op jit(solution)/shard_map/ppermute | solution.py:340
  23.1 2.6 %collective-permute-done.15.far = f32[320,128]{1,0:T(8,128)S(1)} collective-permute-done((f32[320,128]{1,0:T(8,128)S(1)}, f32[320,128]{1,0:T(8,128)S(1)}, u32[]{:S(2)}, u32[]{:S(2)}) %collective-permute-start.15) | collective-permute-done | bytes 163872 | tf_op jit(solution)/shard_map/ppermute | solution.py:340
  25.7 2.0 %collective-permute-start.16 = (f32[320,128]{1,0:T(8,128)S(1)}, f32[320,128]{1,0:T(8,128)S(1)}, u32[]{:S(2)}, u32[]{:S(2)}) collective-permute-start(f32[320,128]{1,0:T(8,128)S(1)} %shard_map.100.refs_2_), channel_id=1, source_target_pairs={{0,1},{1,0},{2,3},{3,2},{4,5},{5,4},{6,7},{7,6},{8,16},{9,17},{10,... | collective-permute-start | bytes 491528 | tf_op jit(solution)/shard_map/ppermute | solution.py:340
  27.8 1.4 %collective-permute-start.5 = (f32[320,128]{1,0:T(8,128)S(1)}, f32[320,128]{1,0:T(8,128)S(1)}, u32[]{:S(2)}, u32[]{:S(2)}) collective-permute-start(f32[320,128]{1,0:T(8,128)S(1)} %shard_map.93.refs_3_), channel_id=1, source_target_pairs={{0,1},{1,0},{2,3},{3,2},{4,5},{5,4},{6,7},{7,6},{8,16},{9,17},{10,... | collective-permute-start | bytes 491528 | tf_op jit(solution)/shard_map/ppermute | solution.py:340
  29.2 1.6 %shard_map.95.total = f32[5,256,128]{2,1,0:T(8,128)S(1)} custom-call(bf16[5,11,256,256]{3,2,1,0:T(8,128)(2,1)S(1)} %shard_map.86.packed, f32[640,128]{1,0:T(8,128)S(1)} %get-tuple-element.24.own, f32[640,128]{1,0:T(8,128)S(1)} %collective-permute-done.8.near), custom_call_target="tpu_custom_call" | custom-call | flops 1342177280 | bytes 8388608 | tf_op jit(solution)/shard_map/pallas_call | solution.py:404
  30.8 7.4 %collective-permute-start.18 = (f32[320,128]{1,0:T(8,128)S(1)}, f32[320,128]{1,0:T(8,128)S(1)}, u32[]{:S(2)}, u32[]{:S(2)}) collective-permute-start(f32[320,128]{1,0:T(8,128)S(1)} %collective-permute-done.16.own), channel_id=1, source_target_pairs={{0,8},{1,2},{2,1},{3,4},{4,3},{5,6},{6,5},{7,15},{8,0},{9,10},{10,... | collective-permute-start | bytes 491528 | tf_op jit(solution)/shard_map/ppermute | solution.py:340
  38.9 1.4 %collective-permute-start.7 = (f32[320,128]{1,0:T(8,128)S(1)}, f32[320,128]{1,0:T(8,128)S(1)}, u32[]{:S(2)}, u32[]{:S(2)}) collective-permute-start(f32[320,128]{1,0:T(8,128)S(1)} %collective-permute-done.5.own), channel_id=1, source_target_pairs={{0,8},{1,2},{2,1},{3,4},{4,3},{5,6},{6,5},{7,15},{8,0},{9,10},{10,... | collective-permute-start | bytes 491528 | tf_op jit(solution)/shard_map/ppermute | solution.py:340
  40.3 1.3 %collective-permute-done.18.far = f32[320,128]{1,0:T(8,128)S(1)} collective-permute-done((f32[320,128]{1,0:T(8,128)S(1)}, f32[320,128]{1,0:T(8,128)S(1)}, u32[]{:S(2)}, u32[]{:S(2)}) %collective-permute-start.18) | collective-permute-done | bytes 163872 | tf_op jit(solution)/shard_map/ppermute | solution.py:340
  41.6 2.7 %collective-permute-start.19 = (f32[320,128]{1,0:T(8,128)S(1)}, f32[320,128]{1,0:T(8,128)S(1)}, u32[]{:S(2)}, u32[]{:S(2)}) collective-permute-start(f32[320,128]{1,0:T(8,128)S(1)} %shard_map.102.refs_4_), channel_id=1, source_target_pairs={{0,8},{1,9},{2,10},{3,11},{4,12},{5,13},{6,14},{7,15},{8,0},{9,1},... | collective-permute-start | bytes 491528 | tf_op jit(solution)/shard_map/ppermute | solution.py:340
  44.3 2.6 %collective-permute-start.10 = (f32[320,128]{1,0:T(8,128)S(1)}, f32[320,128]{1,0:T(8,128)S(1)}, u32[]{:S(2)}, u32[]{:S(2)}) collective-permute-start(f32[320,128]{1,0:T(8,128)S(1)} %shard_map.97.refs_5_), channel_id=1, source_target_pairs={{0,8},{1,9},{2,10},{3,11},{4,12},{5,13},{6,14},{7,15},{8,0},{9,1},... | collective-permute-start | bytes 491528 | tf_op jit(solution)/shard_map/ppermute | solution.py:340
  46.9 2.1 %collective-permute-done.19.own = f32[320,128]{1,0:T(8,128)S(1)} collective-permute-done((f32[320,128]{1,0:T(8,128)S(1)}, f32[320,128]{1,0:T(8,128)S(1)}, u32[]{:S(2)}, u32[]{:S(2)}) %collective-permute-start.19) | collective-permute-done | bytes 163872 | tf_op jit(solution)/shard_map/ppermute | solution.py:340
  49.8 1.7 %collective-permute-start.21 = (f32[320,128]{1,0:T(8,128)S(1)}, f32[320,128]{1,0:T(8,128)S(1)}, u32[]{:S(2)}, u32[]{:S(2)}) collective-permute-start(f32[320,128]{1,0:T(8,128)S(1)} %collective-permute-done.19.own), channel_id=1, source_target_pairs={{0,8},{1,2},{2,1},{3,4},{4,3},{5,6},{6,5},{7,15},{8,0},{9,10},{10,... | collective-permute-start | bytes 491528 | tf_op jit(solution)/shard_map/ppermute | solution.py:340
  51.5 0.9 %shard_map.105 = (f32[1,640,128]{2,1,0:T(8,128)}, f32[1,640,128]{2,1,0:T(8,128)}) custom-call(f32[320,128]{1,0:T(8,128)S(1)} %get-tuple-element.23.refs_0_, f32[320,128]{1,0:T(8,128)S(1)} %get-tuple-element.17.refs_1_, f32[320,128]{1,0:T(8,128)S(1)} %shard_map.100.refs_2_, f32[320,128]{1,0:T(8,128)S(1)} %shard_map.93.refs_3_, ...), custom_call_target="tpu_custom_call" | custom-call | bytes 1310720 | tf_op jit(solution)/shard_map/pallas_call | solution.py:460
  52.7 2.3 %collective-permute-start.12 = (f32[320,128]{1,0:T(8,128)S(1)}, f32[320,128]{1,0:T(8,128)S(1)}, u32[]{:S(2)}, u32[]{:S(2)}) collective-permute-start(f32[320,128]{1,0:T(8,128)S(1)} %collective-permute-done.10.own), channel_id=1, source_target_pairs={{0,8},{1,2},{2,1},{3,4},{4,3},{5,6},{6,5},{7,15},{8,0},{9,10},{10,... | collective-permute-start | bytes 491528 | tf_op jit(solution)/shard_map/ppermute | solution.py:340
  55.0 1.8 %shard_map.103.total = f32[5,256,128]{2,1,0:T(8,128)S(1)} custom-call(bf16[5,11,256,256]{3,2,1,0:T(8,128)(2,1)S(1)} %shard_map.86.packed, f32[320,128]{1,0:T(8,128)S(1)} %collective-permute-done.19.own, f32[320,128]{1,0:T(8,128)S(1)} %collective-permute-done.20.near, f32[5,128,128]{2,1,0:T(8,128)S(1)} %get-tuple-element.18.refs_0_, ...), custom_call_target="tpu_custom_call" | custom-call | flops 1342177280 | bytes 8388608 | tf_op jit(solution)/shard_map/pallas_call | solution.py:404
  57.7 1.8 %shard_map.98.total = f32[5,256,128]{2,1,0:T(8,128)S(1)} custom-call(bf16[5,11,256,256]{3,2,1,0:T(8,128)(2,1)S(1)} %shard_map.86.packed, f32[320,128]{1,0:T(8,128)S(1)} %collective-permute-done.10.own, f32[320,128]{1,0:T(8,128)S(1)} %collective-permute-done.11.near, f32[5,128,128]{2,1,0:T(8,128)S(1)} %get-tuple-element.18.refs_0_, ...), custom_call_target="tpu_custom_call" | custom-call | flops 1342177280 | bytes 8388608 | tf_op jit(solution)/shard_map/pallas_call | solution.py:404
  59.6 1.6 %shard_map.106 = (f32[1,640,128]{2,1,0:T(8,128)}, f32[1,640,128]{2,1,0:T(8,128)}) custom-call(bf16[5,11,256,256]{3,2,1,0:T(8,128)(2,1)S(1)} %shard_map.86.packed, f32[5,256,128]{2,1,0:T(8,128)S(1)} %shard_map.98.total, f32[320,128]{1,0:T(8,128)S(1)} %collective-permute-done.12.far, ...), custom_call_target="tpu_custom_call", output_to_operand_aliasing={{0}: (6, {}), {1}: (7, {})} | custom-call | flops 503316480 | bytes 4194304 | tf_op jit(solution)/shard_map/pallas_call | solution.py:420
  (41 shorter events, 6.4 us)
Async XLA Ops:
  2.4 5.7 %collective-permute-start = (f32[648,128]{1,0:T(8,128)S(1)}, f32[648,128]{1,0:T(8,128)S(1)}, u32[]{:S(2)}, u32[]{:S(2)}) collective-permute-start(f32[648,128]{1,0:T(8,128)S(1)} %get-tuple-element.16.own.refs_0_), channel_id=1, source_target_pairs={{0,1},{1,0},{2,3},{3,2},{4,5},{5,4},{6,7},{7,6},{8,9},{9,8},{10,11... | collective-permute-start | bytes 995336 | tf_op jit(solution)/shard_map/ppermute | solution.py:340
  3.0 7.3 %collective-permute-start.1 = (f32[648,128]{1,0:T(8,128)S(1)}, f32[648,128]{1,0:T(8,128)S(1)}, u32[]{:S(2)}, u32[]{:S(2)}) collective-permute-start(f32[648,128]{1,0:T(8,128)S(1)} %get-tuple-element.16.own.refs_0_), channel_id=1, source_target_pairs={{0,8},{1,2},{2,1},{3,4},{4,3},{5,6},{6,5},{7,15},{8,0},{9,10},{10,... | collective-permute-start | bytes 995336 | tf_op jit(solution)/shard_map/ppermute | solution.py:340
  10.8 7.1 %collective-permute-start.13 = (f32[320,128]{1,0:T(8,128)S(1)}, f32[320,128]{1,0:T(8,128)S(1)}, u32[]{:S(2)}, u32[]{:S(2)}) collective-permute-start(f32[320,128]{1,0:T(8,128)S(1)} %get-tuple-element.23.refs_0_), channel_id=1, source_target_pairs={{0,8},{1,9},{2,10},{3,11},{4,12},{5,13},{6,14},{7,15},{8,0},{9,1},... | collective-permute-start | bytes 491528 | tf_op jit(solution)/shard_map/ppermute | solution.py:340
  12.3 10.1 %collective-permute-start.2 = (f32[320,128]{1,0:T(8,128)S(1)}, f32[320,128]{1,0:T(8,128)S(1)}, u32[]{:S(2)}, u32[]{:S(2)}) collective-permute-start(f32[320,128]{1,0:T(8,128)S(1)} %get-tuple-element.17.refs_1_), channel_id=1, source_target_pairs={{0,8},{1,9},{2,10},{3,11},{4,12},{5,13},{6,14},{7,15},{8,0},{9,1},... | collective-permute-start | bytes 491528 | tf_op jit(solution)/shard_map/ppermute | solution.py:340
  17.9 4.5 %collective-permute-start.14 = (f32[320,128]{1,0:T(8,128)S(1)}, f32[320,128]{1,0:T(8,128)S(1)}, u32[]{:S(2)}, u32[]{:S(2)}) collective-permute-start(f32[320,128]{1,0:T(8,128)S(1)} %collective-permute-done.13.own), channel_id=1, source_target_pairs={{0,1},{1,0},{2,3},{3,2},{4,5},{5,4},{6,7},{7,6},{8,9},{9,8},{10,11... | collective-permute-start | bytes 491528 | tf_op jit(solution)/shard_map/ppermute | solution.py:340
  17.9 11.3 %collective-permute-start.8 = (f32[640,128]{1,0:T(8,128)S(1)}, f32[640,128]{1,0:T(8,128)S(1)}, u32[]{:S(2)}, u32[]{:S(2)}) collective-permute-start(f32[640,128]{1,0:T(8,128)S(1)} %get-tuple-element.24.own), channel_id=1, source_target_pairs={{0,1},{1,0},{2,3},{3,2},{4,5},{5,4},{6,7},{7,6},{8,9},{9,8},{10,11... | collective-permute-start | bytes 983048 | tf_op jit(solution)/shard_map/ppermute | solution.py:340
  18.4 19.9 %collective-permute-start.9 = (f32[640,128]{1,0:T(8,128)S(1)}, f32[640,128]{1,0:T(8,128)S(1)}, u32[]{:S(2)}, u32[]{:S(2)}) collective-permute-start(f32[640,128]{1,0:T(8,128)S(1)} %get-tuple-element.24.own), channel_id=1, source_target_pairs={{0,16},{1,2},{2,1},{3,4},{4,3},{5,6},{6,5},{7,23},{8,24},{9,10},{1... | collective-permute-start | bytes 983048 | tf_op jit(solution)/shard_map/ppermute | solution.py:340
  20.3 5.4 %collective-permute-start.15 = (f32[320,128]{1,0:T(8,128)S(1)}, f32[320,128]{1,0:T(8,128)S(1)}, u32[]{:S(2)}, u32[]{:S(2)}) collective-permute-start(f32[320,128]{1,0:T(8,128)S(1)} %collective-permute-done.13.own), channel_id=1, source_target_pairs={{0,8},{1,2},{2,1},{3,4},{4,3},{5,6},{6,5},{7,15},{8,0},{9,10},{10,... | collective-permute-start | bytes 491528 | tf_op jit(solution)/shard_map/ppermute | solution.py:340
  22.4 5.3 %collective-permute-start.3 = (f32[320,128]{1,0:T(8,128)S(1)}, f32[320,128]{1,0:T(8,128)S(1)}, u32[]{:S(2)}, u32[]{:S(2)}) collective-permute-start(f32[320,128]{1,0:T(8,128)S(1)} %collective-permute-done.2.own), channel_id=1, source_target_pairs={{0,1},{1,0},{2,3},{3,2},{4,5},{5,4},{6,7},{7,6},{8,9},{9,8},{10,11... | collective-permute-start | bytes 491528 | tf_op jit(solution)/shard_map/ppermute | solution.py:340
  22.4 5.4 %collective-permute-start.4 = (f32[320,128]{1,0:T(8,128)S(1)}, f32[320,128]{1,0:T(8,128)S(1)}, u32[]{:S(2)}, u32[]{:S(2)}) collective-permute-start(f32[320,128]{1,0:T(8,128)S(1)} %collective-permute-done.2.own), channel_id=1, source_target_pairs={{0,8},{1,2},{2,1},{3,4},{4,3},{5,6},{6,5},{7,15},{8,0},{9,10},{10,... | collective-permute-start | bytes 491528 | tf_op jit(solution)/shard_map/ppermute | solution.py:340
  25.7 3.5 %collective-permute-start.16 = (f32[320,128]{1,0:T(8,128)S(1)}, f32[320,128]{1,0:T(8,128)S(1)}, u32[]{:S(2)}, u32[]{:S(2)}) collective-permute-start(f32[320,128]{1,0:T(8,128)S(1)} %shard_map.100.refs_2_), channel_id=1, source_target_pairs={{0,1},{1,0},{2,3},{3,2},{4,5},{5,4},{6,7},{7,6},{8,16},{9,17},{10,... | collective-permute-start | bytes 491528 | tf_op jit(solution)/shard_map/ppermute | solution.py:340
  27.8 11.1 %collective-permute-start.5 = (f32[320,128]{1,0:T(8,128)S(1)}, f32[320,128]{1,0:T(8,128)S(1)}, u32[]{:S(2)}, u32[]{:S(2)}) collective-permute-start(f32[320,128]{1,0:T(8,128)S(1)} %shard_map.93.refs_3_), channel_id=1, source_target_pairs={{0,1},{1,0},{2,3},{3,2},{4,5},{5,4},{6,7},{7,6},{8,16},{9,17},{10,... | collective-permute-start | bytes 491528 | tf_op jit(solution)/shard_map/ppermute | solution.py:340
  29.1 11.2 %collective-permute-start.17 = (f32[320,128]{1,0:T(8,128)S(1)}, f32[320,128]{1,0:T(8,128)S(1)}, u32[]{:S(2)}, u32[]{:S(2)}) collective-permute-start(f32[320,128]{1,0:T(8,128)S(1)} %collective-permute-done.16.own), channel_id=1, source_target_pairs={{0,1},{1,0},{2,3},{3,2},{4,5},{5,4},{6,7},{7,6},{8,9},{9,8},{10,11... | collective-permute-start | bytes 491528 | tf_op jit(solution)/shard_map/ppermute | solution.py:340
  30.8 10.7 %collective-permute-start.18 = (f32[320,128]{1,0:T(8,128)S(1)}, f32[320,128]{1,0:T(8,128)S(1)}, u32[]{:S(2)}, u32[]{:S(2)}) collective-permute-start(f32[320,128]{1,0:T(8,128)S(1)} %collective-permute-done.16.own), channel_id=1, source_target_pairs={{0,8},{1,2},{2,1},{3,4},{4,3},{5,6},{6,5},{7,15},{8,0},{9,10},{10,... | collective-permute-start | bytes 491528 | tf_op jit(solution)/shard_map/ppermute | solution.py:340
  38.8 5.5 %collective-permute-start.6 = (f32[320,128]{1,0:T(8,128)S(1)}, f32[320,128]{1,0:T(8,128)S(1)}, u32[]{:S(2)}, u32[]{:S(2)}) collective-permute-start(f32[320,128]{1,0:T(8,128)S(1)} %collective-permute-done.5.own), channel_id=1, source_target_pairs={{0,1},{1,0},{2,3},{3,2},{4,5},{5,4},{6,7},{7,6},{8,9},{9,8},{10,11... | collective-permute-start | bytes 491528 | tf_op jit(solution)/shard_map/ppermute | solution.py:340
  38.9 5.4 %collective-permute-start.7 = (f32[320,128]{1,0:T(8,128)S(1)}, f32[320,128]{1,0:T(8,128)S(1)}, u32[]{:S(2)}, u32[]{:S(2)}) collective-permute-start(f32[320,128]{1,0:T(8,128)S(1)} %collective-permute-done.5.own), channel_id=1, source_target_pairs={{0,8},{1,2},{2,1},{3,4},{4,3},{5,6},{6,5},{7,15},{8,0},{9,10},{10,... | collective-permute-start | bytes 491528 | tf_op jit(solution)/shard_map/ppermute | solution.py:340
  41.6 7.5 %collective-permute-start.19 = (f32[320,128]{1,0:T(8,128)S(1)}, f32[320,128]{1,0:T(8,128)S(1)}, u32[]{:S(2)}, u32[]{:S(2)}) collective-permute-start(f32[320,128]{1,0:T(8,128)S(1)} %shard_map.102.refs_4_), channel_id=1, source_target_pairs={{0,8},{1,9},{2,10},{3,11},{4,12},{5,13},{6,14},{7,15},{8,0},{9,1},... | collective-permute-start | bytes 491528 | tf_op jit(solution)/shard_map/ppermute | solution.py:340
  44.3 8.2 %collective-permute-start.10 = (f32[320,128]{1,0:T(8,128)S(1)}, f32[320,128]{1,0:T(8,128)S(1)}, u32[]{:S(2)}, u32[]{:S(2)}) collective-permute-start(f32[320,128]{1,0:T(8,128)S(1)} %shard_map.97.refs_5_), channel_id=1, source_target_pairs={{0,8},{1,9},{2,10},{3,11},{4,12},{5,13},{6,14},{7,15},{8,0},{9,1},... | collective-permute-start | bytes 491528 | tf_op jit(solution)/shard_map/ppermute | solution.py:340
  49.1 5.9 %collective-permute-start.20 = (f32[320,128]{1,0:T(8,128)S(1)}, f32[320,128]{1,0:T(8,128)S(1)}, u32[]{:S(2)}, u32[]{:S(2)}) collective-permute-start(f32[320,128]{1,0:T(8,128)S(1)} %collective-permute-done.19.own), channel_id=1, source_target_pairs={{0,1},{1,0},{2,3},{3,2},{4,5},{5,4},{6,7},{7,6},{8,9},{9,8},{10,11... | collective-permute-start | bytes 491528 | tf_op jit(solution)/shard_map/ppermute | solution.py:340
  49.8 7.0 %collective-permute-start.21 = (f32[320,128]{1,0:T(8,128)S(1)}, f32[320,128]{1,0:T(8,128)S(1)}, u32[]{:S(2)}, u32[]{:S(2)}) collective-permute-start(f32[320,128]{1,0:T(8,128)S(1)} %collective-permute-done.19.own), channel_id=1, source_target_pairs={{0,8},{1,2},{2,1},{3,4},{4,3},{5,6},{6,5},{7,15},{8,0},{9,10},{10,... | collective-permute-start | bytes 491528 | tf_op jit(solution)/shard_map/ppermute | solution.py:340
  52.6 5.2 %collective-permute-start.11 = (f32[320,128]{1,0:T(8,128)S(1)}, f32[320,128]{1,0:T(8,128)S(1)}, u32[]{:S(2)}, u32[]{:S(2)}) collective-permute-start(f32[320,128]{1,0:T(8,128)S(1)} %collective-permute-done.10.own), channel_id=1, source_target_pairs={{0,1},{1,0},{2,3},{3,2},{4,5},{5,4},{6,7},{7,6},{8,9},{9,8},{10,11... | collective-permute-start | bytes 491528 | tf_op jit(solution)/shard_map/ppermute | solution.py:340
  52.7 6.9 %collective-permute-start.12 = (f32[320,128]{1,0:T(8,128)S(1)}, f32[320,128]{1,0:T(8,128)S(1)}, u32[]{:S(2)}, u32[]{:S(2)}) collective-permute-start(f32[320,128]{1,0:T(8,128)S(1)} %collective-permute-done.10.own), channel_id=1, source_target_pairs={{0,8},{1,2},{2,1},{3,4},{4,3},{5,6},{6,5},{7,15},{8,0},{9,10},{10,... | collective-permute-start | bytes 491528 | tf_op jit(solution)/shard_map/ppermute | solution.py:340

commit v7 on v6

--- a/solution.py
+++ b/solution.py
@@ -176,9 +176,15 @@
     return jnp.where(left, upper, turned(lower)), jnp.where(left, turned(upper), lower)
 
 
+def full_tile(field, t):
+    if len(field) == 1:
+        return field[0][rows_of(t)]
+    return merged(*[part[halves_of(t)] for part in field])
+
+
 def spread(field, scale, sign, tiles, narrow, mirrored, held):
     for t in range(tiles):
-        tile = unpack_tile(field, t) if narrow else field[rows_of(t)]
+        tile = unpack_tile(field[0], t) if narrow else full_tile(field, t)
         if scale is not None:
             tile = tile * (1.0 + sign * scale[t])
         at = 2 * t * TILE
@@ -224,9 +230,10 @@
             out[t] = down_column(source[at : at + 1])
 
 
-def inner_kernel(step, sections, tiles, packed, own, near, *refs):
-    narrow = bool(step)
-    scale, near_scale = refs[:2] if narrow else (None, None)
+def inner_kernel(step, sections, tiles, parts, packed, *refs):
+    narrow = bool(step) and parts == 1
+    own, near, refs = refs[:parts], refs[parts : 2 * parts], refs[2 * parts :]
+    scale, near_scale = refs[:2] if step else (None, None)
     total, held_own, held_near = refs[-3:]
 
     def body():
@@ -243,13 +250,14 @@
     when_active(step or None, sections, body)
 
 
-def outer_kernel(step, sections, lats, tiles, shots, ends, late, packed, total, far, *refs):
-    narrow = bool(step)
-    scale, base, other = None, None, None
-    if narrow:
-        (scale, base), refs = refs[:2], refs[2:]
+def outer_kernel(step, sections, lats, tiles, shots, parts, ends, late, packed, total, *refs):
+    narrow = bool(step) and not ends
+    far, refs = refs[:parts], refs[parts:]
+    scale, base = None, None
+    if step:
+        scale, base, refs = refs[0], refs[1 : 1 + parts], refs[1 + parts :]
     if ends:
-        other, _, _, result_down, result_up, held, leaving, sems = refs
+        _, _, result_down, result_up, held, leaving, sems = refs
     else:
         outs, held = refs[:-1], refs[-1]
     lat = lax.axis_index("lat")
@@ -266,18 +274,19 @@
 
         def finish(j, value):
             at = pl.ds(pl.multiple_of(j * HALF, HALF), HALF)
-            if not narrow:
-                for out, part in zip(outs, parted(combined(value, shots))):
-                    out[at] = part
+            if narrow:
+                value = combined(value + turned(value), shots)
+                outs[0][at] = jnp.where(left_half(HALF), value[:HALF], value[HALF:]) + base[0][at]
                 return
-            value = combined(value + turned(value), shots)
-            part = jnp.where(left_half(HALF), value[:HALF], value[HALF:]) + base[at]
+            value = combined(value, shots)
             if ends:
-                leaving[pl.ds(pl.multiple_of(j * TILE, TILE), TILE)] = merged(other[at], part)
+                value = value + merged(*[part[at] for part in base])
+                leaving[pl.ds(pl.multiple_of(j * TILE, TILE), TILE)] = value
                 pl.when(depth == step)(lambda: copy_of(j, result_down).start())
                 pl.when(depth != step)(lambda: copy_of(j, result_up).start())
-            else:
-                outs[0][at] = part
+                return
+            for out, part in zip(outs, parted(value)):
+                out[at] = part
 
         @pl.when(has_far)
         def _():
@@ -306,8 +315,8 @@
         when_active(step, sections, body)
 
 
-def keep_kernel(sections, tiles, *refs):
-    fields, (result_down, result_up, whole, sems) = refs[:-4], refs[-4:]
+def keep_kernel(sections, tiles, steps, *refs):
+    fields, (result_down, result_up, whole, sems) = refs[: 2 * len(steps)], refs[-4:]
     depth = lax.axis_index("depth")
 
     def put(first, second, result):
@@ -317,8 +326,8 @@
         copy.start()
         copy.wait()
 
-    for step in range(sections - 1):
-        first, second = fields[2 * step : 2 * step + 2]
+    for i, step in enumerate(steps):
+        first, second = fields[2 * i : 2 * i + 2]
         pl.when(depth == step)(functools.partial(put, first, second, result_down))
         pl.when(depth == sections - 1 - step)(functools.partial(put, first, second, result_up))
 
@@ -359,7 +368,7 @@
         return near, move(field, functools.partial(far_of, spare))
 
     def next_door(d):
-        return d ^ 1
+        return (d + sections // 2) % sections
 
     first, second = call(
         functools.partial(prep_kernel, tiles, shots, sections),
@@ -396,29 +405,30 @@
     half = f32(rows // STREAMS, columns)
     result = [f32(1, rows, columns)] * 2
 
-    def held(step):
-        return VMEM((tiles * 2 * TILE, TILE if step else 2 * TILE), jnp.bfloat16)
+    def held(narrow):
+        return VMEM((tiles * 2 * TILE, TILE if narrow else 2 * TILE), jnp.bfloat16)
 
     def inner(step, own, near, *scales):
-        args = [packed, own, near, *scales]
+        args = [packed, *own, *near, *scales]
         return call(
-            functools.partial(inner_kernel, step, sections, tiles),
+            functools.partial(inner_kernel, step, sections, tiles, len(own)),
             out_shape=f32(tiles, 2 * TILE, columns),
             in_specs=[spec(VMEM)] * len(args),
             out_specs=spec(VMEM),
-            scratch_shapes=[held(step)] * 2,
+            scratch_shapes=[held(step and len(own) == 1)] * 2,
             compiler_params=params(),
             cost_estimate=cost(2 * 40 * 256**3, 8 * 2**20),
         )(*args)
 
-    def outer(step, *args, shapes, kept=(), late=False):
-        count = len(args) + 1
+    def outer(step, total, far, *more, shapes, kept=(), late=False):
         ends = bool(kept)
-        scratch = [held(step)]
+        args = [packed, total, *far, *more]
+        count = len(args)
+        scratch = [held(step and not ends)]
         if ends:
             scratch += [VMEM((rows, columns), jnp.float32), pltpu.SemaphoreType.DMA((tiles,))]
         return call(
-            functools.partial(outer_kernel, step, sections, lats, tiles, shots, ends, late),
+            functools.partial(outer_kernel, step, sections, lats, tiles, shots, len(far), ends, late),
             out_shape=shapes,
             in_specs=[spec(VMEM)] * count + [spec(pl.ANY)] * len(kept),
             out_specs=[spec(pl.ANY if ends else VMEM)] * len(shapes),
@@ -426,19 +436,33 @@
             input_output_aliases={count: 0, count + 1: 1} if ends else {},
             compiler_params=params(),
             cost_estimate=cost(2 * 15 * 256**3, 4 * 2**20),
-        )(packed, *args, *kept)
+        )(*args, *kept)
+
+    def keep(steps, kept=()):
+        args = [part for step in steps for part in fields[step]]
+        count = len(args)
+        return call(
+            functools.partial(keep_kernel, sections, tiles, steps),
+            out_shape=result,
+            in_specs=[spec(VMEM)] * count + [spec(pl.ANY)] * len(kept),
+            out_specs=[spec(pl.ANY)] * 2,
+            scratch_shapes=[VMEM((rows, columns), jnp.float32), pltpu.SemaphoreType.DMA(())],
+            input_output_aliases={count: 0, count + 1: 1} if kept else {},
+            compiler_params=params(),
+            cost_estimate=cost(0, 4 * rows * columns * 4),
+        )(*args, *kept)
 
     def cross(step, field):
         return [move(part, functools.partial(across, step)) for part in field]
 
     first_near, first_far = halo(first, next_door)
-    total = inner(0, first, first_near)
-    fields = [outer(0, total, first_far, shapes=[half] * STREAMS)]
-    first_base = outer(0, total, first_far, shapes=[half] * STREAMS, late=True)
+    total = inner(0, [first], [first_near])
+    fields = [outer(0, total, [first_far], shapes=[half] * STREAMS)]
+    first_base = outer(0, total, [first_far], shapes=[half] * STREAMS, late=True)
     arrived = cross(0, fields[0])
 
     second, *_ = lax.optimization_barrier((second, *fields[0]))
-    near, far = halo(second, lambda d: (d + sections // 2) % sections)
+    near, far = halo(second, next_door)
     own_scale, near_scale, far_scale = call(
         functools.partial(scale_kernel, tiles),
         out_shape=[square] * 3,
@@ -447,31 +471,23 @@
         compiler_params=params(),
         cost_estimate=cost(10**6, 4 * rows * columns * 4),
     )(first, first_near, first_far)
-    total = inner(None, second, near)
-    second_base = outer(None, total, far, shapes=[half] * STREAMS)
-
+    total = inner(None, [second], [near])
+    second_base = outer(None, total, [far], shapes=[half] * STREAMS)
+
+    middle = sections // 2
     for step in range(1, sections):
-        bases = first_base if step < sections // 2 else second_base
+        bases = first_base if step < middle else second_base
+        halos = [halo(part, next_door) for part in arrived]
+        nears, fars = zip(*halos)
+        if step == sections - 1:
+            total = inner(step, arrived, nears, own_scale, near_scale)
+            kept = keep(range(middle - 1)) if middle > 1 else ()
+            kept = keep(range(middle - 1, step), kept)
+            return tuple(outer(step, total, fars, far_scale, *bases, shapes=result, kept=kept))
         field = []
         for q in range(STREAMS):
-            near, far = halo(arrived[q], next_door)
-            total = inner(step, arrived[q], near, own_scale, near_scale)
-            if step == sections - 1 and q == STREAMS - 1:
-                kept = call(
-                    functools.partial(keep_kernel, sections, tiles),
-                    out_shape=result,
-                    in_specs=[spec(VMEM)] * (len(fields) * STREAMS),
-                    out_specs=[spec(pl.ANY)] * 2,
-                    scratch_shapes=[VMEM((rows, columns), jnp.float32), pltpu.SemaphoreType.DMA(())],
-                    compiler_params=params(),
-                    cost_estimate=cost(0, 4 * rows * columns * 4),
-                )(*[part for field_ in fields for part in field_])
-                ended = outer(
-                    step, total, far, far_scale, bases[q], field[0], shapes=result, kept=kept
-                )
-                return tuple(ended)
-            (part,) = outer(step, total, far, far_scale, bases[q], shapes=[half])
-            field.append(part)
+            total = inner(step, [arrived[q]], [nears[q]], own_scale, near_scale)
+            field += outer(step, total, [fars[q]], far_scale, bases[q], shapes=[half])
         fields.append(field)
         arrived = cross(step, field)
 

time: 61.6 us -> 61.4 us (level)
  the two profiles are of different devices: /device:TPU:0 before, /device:TPU:1 now
where the time goes in v7:
time: 61.4 us; the launch traced here: 61 us
  starting transfers between devices  28.2 us (46%)
  waiting for transfers between devices  17.3 us (28%)
  Pallas kernels  14.5 us (24%)
  between operations  0.96 us (2%)
    ppermute x22, starting transfers between devices, move(): return lax.ppermute(x, ('depth', 'lat'), pairs)  28.2 us
    ppermute x22, waiting for transfers between devices, move(): return lax.ppermute(x, ('depth', 'lat'), pairs)  17.3 us
    pallas_call x7, Pallas kernels, inner(): call(functools.partial(inner_kernel, step, sections, tiles, len(own)), ou...  5 us
    pallas_call x8, Pallas kernels, outer(): call(functools.partial(outer_kernel, step, sections, lats, tiles, shots,...  3.57 us
    pallas_call x1, Pallas kernels, shards(): call(functools.partial(pack_kernel, tiles, band), out_shape=jax.ShapeDtyp...  2.95 us
    pallas_call x1, Pallas kernels, shards(): call(functools.partial(prep_kernel, tiles, shots, sections), out_shape=[f...  1.76 us
  transfers between devices with their start and end apart: 22, of which 8 were waited for; matrix products, arithmetic and copies ran while one was open for 0% of the time, Pallas kernels for 17%

profile of v7, /device:TPU:1, one launch (start us, length us, event | category | flops | bytes accessed | tf_op | source)
XLA Modules:
  0.0 61.0 jit_solution(3126682017363658491)
XLA Ops:
  0.6 1.8 %shard_map.87 = (f32[648,128]{1,0:T(8,128)S(1)}, f32[640,128]{1,0:T(8,128)S(1)}) custom-call(s32[64]{0:T(128)} %assign_at.1, f32[1,640]{1,0:T(1,128)} %refl_at.1, f32[1,640,128]{2,1,0:T(8,128)} %up_at.1, f32[1,640,128]{2,1,0:T(8,128)} %down_at.1, f32[640,128]{1,0:T(8,128)} %src_at.1), custom_call_target="tpu_custom_call" | custom-call | flops 10000000 | bytes 1638400 | tf_op jit(solution)/shard_map/pallas_call | solution.py:373
  2.5 2.7 %collective-permute-start.1 = (f32[648,128]{1,0:T(8,128)S(1)}, f32[648,128]{1,0:T(8,128)S(1)}, u32[]{:S(2)}, u32[]{:S(2)}) collective-permute-start(f32[648,128]{1,0:T(8,128)S(1)} %get-tuple-element.18.refs_0_), channel_id=1, source_target_pairs={{0,16},{1,2},{2,1},{3,4},{4,3},{5,6},{6,5},{7,23},{8,24},{9,10},{1... | collective-permute-start | bytes 995336 | tf_op jit(solution)/shard_map/ppermute | solution.py:349
  5.2 3.0 %shard_map.86.packed = bf16[5,11,256,256]{3,2,1,0:T(8,128)(2,1)S(1)} custom-call(s32[1,5]{1,0:T(1,128)} %shift_at.1, f32[1,5,9,256,128]{4,3,2,1,0:T(8,128)} %tiles_at.1), custom_call_target="tpu_custom_call" | custom-call | flops 10000000 | bytes 11796480 | tf_op jit(solution)/shard_map/pallas_call | solution.py:390
  8.2 1.6 %shard_map.88.total = f32[5,256,128]{2,1,0:T(8,128)S(1)} custom-call(bf16[5,11,256,256]{3,2,1,0:T(8,128)(2,1)S(1)} %shard_map.86.packed, f32[648,128]{1,0:T(8,128)S(1)} %get-tuple-element.18.refs_0_, f32[648,128]{1,0:T(8,128)S(1)} %collective-permute-done.refs_1_), custom_call_target="tpu_custom_call" | custom-call | flops 1342177280 | bytes 8388608 | tf_op jit(solution)/shard_map/pallas_call | solution.py:413
  10.0 0.9 %shard_map.89 = (f32[320,128]{1,0:T(8,128)S(1)}, f32[320,128]{1,0:T(8,128)S(1)}) custom-call(bf16[5,11,256,256]{3,2,1,0:T(8,128)(2,1)S(1)} %shard_map.86.packed, f32[5,256,128]{2,1,0:T(8,128)S(1)} %shard_map.88.total, f32[648,128]{1,0:T(8,128)S(1)} %collective-permute-done.1.refs_0_.refs_2_), custom_call_target="tpu_custom_call" | custom-call | flops 503316480 | bytes 4194304 | tf_op jit(solution)/shard_map/pallas_call | solution.py:430
  11.6 0.9 %collective-permute-start.11 = (f32[320,128]{1,0:T(8,128)S(1)}, f32[320,128]{1,0:T(8,128)S(1)}, u32[]{:S(2)}, u32[]{:S(2)}) collective-permute-start(f32[320,128]{1,0:T(8,128)S(1)} %get-tuple-element.25.refs_1_), channel_id=1, source_target_pairs={{0,8},{1,9},{2,10},{3,11},{4,12},{5,13},{6,14},{7,15},{8,0},{9,1},... | collective-permute-start | bytes 491528 | tf_op jit(solution)/shard_map/ppermute | solution.py:349
  12.5 4.4 %collective-permute-done.2.refs_0_ = f32[320,128]{1,0:T(8,128)S(1)} collective-permute-done((f32[320,128]{1,0:T(8,128)S(1)}, f32[320,128]{1,0:T(8,128)S(1)}, u32[]{:S(2)}, u32[]{:S(2)}) %collective-permute-start.2) | collective-permute-done | bytes 163872 | tf_op jit(solution)/shard_map/ppermute | solution.py:349
  17.0 1.0 %collective-permute-start.3 = (f32[320,128]{1,0:T(8,128)S(1)}, f32[320,128]{1,0:T(8,128)S(1)}, u32[]{:S(2)}, u32[]{:S(2)}) collective-permute-start(f32[320,128]{1,0:T(8,128)S(1)} %collective-permute-done.2.refs_0_), channel_id=1, source_target_pairs={{0,1},{1,0},{2,3},{3,2},{4,5},{5,4},{6,7},{7,6},{8,9},{9,8},{10,11... | collective-permute-start | bytes 491528 | tf_op jit(solution)/shard_map/ppermute | solution.py:349
  18.0 2.4 %collective-permute-start.9 = (f32[640,128]{1,0:T(8,128)S(1)}, f32[640,128]{1,0:T(8,128)S(1)}, u32[]{:S(2)}, u32[]{:S(2)}) collective-permute-start(f32[640,128]{1,0:T(8,128)S(1)} %get-tuple-element.26.refs_0_), channel_id=1, source_target_pairs={{0,16},{1,2},{2,1},{3,4},{4,3},{5,6},{6,5},{7,23},{8,24},{9,10},{1... | collective-permute-start | bytes 983048 | tf_op jit(solution)/shard_map/ppermute | solution.py:349
  21.2 1.7 %collective-permute-start.13 = (f32[320,128]{1,0:T(8,128)S(1)}, f32[320,128]{1,0:T(8,128)S(1)}, u32[]{:S(2)}, u32[]{:S(2)}) collective-permute-start(f32[320,128]{1,0:T(8,128)S(1)} %collective-permute-done.11.refs_0_), channel_id=1, source_target_pairs={{0,16},{1,2},{2,1},{3,4},{4,3},{5,6},{6,5},{7,23},{8,24},{9,10},{1... | collective-permute-start | bytes 491528 | tf_op jit(solution)/shard_map/ppermute | solution.py:349
  22.8 4.3 %collective-permute-done.4.refs_0_ = f32[320,128]{1,0:T(8,128)S(1)} collective-permute-done((f32[320,128]{1,0:T(8,128)S(1)}, f32[320,128]{1,0:T(8,128)S(1)}, u32[]{:S(2)}, u32[]{:S(2)}) %collective-permute-start.4) | collective-permute-done | bytes 163872 | tf_op jit(solution)/shard_map/ppermute | solution.py:349
  27.3 1.4 %collective-permute-done.13.refs_0_ = f32[320,128]{1,0:T(8,128)S(1)} collective-permute-done((f32[320,128]{1,0:T(8,128)S(1)}, f32[320,128]{1,0:T(8,128)S(1)}, u32[]{:S(2)}, u32[]{:S(2)}) %collective-permute-start.13) | collective-permute-done | bytes 163872 | tf_op jit(solution)/shard_map/ppermute | solution.py:349
  29.2 1.6 %shard_map.95.total = f32[5,256,128]{2,1,0:T(8,128)S(1)} custom-call(bf16[5,11,256,256]{3,2,1,0:T(8,128)(2,1)S(1)} %shard_map.86.packed, f32[640,128]{1,0:T(8,128)S(1)} %get-tuple-element.26.refs_0_, f32[640,128]{1,0:T(8,128)S(1)} %collective-permute-done.8.refs_1_), custom_call_target="tpu_custom_call" | custom-call | flops 1342177280 | bytes 8388608 | tf_op jit(solution)/shard_map/pallas_call | solution.py:413
  30.8 1.8 %collective-permute-start.7 = (f32[320,128]{1,0:T(8,128)S(1)}, f32[320,128]{1,0:T(8,128)S(1)}, u32[]{:S(2)}, u32[]{:S(2)}) collective-permute-start(f32[320,128]{1,0:T(8,128)S(1)} %collective-permute-done.5.refs_0_), channel_id=1, source_target_pairs={{0,16},{1,2},{2,1},{3,4},{4,3},{5,6},{6,5},{7,23},{8,24},{9,10},{1... | collective-permute-start | bytes 491528 | tf_op jit(solution)/shard_map/ppermute | solution.py:349
  32.6 0.9 %shard_map.96 = (f32[320,128]{1,0:T(8,128)S(1)}, f32[320,128]{1,0:T(8,128)S(1)}) custom-call(bf16[5,11,256,256]{3,2,1,0:T(8,128)(2,1)S(1)} %shard_map.86.packed, f32[5,256,128]{2,1,0:T(8,128)S(1)} %shard_map.95.total, f32[640,128]{1,0:T(8,128)S(1)} %collective-permute-done.9.refs_0_), custom_call_target="tpu_custom_call" | custom-call | flops 503316480 | bytes 4194304 | tf_op jit(solution)/shard_map/pallas_call | solution.py:430
  33.5 5.3 %collective-permute-start.15 = (f32[320,128]{1,0:T(8,128)S(1)}, f32[320,128]{1,0:T(8,128)S(1)}, u32[]{:S(2)}, u32[]{:S(2)}) collective-permute-start(f32[320,128]{1,0:T(8,128)S(1)} %collective-permute-done.14.refs_0_), channel_id=1, source_target_pairs={{0,1},{1,0},{2,3},{3,2},{4,5},{5,4},{6,7},{7,6},{8,9},{9,8},{10,11... | collective-permute-start | bytes 491528 | tf_op jit(solution)/shard_map/ppermute | solution.py:349
  38.9 5.6 %collective-permute-start.10 = (f32[320,128]{1,0:T(8,128)S(1)}, f32[320,128]{1,0:T(8,128)S(1)}, u32[]{:S(2)}, u32[]{:S(2)}) collective-permute-start(f32[320,128]{1,0:T(8,128)S(1)} %shard_map.97.refs_2_), channel_id=1, source_target_pairs={{0,8},{1,9},{2,10},{3,11},{4,12},{5,13},{6,14},{7,15},{8,0},{9,1},... | collective-permute-start | bytes 491528 | tf_op jit(solution)/shard_map/ppermute | solution.py:349
  44.5 3.0 %collective-permute-start.17 = (f32[320,128]{1,0:T(8,128)S(1)}, f32[320,128]{1,0:T(8,128)S(1)}, u32[]{:S(2)}, u32[]{:S(2)}) collective-permute-start(f32[320,128]{1,0:T(8,128)S(1)} %shard_map.101.refs_3_), channel_id=1, source_target_pairs={{0,8},{1,9},{2,10},{3,11},{4,12},{5,13},{6,14},{7,15},{8,0},{9,1},... | collective-permute-start | bytes 491528 | tf_op jit(solution)/shard_map/ppermute | solution.py:349
  47.5 1.8 %collective-permute-done.10.refs_0_ = f32[320,128]{1,0:T(8,128)S(1)} collective-permute-done((f32[320,128]{1,0:T(8,128)S(1)}, f32[320,128]{1,0:T(8,128)S(1)}, u32[]{:S(2)}, u32[]{:S(2)}) %collective-permute-start.10) | collective-permute-done | bytes 163872 | tf_op jit(solution)/shard_map/ppermute | solution.py:349
  49.3 2.8 %collective-permute-done.17.refs_1_ = f32[320,128]{1,0:T(8,128)S(1)} collective-permute-done((f32[320,128]{1,0:T(8,128)S(1)}, f32[320,128]{1,0:T(8,128)S(1)}, u32[]{:S(2)}, u32[]{:S(2)}) %collective-permute-start.17) | collective-permute-done | bytes 163872 | tf_op jit(solution)/shard_map/ppermute | solution.py:349
  52.4 1.6 %collective-permute-start.20 = (f32[320,128]{1,0:T(8,128)S(1)}, f32[320,128]{1,0:T(8,128)S(1)}, u32[]{:S(2)}, u32[]{:S(2)}) collective-permute-start(f32[320,128]{1,0:T(8,128)S(1)} %collective-permute-done.10.refs_0_), channel_id=1, source_target_pairs={{0,16},{1,2},{2,1},{3,4},{4,3},{5,6},{6,5},{7,23},{8,24},{9,10},{1... | collective-permute-start | bytes 491528 | tf_op jit(solution)/shard_map/ppermute | solution.py:349
  55.1 1.7 %shard_map.102.total = f32[5,256,128]{2,1,0:T(8,128)S(1)} custom-call(bf16[5,11,256,256]{3,2,1,0:T(8,128)(2,1)S(1)} %shard_map.86.packed, f32[320,128]{1,0:T(8,128)S(1)} %collective-permute-done.10.refs_0_, f32[320,128]{1,0:T(8,128)S(1)} %collective-permute-done.17.refs_1_, f32[320,128]{1,0:T(8,128)S(1)} %collective-permute-done.18.refs_2_, ...), custom_call_target="tpu_custom_call" | custom-call | flops 1342177280 | bytes 8388608 | tf_op jit(solution)/shard_map/pallas_call | solution.py:413
  57.4 1.8 %collective-permute-done.21.refs_1_ = f32[320,128]{1,0:T(8,128)S(1)} collective-permute-done((f32[320,128]{1,0:T(8,128)S(1)}, f32[320,128]{1,0:T(8,128)S(1)}, u32[]{:S(2)}, u32[]{:S(2)}) %collective-permute-start.21) | collective-permute-done | bytes 163872 | tf_op jit(solution)/shard_map/ppermute | solution.py:349
  59.2 1.7 %shard_map.105 = (f32[1,640,128]{2,1,0:T(8,128)}, f32[1,640,128]{2,1,0:T(8,128)}) custom-call(bf16[5,11,256,256]{3,2,1,0:T(8,128)(2,1)S(1)} %shard_map.86.packed, f32[5,256,128]{2,1,0:T(8,128)S(1)} %shard_map.102.total, f32[320,128]{1,0:T(8,128)S(1)} %collective-permute-done.20.refs_0_, ...), custom_call_target="tpu_custom_call", output_to_operand_aliasing={{0}: (7, {}), {1}: (8, {})} | custom-call | flops 503316480 | bytes 4194304 | tf_op jit(solution)/shard_map/pallas_call | solution.py:430
  (40 shorter events, 4.4 us)
Async XLA Ops:
  2.4 5.8 %collective-permute-start = (f32[648,128]{1,0:T(8,128)S(1)}, f32[648,128]{1,0:T(8,128)S(1)}, u32[]{:S(2)}, u32[]{:S(2)}) collective-permute-start(f32[648,128]{1,0:T(8,128)S(1)} %get-tuple-element.18.refs_0_), channel_id=1, source_target_pairs={{0,1},{1,0},{2,3},{3,2},{4,5},{5,4},{6,7},{7,6},{8,9},{9,8},{10,11... | collective-permute-start | bytes 995336 | tf_op jit(solution)/shard_map/ppermute | solution.py:349
  2.5 7.5 %collective-permute-start.1 = (f32[648,128]{1,0:T(8,128)S(1)}, f32[648,128]{1,0:T(8,128)S(1)}, u32[]{:S(2)}, u32[]{:S(2)}) collective-permute-start(f32[648,128]{1,0:T(8,128)S(1)} %get-tuple-element.18.refs_0_), channel_id=1, source_target_pairs={{0,16},{1,2},{2,1},{3,4},{4,3},{5,6},{6,5},{7,23},{8,24},{9,10},{1... | collective-permute-start | bytes 995336 | tf_op jit(solution)/shard_map/ppermute | solution.py:349
  11.0 6.0 %collective-permute-start.2 = (f32[320,128]{1,0:T(8,128)S(1)}, f32[320,128]{1,0:T(8,128)S(1)}, u32[]{:S(2)}, u32[]{:S(2)}) collective-permute-start(f32[320,128]{1,0:T(8,128)S(1)} %get-tuple-element.19.refs_0_), channel_id=1, source_target_pairs={{0,8},{1,9},{2,10},{3,11},{4,12},{5,13},{6,14},{7,15},{8,0},{9,1},... | collective-permute-start | bytes 491528 | tf_op jit(solution)/shard_map/ppermute | solution.py:349
  11.6 9.2 %collective-permute-start.11 = (f32[320,128]{1,0:T(8,128)S(1)}, f32[320,128]{1,0:T(8,128)S(1)}, u32[]{:S(2)}, u32[]{:S(2)}) collective-permute-start(f32[320,128]{1,0:T(8,128)S(1)} %get-tuple-element.25.refs_1_), channel_id=1, source_target_pairs={{0,8},{1,9},{2,10},{3,11},{4,12},{5,13},{6,14},{7,15},{8,0},{9,1},... | collective-permute-start | bytes 491528 | tf_op jit(solution)/shard_map/ppermute | solution.py:349
  17.0 4.2 %collective-permute-start.3 = (f32[320,128]{1,0:T(8,128)S(1)}, f32[320,128]{1,0:T(8,128)S(1)}, u32[]{:S(2)}, u32[]{:S(2)}) collective-permute-start(f32[320,128]{1,0:T(8,128)S(1)} %collective-permute-done.2.refs_0_), channel_id=1, source_target_pairs={{0,1},{1,0},{2,3},{3,2},{4,5},{5,4},{6,7},{7,6},{8,9},{9,8},{10,11... | collective-permute-start | bytes 491528 | tf_op jit(solution)/shard_map/ppermute | solution.py:349
  18.0 11.2 %collective-permute-start.8 = (f32[640,128]{1,0:T(8,128)S(1)}, f32[640,128]{1,0:T(8,128)S(1)}, u32[]{:S(2)}, u32[]{:S(2)}) collective-permute-start(f32[640,128]{1,0:T(8,128)S(1)} %get-tuple-element.26.refs_0_), channel_id=1, source_target_pairs={{0,1},{1,0},{2,3},{3,2},{4,5},{5,4},{6,7},{7,6},{8,9},{9,8},{10,11... | collective-permute-start | bytes 983048 | tf_op jit(solution)/shard_map/ppermute | solution.py:349
  18.0 14.6 %collective-permute-start.9 = (f32[640,128]{1,0:T(8,128)S(1)}, f32[640,128]{1,0:T(8,128)S(1)}, u32[]{:S(2)}, u32[]{:S(2)}) collective-permute-start(f32[640,128]{1,0:T(8,128)S(1)} %get-tuple-element.26.refs_0_), channel_id=1, source_target_pairs={{0,16},{1,2},{2,1},{3,4},{4,3},{5,6},{6,5},{7,23},{8,24},{9,10},{1... | collective-permute-start | bytes 983048 | tf_op jit(solution)/shard_map/ppermute | solution.py:349
  20.7 6.5 %collective-permute-start.4 = (f32[320,128]{1,0:T(8,128)S(1)}, f32[320,128]{1,0:T(8,128)S(1)}, u32[]{:S(2)}, u32[]{:S(2)}) collective-permute-start(f32[320,128]{1,0:T(8,128)S(1)} %collective-permute-done.2.refs_0_), channel_id=1, source_target_pairs={{0,16},{1,2},{2,1},{3,4},{4,3},{5,6},{6,5},{7,23},{8,24},{9,10},{1... | collective-permute-start | bytes 491528 | tf_op jit(solution)/shard_map/ppermute | solution.py:349
  20.8 6.5 %collective-permute-start.12 = (f32[320,128]{1,0:T(8,128)S(1)}, f32[320,128]{1,0:T(8,128)S(1)}, u32[]{:S(2)}, u32[]{:S(2)}) collective-permute-start(f32[320,128]{1,0:T(8,128)S(1)} %collective-permute-done.11.refs_0_), channel_id=1, source_target_pairs={{0,1},{1,0},{2,3},{3,2},{4,5},{5,4},{6,7},{7,6},{8,9},{9,8},{10,11... | collective-permute-start | bytes 491528 | tf_op jit(solution)/shard_map/ppermute | solution.py:349
  21.2 7.5 %collective-permute-start.13 = (f32[320,128]{1,0:T(8,128)S(1)}, f32[320,128]{1,0:T(8,128)S(1)}, u32[]{:S(2)}, u32[]{:S(2)}) collective-permute-start(f32[320,128]{1,0:T(8,128)S(1)} %collective-permute-done.11.refs_0_), channel_id=1, source_target_pairs={{0,16},{1,2},{2,1},{3,4},{4,3},{5,6},{6,5},{7,23},{8,24},{9,10},{1... | collective-permute-start | bytes 491528 | tf_op jit(solution)/shard_map/ppermute | solution.py:349
  27.2 1.9 %collective-permute-start.5 = (f32[320,128]{1,0:T(8,128)S(1)}, f32[320,128]{1,0:T(8,128)S(1)}, u32[]{:S(2)}, u32[]{:S(2)}) collective-permute-start(f32[320,128]{1,0:T(8,128)S(1)} %shard_map.93.refs_0_), channel_id=1, source_target_pairs={{0,1},{1,0},{2,3},{3,2},{4,5},{5,4},{6,7},{7,6},{8,16},{9,17},{10,... | collective-permute-start | bytes 491528 | tf_op jit(solution)/shard_map/ppermute | solution.py:349
  28.7 4.9 %collective-permute-start.14 = (f32[320,128]{1,0:T(8,128)S(1)}, f32[320,128]{1,0:T(8,128)S(1)}, u32[]{:S(2)}, u32[]{:S(2)}) collective-permute-start(f32[320,128]{1,0:T(8,128)S(1)} %shard_map.99.refs_1_), channel_id=1, source_target_pairs={{0,1},{1,0},{2,3},{3,2},{4,5},{5,4},{6,7},{7,6},{8,16},{9,17},{10,... | collective-permute-start | bytes 491528 | tf_op jit(solution)/shard_map/ppermute | solution.py:349
  29.1 9.8 %collective-permute-start.6 = (f32[320,128]{1,0:T(8,128)S(1)}, f32[320,128]{1,0:T(8,128)S(1)}, u32[]{:S(2)}, u32[]{:S(2)}) collective-permute-start(f32[320,128]{1,0:T(8,128)S(1)} %collective-permute-done.5.refs_0_), channel_id=1, source_target_pairs={{0,1},{1,0},{2,3},{3,2},{4,5},{5,4},{6,7},{7,6},{8,9},{9,8},{10,11... | collective-permute-start | bytes 491528 | tf_op jit(solution)/shard_map/ppermute | solution.py:349
  30.8 8.1 %collective-permute-start.7 = (f32[320,128]{1,0:T(8,128)S(1)}, f32[320,128]{1,0:T(8,128)S(1)}, u32[]{:S(2)}, u32[]{:S(2)}) collective-permute-start(f32[320,128]{1,0:T(8,128)S(1)} %collective-permute-done.5.refs_0_), channel_id=1, source_target_pairs={{0,16},{1,2},{2,1},{3,4},{4,3},{5,6},{6,5},{7,23},{8,24},{9,10},{1... | collective-permute-start | bytes 491528 | tf_op jit(solution)/shard_map/ppermute | solution.py:349
  33.5 11.0 %collective-permute-start.15 = (f32[320,128]{1,0:T(8,128)S(1)}, f32[320,128]{1,0:T(8,128)S(1)}, u32[]{:S(2)}, u32[]{:S(2)}) collective-permute-start(f32[320,128]{1,0:T(8,128)S(1)} %collective-permute-done.14.refs_0_), channel_id=1, source_target_pairs={{0,1},{1,0},{2,3},{3,2},{4,5},{5,4},{6,7},{7,6},{8,9},{9,8},{10,11... | collective-permute-start | bytes 491528 | tf_op jit(solution)/shard_map/ppermute | solution.py:349
  38.9 5.7 %collective-permute-start.16 = (f32[320,128]{1,0:T(8,128)S(1)}, f32[320,128]{1,0:T(8,128)S(1)}, u32[]{:S(2)}, u32[]{:S(2)}) collective-permute-start(f32[320,128]{1,0:T(8,128)S(1)} %collective-permute-done.14.refs_0_), channel_id=1, source_target_pairs={{0,16},{1,2},{2,1},{3,4},{4,3},{5,6},{6,5},{7,23},{8,24},{9,10},{1... | collective-permute-start | bytes 491528 | tf_op jit(solution)/shard_map/ppermute | solution.py:349
  38.9 10.4 %collective-permute-start.10 = (f32[320,128]{1,0:T(8,128)S(1)}, f32[320,128]{1,0:T(8,128)S(1)}, u32[]{:S(2)}, u32[]{:S(2)}) collective-permute-start(f32[320,128]{1,0:T(8,128)S(1)} %shard_map.97.refs_2_), channel_id=1, source_target_pairs={{0,8},{1,9},{2,10},{3,11},{4,12},{5,13},{6,14},{7,15},{8,0},{9,1},... | collective-permute-start | bytes 491528 | tf_op jit(solution)/shard_map/ppermute | solution.py:349
  44.5 7.6 %collective-permute-start.17 = (f32[320,128]{1,0:T(8,128)S(1)}, f32[320,128]{1,0:T(8,128)S(1)}, u32[]{:S(2)}, u32[]{:S(2)}) collective-permute-start(f32[320,128]{1,0:T(8,128)S(1)} %shard_map.101.refs_3_), channel_id=1, source_target_pairs={{0,8},{1,9},{2,10},{3,11},{4,12},{5,13},{6,14},{7,15},{8,0},{9,1},... | collective-permute-start | bytes 491528 | tf_op jit(solution)/shard_map/ppermute | solution.py:349
  49.3 5.8 %collective-permute-start.18 = (f32[320,128]{1,0:T(8,128)S(1)}, f32[320,128]{1,0:T(8,128)S(1)}, u32[]{:S(2)}, u32[]{:S(2)}) collective-permute-start(f32[320,128]{1,0:T(8,128)S(1)} %collective-permute-done.10.refs_0_), channel_id=1, source_target_pairs={{0,1},{1,0},{2,3},{3,2},{4,5},{5,4},{6,7},{7,6},{8,9},{9,8},{10,11... | collective-permute-start | bytes 491528 | tf_op jit(solution)/shard_map/ppermute | solution.py:349
  52.1 3.0 %collective-permute-start.19 = (f32[320,128]{1,0:T(8,128)S(1)}, f32[320,128]{1,0:T(8,128)S(1)}, u32[]{:S(2)}, u32[]{:S(2)}) collective-permute-start(f32[320,128]{1,0:T(8,128)S(1)} %collective-permute-done.17.refs_1_), channel_id=1, source_target_pairs={{0,1},{1,0},{2,3},{3,2},{4,5},{5,4},{6,7},{7,6},{8,9},{9,8},{10,11... | collective-permute-start | bytes 491528 | tf_op jit(solution)/shard_map/ppermute | solution.py:349
  52.4 5.0 %collective-permute-start.20 = (f32[320,128]{1,0:T(8,128)S(1)}, f32[320,128]{1,0:T(8,128)S(1)}, u32[]{:S(2)}, u32[]{:S(2)}) collective-permute-start(f32[320,128]{1,0:T(8,128)S(1)} %collective-permute-done.10.refs_0_), channel_id=1, source_target_pairs={{0,16},{1,2},{2,1},{3,4},{4,3},{5,6},{6,5},{7,23},{8,24},{9,10},{1... | collective-permute-start | bytes 491528 | tf_op jit(solution)/shard_map/ppermute | solution.py:349
  53.9 5.2 %collective-permute-start.21 = (f32[320,128]{1,0:T(8,128)S(1)}, f32[320,128]{1,0:T(8,128)S(1)}, u32[]{:S(2)}, u32[]{:S(2)}) collective-permute-start(f32[320,128]{1,0:T(8,128)S(1)} %collective-permute-done.17.refs_1_), channel_id=1, source_target_pairs={{0,16},{1,2},{2,1},{3,4},{4,3},{5,6},{6,5},{7,23},{8,24},{9,10},{1... | collective-permute-start | bytes 491528 | tf_op jit(solution)/shard_map/ppermute | solution.py:349

commit v8 on v7

--- a/solution.py
+++ b/solution.py
@@ -53,36 +53,19 @@
     return high, low
 
 
-def prep_kernel(tiles, shots, sections, assign_at, refl_at, up_at, down_at, src_at, first, second, assign, refl, up, down, src, sems):
+def prep_kernel(tiles, shots, sections, assign_at, refl_at, up_at, down_at, src_at, first, second, *refs):
+    *streams, assign, refl, up, down, src, pick, sems = refs
     depth = lax.axis_index("depth")
     loads = [
         pltpu.make_async_copy(assign_at, assign, sems.at[0]),
         pltpu.make_async_copy(refl_at, refl, sems.at[1]),
-        pltpu.make_async_copy(up_at, up, sems.at[2]),
-        pltpu.make_async_copy(down_at, down, sems.at[3]),
-        pltpu.make_async_copy(src_at, src, sems.at[4]),
+        pltpu.make_async_copy(src_at, src, sems.at[2]),
+        pltpu.make_async_copy(up_at, up, sems.at[3]),
+        pltpu.make_async_copy(down_at, down, sems.at[4]),
     ]
     for load in loads:
         load.start()
-    for load in loads:
-        load.wait()
-    descends = depth < sections // 2
-
-    def write(of_up, of_down):
-        for j in range(tiles):
-            row = refl[0:1, rows_of(j)]
-            r = down_column(row)
-            of_up[rows_of(j)] = -(r * up[0, rows_of(j)])
-            of_down[rows_of(j)] = r * down[0, rows_of(j)]
-            first[tiles * TILE + j : tiles * TILE + j + 1] = row
-
-    @pl.when(descends)
-    def _():
-        write(first, second)
-
-    @pl.when(jnp.logical_not(descends))
-    def _():
-        write(second, first)
+    loads[0].wait()
 
     @pl.when(depth == 0)
     def _():
@@ -95,35 +78,51 @@
                 wanted = jnp.where(lane == at, shot, wanted)
                 wanted = jnp.where(lane == at + shots, shot + TILE // 2, wanted)
         source = lax.broadcasted_iota(jnp.int32, (TILE, TILE), 0)
-        pick = (source == jnp.broadcast_to(wanted[0:1], (TILE, TILE))).astype(jnp.float32).astype(jnp.bfloat16)
+        found = source == jnp.broadcast_to(wanted[0:1], (TILE, TILE))
+        pick[...] = found.astype(jnp.float32).astype(jnp.bfloat16)
+
+    for load in loads[1:]:
+        load.wait()
+    descends = depth < sections // 2
+
+    def of_up(j):
+        return -(down_column(refl[0:1, rows_of(j)]) * up[0, rows_of(j)])
+
+    def of_down(j):
+        return down_column(refl[0:1, rows_of(j)]) * down[0, rows_of(j)]
+
+    def put(j, tile, later):
+        first[rows_of(j)] = tile
+        for stream, part in zip(streams, parted(tile)):
+            stream[halves_of(j)] = part
+        second[rows_of(j)] = later
+
+    for j in range(tiles):
+        row = refl[0:1, rows_of(j)]
+        first[tiles * TILE + j : tiles * TILE + j + 1] = row
+        streams[0][tiles * HALF + j : tiles * HALF + j + 1] = row
+
+    @pl.when(descends & (depth > 0))
+    def _():
+        for j in range(tiles):
+            put(j, of_up(j), of_down(j))
+
+    @pl.when(jnp.logical_not(descends))
+    def _():
+        for j in range(tiles):
+            put(j, of_down(j), of_up(j))
+
+    @pl.when(depth == 0)
+    def _():
         for j in range(tiles):
             x = src[rows_of(j)]
             high = x.astype(jnp.bfloat16)
             mid, low = split(x - high.astype(jnp.float32))
-            entering = jnp.dot(low, pick, preferred_element_type=jnp.float32)
-            entering += jnp.dot(mid, pick, preferred_element_type=jnp.float32)
-            entering += jnp.dot(high, pick, preferred_element_type=jnp.float32)
+            entering = jnp.dot(low, pick[...], preferred_element_type=jnp.float32)
+            entering += jnp.dot(mid, pick[...], preferred_element_type=jnp.float32)
+            entering += jnp.dot(high, pick[...], preferred_element_type=jnp.float32)
             r = down_column(refl[0:1, rows_of(j)])
-            first[rows_of(j)] = (1.0 + r) * entering + first[rows_of(j)]
-
-
-def pack_kernel(tiles, band, shift_at, tiles_at, out, shift, held, sems):
-    loads = [pltpu.make_async_copy(shift_at, shift, sems.at[tiles])]
-    loads += [pltpu.make_async_copy(tiles_at.at[0, j], held.at[j], sems.at[j]) for j in range(tiles)]
-    for load in loads:
-        load.start()
-    loads[0].wait()
-    for j in range(tiles):
-        loads[1 + j].wait()
-        move = shift[0, j]
-        for k in range(band):
-            high, low = split(held[j, k])
-            slot = k + 1 + move
-            out[j, slot, :, :TILE] = high
-            out[j, slot, :, TILE:] = low
-        zero = jnp.zeros(out.shape[2:], jnp.bfloat16)
-        out[j, jnp.where(move >= 0, 0, band)] = zero
-        out[j, jnp.where(move <= 0, band + 1, 1)] = zero
+            put(j, (1.0 + r) * entering + of_up(j), of_down(j))
 
 
 def doubled(tile):
@@ -226,8 +225,34 @@
 def scale_kernel(tiles, *refs):
     for source, out in zip(refs[:3], refs[3:]):
         for t in range(tiles):
-            at = tiles * TILE + t
+            at = source.shape[0] - 8 + t
             out[t] = down_column(source[at : at + 1])
+
+
+def pack_kernel(tiles, band, shift_at, tiles_at, own, near, packed, total, shift, raw, held_own, held_near, sems):
+    loads = [pltpu.make_async_copy(shift_at, shift, sems.at[tiles])]
+    loads += [pltpu.make_async_copy(tiles_at.at[0, j], raw.at[j], sems.at[j]) for j in range(tiles)]
+    for load in loads:
+        load.start()
+    low_side = lax.rem(lax.axis_index("lat"), 2) == 1
+    spread([own], None, None, tiles, False, None, held_own)
+    spread([near], None, None, tiles, False, low_side, held_near)
+    zero = jnp.zeros(packed.shape[2:], jnp.bfloat16)
+    loads[0].wait()
+    for j in range(tiles):
+        loads[1 + j].wait()
+        move = shift[0, j]
+        for k in range(band):
+            high, low = split(raw[j, k])
+            slot = k + 1 + move
+            packed[j, slot, :, :TILE] = high
+            packed[j, slot, :, TILE:] = low
+        packed[j, jnp.where(move >= 0, 0, band)] = zero
+        packed[j, jnp.where(move <= 0, band + 1, 1)] = zero
+        total[j] = product(packed, held_own, j, range(tiles - j, 2 * tiles - j), False)
+    for jj in range(tiles):
+        j, value = side_product(packed, held_near, tiles, jj, low_side, False)
+        total[j] = total[j] + value
 
 
 def inner_kernel(step, sections, tiles, parts, packed, *refs):
@@ -250,8 +275,8 @@
     when_active(step or None, sections, body)
 
 
-def outer_kernel(step, sections, lats, tiles, shots, parts, ends, late, packed, total, *refs):
-    narrow = bool(step) and not ends
+def outer_kernel(step, sections, lats, tiles, shots, parts, stream, ends, late, packed, total, *refs):
+    narrow = stream is not None
     far, refs = refs[:parts], refs[parts:]
     scale, base = None, None
     if step:
@@ -272,13 +297,22 @@
             at = pl.ds(pl.multiple_of(j * TILE, TILE), TILE)
             return pltpu.make_async_copy(leaving.at[at], result.at[0, at], sems.at[j])
 
-        def finish(j, value):
+        def finish(j, value, more):
             at = pl.ds(pl.multiple_of(j * HALF, HALF), HALF)
+            if narrow and step == 0:
+                mine = left_half(2 * TILE) if stream == 0 else jnp.logical_not(left_half(2 * TILE))
+                value = jnp.where(mine, value, turned(value))
+                if more is not None:
+                    value = value + (more + turned(more))
+            else:
+                value = value if more is None else value + more
+                if narrow:
+                    value = value + turned(value)
+            value = combined(value, shots)
             if narrow:
-                value = combined(value + turned(value), shots)
-                outs[0][at] = jnp.where(left_half(HALF), value[:HALF], value[HALF:]) + base[0][at]
+                value = jnp.where(left_half(HALF), value[:HALF], value[HALF:])
+                outs[0][at] = value if base is None else value + base[0][at]
                 return
-            value = combined(value, shots)
             if ends:
                 value = value + merged(*[part[at] for part in base])
                 leaving[pl.ds(pl.multiple_of(j * TILE, TILE), TILE)] = value
@@ -293,12 +327,12 @@
             spread(far, scale, sign, tiles, narrow, low_side, held)
             for jj in range(tiles):
                 j, value = side_product(packed, held, tiles, jj, low_side, narrow)
-                finish(j, total[j] + value)
+                finish(j, total[j], value)
 
         @pl.when(jnp.logical_not(has_far))
         def _():
             for j in range(tiles):
-                finish(j, total[j])
+                finish(j, total[j], None)
 
         if ends:
 
@@ -370,39 +404,26 @@
     def next_door(d):
         return (d + sections // 2) % sections
 
-    first, second = call(
+    half = f32(rows // STREAMS, columns)
+    first, second, *streams = call(
         functools.partial(prep_kernel, tiles, shots, sections),
-        out_shape=[f32(rows + 8, columns), f32(rows, columns)],
+        out_shape=[f32(rows + 8, columns), f32(rows, columns), f32(rows // STREAMS + 8, columns), half],
         in_specs=[spec(pltpu.HBM)] * 5,
-        out_specs=[spec(VMEM)] * 2,
+        out_specs=[spec(VMEM)] * 4,
         scratch_shapes=[
             pltpu.SMEM(assignment.shape, jnp.int32),
             VMEM(reflectivity.shape, jnp.float32),
             VMEM(up_stored.shape, jnp.float32),
             VMEM(down_stored.shape, jnp.float32),
             VMEM(sources.shape, jnp.float32),
+            VMEM((TILE, TILE), jnp.bfloat16),
             pltpu.SemaphoreType.DMA((5,)),
         ],
         compiler_params=params(),
         cost_estimate=cost(10**7, 5 * rows * columns * 4),
     )(*map(in_hbm, (assignment, reflectivity, up_stored, down_stored, sources)))
 
-    packed = call(
-        functools.partial(pack_kernel, tiles, band),
-        out_shape=jax.ShapeDtypeStruct((tiles, band + 2, 2 * TILE, 2 * TILE), jnp.bfloat16),
-        in_specs=[spec(pltpu.HBM)] * 2,
-        out_specs=spec(VMEM),
-        scratch_shapes=[
-            pltpu.SMEM(band_shift.shape, jnp.int32),
-            VMEM(operator.shape[1:], jnp.float32),
-            pltpu.SemaphoreType.DMA((tiles + 1,)),
-        ],
-        compiler_params=params(),
-        cost_estimate=cost(10**7, 2 * operator.size * 4),
-    )(in_hbm(band_shift), in_hbm(operator))
-
     square = f32(tiles, TILE, columns)
-    half = f32(rows // STREAMS, columns)
     result = [f32(1, rows, columns)] * 2
 
     def held(narrow):
@@ -420,15 +441,15 @@
             cost_estimate=cost(2 * 40 * 256**3, 8 * 2**20),
         )(*args)
 
-    def outer(step, total, far, *more, shapes, kept=(), late=False):
+    def outer(step, total, far, *more, shapes, stream=None, kept=(), late=False):
         ends = bool(kept)
         args = [packed, total, *far, *more]
         count = len(args)
-        scratch = [held(step and not ends)]
+        scratch = [held(stream is not None)]
         if ends:
             scratch += [VMEM((rows, columns), jnp.float32), pltpu.SemaphoreType.DMA((tiles,))]
         return call(
-            functools.partial(outer_kernel, step, sections, lats, tiles, shots, len(far), ends, late),
+            functools.partial(outer_kernel, step, sections, lats, tiles, shots, len(far), stream, ends, late),
             out_shape=shapes,
             in_specs=[spec(VMEM)] * count + [spec(pl.ANY)] * len(kept),
             out_specs=[spec(pl.ANY if ends else VMEM)] * len(shapes),
@@ -455,10 +476,31 @@
     def cross(step, field):
         return [move(part, functools.partial(across, step)) for part in field]
 
-    first_near, first_far = halo(first, next_door)
-    total = inner(0, [first], [first_near])
-    fields = [outer(0, total, [first_far], shapes=[half] * STREAMS)]
-    first_base = outer(0, total, [first_far], shapes=[half] * STREAMS, late=True)
+    first_near = move(first, near_of)
+    first_fars = [move(part, functools.partial(far_of, next_door)) for part in streams]
+    packed, total = call(
+        functools.partial(pack_kernel, tiles, band),
+        out_shape=[
+            jax.ShapeDtypeStruct((tiles, band + 2, 2 * TILE, 2 * TILE), jnp.bfloat16),
+            f32(tiles, 2 * TILE, columns),
+        ],
+        in_specs=[spec(pltpu.HBM)] * 2 + [spec(VMEM)] * 2,
+        out_specs=[spec(VMEM)] * 2,
+        scratch_shapes=[
+            pltpu.SMEM(band_shift.shape, jnp.int32),
+            VMEM(operator.shape[1:], jnp.float32),
+            held(False),
+            held(False),
+            pltpu.SemaphoreType.DMA((tiles + 1,)),
+        ],
+        compiler_params=params(),
+        cost_estimate=cost(2 * 40 * 256**3, 2 * operator.size * 4),
+    )(in_hbm(band_shift), in_hbm(operator), first, first_near)
+    field = []
+    for q in range(STREAMS):
+        field += outer(0, total, [first_fars[q]], shapes=[half], stream=q)
+    fields = [field]
+    first_base = outer(0, total, first_fars, shapes=[half] * STREAMS, late=True)
     arrived = cross(0, fields[0])
 
     second, *_ = lax.optimization_barrier((second, *fields[0]))
@@ -470,7 +512,7 @@
         out_specs=[spec(VMEM)] * 3,
         compiler_params=params(),
         cost_estimate=cost(10**6, 4 * rows * columns * 4),
-    )(first, first_near, first_far)
+    )(first, first_near, first_fars[0])
     total = inner(None, [second], [near])
     second_base = outer(None, total, [far], shapes=[half] * STREAMS)
 
@@ -487,7 +529,7 @@
         field = []
         for q in range(STREAMS):
             total = inner(step, [arrived[q]], [nears[q]], own_scale, near_scale)
-            field += outer(step, total, [fars[q]], far_scale, bases[q], shapes=[half])
+            field += outer(step, total, [fars[q]], far_scale, bases[q], shapes=[half], stream=q)
         fields.append(field)
         arrived = cross(step, field)
 

time: 61.4 us -> 62 us (level)
  Pallas kernels: 14.5 us -> 16.6 us
  starting transfers between devices: 28.2 us -> 27.2 us
  waiting for transfers between devices: 17.3 us -> 16.5 us
    pallas_call x1, Pallas kernels: 2.95 us -> 5.32 us  [shards(): call(functools.partial(pack_kernel, tiles, band), out_shape=[jax.ShapeDty...]
    pallas_call x7 -> x6, Pallas kernels: 5 us -> 3.38 us  [inner(): call(functools.partial(inner_kernel, step, sections, tiles, len(own)), ou...]
    pallas_call x8 -> x9, Pallas kernels: 3.57 us -> 4.78 us  [outer(): call(functools.partial(outer_kernel, step, sections, lats, tiles, shots,...]
    ppermute x22 -> x23, starting transfers between devices: 28.2 us -> 27.2 us  [move(): return lax.ppermute(x, ('depth', 'lat'), pairs)]
    ppermute x22 -> x23, waiting for transfers between devices: 17.3 us -> 16.5 us  [move(): return lax.ppermute(x, ('depth', 'lat'), pairs)]
  transfers between devices with their start and end apart: 22 -> 23, of which waited for: 8 -> 7; matrix products, arithmetic and copies ran while one was open for 0% -> 0% of each run, Pallas kernels for 17% -> 22%
where the time goes in v8:
time: 62 us; the launch traced here: 61.3 us
  starting transfers between devices  27.2 us (44%)
  Pallas kernels  16.6 us (27%)
  waiting for transfers between devices  16.5 us (27%)
  between operations  0.99 us (2%)
    ppermute x23, starting transfers between devices, move(): return lax.ppermute(x, ('depth', 'lat'), pairs)  27.2 us
    ppermute x23, waiting for transfers between devices, move(): return lax.ppermute(x, ('depth', 'lat'), pairs)  16.5 us
    pallas_call x1, Pallas kernels, shards(): call(functools.partial(pack_kernel, tiles, band), out_shape=[jax.ShapeDty...  5.32 us
    pallas_call x9, Pallas kernels, outer(): call(functools.partial(outer_kernel, step, sections, lats, tiles, shots,...  4.78 us
    pallas_call x6, Pallas kernels, inner(): call(functools.partial(inner_kernel, step, sections, tiles, len(own)), ou...  3.38 us
    pallas_call x1, Pallas kernels, shards(): call(functools.partial(prep_kernel, tiles, shots, sections), out_shape=[f...  1.61 us
  transfers between devices with their start and end apart: 23, of which 7 were waited for; matrix products, arithmetic and copies ran while one was open for 0% of the time, Pallas kernels for 22%

profile of v8, /device:TPU:1, one launch (start us, length us, event | category | flops | bytes accessed | tf_op | source)
XLA Modules:
  0.0 61.3 jit_solution(6697325327689407258)
XLA Ops:
  0.6 1.6 %shard_map.86 = (f32[648,128]{1,0:T(8,128)S(1)}, f32[640,128]{1,0:T(8,128)S(1)}, f32[328,128]{1,0:T(8,128)S(1)}, f32[320,128]{1,0:T(8,128)S(1)}) custom-call(s32[64]{0:T(128)} %assign_at.1, f32[1,640]{1,0:T(1,128)} %refl_at.1, f32[1,640,128]{2,1,0:T(8,128)} %up_at.1, f32[1,640,128]{2,1,0:T(8,128)} %down_at.1, f32[640,128]{1,0:T(8,128)} %src_at.1), custom_call_target="tpu_custom_call" | custom-call | flops 10000000 | bytes 1638400 | tf_op jit(solution)/shard_map/pallas_call | solution.py:408
  2.3 2.7 %collective-permute-start.1 = (f32[328,128]{1,0:T(8,128)S(1)}, f32[328,128]{1,0:T(8,128)S(1)}, u32[]{:S(2)}, u32[]{:S(2)}) collective-permute-start(f32[328,128]{1,0:T(8,128)S(1)} %get-tuple-element.23), channel_id=1, source_target_pairs={{0,16},{1,2},{2,1},{3,4},{4,3},{5,6},{6,5},{7,23},{8,24},{9,10},{1... | collective-permute-start | bytes 503816 | tf_op jit(solution)/shard_map/ppermute | solution.py:383
  5.2 5.3 %shard_map.87 = (bf16[5,11,256,256]{3,2,1,0:T(8,128)(2,1)S(1)}, f32[5,256,128]{2,1,0:T(8,128)S(1)}) custom-call(s32[1,5]{1,0:T(1,128)} %shift_at.1, f32[1,5,9,256,128]{4,3,2,1,0:T(8,128)} %tiles_at.1, f32[648,128]{1,0:T(8,128)S(1)} %get-tuple-element.20.own.refs_0_, f32[648,128]{1,0:T(8,128)S(1)} %collective-permute-done.near.refs_1_), custom_call_target="tpu_custom_call" | custom-call | flops 1342177280 | bytes 11796480 | tf_op jit(solution)/shard_map/pallas_call | solution.py:481
  10.5 1.1 %shard_map.88.refs_0_ = f32[320,128]{1,0:T(8,128)S(1)} custom-call(bf16[5,11,256,256]{3,2,1,0:T(8,128)(2,1)S(1)} %get-tuple-element.21.packed, f32[5,256,128]{2,1,0:T(8,128)S(1)} %get-tuple-element.22.total, f32[328,128]{1,0:T(8,128)S(1)} %collective-permute-done.1.refs_0_.refs_2_), custom_call_target="tpu_custom_call" | custom-call | flops 503316480 | bytes 4194304 | tf_op jit(solution)/shard_map/pallas_call | solution.py:451
  12.1 1.1 %shard_map.94.refs_1_ = f32[320,128]{1,0:T(8,128)S(1)} custom-call(bf16[5,11,256,256]{3,2,1,0:T(8,128)(2,1)S(1)} %get-tuple-element.21.packed, f32[5,256,128]{2,1,0:T(8,128)S(1)} %get-tuple-element.22.total, f32[320,128]{1,0:T(8,128)S(1)} %collective-permute-done.5.refs_1_.refs_0_), custom_call_target="tpu_custom_call" | custom-call | flops 503316480 | bytes 4194304 | tf_op jit(solution)/shard_map/pallas_call | solution.py:451
  13.3 4.3 %collective-permute-done.2.refs_0_ = f32[320,128]{1,0:T(8,128)S(1)} collective-permute-done((f32[320,128]{1,0:T(8,128)S(1)}, f32[320,128]{1,0:T(8,128)S(1)}, u32[]{:S(2)}, u32[]{:S(2)}) %collective-permute-start.2) | collective-permute-done | bytes 163872 | tf_op jit(solution)/shard_map/ppermute | solution.py:383
  17.6 1.0 %collective-permute-start.3 = (f32[320,128]{1,0:T(8,128)S(1)}, f32[320,128]{1,0:T(8,128)S(1)}, u32[]{:S(2)}, u32[]{:S(2)}) collective-permute-start(f32[320,128]{1,0:T(8,128)S(1)} %collective-permute-done.2.refs_0_), channel_id=1, source_target_pairs={{0,1},{1,0},{2,3},{3,2},{4,5},{5,4},{6,7},{7,6},{8,9},{9,8},{10,11... | collective-permute-start | bytes 491528 | tf_op jit(solution)/shard_map/ppermute | solution.py:383
  18.6 2.3 %collective-permute-start.10 = (f32[640,128]{1,0:T(8,128)S(1)}, f32[640,128]{1,0:T(8,128)S(1)}, u32[]{:S(2)}, u32[]{:S(2)}) collective-permute-start(f32[640,128]{1,0:T(8,128)S(1)} %get-tuple-element.30.refs_0_), channel_id=1, source_target_pairs={{0,16},{1,2},{2,1},{3,4},{4,3},{5,6},{6,5},{7,23},{8,24},{9,10},{1... | collective-permute-start | bytes 983048 | tf_op jit(solution)/shard_map/ppermute | solution.py:383
  21.8 1.6 %collective-permute-start.14 = (f32[320,128]{1,0:T(8,128)S(1)}, f32[320,128]{1,0:T(8,128)S(1)}, u32[]{:S(2)}, u32[]{:S(2)}) collective-permute-start(f32[320,128]{1,0:T(8,128)S(1)} %collective-permute-done.12.refs_0_), channel_id=1, source_target_pairs={{0,16},{1,2},{2,1},{3,4},{4,3},{5,6},{6,5},{7,23},{8,24},{9,10},{1... | collective-permute-start | bytes 491528 | tf_op jit(solution)/shard_map/ppermute | solution.py:383
  23.4 4.3 %collective-permute-done.4.refs_0_ = f32[320,128]{1,0:T(8,128)S(1)} collective-permute-done((f32[320,128]{1,0:T(8,128)S(1)}, f32[320,128]{1,0:T(8,128)S(1)}, u32[]{:S(2)}, u32[]{:S(2)}) %collective-permute-start.4) | collective-permute-done | bytes 163872 | tf_op jit(solution)/shard_map/ppermute | solution.py:383
  27.9 1.3 %collective-permute-done.14.refs_0_ = f32[320,128]{1,0:T(8,128)S(1)} collective-permute-done((f32[320,128]{1,0:T(8,128)S(1)}, f32[320,128]{1,0:T(8,128)S(1)}, u32[]{:S(2)}, u32[]{:S(2)}) %collective-permute-start.14) | collective-permute-done | bytes 163872 | tf_op jit(solution)/shard_map/ppermute | solution.py:383
  29.8 1.6 %shard_map.95.total = f32[5,256,128]{2,1,0:T(8,128)S(1)} custom-call(bf16[5,11,256,256]{3,2,1,0:T(8,128)(2,1)S(1)} %get-tuple-element.21.packed, f32[640,128]{1,0:T(8,128)S(1)} %get-tuple-element.30.refs_0_, f32[640,128]{1,0:T(8,128)S(1)} %collective-permute-done.9.refs_1_), custom_call_target="tpu_custom_call" | custom-call | flops 1342177280 | bytes 8388608 | tf_op jit(solution)/shard_map/pallas_call | solution.py:434
  31.4 1.7 %collective-permute-start.8 = (f32[320,128]{1,0:T(8,128)S(1)}, f32[320,128]{1,0:T(8,128)S(1)}, u32[]{:S(2)}, u32[]{:S(2)}) collective-permute-start(f32[320,128]{1,0:T(8,128)S(1)} %collective-permute-done.6.refs_0_), channel_id=1, source_target_pairs={{0,16},{1,2},{2,1},{3,4},{4,3},{5,6},{6,5},{7,23},{8,24},{9,10},{1... | collective-permute-start | bytes 491528 | tf_op jit(solution)/shard_map/ppermute | solution.py:383
  33.1 0.9 %shard_map.96 = (f32[320,128]{1,0:T(8,128)S(1)}, f32[320,128]{1,0:T(8,128)S(1)}) custom-call(bf16[5,11,256,256]{3,2,1,0:T(8,128)(2,1)S(1)} %get-tuple-element.21.packed, f32[5,256,128]{2,1,0:T(8,128)S(1)} %shard_map.95.total, f32[640,128]{1,0:T(8,128)S(1)} %collective-permute-done.10.refs_0_), custom_call_target="tpu_custom_call" | custom-call | flops 503316480 | bytes 4194304 | tf_op jit(solution)/shard_map/pallas_call | solution.py:451
  34.1 5.4 %collective-permute-start.16 = (f32[320,128]{1,0:T(8,128)S(1)}, f32[320,128]{1,0:T(8,128)S(1)}, u32[]{:S(2)}, u32[]{:S(2)}) collective-permute-start(f32[320,128]{1,0:T(8,128)S(1)} %collective-permute-done.15.refs_0_), channel_id=1, source_target_pairs={{0,1},{1,0},{2,3},{3,2},{4,5},{5,4},{6,7},{7,6},{8,9},{9,8},{10,11... | collective-permute-start | bytes 491528 | tf_op jit(solution)/shard_map/ppermute | solution.py:383
  39.5 5.6 %collective-permute-start.11 = (f32[320,128]{1,0:T(8,128)S(1)}, f32[320,128]{1,0:T(8,128)S(1)}, u32[]{:S(2)}, u32[]{:S(2)}) collective-permute-start(f32[320,128]{1,0:T(8,128)S(1)} %shard_map.97.refs_2_), channel_id=1, source_target_pairs={{0,8},{1,9},{2,10},{3,11},{4,12},{5,13},{6,14},{7,15},{8,0},{9,1},... | collective-permute-start | bytes 491528 | tf_op jit(solution)/shard_map/ppermute | solution.py:383
  45.2 3.0 %collective-permute-start.18 = (f32[320,128]{1,0:T(8,128)S(1)}, f32[320,128]{1,0:T(8,128)S(1)}, u32[]{:S(2)}, u32[]{:S(2)}) collective-permute-start(f32[320,128]{1,0:T(8,128)S(1)} %shard_map.101.refs_3_), channel_id=1, source_target_pairs={{0,8},{1,9},{2,10},{3,11},{4,12},{5,13},{6,14},{7,15},{8,0},{9,1},... | collective-permute-start | bytes 491528 | tf_op jit(solution)/shard_map/ppermute | solution.py:383
  48.2 1.8 %collective-permute-done.11.refs_0_ = f32[320,128]{1,0:T(8,128)S(1)} collective-permute-done((f32[320,128]{1,0:T(8,128)S(1)}, f32[320,128]{1,0:T(8,128)S(1)}, u32[]{:S(2)}, u32[]{:S(2)}) %collective-permute-start.11) | collective-permute-done | bytes 163872 | tf_op jit(solution)/shard_map/ppermute | solution.py:383
  50.0 2.6 %collective-permute-done.18.refs_1_ = f32[320,128]{1,0:T(8,128)S(1)} collective-permute-done((f32[320,128]{1,0:T(8,128)S(1)}, f32[320,128]{1,0:T(8,128)S(1)}, u32[]{:S(2)}, u32[]{:S(2)}) %collective-permute-start.18) | collective-permute-done | bytes 163872 | tf_op jit(solution)/shard_map/ppermute | solution.py:383
  52.7 1.7 %collective-permute-start.21 = (f32[320,128]{1,0:T(8,128)S(1)}, f32[320,128]{1,0:T(8,128)S(1)}, u32[]{:S(2)}, u32[]{:S(2)}) collective-permute-start(f32[320,128]{1,0:T(8,128)S(1)} %collective-permute-done.11.refs_0_), channel_id=1, source_target_pairs={{0,16},{1,2},{2,1},{3,4},{4,3},{5,6},{6,5},{7,23},{8,24},{9,10},{1... | collective-permute-start | bytes 491528 | tf_op jit(solution)/shard_map/ppermute | solution.py:383
  54.4 0.9 %shard_map.103 = (f32[1,640,128]{2,1,0:T(8,128)}, f32[1,640,128]{2,1,0:T(8,128)}) custom-call(f32[320,128]{1,0:T(8,128)S(1)} %shard_map.88.refs_0_, f32[320,128]{1,0:T(8,128)S(1)} %shard_map.94.refs_1_), custom_call_target="tpu_custom_call" | custom-call | bytes 1310720 | tf_op jit(solution)/shard_map/pallas_call | solution.py:465
  55.6 1.7 %shard_map.102.total = f32[5,256,128]{2,1,0:T(8,128)S(1)} custom-call(bf16[5,11,256,256]{3,2,1,0:T(8,128)(2,1)S(1)} %get-tuple-element.21.packed, f32[320,128]{1,0:T(8,128)S(1)} %collective-permute-done.11.refs_0_, f32[320,128]{1,0:T(8,128)S(1)} %collective-permute-done.18.refs_1_, f32[320,128]{1,0:T(8,128)S(1)} %collective-permute-done.19.refs_2_, ...), custom_call_target="tpu_custom_call" | custom-call | flops 1342177280 | bytes 8388608 | tf_op jit(solution)/shard_map/pallas_call | solution.py:434
  57.7 1.8 %collective-permute-done.22.refs_1_ = f32[320,128]{1,0:T(8,128)S(1)} collective-permute-done((f32[320,128]{1,0:T(8,128)S(1)}, f32[320,128]{1,0:T(8,128)S(1)}, u32[]{:S(2)}, u32[]{:S(2)}) %collective-permute-start.22) | collective-permute-done | bytes 163872 | tf_op jit(solution)/shard_map/ppermute | solution.py:383
  59.4 1.7 %shard_map.105 = (f32[1,640,128]{2,1,0:T(8,128)}, f32[1,640,128]{2,1,0:T(8,128)}) custom-call(bf16[5,11,256,256]{3,2,1,0:T(8,128)(2,1)S(1)} %get-tuple-element.21.packed, f32[5,256,128]{2,1,0:T(8,128)S(1)} %shard_map.102.total, f32[320,128]{1,0:T(8,128)S(1)} %collective-permute-done.21.refs_0_, ...), custom_call_target="tpu_custom_call", output_to_operand_aliasing={{0}: (7, {}), {1}: (8, {})} | custom-call | flops 503316480 | bytes 4194304 | tf_op jit(solution)/shard_map/pallas_call | solution.py:451
  (42 shorter events, 3.2 us)
Async XLA Ops:
  2.3 2.9 %collective-permute-start = (f32[648,128]{1,0:T(8,128)S(1)}, f32[648,128]{1,0:T(8,128)S(1)}, u32[]{:S(2)}, u32[]{:S(2)}) collective-permute-start(f32[648,128]{1,0:T(8,128)S(1)} %get-tuple-element.20.own.refs_0_), channel_id=1, source_target_pairs={{0,1},{1,0},{2,3},{3,2},{4,5},{5,4},{6,7},{7,6},{8,9},{9,8},{10,11... | collective-permute-start | bytes 995336 | tf_op jit(solution)/shard_map/ppermute | solution.py:383
  2.3 8.1 %collective-permute-start.1 = (f32[328,128]{1,0:T(8,128)S(1)}, f32[328,128]{1,0:T(8,128)S(1)}, u32[]{:S(2)}, u32[]{:S(2)}) collective-permute-start(f32[328,128]{1,0:T(8,128)S(1)} %get-tuple-element.23), channel_id=1, source_target_pairs={{0,16},{1,2},{2,1},{3,4},{4,3},{5,6},{6,5},{7,23},{8,24},{9,10},{1... | collective-permute-start | bytes 503816 | tf_op jit(solution)/shard_map/ppermute | solution.py:383
  5.1 7.1 %collective-permute-start.5 = (f32[320,128]{1,0:T(8,128)S(1)}, f32[320,128]{1,0:T(8,128)S(1)}, u32[]{:S(2)}, u32[]{:S(2)}) collective-permute-start(f32[320,128]{1,0:T(8,128)S(1)} %get-tuple-element.27), channel_id=1, source_target_pairs={{0,16},{1,2},{2,1},{3,4},{4,3},{5,6},{6,5},{7,23},{8,24},{9,10},{1... | collective-permute-start | bytes 491528 | tf_op jit(solution)/shard_map/ppermute | solution.py:383
  11.6 6.0 %collective-permute-start.2 = (f32[320,128]{1,0:T(8,128)S(1)}, f32[320,128]{1,0:T(8,128)S(1)}, u32[]{:S(2)}, u32[]{:S(2)}) collective-permute-start(f32[320,128]{1,0:T(8,128)S(1)} %shard_map.88.refs_0_), channel_id=1, source_target_pairs={{0,8},{1,9},{2,10},{3,11},{4,12},{5,13},{6,14},{7,15},{8,0},{9,1},... | collective-permute-start | bytes 491528 | tf_op jit(solution)/shard_map/ppermute | solution.py:383
  13.2 8.1 %collective-permute-start.12 = (f32[320,128]{1,0:T(8,128)S(1)}, f32[320,128]{1,0:T(8,128)S(1)}, u32[]{:S(2)}, u32[]{:S(2)}) collective-permute-start(f32[320,128]{1,0:T(8,128)S(1)} %shard_map.94.refs_1_), channel_id=1, source_target_pairs={{0,8},{1,9},{2,10},{3,11},{4,12},{5,13},{6,14},{7,15},{8,0},{9,1},... | collective-permute-start | bytes 491528 | tf_op jit(solution)/shard_map/ppermute | solution.py:383
  17.6 4.2 %collective-permute-start.3 = (f32[320,128]{1,0:T(8,128)S(1)}, f32[320,128]{1,0:T(8,128)S(1)}, u32[]{:S(2)}, u32[]{:S(2)}) collective-permute-start(f32[320,128]{1,0:T(8,128)S(1)} %collective-permute-done.2.refs_0_), channel_id=1, source_target_pairs={{0,1},{1,0},{2,3},{3,2},{4,5},{5,4},{6,7},{7,6},{8,9},{9,8},{10,11... | collective-permute-start | bytes 491528 | tf_op jit(solution)/shard_map/ppermute | solution.py:383
  18.6 11.2 %collective-permute-start.9 = (f32[640,128]{1,0:T(8,128)S(1)}, f32[640,128]{1,0:T(8,128)S(1)}, u32[]{:S(2)}, u32[]{:S(2)}) collective-permute-start(f32[640,128]{1,0:T(8,128)S(1)} %get-tuple-element.30.refs_0_), channel_id=1, source_target_pairs={{0,1},{1,0},{2,3},{3,2},{4,5},{5,4},{6,7},{7,6},{8,9},{9,8},{10,11... | collective-permute-start | bytes 983048 | tf_op jit(solution)/shard_map/ppermute | solution.py:383
  18.6 14.6 %collective-permute-start.10 = (f32[640,128]{1,0:T(8,128)S(1)}, f32[640,128]{1,0:T(8,128)S(1)}, u32[]{:S(2)}, u32[]{:S(2)}) collective-permute-start(f32[640,128]{1,0:T(8,128)S(1)} %get-tuple-element.30.refs_0_), channel_id=1, source_target_pairs={{0,16},{1,2},{2,1},{3,4},{4,3},{5,6},{6,5},{7,23},{8,24},{9,10},{1... | collective-permute-start | bytes 983048 | tf_op jit(solution)/shard_map/ppermute | solution.py:383
  21.2 6.5 %collective-permute-start.4 = (f32[320,128]{1,0:T(8,128)S(1)}, f32[320,128]{1,0:T(8,128)S(1)}, u32[]{:S(2)}, u32[]{:S(2)}) collective-permute-start(f32[320,128]{1,0:T(8,128)S(1)} %collective-permute-done.2.refs_0_), channel_id=1, source_target_pairs={{0,16},{1,2},{2,1},{3,4},{4,3},{5,6},{6,5},{7,23},{8,24},{9,10},{1... | collective-permute-start | bytes 491528 | tf_op jit(solution)/shard_map/ppermute | solution.py:383
  21.3 6.6 %collective-permute-start.13 = (f32[320,128]{1,0:T(8,128)S(1)}, f32[320,128]{1,0:T(8,128)S(1)}, u32[]{:S(2)}, u32[]{:S(2)}) collective-permute-start(f32[320,128]{1,0:T(8,128)S(1)} %collective-permute-done.12.refs_0_), channel_id=1, source_target_pairs={{0,1},{1,0},{2,3},{3,2},{4,5},{5,4},{6,7},{7,6},{8,9},{9,8},{10,11... | collective-permute-start | bytes 491528 | tf_op jit(solution)/shard_map/ppermute | solution.py:383
  21.8 7.5 %collective-permute-start.14 = (f32[320,128]{1,0:T(8,128)S(1)}, f32[320,128]{1,0:T(8,128)S(1)}, u32[]{:S(2)}, u32[]{:S(2)}) collective-permute-start(f32[320,128]{1,0:T(8,128)S(1)} %collective-permute-done.12.refs_0_), channel_id=1, source_target_pairs={{0,16},{1,2},{2,1},{3,4},{4,3},{5,6},{6,5},{7,23},{8,24},{9,10},{1... | collective-permute-start | bytes 491528 | tf_op jit(solution)/shard_map/ppermute | solution.py:383
  27.7 1.9 %collective-permute-start.6 = (f32[320,128]{1,0:T(8,128)S(1)}, f32[320,128]{1,0:T(8,128)S(1)}, u32[]{:S(2)}, u32[]{:S(2)}) collective-permute-start(f32[320,128]{1,0:T(8,128)S(1)} %shard_map.92.refs_0_), channel_id=1, source_target_pairs={{0,1},{1,0},{2,3},{3,2},{4,5},{5,4},{6,7},{7,6},{8,16},{9,17},{10,... | collective-permute-start | bytes 491528 | tf_op jit(solution)/shard_map/ppermute | solution.py:383
  29.3 4.8 %collective-permute-start.15 = (f32[320,128]{1,0:T(8,128)S(1)}, f32[320,128]{1,0:T(8,128)S(1)}, u32[]{:S(2)}, u32[]{:S(2)}) collective-permute-start(f32[320,128]{1,0:T(8,128)S(1)} %shard_map.99.refs_1_), channel_id=1, source_target_pairs={{0,1},{1,0},{2,3},{3,2},{4,5},{5,4},{6,7},{7,6},{8,16},{9,17},{10,... | collective-permute-start | bytes 491528 | tf_op jit(solution)/shard_map/ppermute | solution.py:383
  29.7 9.9 %collective-permute-start.7 = (f32[320,128]{1,0:T(8,128)S(1)}, f32[320,128]{1,0:T(8,128)S(1)}, u32[]{:S(2)}, u32[]{:S(2)}) collective-permute-start(f32[320,128]{1,0:T(8,128)S(1)} %collective-permute-done.6.refs_0_), channel_id=1, source_target_pairs={{0,1},{1,0},{2,3},{3,2},{4,5},{5,4},{6,7},{7,6},{8,9},{9,8},{10,11... | collective-permute-start | bytes 491528 | tf_op jit(solution)/shard_map/ppermute | solution.py:383
  31.4 8.1 %collective-permute-start.8 = (f32[320,128]{1,0:T(8,128)S(1)}, f32[320,128]{1,0:T(8,128)S(1)}, u32[]{:S(2)}, u32[]{:S(2)}) collective-permute-start(f32[320,128]{1,0:T(8,128)S(1)} %collective-permute-done.6.refs_0_), channel_id=1, source_target_pairs={{0,16},{1,2},{2,1},{3,4},{4,3},{5,6},{6,5},{7,23},{8,24},{9,10},{1... | collective-permute-start | bytes 491528 | tf_op jit(solution)/shard_map/ppermute | solution.py:383
  34.1 11.1 %collective-permute-start.16 = (f32[320,128]{1,0:T(8,128)S(1)}, f32[320,128]{1,0:T(8,128)S(1)}, u32[]{:S(2)}, u32[]{:S(2)}) collective-permute-start(f32[320,128]{1,0:T(8,128)S(1)} %collective-permute-done.15.refs_0_), channel_id=1, source_target_pairs={{0,1},{1,0},{2,3},{3,2},{4,5},{5,4},{6,7},{7,6},{8,9},{9,8},{10,11... | collective-permute-start | bytes 491528 | tf_op jit(solution)/shard_map/ppermute | solution.py:383
  39.5 5.7 %collective-permute-start.17 = (f32[320,128]{1,0:T(8,128)S(1)}, f32[320,128]{1,0:T(8,128)S(1)}, u32[]{:S(2)}, u32[]{:S(2)}) collective-permute-start(f32[320,128]{1,0:T(8,128)S(1)} %collective-permute-done.15.refs_0_), channel_id=1, source_target_pairs={{0,16},{1,2},{2,1},{3,4},{4,3},{5,6},{6,5},{7,23},{8,24},{9,10},{1... | collective-permute-start | bytes 491528 | tf_op jit(solution)/shard_map/ppermute | solution.py:383
  39.5 10.4 %collective-permute-start.11 = (f32[320,128]{1,0:T(8,128)S(1)}, f32[320,128]{1,0:T(8,128)S(1)}, u32[]{:S(2)}, u32[]{:S(2)}) collective-permute-start(f32[320,128]{1,0:T(8,128)S(1)} %shard_map.97.refs_2_), channel_id=1, source_target_pairs={{0,8},{1,9},{2,10},{3,11},{4,12},{5,13},{6,14},{7,15},{8,0},{9,1},... | collective-permute-start | bytes 491528 | tf_op jit(solution)/shard_map/ppermute | solution.py:383
  45.2 7.4 %collective-permute-start.18 = (f32[320,128]{1,0:T(8,128)S(1)}, f32[320,128]{1,0:T(8,128)S(1)}, u32[]{:S(2)}, u32[]{:S(2)}) collective-permute-start(f32[320,128]{1,0:T(8,128)S(1)} %shard_map.101.refs_3_), channel_id=1, source_target_pairs={{0,8},{1,9},{2,10},{3,11},{4,12},{5,13},{6,14},{7,15},{8,0},{9,1},... | collective-permute-start | bytes 491528 | tf_op jit(solution)/shard_map/ppermute | solution.py:383
  49.9 5.6 %collective-permute-start.19 = (f32[320,128]{1,0:T(8,128)S(1)}, f32[320,128]{1,0:T(8,128)S(1)}, u32[]{:S(2)}, u32[]{:S(2)}) collective-permute-start(f32[320,128]{1,0:T(8,128)S(1)} %collective-permute-done.11.refs_0_), channel_id=1, source_target_pairs={{0,1},{1,0},{2,3},{3,2},{4,5},{5,4},{6,7},{7,6},{8,9},{9,8},{10,11... | collective-permute-start | bytes 491528 | tf_op jit(solution)/shard_map/ppermute | solution.py:383
  52.6 3.0 %collective-permute-start.20 = (f32[320,128]{1,0:T(8,128)S(1)}, f32[320,128]{1,0:T(8,128)S(1)}, u32[]{:S(2)}, u32[]{:S(2)}) collective-permute-start(f32[320,128]{1,0:T(8,128)S(1)} %collective-permute-done.18.refs_1_), channel_id=1, source_target_pairs={{0,1},{1,0},{2,3},{3,2},{4,5},{5,4},{6,7},{7,6},{8,9},{9,8},{10,11... | collective-permute-start | bytes 491528 | tf_op jit(solution)/shard_map/ppermute | solution.py:383
  52.7 5.0 %collective-permute-start.21 = (f32[320,128]{1,0:T(8,128)S(1)}, f32[320,128]{1,0:T(8,128)S(1)}, u32[]{:S(2)}, u32[]{:S(2)}) collective-permute-start(f32[320,128]{1,0:T(8,128)S(1)} %collective-permute-done.11.refs_0_), channel_id=1, source_target_pairs={{0,16},{1,2},{2,1},{3,4},{4,3},{5,6},{6,5},{7,23},{8,24},{9,10},{1... | collective-permute-start | bytes 491528 | tf_op jit(solution)/shard_map/ppermute | solution.py:383
  54.4 5.1 %collective-permute-start.22 = (f32[320,128]{1,0:T(8,128)S(1)}, f32[320,128]{1,0:T(8,128)S(1)}, u32[]{:S(2)}, u32[]{:S(2)}) collective-permute-start(f32[320,128]{1,0:T(8,128)S(1)} %collective-permute-done.18.refs_1_), channel_id=1, source_target_pairs={{0,16},{1,2},{2,1},{3,4},{4,3},{5,6},{6,5},{7,23},{8,24},{9,10},{1... | collective-permute-start | bytes 491528 | tf_op jit(solution)/shard_map/ppermute | solution.py:383

commit v9 on v7

--- a/solution.py
+++ b/solution.py
@@ -13,6 +13,7 @@
 VMEM = pltpu.VMEM
 LIMIT = 16 * 2**20
 STREAMS = 2
+CHUNKS = (3, 2)
 
 
 def spec(space):
@@ -152,9 +153,25 @@
     return slice(t * HALF, (t + 1) * HALF)
 
 
-def unpack_tile(chunk, t):
-    part = chunk[halves_of(t)]
-    return jnp.concatenate([part, turned(part)], axis=0)
+def part_tile(part, t):
+    for chunk in part:
+        count = chunk.shape[0] // HALF
+        if t < count:
+            return chunk[halves_of(t)]
+        t -= count
+
+
+def unpack_tile(part, t):
+    tile = part_tile(part, t)
+    return jnp.concatenate([tile, turned(tile)], axis=0)
+
+
+def grouped(refs, layout):
+    out = []
+    for count in layout:
+        out.append(refs[:count])
+        refs = refs[count:]
+    return out, refs
 
 
 def stream_line(tile):
@@ -178,8 +195,8 @@
 
 def full_tile(field, t):
     if len(field) == 1:
-        return field[0][rows_of(t)]
-    return merged(*[part[halves_of(t)] for part in field])
+        return field[0][0][rows_of(t)]
+    return merged(*[part_tile(part, t) for part in field])
 
 
 def spread(field, scale, sign, tiles, narrow, mirrored, held):
@@ -230,9 +247,14 @@
             out[t] = down_column(source[at : at + 1])
 
 
-def inner_kernel(step, sections, tiles, parts, packed, *refs):
-    narrow = bool(step) and parts == 1
-    own, near, refs = refs[:parts], refs[parts : 2 * parts], refs[2 * parts :]
+def mark_kernel(out):
+    out[...] = jnp.zeros_like(out)
+
+
+def inner_kernel(step, sections, tiles, layout, packed, *refs):
+    narrow = bool(step) and len(layout) == 1
+    own, refs = grouped(refs, layout)
+    near, refs = grouped(refs, layout)
     scale, near_scale = refs[:2] if step else (None, None)
     total, held_own, held_near = refs[-3:]
 
@@ -250,9 +272,10 @@
     when_active(step or None, sections, body)
 
 
-def outer_kernel(step, sections, lats, tiles, shots, parts, ends, late, packed, total, *refs):
+def outer_kernel(step, sections, lats, tiles, shots, layout, ends, late, packed, total, *refs):
     narrow = bool(step) and not ends
-    far, refs = refs[:parts], refs[parts:]
+    parts = len(layout)
+    far, refs = grouped(refs, layout)
     scale, base = None, None
     if step:
         scale, base, refs = refs[0], refs[1 : 1 + parts], refs[1 + parts :]
@@ -272,11 +295,25 @@
             at = pl.ds(pl.multiple_of(j * TILE, TILE), TILE)
             return pltpu.make_async_copy(leaving.at[at], result.at[0, at], sems.at[j])
 
+        def store(j, value):
+            first = 0
+            for out in outs:
+                count = out.shape[0] // HALF
+
+                def put(out=out, first=first):
+                    out[pl.ds(pl.multiple_of((j - first) * HALF, HALF), HALF)] = value
+
+                if len(outs) == 1:
+                    put()
+                else:
+                    pl.when((j >= first) & (j < first + count))(put)
+                first += count
+
         def finish(j, value):
             at = pl.ds(pl.multiple_of(j * HALF, HALF), HALF)
             if narrow:
                 value = combined(value + turned(value), shots)
-                outs[0][at] = jnp.where(left_half(HALF), value[:HALF], value[HALF:]) + base[0][at]
+                store(j, jnp.where(left_half(HALF), value[:HALF], value[HALF:]) + base[0][at])
                 return
             value = combined(value, shots)
             if ends:
@@ -315,13 +352,14 @@
         when_active(step, sections, body)
 
 
-def keep_kernel(sections, tiles, steps, *refs):
-    fields, (result_down, result_up, whole, sems) = refs[: 2 * len(steps)], refs[-4:]
+def keep_kernel(sections, tiles, steps, layout, *refs):
+    result_down, result_up, whole, sems = refs[-4:]
+    fields, _ = grouped(refs, layout)
     depth = lax.axis_index("depth")
 
     def put(first, second, result):
         for j in range(tiles):
-            whole[rows_of(j)] = merged(first[halves_of(j)], second[halves_of(j)])
+            whole[rows_of(j)] = merged(part_tile(first, j), part_tile(second, j))
         copy = pltpu.make_async_copy(whole, result.at[0], sems)
         copy.start()
         copy.wait()
@@ -337,7 +375,7 @@
     _, columns = sources.shape
     shots = columns // 4
     rows = tiles * TILE
-    if sections % 2 or lats % 2 or tiles != band // 2 + 1 or columns != TILE:
+    if sections % 2 or lats % 2 or tiles != band // 2 + 1 or columns != TILE or tiles != sum(CHUNKS):
         raise ValueError("unsupported sizes")
 
     def move(x, partner):
@@ -409,9 +447,9 @@
         return VMEM((tiles * 2 * TILE, TILE if narrow else 2 * TILE), jnp.bfloat16)
 
     def inner(step, own, near, *scales):
-        args = [packed, *own, *near, *scales]
+        args = [packed, *flat(own), *flat(near), *scales]
         return call(
-            functools.partial(inner_kernel, step, sections, tiles, len(own)),
+            functools.partial(inner_kernel, step, sections, tiles, [len(part) for part in own]),
             out_shape=f32(tiles, 2 * TILE, columns),
             in_specs=[spec(VMEM)] * len(args),
             out_specs=spec(VMEM),
@@ -422,13 +460,15 @@
 
     def outer(step, total, far, *more, shapes, kept=(), late=False):
         ends = bool(kept)
-        args = [packed, total, *far, *more]
+        args = [packed, total, *flat(far), *more]
         count = len(args)
         scratch = [held(step and not ends)]
         if ends:
             scratch += [VMEM((rows, columns), jnp.float32), pltpu.SemaphoreType.DMA((tiles,))]
         return call(
-            functools.partial(outer_kernel, step, sections, lats, tiles, shots, len(far), ends, late),
+            functools.partial(
+                outer_kernel, step, sections, lats, tiles, shots, [len(part) for part in far], ends, late
+            ),
             out_shape=shapes,
             in_specs=[spec(VMEM)] * count + [spec(pl.ANY)] * len(kept),
             out_specs=[spec(pl.ANY if ends else VMEM)] * len(shapes),
@@ -439,10 +479,11 @@
         )(*args, *kept)
 
     def keep(steps, kept=()):
-        args = [part for step in steps for part in fields[step]]
+        parts = [part for step in steps for part in fields[step]]
+        args = flat(parts)
         count = len(args)
         return call(
-            functools.partial(keep_kernel, sections, tiles, steps),
+            functools.partial(keep_kernel, sections, tiles, steps, [len(part) for part in parts]),
             out_shape=result,
             in_specs=[spec(VMEM)] * count + [spec(pl.ANY)] * len(kept),
             out_specs=[spec(pl.ANY)] * 2,
@@ -452,16 +493,23 @@
             cost_estimate=cost(0, 4 * rows * columns * 4),
         )(*args, *kept)
 
+    def flat(parts):
+        return [chunk for part in parts for chunk in part]
+
     def cross(step, field):
-        return [move(part, functools.partial(across, step)) for part in field]
+        def one(chunk):
+            return move(chunk, functools.partial(across, step))
+
+        return [[one(chunk) for chunk in part] for part in field]
 
     first_near, first_far = halo(first, next_door)
-    total = inner(0, [first], [first_near])
-    fields = [outer(0, total, [first_far], shapes=[half] * STREAMS)]
-    first_base = outer(0, total, [first_far], shapes=[half] * STREAMS, late=True)
+    total = inner(0, [[first]], [[first_near]])
+    field = outer(0, total, [[first_far]], shapes=[half] * STREAMS)
+    fields = [[[part] for part in field]]
+    first_base = outer(0, total, [[first_far]], shapes=[half] * STREAMS, late=True)
     arrived = cross(0, fields[0])
 
-    second, *_ = lax.optimization_barrier((second, *fields[0]))
+    second, *_ = lax.optimization_barrier((second, *field))
     near, far = halo(second, next_door)
     own_scale, near_scale, far_scale = call(
         functools.partial(scale_kernel, tiles),
@@ -471,23 +519,37 @@
         compiler_params=params(),
         cost_estimate=cost(10**6, 4 * rows * columns * 4),
     )(first, first_near, first_far)
-    total = inner(None, [second], [near])
-    second_base = outer(None, total, [far], shapes=[half] * STREAMS)
+    total = inner(None, [[second]], [[near]])
+    second_base = outer(None, total, [[far]], shapes=[half] * STREAMS)
 
     middle = sections // 2
     for step in range(1, sections):
         bases = first_base if step < middle else second_base
-        halos = [halo(part, next_door) for part in arrived]
-        nears, fars = zip(*halos)
+        nears, fars = [], []
+        for part in arrived:
+            halos = [halo(chunk, next_door) for chunk in part]
+            nears.append([near for near, _ in halos])
+            fars.append([far for _, far in halos])
         if step == sections - 1:
-            total = inner(step, arrived, nears, own_scale, near_scale)
+            mark = call(
+                mark_kernel,
+                out_shape=f32(8, columns),
+                in_specs=[],
+                out_specs=spec(VMEM),
+                compiler_params=params(),
+                cost_estimate=cost(0, 1),
+            )()
+            total = inner(step, arrived, nears, own_scale, near_scale, mark)
             kept = keep(range(middle - 1)) if middle > 1 else ()
             kept = keep(range(middle - 1, step), kept)
             return tuple(outer(step, total, fars, far_scale, *bases, shapes=result, kept=kept))
         field = []
         for q in range(STREAMS):
             total = inner(step, [arrived[q]], [nears[q]], own_scale, near_scale)
-            field += outer(step, total, [fars[q]], far_scale, bases[q], shapes=[half])
+            shapes = [half]
+            if step == sections - 2 and q == STREAMS - 1:
+                shapes = [f32(count * HALF, columns) for count in CHUNKS]
+            field.append(outer(step, total, [fars[q]], far_scale, bases[q], shapes=shapes))
         fields.append(field)
         arrived = cross(step, field)
 

time: 61.4 us -> 64 us (1.042)
  starting transfers between devices: 28.2 us -> 34.3 us
  waiting for transfers between devices: 17.3 us -> 13.6 us
    ppermute x22 -> x25, starting transfers between devices: 28.2 us -> 34.3 us  [move(): return lax.ppermute(x, ('depth', 'lat'), pairs)]
    ppermute x22 -> x25, waiting for transfers between devices: 17.3 us -> 13.6 us  [move(): return lax.ppermute(x, ('depth', 'lat'), pairs)]
    pallas_call x9 -> x10, Pallas kernels: 5.92 us -> 5.98 us  [the longest x7 5.06 us: inner(): call(functools.partial(inner_kernel, step, sections, tiles, [len(part) fo...]
  transfers between devices with their start and end apart: 22 -> 25, of which waited for: 8 -> 8; matrix products, arithmetic and copies ran while one was open for 0% -> 0% of each run, Pallas kernels for 17% -> 16%
where the time goes in v9:
time: 64 us; the launch traced here: 63.4 us
  starting transfers between devices  34.3 us (54%)
  Pallas kernels  14.6 us (23%)
  waiting for transfers between devices  13.6 us (21%)
  between operations  0.95 us (1%)
    ppermute x25, starting transfers between devices, move(): return lax.ppermute(x, ('depth', 'lat'), pairs)  34.3 us
    ppermute x25, waiting for transfers between devices, move(): return lax.ppermute(x, ('depth', 'lat'), pairs)  13.6 us
    pallas_call x7, Pallas kernels, inner(): call(functools.partial(inner_kernel, step, sections, tiles, [len(part) fo...  5.06 us
    pallas_call x8, Pallas kernels, outer(): call(functools.partial(outer_kernel, step, sections, lats, tiles, shots,...  3.62 us
    pallas_call x1, Pallas kernels, shards(): call(functools.partial(pack_kernel, tiles, band), out_shape=jax.ShapeDtyp...  2.95 us
    pallas_call x1, Pallas kernels, shards(): call(functools.partial(prep_kernel, tiles, shots, sections), out_shape=[f...  1.76 us
  transfers between devices with their start and end apart: 25, of which 8 were waited for; matrix products, arithmetic and copies ran while one was open for 0% of the time, Pallas kernels for 16%

profile of v9, /device:TPU:1, one launch (start us, length us, event | category | flops | bytes accessed | tf_op | source)
XLA Modules:
  0.0 63.4 jit_solution(17913473476633510604)
XLA Ops:
  0.6 1.8 %shard_map.87 = (f32[648,128]{1,0:T(8,128)S(1)}, f32[640,128]{1,0:T(8,128)S(1)}) custom-call(s32[64]{0:T(128)} %assign_at.1, f32[1,640]{1,0:T(1,128)} %refl_at.1, f32[1,640,128]{2,1,0:T(8,128)} %up_at.1, f32[1,640,128]{2,1,0:T(8,128)} %down_at.1, f32[640,128]{1,0:T(8,128)} %src_at.1), custom_call_target="tpu_custom_call" | custom-call | flops 10000000 | bytes 1638400 | tf_op jit(solution)/shard_map/pallas_call | solution.py:411
  2.5 2.7 %collective-permute-start.1 = (f32[648,128]{1,0:T(8,128)S(1)}, f32[648,128]{1,0:T(8,128)S(1)}, u32[]{:S(2)}, u32[]{:S(2)}) collective-permute-start(f32[648,128]{1,0:T(8,128)S(1)} %get-tuple-element.20.refs_0_), channel_id=1, source_target_pairs={{0,16},{1,2},{2,1},{3,4},{4,3},{5,6},{6,5},{7,23},{8,24},{9,10},{1... | collective-permute-start | bytes 995336 | tf_op jit(solution)/shard_map/ppermute | solution.py:387
  5.2 3.0 %shard_map.86.packed = bf16[5,11,256,256]{3,2,1,0:T(8,128)(2,1)S(1)} custom-call(s32[1,5]{1,0:T(1,128)} %shift_at.1, f32[1,5,9,256,128]{4,3,2,1,0:T(8,128)} %tiles_at.1), custom_call_target="tpu_custom_call" | custom-call | flops 10000000 | bytes 11796480 | tf_op jit(solution)/shard_map/pallas_call | solution.py:428
  8.2 1.6 %shard_map.88.total = f32[5,256,128]{2,1,0:T(8,128)S(1)} custom-call(bf16[5,11,256,256]{3,2,1,0:T(8,128)(2,1)S(1)} %shard_map.86.packed, f32[648,128]{1,0:T(8,128)S(1)} %get-tuple-element.20.refs_0_, f32[648,128]{1,0:T(8,128)S(1)} %collective-permute-done.refs_1_), custom_call_target="tpu_custom_call" | custom-call | flops 1342177280 | bytes 8388608 | tf_op jit(solution)/shard_map/pallas_call | solution.py:451
  10.0 0.9 %shard_map.89 = (f32[320,128]{1,0:T(8,128)S(1)}, f32[320,128]{1,0:T(8,128)S(1)}) custom-call(bf16[5,11,256,256]{3,2,1,0:T(8,128)(2,1)S(1)} %shard_map.86.packed, f32[5,256,128]{2,1,0:T(8,128)S(1)} %shard_map.88.total, f32[648,128]{1,0:T(8,128)S(1)} %collective-permute-done.1.refs_0_.refs_2_), custom_call_target="tpu_custom_call" | custom-call | flops 503316480 | bytes 4194304 | tf_op jit(solution)/shard_map/pallas_call | solution.py:468
  12.5 4.5 %collective-permute-done.2.refs_0_ = f32[320,128]{1,0:T(8,128)S(1)} collective-permute-done((f32[320,128]{1,0:T(8,128)S(1)}, f32[320,128]{1,0:T(8,128)S(1)}, u32[]{:S(2)}, u32[]{:S(2)}) %collective-permute-start.2) | collective-permute-done | bytes 163872 | tf_op jit(solution)/shard_map/ppermute | solution.py:387
  17.0 1.0 %collective-permute-start.3 = (f32[320,128]{1,0:T(8,128)S(1)}, f32[320,128]{1,0:T(8,128)S(1)}, u32[]{:S(2)}, u32[]{:S(2)}) collective-permute-start(f32[320,128]{1,0:T(8,128)S(1)} %collective-permute-done.2.refs_0_), channel_id=1, source_target_pairs={{0,1},{1,0},{2,3},{3,2},{4,5},{5,4},{6,7},{7,6},{8,9},{9,8},{10,11... | collective-permute-start | bytes 491528 | tf_op jit(solution)/shard_map/ppermute | solution.py:387
  18.0 2.4 %collective-permute-start.9 = (f32[640,128]{1,0:T(8,128)S(1)}, f32[640,128]{1,0:T(8,128)S(1)}, u32[]{:S(2)}, u32[]{:S(2)}) collective-permute-start(f32[640,128]{1,0:T(8,128)S(1)} %get-tuple-element.28.refs_0_), channel_id=1, source_target_pairs={{0,16},{1,2},{2,1},{3,4},{4,3},{5,6},{6,5},{7,23},{8,24},{9,10},{1... | collective-permute-start | bytes 983048 | tf_op jit(solution)/shard_map/ppermute | solution.py:387
  21.2 1.7 %collective-permute-start.13 = (f32[320,128]{1,0:T(8,128)S(1)}, f32[320,128]{1,0:T(8,128)S(1)}, u32[]{:S(2)}, u32[]{:S(2)}) collective-permute-start(f32[320,128]{1,0:T(8,128)S(1)} %collective-permute-done.11.refs_0_), channel_id=1, source_target_pairs={{0,16},{1,2},{2,1},{3,4},{4,3},{5,6},{6,5},{7,23},{8,24},{9,10},{1... | collective-permute-start | bytes 491528 | tf_op jit(solution)/shard_map/ppermute | solution.py:387
  22.8 4.3 %collective-permute-done.4.refs_0_ = f32[320,128]{1,0:T(8,128)S(1)} collective-permute-done((f32[320,128]{1,0:T(8,128)S(1)}, f32[320,128]{1,0:T(8,128)S(1)}, u32[]{:S(2)}, u32[]{:S(2)}) %collective-permute-start.4) | collective-permute-done | bytes 163872 | tf_op jit(solution)/shard_map/ppermute | solution.py:387
  27.3 1.4 %collective-permute-done.13.refs_0_ = f32[320,128]{1,0:T(8,128)S(1)} collective-permute-done((f32[320,128]{1,0:T(8,128)S(1)}, f32[320,128]{1,0:T(8,128)S(1)}, u32[]{:S(2)}, u32[]{:S(2)}) %collective-permute-start.13) | collective-permute-done | bytes 163872 | tf_op jit(solution)/shard_map/ppermute | solution.py:387
  29.2 1.7 %shard_map.95.total = f32[5,256,128]{2,1,0:T(8,128)S(1)} custom-call(bf16[5,11,256,256]{3,2,1,0:T(8,128)(2,1)S(1)} %shard_map.86.packed, f32[640,128]{1,0:T(8,128)S(1)} %get-tuple-element.28.refs_0_, f32[640,128]{1,0:T(8,128)S(1)} %collective-permute-done.8.refs_1_), custom_call_target="tpu_custom_call" | custom-call | flops 1342177280 | bytes 8388608 | tf_op jit(solution)/shard_map/pallas_call | solution.py:451
  30.8 1.8 %collective-permute-start.7 = (f32[320,128]{1,0:T(8,128)S(1)}, f32[320,128]{1,0:T(8,128)S(1)}, u32[]{:S(2)}, u32[]{:S(2)}) collective-permute-start(f32[320,128]{1,0:T(8,128)S(1)} %collective-permute-done.5.refs_0_), channel_id=1, source_target_pairs={{0,16},{1,2},{2,1},{3,4},{4,3},{5,6},{6,5},{7,23},{8,24},{9,10},{1... | collective-permute-start | bytes 491528 | tf_op jit(solution)/shard_map/ppermute | solution.py:387
  32.6 0.9 %shard_map.96 = (f32[320,128]{1,0:T(8,128)S(1)}, f32[320,128]{1,0:T(8,128)S(1)}) custom-call(bf16[5,11,256,256]{3,2,1,0:T(8,128)(2,1)S(1)} %shard_map.86.packed, f32[5,256,128]{2,1,0:T(8,128)S(1)} %shard_map.95.total, f32[640,128]{1,0:T(8,128)S(1)} %collective-permute-done.9.refs_0_), custom_call_target="tpu_custom_call" | custom-call | flops 503316480 | bytes 4194304 | tf_op jit(solution)/shard_map/pallas_call | solution.py:468
  33.6 5.3 %collective-permute-start.15 = (f32[320,128]{1,0:T(8,128)S(1)}, f32[320,128]{1,0:T(8,128)S(1)}, u32[]{:S(2)}, u32[]{:S(2)}) collective-permute-start(f32[320,128]{1,0:T(8,128)S(1)} %collective-permute-done.14.refs_0_), channel_id=1, source_target_pairs={{0,1},{1,0},{2,3},{3,2},{4,5},{5,4},{6,7},{7,6},{8,9},{9,8},{10,11... | collective-permute-start | bytes 491528 | tf_op jit(solution)/shard_map/ppermute | solution.py:387
  39.0 5.7 %collective-permute-start.10 = (f32[320,128]{1,0:T(8,128)S(1)}, f32[320,128]{1,0:T(8,128)S(1)}, u32[]{:S(2)}, u32[]{:S(2)}) collective-permute-start(f32[320,128]{1,0:T(8,128)S(1)} %shard_map.97.refs_2_), channel_id=1, source_target_pairs={{0,8},{1,9},{2,10},{3,11},{4,12},{5,13},{6,14},{7,15},{8,0},{9,1},... | collective-permute-start | bytes 491528 | tf_op jit(solution)/shard_map/ppermute | solution.py:387
  44.7 3.9 %collective-permute-start.17 = (f32[192,128]{1,0:T(8,128)S(1)}, f32[192,128]{1,0:T(8,128)S(1)}, u32[]{:S(2)}, u32[]{:S(2)}) collective-permute-start(f32[192,128]{1,0:T(8,128)S(1)} %get-tuple-element.32.refs_3_), channel_id=1, source_target_pairs={{0,8},{1,9},{2,10},{3,11},{4,12},{5,13},{6,14},{7,15},{8,0},{9,1},... | collective-permute-start | bytes 294920 | tf_op jit(solution)/shard_map/ppermute | solution.py:387
  49.4 1.5 %collective-permute-start.18 = (f32[128,128]{1,0:T(8,128)S(1)}, f32[128,128]{1,0:T(8,128)S(1)}, u32[]{:S(2)}, u32[]{:S(2)}) collective-permute-start(f32[128,128]{1,0:T(8,128)S(1)} %get-tuple-element.33.refs_4_), channel_id=1, source_target_pairs={{0,8},{1,9},{2,10},{3,11},{4,12},{5,13},{6,14},{7,15},{8,0},{9,1},... | collective-permute-start | bytes 196616 | tf_op jit(solution)/shard_map/ppermute | solution.py:387
  52.6 1.7 %collective-permute-start.21 = (f32[128,128]{1,0:T(8,128)S(1)}, f32[128,128]{1,0:T(8,128)S(1)}, u32[]{:S(2)}, u32[]{:S(2)}) collective-permute-start(f32[128,128]{1,0:T(8,128)S(1)} %collective-permute-done.18.refs_2_), channel_id=1, source_target_pairs={{0,1},{1,0},{2,3},{3,2},{4,5},{5,4},{6,7},{7,6},{8,9},{9,8},{10,11... | collective-permute-start | bytes 196616 | tf_op jit(solution)/shard_map/ppermute | solution.py:387
  54.2 1.3 %collective-permute-start.22 = (f32[320,128]{1,0:T(8,128)S(1)}, f32[320,128]{1,0:T(8,128)S(1)}, u32[]{:S(2)}, u32[]{:S(2)}) collective-permute-start(f32[320,128]{1,0:T(8,128)S(1)} %collective-permute-done.10.refs_0_), channel_id=1, source_target_pairs={{0,16},{1,2},{2,1},{3,4},{4,3},{5,6},{6,5},{7,23},{8,24},{9,10},{1... | collective-permute-start | bytes 491528 | tf_op jit(solution)/shard_map/ppermute | solution.py:387
  57.0 1.3 %collective-permute-start.23 = (f32[192,128]{1,0:T(8,128)S(1)}, f32[192,128]{1,0:T(8,128)S(1)}, u32[]{:S(2)}, u32[]{:S(2)}) collective-permute-start(f32[192,128]{1,0:T(8,128)S(1)} %collective-permute-done.17.refs_1_), channel_id=1, source_target_pairs={{0,16},{1,2},{2,1},{3,4},{4,3},{5,6},{6,5},{7,23},{8,24},{9,10},{1... | collective-permute-start | bytes 294920 | tf_op jit(solution)/shard_map/ppermute | solution.py:387
  58.3 1.8 %shard_map.103.total = f32[5,256,128]{2,1,0:T(8,128)S(1)} custom-call(bf16[5,11,256,256]{3,2,1,0:T(8,128)(2,1)S(1)} %shard_map.86.packed, f32[320,128]{1,0:T(8,128)S(1)} %collective-permute-done.10.refs_0_, f32[192,128]{1,0:T(8,128)S(1)} %collective-permute-done.17.refs_1_, f32[128,128]{1,0:T(8,128)S(1)} %collective-permute-done.18.refs_2_, ...), custom_call_target="tpu_custom_call" | custom-call | flops 1342177280 | bytes 8388608 | tf_op jit(solution)/shard_map/pallas_call | solution.py:451
  60.5 1.1 %collective-permute-done.23.refs_1_ = f32[192,128]{1,0:T(8,128)S(1)} collective-permute-done((f32[192,128]{1,0:T(8,128)S(1)}, f32[192,128]{1,0:T(8,128)S(1)}, u32[]{:S(2)}, u32[]{:S(2)}) %collective-permute-start.23) | collective-permute-done | bytes 98336 | tf_op jit(solution)/shard_map/ppermute | solution.py:387
  61.6 1.7 %shard_map.106 = (f32[1,640,128]{2,1,0:T(8,128)}, f32[1,640,128]{2,1,0:T(8,128)}) custom-call(bf16[5,11,256,256]{3,2,1,0:T(8,128)(2,1)S(1)} %shard_map.86.packed, f32[5,256,128]{2,1,0:T(8,128)S(1)} %shard_map.103.total, f32[320,128]{1,0:T(8,128)S(1)} %collective-permute-done.22.refs_0_, ...), custom_call_target="tpu_custom_call", output_to_operand_aliasing={{0}: (8, {}), {1}: (9, {})} | custom-call | flops 503316480 | bytes 4194304 | tf_op jit(solution)/shard_map/pallas_call | solution.py:468
  (47 shorter events, 7.6 us)
Async XLA Ops:
  2.4 5.8 %collective-permute-start = (f32[648,128]{1,0:T(8,128)S(1)}, f32[648,128]{1,0:T(8,128)S(1)}, u32[]{:S(2)}, u32[]{:S(2)}) collective-permute-start(f32[648,128]{1,0:T(8,128)S(1)} %get-tuple-element.20.refs_0_), channel_id=1, source_target_pairs={{0,1},{1,0},{2,3},{3,2},{4,5},{5,4},{6,7},{7,6},{8,9},{9,8},{10,11... | collective-permute-start | bytes 995336 | tf_op jit(solution)/shard_map/ppermute | solution.py:387
  2.5 7.5 %collective-permute-start.1 = (f32[648,128]{1,0:T(8,128)S(1)}, f32[648,128]{1,0:T(8,128)S(1)}, u32[]{:S(2)}, u32[]{:S(2)}) collective-permute-start(f32[648,128]{1,0:T(8,128)S(1)} %get-tuple-element.20.refs_0_), channel_id=1, source_target_pairs={{0,16},{1,2},{2,1},{3,4},{4,3},{5,6},{6,5},{7,23},{8,24},{9,10},{1... | collective-permute-start | bytes 995336 | tf_op jit(solution)/shard_map/ppermute | solution.py:387
  11.0 6.0 %collective-permute-start.2 = (f32[320,128]{1,0:T(8,128)S(1)}, f32[320,128]{1,0:T(8,128)S(1)}, u32[]{:S(2)}, u32[]{:S(2)}) collective-permute-start(f32[320,128]{1,0:T(8,128)S(1)} %get-tuple-element.21.refs_0_), channel_id=1, source_target_pairs={{0,8},{1,9},{2,10},{3,11},{4,12},{5,13},{6,14},{7,15},{8,0},{9,1},... | collective-permute-start | bytes 491528 | tf_op jit(solution)/shard_map/ppermute | solution.py:387
  11.6 9.2 %collective-permute-start.11 = (f32[320,128]{1,0:T(8,128)S(1)}, f32[320,128]{1,0:T(8,128)S(1)}, u32[]{:S(2)}, u32[]{:S(2)}) collective-permute-start(f32[320,128]{1,0:T(8,128)S(1)} %get-tuple-element.27.refs_1_), channel_id=1, source_target_pairs={{0,8},{1,9},{2,10},{3,11},{4,12},{5,13},{6,14},{7,15},{8,0},{9,1},... | collective-permute-start | bytes 491528 | tf_op jit(solution)/shard_map/ppermute | solution.py:387
  17.0 4.2 %collective-permute-start.3 = (f32[320,128]{1,0:T(8,128)S(1)}, f32[320,128]{1,0:T(8,128)S(1)}, u32[]{:S(2)}, u32[]{:S(2)}) collective-permute-start(f32[320,128]{1,0:T(8,128)S(1)} %collective-permute-done.2.refs_0_), channel_id=1, source_target_pairs={{0,1},{1,0},{2,3},{3,2},{4,5},{5,4},{6,7},{7,6},{8,9},{9,8},{10,11... | collective-permute-start | bytes 491528 | tf_op jit(solution)/shard_map/ppermute | solution.py:387
  18.0 11.2 %collective-permute-start.8 = (f32[640,128]{1,0:T(8,128)S(1)}, f32[640,128]{1,0:T(8,128)S(1)}, u32[]{:S(2)}, u32[]{:S(2)}) collective-permute-start(f32[640,128]{1,0:T(8,128)S(1)} %get-tuple-element.28.refs_0_), channel_id=1, source_target_pairs={{0,1},{1,0},{2,3},{3,2},{4,5},{5,4},{6,7},{7,6},{8,9},{9,8},{10,11... | collective-permute-start | bytes 983048 | tf_op jit(solution)/shard_map/ppermute | solution.py:387
  18.0 14.7 %collective-permute-start.9 = (f32[640,128]{1,0:T(8,128)S(1)}, f32[640,128]{1,0:T(8,128)S(1)}, u32[]{:S(2)}, u32[]{:S(2)}) collective-permute-start(f32[640,128]{1,0:T(8,128)S(1)} %get-tuple-element.28.refs_0_), channel_id=1, source_target_pairs={{0,16},{1,2},{2,1},{3,4},{4,3},{5,6},{6,5},{7,23},{8,24},{9,10},{1... | collective-permute-start | bytes 983048 | tf_op jit(solution)/shard_map/ppermute | solution.py:387
  20.7 6.5 %collective-permute-start.4 = (f32[320,128]{1,0:T(8,128)S(1)}, f32[320,128]{1,0:T(8,128)S(1)}, u32[]{:S(2)}, u32[]{:S(2)}) collective-permute-start(f32[320,128]{1,0:T(8,128)S(1)} %collective-permute-done.2.refs_0_), channel_id=1, source_target_pairs={{0,16},{1,2},{2,1},{3,4},{4,3},{5,6},{6,5},{7,23},{8,24},{9,10},{1... | collective-permute-start | bytes 491528 | tf_op jit(solution)/shard_map/ppermute | solution.py:387
  20.8 6.5 %collective-permute-start.12 = (f32[320,128]{1,0:T(8,128)S(1)}, f32[320,128]{1,0:T(8,128)S(1)}, u32[]{:S(2)}, u32[]{:S(2)}) collective-permute-start(f32[320,128]{1,0:T(8,128)S(1)} %collective-permute-done.11.refs_0_), channel_id=1, source_target_pairs={{0,1},{1,0},{2,3},{3,2},{4,5},{5,4},{6,7},{7,6},{8,9},{9,8},{10,11... | collective-permute-start | bytes 491528 | tf_op jit(solution)/shard_map/ppermute | solution.py:387
  21.2 7.5 %collective-permute-start.13 = (f32[320,128]{1,0:T(8,128)S(1)}, f32[320,128]{1,0:T(8,128)S(1)}, u32[]{:S(2)}, u32[]{:S(2)}) collective-permute-start(f32[320,128]{1,0:T(8,128)S(1)} %collective-permute-done.11.refs_0_), channel_id=1, source_target_pairs={{0,16},{1,2},{2,1},{3,4},{4,3},{5,6},{6,5},{7,23},{8,24},{9,10},{1... | collective-permute-start | bytes 491528 | tf_op jit(solution)/shard_map/ppermute | solution.py:387
  28.7 4.9 %collective-permute-start.14 = (f32[320,128]{1,0:T(8,128)S(1)}, f32[320,128]{1,0:T(8,128)S(1)}, u32[]{:S(2)}, u32[]{:S(2)}) collective-permute-start(f32[320,128]{1,0:T(8,128)S(1)} %shard_map.99.refs_1_), channel_id=1, source_target_pairs={{0,1},{1,0},{2,3},{3,2},{4,5},{5,4},{6,7},{7,6},{8,16},{9,17},{10,... | collective-permute-start | bytes 491528 | tf_op jit(solution)/shard_map/ppermute | solution.py:387
  29.1 9.9 %collective-permute-start.6 = (f32[320,128]{1,0:T(8,128)S(1)}, f32[320,128]{1,0:T(8,128)S(1)}, u32[]{:S(2)}, u32[]{:S(2)}) collective-permute-start(f32[320,128]{1,0:T(8,128)S(1)} %collective-permute-done.5.refs_0_), channel_id=1, source_target_pairs={{0,1},{1,0},{2,3},{3,2},{4,5},{5,4},{6,7},{7,6},{8,9},{9,8},{10,11... | collective-permute-start | bytes 491528 | tf_op jit(solution)/shard_map/ppermute | solution.py:387
  30.8 8.1 %collective-permute-start.7 = (f32[320,128]{1,0:T(8,128)S(1)}, f32[320,128]{1,0:T(8,128)S(1)}, u32[]{:S(2)}, u32[]{:S(2)}) collective-permute-start(f32[320,128]{1,0:T(8,128)S(1)} %collective-permute-done.5.refs_0_), channel_id=1, source_target_pairs={{0,16},{1,2},{2,1},{3,4},{4,3},{5,6},{6,5},{7,23},{8,24},{9,10},{1... | collective-permute-start | bytes 491528 | tf_op jit(solution)/shard_map/ppermute | solution.py:387
  33.6 11.1 %collective-permute-start.15 = (f32[320,128]{1,0:T(8,128)S(1)}, f32[320,128]{1,0:T(8,128)S(1)}, u32[]{:S(2)}, u32[]{:S(2)}) collective-permute-start(f32[320,128]{1,0:T(8,128)S(1)} %collective-permute-done.14.refs_0_), channel_id=1, source_target_pairs={{0,1},{1,0},{2,3},{3,2},{4,5},{5,4},{6,7},{7,6},{8,9},{9,8},{10,11... | collective-permute-start | bytes 491528 | tf_op jit(solution)/shard_map/ppermute | solution.py:387
  38.9 5.8 %collective-permute-start.16 = (f32[320,128]{1,0:T(8,128)S(1)}, f32[320,128]{1,0:T(8,128)S(1)}, u32[]{:S(2)}, u32[]{:S(2)}) collective-permute-start(f32[320,128]{1,0:T(8,128)S(1)} %collective-permute-done.14.refs_0_), channel_id=1, source_target_pairs={{0,16},{1,2},{2,1},{3,4},{4,3},{5,6},{6,5},{7,23},{8,24},{9,10},{1... | collective-permute-start | bytes 491528 | tf_op jit(solution)/shard_map/ppermute | solution.py:387
  39.0 10.5 %collective-permute-start.10 = (f32[320,128]{1,0:T(8,128)S(1)}, f32[320,128]{1,0:T(8,128)S(1)}, u32[]{:S(2)}, u32[]{:S(2)}) collective-permute-start(f32[320,128]{1,0:T(8,128)S(1)} %shard_map.97.refs_2_), channel_id=1, source_target_pairs={{0,8},{1,9},{2,10},{3,11},{4,12},{5,13},{6,14},{7,15},{8,0},{9,1},... | collective-permute-start | bytes 491528 | tf_op jit(solution)/shard_map/ppermute | solution.py:387
  44.7 6.2 %collective-permute-start.17 = (f32[192,128]{1,0:T(8,128)S(1)}, f32[192,128]{1,0:T(8,128)S(1)}, u32[]{:S(2)}, u32[]{:S(2)}) collective-permute-start(f32[192,128]{1,0:T(8,128)S(1)} %get-tuple-element.32.refs_3_), channel_id=1, source_target_pairs={{0,8},{1,9},{2,10},{3,11},{4,12},{5,13},{6,14},{7,15},{8,0},{9,1},... | collective-permute-start | bytes 294920 | tf_op jit(solution)/shard_map/ppermute | solution.py:387
  49.4 8.8 %collective-permute-start.19 = (f32[320,128]{1,0:T(8,128)S(1)}, f32[320,128]{1,0:T(8,128)S(1)}, u32[]{:S(2)}, u32[]{:S(2)}) collective-permute-start(f32[320,128]{1,0:T(8,128)S(1)} %collective-permute-done.10.refs_0_), channel_id=1, source_target_pairs={{0,1},{1,0},{2,3},{3,2},{4,5},{5,4},{6,7},{7,6},{8,9},{9,8},{10,11... | collective-permute-start | bytes 491528 | tf_op jit(solution)/shard_map/ppermute | solution.py:387
  49.4 3.1 %collective-permute-start.18 = (f32[128,128]{1,0:T(8,128)S(1)}, f32[128,128]{1,0:T(8,128)S(1)}, u32[]{:S(2)}, u32[]{:S(2)}) collective-permute-start(f32[128,128]{1,0:T(8,128)S(1)} %get-tuple-element.33.refs_4_), channel_id=1, source_target_pairs={{0,8},{1,9},{2,10},{3,11},{4,12},{5,13},{6,14},{7,15},{8,0},{9,1},... | collective-permute-start | bytes 196616 | tf_op jit(solution)/shard_map/ppermute | solution.py:387
  50.9 7.4 %collective-permute-start.20 = (f32[192,128]{1,0:T(8,128)S(1)}, f32[192,128]{1,0:T(8,128)S(1)}, u32[]{:S(2)}, u32[]{:S(2)}) collective-permute-start(f32[192,128]{1,0:T(8,128)S(1)} %collective-permute-done.17.refs_1_), channel_id=1, source_target_pairs={{0,1},{1,0},{2,3},{3,2},{4,5},{5,4},{6,7},{7,6},{8,9},{9,8},{10,11... | collective-permute-start | bytes 294920 | tf_op jit(solution)/shard_map/ppermute | solution.py:387
  52.6 4.4 %collective-permute-start.21 = (f32[128,128]{1,0:T(8,128)S(1)}, f32[128,128]{1,0:T(8,128)S(1)}, u32[]{:S(2)}, u32[]{:S(2)}) collective-permute-start(f32[128,128]{1,0:T(8,128)S(1)} %collective-permute-done.18.refs_2_), channel_id=1, source_target_pairs={{0,1},{1,0},{2,3},{3,2},{4,5},{5,4},{6,7},{7,6},{8,9},{9,8},{10,11... | collective-permute-start | bytes 196616 | tf_op jit(solution)/shard_map/ppermute | solution.py:387
  54.2 7.3 %collective-permute-start.22 = (f32[320,128]{1,0:T(8,128)S(1)}, f32[320,128]{1,0:T(8,128)S(1)}, u32[]{:S(2)}, u32[]{:S(2)}) collective-permute-start(f32[320,128]{1,0:T(8,128)S(1)} %collective-permute-done.10.refs_0_), channel_id=1, source_target_pairs={{0,16},{1,2},{2,1},{3,4},{4,3},{5,6},{6,5},{7,23},{8,24},{9,10},{1... | collective-permute-start | bytes 491528 | tf_op jit(solution)/shard_map/ppermute | solution.py:387
  56.5 4.1 %collective-permute-start.24 = (f32[128,128]{1,0:T(8,128)S(1)}, f32[128,128]{1,0:T(8,128)S(1)}, u32[]{:S(2)}, u32[]{:S(2)}) collective-permute-start(f32[128,128]{1,0:T(8,128)S(1)} %collective-permute-done.18.refs_2_), channel_id=1, source_target_pairs={{0,16},{1,2},{2,1},{3,4},{4,3},{5,6},{6,5},{7,23},{8,24},{9,10},{1... | collective-permute-start | bytes 196616 | tf_op jit(solution)/shard_map/ppermute | solution.py:387
  57.0 4.6 %collective-permute-start.23 = (f32[192,128]{1,0:T(8,128)S(1)}, f32[192,128]{1,0:T(8,128)S(1)}, u32[]{:S(2)}, u32[]{:S(2)}) collective-permute-start(f32[192,128]{1,0:T(8,128)S(1)} %collective-permute-done.17.refs_1_), channel_id=1, source_target_pairs={{0,16},{1,2},{2,1},{3,4},{4,3},{5,6},{6,5},{7,23},{8,24},{9,10},{1... | collective-permute-start | bytes 294920 | tf_op jit(solution)/shard_map/ppermute | solution.py:387
  (1 other events, 1.9 us)

commit v10 on v9

--- a/solution.py
+++ b/solution.py
@@ -199,6 +199,16 @@
     return merged(*[part_tile(part, t) for part in field])
 
 
+def aligned(j, size):
+    return j * size if isinstance(j, int) else pl.multiple_of(j * size, size)
+
+
+def choose(condition, this, that):
+    if isinstance(condition, bool):
+        return this if condition else that
+    return jnp.where(condition, this, that)
+
+
 def spread(field, scale, sign, tiles, narrow, mirrored, held):
     for t in range(tiles):
         tile = unpack_tile(field[0], t) if narrow else full_tile(field, t)
@@ -206,7 +216,8 @@
             tile = tile * (1.0 + sign * scale[t])
         at = 2 * t * TILE
         if mirrored is not None:
-            at = pl.multiple_of(jnp.where(mirrored, 2 * (tiles - 1 - t) * TILE, at), 2 * TILE)
+            at = choose(mirrored, 2 * (tiles - 1 - t) * TILE, at)
+            at = at if isinstance(at, int) else pl.multiple_of(at, 2 * TILE)
         held[pl.ds(at, 2 * TILE)] = stream_line(tile) if narrow else doubled(tile)
 
 
@@ -220,8 +231,8 @@
 
 
 def side_product(packed, held, tiles, jj, low_side, narrow):
-    j = jnp.where(low_side, tiles - 1 - jj, jj)
-    slots = [jnp.where(low_side, jj - t, 2 * tiles + t - jj) for t in range(jj + 1)]
+    j = choose(low_side, tiles - 1 - jj, jj)
+    slots = [choose(low_side, jj - t, 2 * tiles + t - jj) for t in range(jj + 1)]
     return j, product(packed, held, j, slots, narrow)
 
 
@@ -296,21 +307,17 @@
             return pltpu.make_async_copy(leaving.at[at], result.at[0, at], sems.at[j])
 
         def store(j, value):
-            first = 0
+            if len(outs) == 1:
+                outs[0][pl.ds(aligned(j, HALF), HALF)] = value
+                return
             for out in outs:
                 count = out.shape[0] // HALF
-
-                def put(out=out, first=first):
-                    out[pl.ds(pl.multiple_of((j - first) * HALF, HALF), HALF)] = value
-
-                if len(outs) == 1:
-                    put()
-                else:
-                    pl.when((j >= first) & (j < first + count))(put)
-                first += count
+                if 0 <= j < count:
+                    out[halves_of(j)] = value
+                j -= count
 
         def finish(j, value):
-            at = pl.ds(pl.multiple_of(j * HALF, HALF), HALF)
+            at = pl.ds(aligned(j, HALF), HALF)
             if narrow:
                 value = combined(value + turned(value), shots)
                 store(j, jnp.where(left_half(HALF), value[:HALF], value[HALF:]) + base[0][at])
@@ -325,12 +332,17 @@
             for out, part in zip(outs, parted(value)):
                 out[at] = part
 
-        @pl.when(has_far)
-        def _():
-            spread(far, scale, sign, tiles, narrow, low_side, held)
+        def with_far(low):
+            spread(far, scale, sign, tiles, narrow, low, held)
             for jj in range(tiles):
-                j, value = side_product(packed, held, tiles, jj, low_side, narrow)
+                j, value = side_product(packed, held, tiles, jj, low, narrow)
                 finish(j, total[j] + value)
+
+        if narrow and len(outs) > 1:
+            pl.when(has_far & low_side)(lambda: with_far(True))
+            pl.when(has_far & jnp.logical_not(low_side))(lambda: with_far(False))
+        else:
+            pl.when(has_far)(lambda: with_far(low_side))
 
         @pl.when(jnp.logical_not(has_far))
         def _():
@@ -531,15 +543,18 @@
             nears.append([near for near, _ in halos])
             fars.append([far for _, far in halos])
         if step == sections - 1:
-            mark = call(
-                mark_kernel,
-                out_shape=f32(8, columns),
-                in_specs=[],
-                out_specs=spec(VMEM),
-                compiler_params=params(),
-                cost_estimate=cost(0, 1),
-            )()
-            total = inner(step, arrived, nears, own_scale, near_scale, mark)
+            marks = [
+                call(
+                    mark_kernel,
+                    out_shape=f32(8, columns),
+                    in_specs=[],
+                    out_specs=spec(VMEM),
+                    compiler_params=pltpu.CompilerParams(vmem_limit_bytes=LIMIT, has_side_effects=True),
+                    cost_estimate=cost(0, 1),
+                )()
+                for _ in range(STREAMS)
+            ]
+            total = inner(step, arrived, nears, own_scale, near_scale, *marks)
             kept = keep(range(middle - 1)) if middle > 1 else ()
             kept = keep(range(middle - 1, step), kept)
             return tuple(outer(step, total, fars, far_scale, *bases, shapes=result, kept=kept))

time: 64 us -> 64.1 us (level)
  waiting for transfers between devices: 13.6 us -> 14.3 us
  starting transfers between devices: 34.3 us -> 33.6 us
    ppermute x25, waiting for transfers between devices: 13.6 us -> 14.3 us  [move(): return lax.ppermute(x, ('depth', 'lat'), pairs)]
    ppermute x25, starting transfers between devices: 34.3 us -> 33.6 us  [move(): return lax.ppermute(x, ('depth', 'lat'), pairs)]
where the time goes in v10:
time: 64.1 us; the launch traced here: 63.5 us
  starting transfers between devices  33.6 us (52%)
  Pallas kernels  14.7 us (23%)
  waiting for transfers between devices  14.3 us (22%)
  between operations  0.95 us (1%)
    ppermute x25, starting transfers between devices, move(): return lax.ppermute(x, ('depth', 'lat'), pairs)  33.6 us
    ppermute x25, waiting for transfers between devices, move(): return lax.ppermute(x, ('depth', 'lat'), pairs)  14.3 us
    pallas_call x7, Pallas kernels, inner(): call(functools.partial(inner_kernel, step, sections, tiles, [len(part) fo...  5.1 us
    pallas_call x8, Pallas kernels, outer(): call(functools.partial(outer_kernel, step, sections, lats, tiles, shots,...  3.63 us
    pallas_call x1, Pallas kernels, shards(): call(functools.partial(pack_kernel, tiles, band), out_shape=jax.ShapeDtyp...  2.95 us
    pallas_call x1, Pallas kernels, shards(): call(functools.partial(prep_kernel, tiles, shots, sections), out_shape=[f...  1.76 us
  transfers between devices with their start and end apart: 25, of which 8 were waited for; matrix products, arithmetic and copies ran while one was open for 0% of the time, Pallas kernels for 16%

profile of v10, /device:TPU:1, one launch (start us, length us, event | category | flops | bytes accessed | tf_op | source)
XLA Modules:
  0.0 63.5 jit_solution(11589158641023927858)
XLA Ops:
  0.6 1.8 %shard_map.87 = (f32[648,128]{1,0:T(8,128)S(1)}, f32[640,128]{1,0:T(8,128)S(1)}) custom-call(s32[64]{0:T(128)} %assign_at.1, f32[1,640]{1,0:T(1,128)} %refl_at.1, f32[1,640,128]{2,1,0:T(8,128)} %up_at.1, f32[1,640,128]{2,1,0:T(8,128)} %down_at.1, f32[640,128]{1,0:T(8,128)} %src_at.1), custom_call_target="tpu_custom_call" | custom-call | flops 10000000 | bytes 1638400 | tf_op jit(solution)/shard_map/pallas_call | solution.py:423
  2.5 2.7 %collective-permute-start.1 = (f32[648,128]{1,0:T(8,128)S(1)}, f32[648,128]{1,0:T(8,128)S(1)}, u32[]{:S(2)}, u32[]{:S(2)}) collective-permute-start(f32[648,128]{1,0:T(8,128)S(1)} %get-tuple-element.20.refs_0_), channel_id=1, source_target_pairs={{0,16},{1,2},{2,1},{3,4},{4,3},{5,6},{6,5},{7,23},{8,24},{9,10},{1... | collective-permute-start | bytes 995336 | tf_op jit(solution)/shard_map/ppermute | solution.py:399
  5.2 3.0 %shard_map.86.packed = bf16[5,11,256,256]{3,2,1,0:T(8,128)(2,1)S(1)} custom-call(s32[1,5]{1,0:T(1,128)} %shift_at.1, f32[1,5,9,256,128]{4,3,2,1,0:T(8,128)} %tiles_at.1), custom_call_target="tpu_custom_call" | custom-call | flops 10000000 | bytes 11796480 | tf_op jit(solution)/shard_map/pallas_call | solution.py:440
  8.2 1.7 %shard_map.88.total = f32[5,256,128]{2,1,0:T(8,128)S(1)} custom-call(bf16[5,11,256,256]{3,2,1,0:T(8,128)(2,1)S(1)} %shard_map.86.packed, f32[648,128]{1,0:T(8,128)S(1)} %get-tuple-element.20.refs_0_, f32[648,128]{1,0:T(8,128)S(1)} %collective-permute-done.refs_1_), custom_call_target="tpu_custom_call" | custom-call | flops 1342177280 | bytes 8388608 | tf_op jit(solution)/shard_map/pallas_call | solution.py:463
  10.0 0.9 %shard_map.89 = (f32[320,128]{1,0:T(8,128)S(1)}, f32[320,128]{1,0:T(8,128)S(1)}) custom-call(bf16[5,11,256,256]{3,2,1,0:T(8,128)(2,1)S(1)} %shard_map.86.packed, f32[5,256,128]{2,1,0:T(8,128)S(1)} %shard_map.88.total, f32[648,128]{1,0:T(8,128)S(1)} %collective-permute-done.1.refs_0_.refs_2_), custom_call_target="tpu_custom_call" | custom-call | flops 503316480 | bytes 4194304 | tf_op jit(solution)/shard_map/pallas_call | solution.py:480
  12.5 4.5 %collective-permute-done.2.refs_0_ = f32[320,128]{1,0:T(8,128)S(1)} collective-permute-done((f32[320,128]{1,0:T(8,128)S(1)}, f32[320,128]{1,0:T(8,128)S(1)}, u32[]{:S(2)}, u32[]{:S(2)}) %collective-permute-start.2) | collective-permute-done | bytes 163872 | tf_op jit(solution)/shard_map/ppermute | solution.py:399
  17.0 1.0 %collective-permute-start.3 = (f32[320,128]{1,0:T(8,128)S(1)}, f32[320,128]{1,0:T(8,128)S(1)}, u32[]{:S(2)}, u32[]{:S(2)}) collective-permute-start(f32[320,128]{1,0:T(8,128)S(1)} %collective-permute-done.2.refs_0_), channel_id=1, source_target_pairs={{0,1},{1,0},{2,3},{3,2},{4,5},{5,4},{6,7},{7,6},{8,9},{9,8},{10,11... | collective-permute-start | bytes 491528 | tf_op jit(solution)/shard_map/ppermute | solution.py:399
  18.0 2.4 %collective-permute-start.9 = (f32[640,128]{1,0:T(8,128)S(1)}, f32[640,128]{1,0:T(8,128)S(1)}, u32[]{:S(2)}, u32[]{:S(2)}) collective-permute-start(f32[640,128]{1,0:T(8,128)S(1)} %get-tuple-element.28.refs_0_), channel_id=1, source_target_pairs={{0,16},{1,2},{2,1},{3,4},{4,3},{5,6},{6,5},{7,23},{8,24},{9,10},{1... | collective-permute-start | bytes 983048 | tf_op jit(solution)/shard_map/ppermute | solution.py:399
  21.2 1.7 %collective-permute-start.13 = (f32[320,128]{1,0:T(8,128)S(1)}, f32[320,128]{1,0:T(8,128)S(1)}, u32[]{:S(2)}, u32[]{:S(2)}) collective-permute-start(f32[320,128]{1,0:T(8,128)S(1)} %collective-permute-done.11.refs_0_), channel_id=1, source_target_pairs={{0,16},{1,2},{2,1},{3,4},{4,3},{5,6},{6,5},{7,23},{8,24},{9,10},{1... | collective-permute-start | bytes 491528 | tf_op jit(solution)/shard_map/ppermute | solution.py:399
  22.9 4.3 %collective-permute-done.4.refs_0_ = f32[320,128]{1,0:T(8,128)S(1)} collective-permute-done((f32[320,128]{1,0:T(8,128)S(1)}, f32[320,128]{1,0:T(8,128)S(1)}, u32[]{:S(2)}, u32[]{:S(2)}) %collective-permute-start.4) | collective-permute-done | bytes 163872 | tf_op jit(solution)/shard_map/ppermute | solution.py:399
  27.3 1.4 %collective-permute-done.13.refs_0_ = f32[320,128]{1,0:T(8,128)S(1)} collective-permute-done((f32[320,128]{1,0:T(8,128)S(1)}, f32[320,128]{1,0:T(8,128)S(1)}, u32[]{:S(2)}, u32[]{:S(2)}) %collective-permute-start.13) | collective-permute-done | bytes 163872 | tf_op jit(solution)/shard_map/ppermute | solution.py:399
  29.2 1.7 %shard_map.95.total = f32[5,256,128]{2,1,0:T(8,128)S(1)} custom-call(bf16[5,11,256,256]{3,2,1,0:T(8,128)(2,1)S(1)} %shard_map.86.packed, f32[640,128]{1,0:T(8,128)S(1)} %get-tuple-element.28.refs_0_, f32[640,128]{1,0:T(8,128)S(1)} %collective-permute-done.8.refs_1_), custom_call_target="tpu_custom_call" | custom-call | flops 1342177280 | bytes 8388608 | tf_op jit(solution)/shard_map/pallas_call | solution.py:463
  30.8 1.8 %collective-permute-start.7 = (f32[320,128]{1,0:T(8,128)S(1)}, f32[320,128]{1,0:T(8,128)S(1)}, u32[]{:S(2)}, u32[]{:S(2)}) collective-permute-start(f32[320,128]{1,0:T(8,128)S(1)} %collective-permute-done.5.refs_0_), channel_id=1, source_target_pairs={{0,16},{1,2},{2,1},{3,4},{4,3},{5,6},{6,5},{7,23},{8,24},{9,10},{1... | collective-permute-start | bytes 491528 | tf_op jit(solution)/shard_map/ppermute | solution.py:399
  33.6 5.4 %collective-permute-start.15 = (f32[320,128]{1,0:T(8,128)S(1)}, f32[320,128]{1,0:T(8,128)S(1)}, u32[]{:S(2)}, u32[]{:S(2)}) collective-permute-start(f32[320,128]{1,0:T(8,128)S(1)} %collective-permute-done.14.refs_0_), channel_id=1, source_target_pairs={{0,1},{1,0},{2,3},{3,2},{4,5},{5,4},{6,7},{7,6},{8,9},{9,8},{10,11... | collective-permute-start | bytes 491528 | tf_op jit(solution)/shard_map/ppermute | solution.py:399
  39.0 5.8 %collective-permute-start.10 = (f32[320,128]{1,0:T(8,128)S(1)}, f32[320,128]{1,0:T(8,128)S(1)}, u32[]{:S(2)}, u32[]{:S(2)}) collective-permute-start(f32[320,128]{1,0:T(8,128)S(1)} %shard_map.97.refs_2_), channel_id=1, source_target_pairs={{0,8},{1,9},{2,10},{3,11},{4,12},{5,13},{6,14},{7,15},{8,0},{9,1},... | collective-permute-start | bytes 491528 | tf_op jit(solution)/shard_map/ppermute | solution.py:399
  44.8 3.1 %collective-permute-start.17 = (f32[192,128]{1,0:T(8,128)S(1)}, f32[192,128]{1,0:T(8,128)S(1)}, u32[]{:S(2)}, u32[]{:S(2)}) collective-permute-start(f32[192,128]{1,0:T(8,128)S(1)} %get-tuple-element.32.refs_3_), channel_id=1, source_target_pairs={{0,8},{1,9},{2,10},{3,11},{4,12},{5,13},{6,14},{7,15},{8,0},{9,1},... | collective-permute-start | bytes 294920 | tf_op jit(solution)/shard_map/ppermute | solution.py:399
  47.9 1.6 %collective-permute-done.10.refs_0_ = f32[320,128]{1,0:T(8,128)S(1)} collective-permute-done((f32[320,128]{1,0:T(8,128)S(1)}, f32[320,128]{1,0:T(8,128)S(1)}, u32[]{:S(2)}, u32[]{:S(2)}) %collective-permute-start.10) | collective-permute-done | bytes 163872 | tf_op jit(solution)/shard_map/ppermute | solution.py:399
  49.5 1.5 %collective-permute-start.18 = (f32[128,128]{1,0:T(8,128)S(1)}, f32[128,128]{1,0:T(8,128)S(1)}, u32[]{:S(2)}, u32[]{:S(2)}) collective-permute-start(f32[128,128]{1,0:T(8,128)S(1)} %get-tuple-element.33.refs_4_), channel_id=1, source_target_pairs={{0,8},{1,9},{2,10},{3,11},{4,12},{5,13},{6,14},{7,15},{8,0},{9,1},... | collective-permute-start | bytes 196616 | tf_op jit(solution)/shard_map/ppermute | solution.py:399
  52.7 1.7 %collective-permute-start.21 = (f32[128,128]{1,0:T(8,128)S(1)}, f32[128,128]{1,0:T(8,128)S(1)}, u32[]{:S(2)}, u32[]{:S(2)}) collective-permute-start(f32[128,128]{1,0:T(8,128)S(1)} %collective-permute-done.18.refs_2_), channel_id=1, source_target_pairs={{0,1},{1,0},{2,3},{3,2},{4,5},{5,4},{6,7},{7,6},{8,9},{9,8},{10,11... | collective-permute-start | bytes 196616 | tf_op jit(solution)/shard_map/ppermute | solution.py:399
  54.3 1.3 %collective-permute-start.22 = (f32[320,128]{1,0:T(8,128)S(1)}, f32[320,128]{1,0:T(8,128)S(1)}, u32[]{:S(2)}, u32[]{:S(2)}) collective-permute-start(f32[320,128]{1,0:T(8,128)S(1)} %collective-permute-done.10.refs_0_), channel_id=1, source_target_pairs={{0,16},{1,2},{2,1},{3,4},{4,3},{5,6},{6,5},{7,23},{8,24},{9,10},{1... | collective-permute-start | bytes 491528 | tf_op jit(solution)/shard_map/ppermute | solution.py:399
  57.1 1.3 %collective-permute-start.23 = (f32[192,128]{1,0:T(8,128)S(1)}, f32[192,128]{1,0:T(8,128)S(1)}, u32[]{:S(2)}, u32[]{:S(2)}) collective-permute-start(f32[192,128]{1,0:T(8,128)S(1)} %collective-permute-done.17.refs_1_), channel_id=1, source_target_pairs={{0,16},{1,2},{2,1},{3,4},{4,3},{5,6},{6,5},{7,23},{8,24},{9,10},{1... | collective-permute-start | bytes 294920 | tf_op jit(solution)/shard_map/ppermute | solution.py:399
  58.4 1.8 %shard_map.104.total = f32[5,256,128]{2,1,0:T(8,128)S(1)} custom-call(bf16[5,11,256,256]{3,2,1,0:T(8,128)(2,1)S(1)} %shard_map.86.packed, f32[320,128]{1,0:T(8,128)S(1)} %collective-permute-done.10.refs_0_, f32[192,128]{1,0:T(8,128)S(1)} %collective-permute-done.17.refs_1_, f32[128,128]{1,0:T(8,128)S(1)} %collective-permute-done.18.refs_2_, ...), custom_call_target="tpu_custom_call" | custom-call | flops 1342177280 | bytes 8388608 | tf_op jit(solution)/shard_map/pallas_call | solution.py:463
  60.6 1.1 %collective-permute-done.23.refs_1_ = f32[192,128]{1,0:T(8,128)S(1)} collective-permute-done((f32[192,128]{1,0:T(8,128)S(1)}, f32[192,128]{1,0:T(8,128)S(1)}, u32[]{:S(2)}, u32[]{:S(2)}) %collective-permute-start.23) | collective-permute-done | bytes 98336 | tf_op jit(solution)/shard_map/ppermute | solution.py:399
  61.7 1.7 %shard_map.107 = (f32[1,640,128]{2,1,0:T(8,128)}, f32[1,640,128]{2,1,0:T(8,128)}) custom-call(bf16[5,11,256,256]{3,2,1,0:T(8,128)(2,1)S(1)} %shard_map.86.packed, f32[5,256,128]{2,1,0:T(8,128)S(1)} %shard_map.104.total, f32[320,128]{1,0:T(8,128)S(1)} %collective-permute-done.22.refs_0_, ...), custom_call_target="tpu_custom_call", output_to_operand_aliasing={{0}: (8, {}), {1}: (9, {})} | custom-call | flops 503316480 | bytes 4194304 | tf_op jit(solution)/shard_map/pallas_call | solution.py:480
  (48 shorter events, 7.8 us)
Async XLA Ops:
  2.4 5.8 %collective-permute-start = (f32[648,128]{1,0:T(8,128)S(1)}, f32[648,128]{1,0:T(8,128)S(1)}, u32[]{:S(2)}, u32[]{:S(2)}) collective-permute-start(f32[648,128]{1,0:T(8,128)S(1)} %get-tuple-element.20.refs_0_), channel_id=1, source_target_pairs={{0,1},{1,0},{2,3},{3,2},{4,5},{5,4},{6,7},{7,6},{8,9},{9,8},{10,11... | collective-permute-start | bytes 995336 | tf_op jit(solution)/shard_map/ppermute | solution.py:399
  2.5 7.5 %collective-permute-start.1 = (f32[648,128]{1,0:T(8,128)S(1)}, f32[648,128]{1,0:T(8,128)S(1)}, u32[]{:S(2)}, u32[]{:S(2)}) collective-permute-start(f32[648,128]{1,0:T(8,128)S(1)} %get-tuple-element.20.refs_0_), channel_id=1, source_target_pairs={{0,16},{1,2},{2,1},{3,4},{4,3},{5,6},{6,5},{7,23},{8,24},{9,10},{1... | collective-permute-start | bytes 995336 | tf_op jit(solution)/shard_map/ppermute | solution.py:399
  11.0 6.0 %collective-permute-start.2 = (f32[320,128]{1,0:T(8,128)S(1)}, f32[320,128]{1,0:T(8,128)S(1)}, u32[]{:S(2)}, u32[]{:S(2)}) collective-permute-start(f32[320,128]{1,0:T(8,128)S(1)} %get-tuple-element.21.refs_0_), channel_id=1, source_target_pairs={{0,8},{1,9},{2,10},{3,11},{4,12},{5,13},{6,14},{7,15},{8,0},{9,1},... | collective-permute-start | bytes 491528 | tf_op jit(solution)/shard_map/ppermute | solution.py:399
  11.6 9.2 %collective-permute-start.11 = (f32[320,128]{1,0:T(8,128)S(1)}, f32[320,128]{1,0:T(8,128)S(1)}, u32[]{:S(2)}, u32[]{:S(2)}) collective-permute-start(f32[320,128]{1,0:T(8,128)S(1)} %get-tuple-element.27.refs_1_), channel_id=1, source_target_pairs={{0,8},{1,9},{2,10},{3,11},{4,12},{5,13},{6,14},{7,15},{8,0},{9,1},... | collective-permute-start | bytes 491528 | tf_op jit(solution)/shard_map/ppermute | solution.py:399
  17.0 4.2 %collective-permute-start.3 = (f32[320,128]{1,0:T(8,128)S(1)}, f32[320,128]{1,0:T(8,128)S(1)}, u32[]{:S(2)}, u32[]{:S(2)}) collective-permute-start(f32[320,128]{1,0:T(8,128)S(1)} %collective-permute-done.2.refs_0_), channel_id=1, source_target_pairs={{0,1},{1,0},{2,3},{3,2},{4,5},{5,4},{6,7},{7,6},{8,9},{9,8},{10,11... | collective-permute-start | bytes 491528 | tf_op jit(solution)/shard_map/ppermute | solution.py:399
  18.0 11.2 %collective-permute-start.8 = (f32[640,128]{1,0:T(8,128)S(1)}, f32[640,128]{1,0:T(8,128)S(1)}, u32[]{:S(2)}, u32[]{:S(2)}) collective-permute-start(f32[640,128]{1,0:T(8,128)S(1)} %get-tuple-element.28.refs_0_), channel_id=1, source_target_pairs={{0,1},{1,0},{2,3},{3,2},{4,5},{5,4},{6,7},{7,6},{8,9},{9,8},{10,11... | collective-permute-start | bytes 983048 | tf_op jit(solution)/shard_map/ppermute | solution.py:399
  18.0 14.7 %collective-permute-start.9 = (f32[640,128]{1,0:T(8,128)S(1)}, f32[640,128]{1,0:T(8,128)S(1)}, u32[]{:S(2)}, u32[]{:S(2)}) collective-permute-start(f32[640,128]{1,0:T(8,128)S(1)} %get-tuple-element.28.refs_0_), channel_id=1, source_target_pairs={{0,16},{1,2},{2,1},{3,4},{4,3},{5,6},{6,5},{7,23},{8,24},{9,10},{1... | collective-permute-start | bytes 983048 | tf_op jit(solution)/shard_map/ppermute | solution.py:399
  20.7 6.5 %collective-permute-start.4 = (f32[320,128]{1,0:T(8,128)S(1)}, f32[320,128]{1,0:T(8,128)S(1)}, u32[]{:S(2)}, u32[]{:S(2)}) collective-permute-start(f32[320,128]{1,0:T(8,128)S(1)} %collective-permute-done.2.refs_0_), channel_id=1, source_target_pairs={{0,16},{1,2},{2,1},{3,4},{4,3},{5,6},{6,5},{7,23},{8,24},{9,10},{1... | collective-permute-start | bytes 491528 | tf_op jit(solution)/shard_map/ppermute | solution.py:399
  20.8 6.5 %collective-permute-start.12 = (f32[320,128]{1,0:T(8,128)S(1)}, f32[320,128]{1,0:T(8,128)S(1)}, u32[]{:S(2)}, u32[]{:S(2)}) collective-permute-start(f32[320,128]{1,0:T(8,128)S(1)} %collective-permute-done.11.refs_0_), channel_id=1, source_target_pairs={{0,1},{1,0},{2,3},{3,2},{4,5},{5,4},{6,7},{7,6},{8,9},{9,8},{10,11... | collective-permute-start | bytes 491528 | tf_op jit(solution)/shard_map/ppermute | solution.py:399
  21.2 7.5 %collective-permute-start.13 = (f32[320,128]{1,0:T(8,128)S(1)}, f32[320,128]{1,0:T(8,128)S(1)}, u32[]{:S(2)}, u32[]{:S(2)}) collective-permute-start(f32[320,128]{1,0:T(8,128)S(1)} %collective-permute-done.11.refs_0_), channel_id=1, source_target_pairs={{0,16},{1,2},{2,1},{3,4},{4,3},{5,6},{6,5},{7,23},{8,24},{9,10},{1... | collective-permute-start | bytes 491528 | tf_op jit(solution)/shard_map/ppermute | solution.py:399
  28.7 4.9 %collective-permute-start.14 = (f32[320,128]{1,0:T(8,128)S(1)}, f32[320,128]{1,0:T(8,128)S(1)}, u32[]{:S(2)}, u32[]{:S(2)}) collective-permute-start(f32[320,128]{1,0:T(8,128)S(1)} %shard_map.99.refs_1_), channel_id=1, source_target_pairs={{0,1},{1,0},{2,3},{3,2},{4,5},{5,4},{6,7},{7,6},{8,16},{9,17},{10,... | collective-permute-start | bytes 491528 | tf_op jit(solution)/shard_map/ppermute | solution.py:399
  29.1 9.9 %collective-permute-start.6 = (f32[320,128]{1,0:T(8,128)S(1)}, f32[320,128]{1,0:T(8,128)S(1)}, u32[]{:S(2)}, u32[]{:S(2)}) collective-permute-start(f32[320,128]{1,0:T(8,128)S(1)} %collective-permute-done.5.refs_0_), channel_id=1, source_target_pairs={{0,1},{1,0},{2,3},{3,2},{4,5},{5,4},{6,7},{7,6},{8,9},{9,8},{10,11... | collective-permute-start | bytes 491528 | tf_op jit(solution)/shard_map/ppermute | solution.py:399
  30.8 8.1 %collective-permute-start.7 = (f32[320,128]{1,0:T(8,128)S(1)}, f32[320,128]{1,0:T(8,128)S(1)}, u32[]{:S(2)}, u32[]{:S(2)}) collective-permute-start(f32[320,128]{1,0:T(8,128)S(1)} %collective-permute-done.5.refs_0_), channel_id=1, source_target_pairs={{0,16},{1,2},{2,1},{3,4},{4,3},{5,6},{6,5},{7,23},{8,24},{9,10},{1... | collective-permute-start | bytes 491528 | tf_op jit(solution)/shard_map/ppermute | solution.py:399
  33.6 11.2 %collective-permute-start.15 = (f32[320,128]{1,0:T(8,128)S(1)}, f32[320,128]{1,0:T(8,128)S(1)}, u32[]{:S(2)}, u32[]{:S(2)}) collective-permute-start(f32[320,128]{1,0:T(8,128)S(1)} %collective-permute-done.14.refs_0_), channel_id=1, source_target_pairs={{0,1},{1,0},{2,3},{3,2},{4,5},{5,4},{6,7},{7,6},{8,9},{9,8},{10,11... | collective-permute-start | bytes 491528 | tf_op jit(solution)/shard_map/ppermute | solution.py:399
  39.0 5.8 %collective-permute-start.16 = (f32[320,128]{1,0:T(8,128)S(1)}, f32[320,128]{1,0:T(8,128)S(1)}, u32[]{:S(2)}, u32[]{:S(2)}) collective-permute-start(f32[320,128]{1,0:T(8,128)S(1)} %collective-permute-done.14.refs_0_), channel_id=1, source_target_pairs={{0,16},{1,2},{2,1},{3,4},{4,3},{5,6},{6,5},{7,23},{8,24},{9,10},{1... | collective-permute-start | bytes 491528 | tf_op jit(solution)/shard_map/ppermute | solution.py:399
  39.0 10.5 %collective-permute-start.10 = (f32[320,128]{1,0:T(8,128)S(1)}, f32[320,128]{1,0:T(8,128)S(1)}, u32[]{:S(2)}, u32[]{:S(2)}) collective-permute-start(f32[320,128]{1,0:T(8,128)S(1)} %shard_map.97.refs_2_), channel_id=1, source_target_pairs={{0,8},{1,9},{2,10},{3,11},{4,12},{5,13},{6,14},{7,15},{8,0},{9,1},... | collective-permute-start | bytes 491528 | tf_op jit(solution)/shard_map/ppermute | solution.py:399
  44.8 6.2 %collective-permute-start.17 = (f32[192,128]{1,0:T(8,128)S(1)}, f32[192,128]{1,0:T(8,128)S(1)}, u32[]{:S(2)}, u32[]{:S(2)}) collective-permute-start(f32[192,128]{1,0:T(8,128)S(1)} %get-tuple-element.32.refs_3_), channel_id=1, source_target_pairs={{0,8},{1,9},{2,10},{3,11},{4,12},{5,13},{6,14},{7,15},{8,0},{9,1},... | collective-permute-start | bytes 294920 | tf_op jit(solution)/shard_map/ppermute | solution.py:399
  49.5 8.8 %collective-permute-start.19 = (f32[320,128]{1,0:T(8,128)S(1)}, f32[320,128]{1,0:T(8,128)S(1)}, u32[]{:S(2)}, u32[]{:S(2)}) collective-permute-start(f32[320,128]{1,0:T(8,128)S(1)} %collective-permute-done.10.refs_0_), channel_id=1, source_target_pairs={{0,1},{1,0},{2,3},{3,2},{4,5},{5,4},{6,7},{7,6},{8,9},{9,8},{10,11... | collective-permute-start | bytes 491528 | tf_op jit(solution)/shard_map/ppermute | solution.py:399
  49.5 3.1 %collective-permute-start.18 = (f32[128,128]{1,0:T(8,128)S(1)}, f32[128,128]{1,0:T(8,128)S(1)}, u32[]{:S(2)}, u32[]{:S(2)}) collective-permute-start(f32[128,128]{1,0:T(8,128)S(1)} %get-tuple-element.33.refs_4_), channel_id=1, source_target_pairs={{0,8},{1,9},{2,10},{3,11},{4,12},{5,13},{6,14},{7,15},{8,0},{9,1},... | collective-permute-start | bytes 196616 | tf_op jit(solution)/shard_map/ppermute | solution.py:399
  51.0 7.4 %collective-permute-start.20 = (f32[192,128]{1,0:T(8,128)S(1)}, f32[192,128]{1,0:T(8,128)S(1)}, u32[]{:S(2)}, u32[]{:S(2)}) collective-permute-start(f32[192,128]{1,0:T(8,128)S(1)} %collective-permute-done.17.refs_1_), channel_id=1, source_target_pairs={{0,1},{1,0},{2,3},{3,2},{4,5},{5,4},{6,7},{7,6},{8,9},{9,8},{10,11... | collective-permute-start | bytes 294920 | tf_op jit(solution)/shard_map/ppermute | solution.py:399
  52.7 4.4 %collective-permute-start.21 = (f32[128,128]{1,0:T(8,128)S(1)}, f32[128,128]{1,0:T(8,128)S(1)}, u32[]{:S(2)}, u32[]{:S(2)}) collective-permute-start(f32[128,128]{1,0:T(8,128)S(1)} %collective-permute-done.18.refs_2_), channel_id=1, source_target_pairs={{0,1},{1,0},{2,3},{3,2},{4,5},{5,4},{6,7},{7,6},{8,9},{9,8},{10,11... | collective-permute-start | bytes 196616 | tf_op jit(solution)/shard_map/ppermute | solution.py:399
  54.3 7.3 %collective-permute-start.22 = (f32[320,128]{1,0:T(8,128)S(1)}, f32[320,128]{1,0:T(8,128)S(1)}, u32[]{:S(2)}, u32[]{:S(2)}) collective-permute-start(f32[320,128]{1,0:T(8,128)S(1)} %collective-permute-done.10.refs_0_), channel_id=1, source_target_pairs={{0,16},{1,2},{2,1},{3,4},{4,3},{5,6},{6,5},{7,23},{8,24},{9,10},{1... | collective-permute-start | bytes 491528 | tf_op jit(solution)/shard_map/ppermute | solution.py:399
  56.5 4.1 %collective-permute-start.24 = (f32[128,128]{1,0:T(8,128)S(1)}, f32[128,128]{1,0:T(8,128)S(1)}, u32[]{:S(2)}, u32[]{:S(2)}) collective-permute-start(f32[128,128]{1,0:T(8,128)S(1)} %collective-permute-done.18.refs_2_), channel_id=1, source_target_pairs={{0,16},{1,2},{2,1},{3,4},{4,3},{5,6},{6,5},{7,23},{8,24},{9,10},{1... | collective-permute-start | bytes 196616 | tf_op jit(solution)/shard_map/ppermute | solution.py:399
  57.1 4.6 %collective-permute-start.23 = (f32[192,128]{1,0:T(8,128)S(1)}, f32[192,128]{1,0:T(8,128)S(1)}, u32[]{:S(2)}, u32[]{:S(2)}) collective-permute-start(f32[192,128]{1,0:T(8,128)S(1)} %collective-permute-done.17.refs_1_), channel_id=1, source_target_pairs={{0,16},{1,2},{2,1},{3,4},{4,3},{5,6},{6,5},{7,23},{8,24},{9,10},{1... | collective-permute-start | bytes 294920 | tf_op jit(solution)/shard_map/ppermute | solution.py:399
  (1 other events, 1.9 us)

commit v11 on v10

--- a/solution.py
+++ b/solution.py
@@ -13,7 +13,7 @@
 VMEM = pltpu.VMEM
 LIMIT = 16 * 2**20
 STREAMS = 2
-CHUNKS = (3, 2)
+CHUNKS = (2, 3)
 
 
 def spec(space):
@@ -54,36 +54,19 @@
     return high, low
 
 
-def prep_kernel(tiles, shots, sections, assign_at, refl_at, up_at, down_at, src_at, first, second, assign, refl, up, down, src, sems):
+def prep_kernel(tiles, shots, sections, assign_at, refl_at, up_at, down_at, src_at, first, second, *refs):
+    assign, refl, up, down, src, pick, sems = refs
     depth = lax.axis_index("depth")
     loads = [
         pltpu.make_async_copy(assign_at, assign, sems.at[0]),
         pltpu.make_async_copy(refl_at, refl, sems.at[1]),
-        pltpu.make_async_copy(up_at, up, sems.at[2]),
-        pltpu.make_async_copy(down_at, down, sems.at[3]),
-        pltpu.make_async_copy(src_at, src, sems.at[4]),
+        pltpu.make_async_copy(src_at, src, sems.at[2]),
+        pltpu.make_async_copy(up_at, up, sems.at[3]),
+        pltpu.make_async_copy(down_at, down, sems.at[4]),
     ]
     for load in loads:
         load.start()
-    for load in loads:
-        load.wait()
-    descends = depth < sections // 2
-
-    def write(of_up, of_down):
-        for j in range(tiles):
-            row = refl[0:1, rows_of(j)]
-            r = down_column(row)
-            of_up[rows_of(j)] = -(r * up[0, rows_of(j)])
-            of_down[rows_of(j)] = r * down[0, rows_of(j)]
-            first[tiles * TILE + j : tiles * TILE + j + 1] = row
-
-    @pl.when(descends)
-    def _():
-        write(first, second)
-
-    @pl.when(jnp.logical_not(descends))
-    def _():
-        write(second, first)
+    loads[0].wait()
 
     @pl.when(depth == 0)
     def _():
@@ -96,16 +79,46 @@
                 wanted = jnp.where(lane == at, shot, wanted)
                 wanted = jnp.where(lane == at + shots, shot + TILE // 2, wanted)
         source = lax.broadcasted_iota(jnp.int32, (TILE, TILE), 0)
-        pick = (source == jnp.broadcast_to(wanted[0:1], (TILE, TILE))).astype(jnp.float32).astype(jnp.bfloat16)
+        found = source == jnp.broadcast_to(wanted[0:1], (TILE, TILE))
+        pick[...] = found.astype(jnp.float32).astype(jnp.bfloat16)
+
+    for load in loads[1:]:
+        load.wait()
+    descends = depth < sections // 2
+
+    def of_up(j):
+        return -(down_column(refl[0:1, rows_of(j)]) * up[0, rows_of(j)])
+
+    def of_down(j):
+        return down_column(refl[0:1, rows_of(j)]) * down[0, rows_of(j)]
+
+    for j in range(tiles):
+        first[tiles * TILE + j : tiles * TILE + j + 1] = refl[0:1, rows_of(j)]
+
+    @pl.when(descends & (depth > 0))
+    def _():
+        for j in range(tiles):
+            first[rows_of(j)] = of_up(j)
+            second[rows_of(j)] = of_down(j)
+
+    @pl.when(jnp.logical_not(descends))
+    def _():
+        for j in range(tiles):
+            first[rows_of(j)] = of_down(j)
+            second[rows_of(j)] = of_up(j)
+
+    @pl.when(depth == 0)
+    def _():
         for j in range(tiles):
             x = src[rows_of(j)]
             high = x.astype(jnp.bfloat16)
             mid, low = split(x - high.astype(jnp.float32))
-            entering = jnp.dot(low, pick, preferred_element_type=jnp.float32)
-            entering += jnp.dot(mid, pick, preferred_element_type=jnp.float32)
-            entering += jnp.dot(high, pick, preferred_element_type=jnp.float32)
+            entering = jnp.dot(low, pick[...], preferred_element_type=jnp.float32)
+            entering += jnp.dot(mid, pick[...], preferred_element_type=jnp.float32)
+            entering += jnp.dot(high, pick[...], preferred_element_type=jnp.float32)
             r = down_column(refl[0:1, rows_of(j)])
-            first[rows_of(j)] = (1.0 + r) * entering + first[rows_of(j)]
+            first[rows_of(j)] = (1.0 + r) * entering + of_up(j)
+            second[rows_of(j)] = of_down(j)
 
 
 def pack_kernel(tiles, band, shift_at, tiles_at, out, shift, held, sems):
@@ -431,6 +444,7 @@
             VMEM(up_stored.shape, jnp.float32),
             VMEM(down_stored.shape, jnp.float32),
             VMEM(sources.shape, jnp.float32),
+            VMEM((TILE, TILE), jnp.bfloat16),
             pltpu.SemaphoreType.DMA((5,)),
         ],
         compiler_params=params(),

time: 64.1 us -> 64.2 us (level)
  no operation moved by 1% of the time
where the time goes in v11:
time: 64.2 us; the launch traced here: 63.6 us
  starting transfers between devices  33.8 us (53%)
  Pallas kernels  14.4 us (22%)
  waiting for transfers between devices  14.4 us (22%)
  between operations  0.95 us (1%)
    ppermute x25, starting transfers between devices, move(): return lax.ppermute(x, ('depth', 'lat'), pairs)  33.8 us
    ppermute x25, waiting for transfers between devices, move(): return lax.ppermute(x, ('depth', 'lat'), pairs)  14.4 us
    pallas_call x7, Pallas kernels, inner(): call(functools.partial(inner_kernel, step, sections, tiles, [len(part) fo...  5.08 us
    pallas_call x8, Pallas kernels, outer(): call(functools.partial(outer_kernel, step, sections, lats, tiles, shots,...  3.63 us
    pallas_call x1, Pallas kernels, shards(): call(functools.partial(pack_kernel, tiles, band), out_shape=jax.ShapeDtyp...  2.95 us
    pallas_call x1, Pallas kernels, shards(): call(functools.partial(prep_kernel, tiles, shots, sections), out_shape=[f...  1.53 us
  transfers between devices with their start and end apart: 25, of which 8 were waited for; matrix products, arithmetic and copies ran while one was open for 0% of the time, Pallas kernels for 16%

profile of v11, /device:TPU:1, one launch (start us, length us, event | category | flops | bytes accessed | tf_op | source)
XLA Modules:
  0.0 63.6 jit_solution(14813844215196072350)
XLA Ops:
  0.6 1.5 %shard_map.87 = (f32[648,128]{1,0:T(8,128)S(1)}, f32[640,128]{1,0:T(8,128)S(1)}) custom-call(s32[64]{0:T(128)} %assign_at.1, f32[1,640]{1,0:T(1,128)} %refl_at.1, f32[1,640,128]{2,1,0:T(8,128)} %up_at.1, f32[1,640,128]{2,1,0:T(8,128)} %down_at.1, f32[640,128]{1,0:T(8,128)} %src_at.1), custom_call_target="tpu_custom_call" | custom-call | flops 10000000 | bytes 1638400 | tf_op jit(solution)/shard_map/pallas_call | solution.py:436
  2.3 2.7 %collective-permute-start.1 = (f32[648,128]{1,0:T(8,128)S(1)}, f32[648,128]{1,0:T(8,128)S(1)}, u32[]{:S(2)}, u32[]{:S(2)}) collective-permute-start(f32[648,128]{1,0:T(8,128)S(1)} %get-tuple-element.20.refs_0_), channel_id=1, source_target_pairs={{0,16},{1,2},{2,1},{3,4},{4,3},{5,6},{6,5},{7,23},{8,24},{9,10},{1... | collective-permute-start | bytes 995336 | tf_op jit(solution)/shard_map/ppermute | solution.py:412
  5.0 3.0 %shard_map.86.packed = bf16[5,11,256,256]{3,2,1,0:T(8,128)(2,1)S(1)} custom-call(s32[1,5]{1,0:T(1,128)} %shift_at.1, f32[1,5,9,256,128]{4,3,2,1,0:T(8,128)} %tiles_at.1), custom_call_target="tpu_custom_call" | custom-call | flops 10000000 | bytes 11796480 | tf_op jit(solution)/shard_map/pallas_call | solution.py:454
  8.0 1.7 %shard_map.88.total = f32[5,256,128]{2,1,0:T(8,128)S(1)} custom-call(bf16[5,11,256,256]{3,2,1,0:T(8,128)(2,1)S(1)} %shard_map.86.packed, f32[648,128]{1,0:T(8,128)S(1)} %get-tuple-element.20.refs_0_, f32[648,128]{1,0:T(8,128)S(1)} %collective-permute-done.refs_1_), custom_call_target="tpu_custom_call" | custom-call | flops 1342177280 | bytes 8388608 | tf_op jit(solution)/shard_map/pallas_call | solution.py:477
  10.0 0.9 %shard_map.89 = (f32[320,128]{1,0:T(8,128)S(1)}, f32[320,128]{1,0:T(8,128)S(1)}) custom-call(bf16[5,11,256,256]{3,2,1,0:T(8,128)(2,1)S(1)} %shard_map.86.packed, f32[5,256,128]{2,1,0:T(8,128)S(1)} %shard_map.88.total, f32[648,128]{1,0:T(8,128)S(1)} %collective-permute-done.1.refs_0_.refs_2_), custom_call_target="tpu_custom_call" | custom-call | flops 503316480 | bytes 4194304 | tf_op jit(solution)/shard_map/pallas_call | solution.py:494
  12.5 4.3 %collective-permute-done.2.refs_0_ = f32[320,128]{1,0:T(8,128)S(1)} collective-permute-done((f32[320,128]{1,0:T(8,128)S(1)}, f32[320,128]{1,0:T(8,128)S(1)}, u32[]{:S(2)}, u32[]{:S(2)}) %collective-permute-start.2) | collective-permute-done | bytes 163872 | tf_op jit(solution)/shard_map/ppermute | solution.py:412
  16.8 1.2 %collective-permute-start.3 = (f32[320,128]{1,0:T(8,128)S(1)}, f32[320,128]{1,0:T(8,128)S(1)}, u32[]{:S(2)}, u32[]{:S(2)}) collective-permute-start(f32[320,128]{1,0:T(8,128)S(1)} %collective-permute-done.2.refs_0_), channel_id=1, source_target_pairs={{0,1},{1,0},{2,3},{3,2},{4,5},{5,4},{6,7},{7,6},{8,9},{9,8},{10,11... | collective-permute-start | bytes 491528 | tf_op jit(solution)/shard_map/ppermute | solution.py:412
  18.0 2.1 %collective-permute-start.9 = (f32[640,128]{1,0:T(8,128)S(1)}, f32[640,128]{1,0:T(8,128)S(1)}, u32[]{:S(2)}, u32[]{:S(2)}) collective-permute-start(f32[640,128]{1,0:T(8,128)S(1)} %get-tuple-element.28.refs_0_), channel_id=1, source_target_pairs={{0,16},{1,2},{2,1},{3,4},{4,3},{5,6},{6,5},{7,23},{8,24},{9,10},{1... | collective-permute-start | bytes 983048 | tf_op jit(solution)/shard_map/ppermute | solution.py:412
  21.1 1.5 %collective-permute-start.13 = (f32[320,128]{1,0:T(8,128)S(1)}, f32[320,128]{1,0:T(8,128)S(1)}, u32[]{:S(2)}, u32[]{:S(2)}) collective-permute-start(f32[320,128]{1,0:T(8,128)S(1)} %collective-permute-done.11.refs_0_), channel_id=1, source_target_pairs={{0,16},{1,2},{2,1},{3,4},{4,3},{5,6},{6,5},{7,23},{8,24},{9,10},{1... | collective-permute-start | bytes 491528 | tf_op jit(solution)/shard_map/ppermute | solution.py:412
  22.6 4.3 %collective-permute-done.4.refs_0_ = f32[320,128]{1,0:T(8,128)S(1)} collective-permute-done((f32[320,128]{1,0:T(8,128)S(1)}, f32[320,128]{1,0:T(8,128)S(1)}, u32[]{:S(2)}, u32[]{:S(2)}) %collective-permute-start.4) | collective-permute-done | bytes 163872 | tf_op jit(solution)/shard_map/ppermute | solution.py:412
  27.4 1.3 %collective-permute-done.13.refs_0_ = f32[320,128]{1,0:T(8,128)S(1)} collective-permute-done((f32[320,128]{1,0:T(8,128)S(1)}, f32[320,128]{1,0:T(8,128)S(1)}, u32[]{:S(2)}, u32[]{:S(2)}) %collective-permute-start.13) | collective-permute-done | bytes 163872 | tf_op jit(solution)/shard_map/ppermute | solution.py:412
  29.2 1.7 %shard_map.95.total = f32[5,256,128]{2,1,0:T(8,128)S(1)} custom-call(bf16[5,11,256,256]{3,2,1,0:T(8,128)(2,1)S(1)} %shard_map.86.packed, f32[640,128]{1,0:T(8,128)S(1)} %get-tuple-element.28.refs_0_, f32[640,128]{1,0:T(8,128)S(1)} %collective-permute-done.8.refs_1_), custom_call_target="tpu_custom_call" | custom-call | flops 1342177280 | bytes 8388608 | tf_op jit(solution)/shard_map/pallas_call | solution.py:477
  30.9 1.5 %collective-permute-start.7 = (f32[320,128]{1,0:T(8,128)S(1)}, f32[320,128]{1,0:T(8,128)S(1)}, u32[]{:S(2)}, u32[]{:S(2)}) collective-permute-start(f32[320,128]{1,0:T(8,128)S(1)} %collective-permute-done.5.refs_0_), channel_id=1, source_target_pairs={{0,16},{1,2},{2,1},{3,4},{4,3},{5,6},{6,5},{7,23},{8,24},{9,10},{1... | collective-permute-start | bytes 491528 | tf_op jit(solution)/shard_map/ppermute | solution.py:412
  33.4 5.7 %collective-permute-start.15 = (f32[320,128]{1,0:T(8,128)S(1)}, f32[320,128]{1,0:T(8,128)S(1)}, u32[]{:S(2)}, u32[]{:S(2)}) collective-permute-start(f32[320,128]{1,0:T(8,128)S(1)} %collective-permute-done.14.refs_0_), channel_id=1, source_target_pairs={{0,1},{1,0},{2,3},{3,2},{4,5},{5,4},{6,7},{7,6},{8,9},{9,8},{10,11... | collective-permute-start | bytes 491528 | tf_op jit(solution)/shard_map/ppermute | solution.py:412
  39.1 5.8 %collective-permute-start.10 = (f32[320,128]{1,0:T(8,128)S(1)}, f32[320,128]{1,0:T(8,128)S(1)}, u32[]{:S(2)}, u32[]{:S(2)}) collective-permute-start(f32[320,128]{1,0:T(8,128)S(1)} %shard_map.97.refs_2_), channel_id=1, source_target_pairs={{0,8},{1,9},{2,10},{3,11},{4,12},{5,13},{6,14},{7,15},{8,0},{9,1},... | collective-permute-start | bytes 491528 | tf_op jit(solution)/shard_map/ppermute | solution.py:412
  44.9 3.1 %collective-permute-start.18 = (f32[192,128]{1,0:T(8,128)S(1)}, f32[192,128]{1,0:T(8,128)S(1)}, u32[]{:S(2)}, u32[]{:S(2)}) collective-permute-start(f32[192,128]{1,0:T(8,128)S(1)} %get-tuple-element.33.refs_4_), channel_id=1, source_target_pairs={{0,8},{1,9},{2,10},{3,11},{4,12},{5,13},{6,14},{7,15},{8,0},{9,1},... | collective-permute-start | bytes 294920 | tf_op jit(solution)/shard_map/ppermute | solution.py:412
  48.0 1.6 %collective-permute-done.10.refs_0_ = f32[320,128]{1,0:T(8,128)S(1)} collective-permute-done((f32[320,128]{1,0:T(8,128)S(1)}, f32[320,128]{1,0:T(8,128)S(1)}, u32[]{:S(2)}, u32[]{:S(2)}) %collective-permute-start.10) | collective-permute-done | bytes 163872 | tf_op jit(solution)/shard_map/ppermute | solution.py:412
  49.6 1.5 %collective-permute-start.17 = (f32[128,128]{1,0:T(8,128)S(1)}, f32[128,128]{1,0:T(8,128)S(1)}, u32[]{:S(2)}, u32[]{:S(2)}) collective-permute-start(f32[128,128]{1,0:T(8,128)S(1)} %get-tuple-element.32.refs_3_), channel_id=1, source_target_pairs={{0,8},{1,9},{2,10},{3,11},{4,12},{5,13},{6,14},{7,15},{8,0},{9,1},... | collective-permute-start | bytes 196616 | tf_op jit(solution)/shard_map/ppermute | solution.py:412
  52.7 1.7 %collective-permute-start.20 = (f32[128,128]{1,0:T(8,128)S(1)}, f32[128,128]{1,0:T(8,128)S(1)}, u32[]{:S(2)}, u32[]{:S(2)}) collective-permute-start(f32[128,128]{1,0:T(8,128)S(1)} %collective-permute-done.17.refs_1_), channel_id=1, source_target_pairs={{0,1},{1,0},{2,3},{3,2},{4,5},{5,4},{6,7},{7,6},{8,9},{9,8},{10,11... | collective-permute-start | bytes 196616 | tf_op jit(solution)/shard_map/ppermute | solution.py:412
  54.4 1.3 %collective-permute-start.22 = (f32[320,128]{1,0:T(8,128)S(1)}, f32[320,128]{1,0:T(8,128)S(1)}, u32[]{:S(2)}, u32[]{:S(2)}) collective-permute-start(f32[320,128]{1,0:T(8,128)S(1)} %collective-permute-done.10.refs_0_), channel_id=1, source_target_pairs={{0,16},{1,2},{2,1},{3,4},{4,3},{5,6},{6,5},{7,23},{8,24},{9,10},{1... | collective-permute-start | bytes 491528 | tf_op jit(solution)/shard_map/ppermute | solution.py:412
  57.1 1.3 %collective-permute-start.24 = (f32[192,128]{1,0:T(8,128)S(1)}, f32[192,128]{1,0:T(8,128)S(1)}, u32[]{:S(2)}, u32[]{:S(2)}) collective-permute-start(f32[192,128]{1,0:T(8,128)S(1)} %collective-permute-done.18.refs_2_), channel_id=1, source_target_pairs={{0,16},{1,2},{2,1},{3,4},{4,3},{5,6},{6,5},{7,23},{8,24},{9,10},{1... | collective-permute-start | bytes 294920 | tf_op jit(solution)/shard_map/ppermute | solution.py:412
  58.4 1.8 %shard_map.104.total = f32[5,256,128]{2,1,0:T(8,128)S(1)} custom-call(bf16[5,11,256,256]{3,2,1,0:T(8,128)(2,1)S(1)} %shard_map.86.packed, f32[320,128]{1,0:T(8,128)S(1)} %collective-permute-done.10.refs_0_, f32[128,128]{1,0:T(8,128)S(1)} %collective-permute-done.17.refs_1_, f32[192,128]{1,0:T(8,128)S(1)} %collective-permute-done.18.refs_2_, ...), custom_call_target="tpu_custom_call" | custom-call | flops 1342177280 | bytes 8388608 | tf_op jit(solution)/shard_map/pallas_call | solution.py:477
  60.7 1.1 %collective-permute-done.24.refs_2_ = f32[192,128]{1,0:T(8,128)S(1)} collective-permute-done((f32[192,128]{1,0:T(8,128)S(1)}, f32[192,128]{1,0:T(8,128)S(1)}, u32[]{:S(2)}, u32[]{:S(2)}) %collective-permute-start.24) | collective-permute-done | bytes 98336 | tf_op jit(solution)/shard_map/ppermute | solution.py:412
  61.7 1.7 %shard_map.107 = (f32[1,640,128]{2,1,0:T(8,128)}, f32[1,640,128]{2,1,0:T(8,128)}) custom-call(bf16[5,11,256,256]{3,2,1,0:T(8,128)(2,1)S(1)} %shard_map.86.packed, f32[5,256,128]{2,1,0:T(8,128)S(1)} %shard_map.104.total, f32[320,128]{1,0:T(8,128)S(1)} %collective-permute-done.22.refs_0_, ...), custom_call_target="tpu_custom_call", output_to_operand_aliasing={{0}: (8, {}), {1}: (9, {})} | custom-call | flops 503316480 | bytes 4194304 | tf_op jit(solution)/shard_map/pallas_call | solution.py:494
  (48 shorter events, 8.4 us)
Async XLA Ops:
  2.2 5.8 %collective-permute-start = (f32[648,128]{1,0:T(8,128)S(1)}, f32[648,128]{1,0:T(8,128)S(1)}, u32[]{:S(2)}, u32[]{:S(2)}) collective-permute-start(f32[648,128]{1,0:T(8,128)S(1)} %get-tuple-element.20.refs_0_), channel_id=1, source_target_pairs={{0,1},{1,0},{2,3},{3,2},{4,5},{5,4},{6,7},{7,6},{8,9},{9,8},{10,11... | collective-permute-start | bytes 995336 | tf_op jit(solution)/shard_map/ppermute | solution.py:412
  2.3 7.7 %collective-permute-start.1 = (f32[648,128]{1,0:T(8,128)S(1)}, f32[648,128]{1,0:T(8,128)S(1)}, u32[]{:S(2)}, u32[]{:S(2)}) collective-permute-start(f32[648,128]{1,0:T(8,128)S(1)} %get-tuple-element.20.refs_0_), channel_id=1, source_target_pairs={{0,16},{1,2},{2,1},{3,4},{4,3},{5,6},{6,5},{7,23},{8,24},{9,10},{1... | collective-permute-start | bytes 995336 | tf_op jit(solution)/shard_map/ppermute | solution.py:412
  10.9 5.9 %collective-permute-start.2 = (f32[320,128]{1,0:T(8,128)S(1)}, f32[320,128]{1,0:T(8,128)S(1)}, u32[]{:S(2)}, u32[]{:S(2)}) collective-permute-start(f32[320,128]{1,0:T(8,128)S(1)} %get-tuple-element.21.refs_0_), channel_id=1, source_target_pairs={{0,8},{1,9},{2,10},{3,11},{4,12},{5,13},{6,14},{7,15},{8,0},{9,1},... | collective-permute-start | bytes 491528 | tf_op jit(solution)/shard_map/ppermute | solution.py:412
  11.7 8.9 %collective-permute-start.11 = (f32[320,128]{1,0:T(8,128)S(1)}, f32[320,128]{1,0:T(8,128)S(1)}, u32[]{:S(2)}, u32[]{:S(2)}) collective-permute-start(f32[320,128]{1,0:T(8,128)S(1)} %get-tuple-element.27.refs_1_), channel_id=1, source_target_pairs={{0,8},{1,9},{2,10},{3,11},{4,12},{5,13},{6,14},{7,15},{8,0},{9,1},... | collective-permute-start | bytes 491528 | tf_op jit(solution)/shard_map/ppermute | solution.py:412
  16.8 4.3 %collective-permute-start.3 = (f32[320,128]{1,0:T(8,128)S(1)}, f32[320,128]{1,0:T(8,128)S(1)}, u32[]{:S(2)}, u32[]{:S(2)}) collective-permute-start(f32[320,128]{1,0:T(8,128)S(1)} %collective-permute-done.2.refs_0_), channel_id=1, source_target_pairs={{0,1},{1,0},{2,3},{3,2},{4,5},{5,4},{6,7},{7,6},{8,9},{9,8},{10,11... | collective-permute-start | bytes 491528 | tf_op jit(solution)/shard_map/ppermute | solution.py:412
  18.0 11.2 %collective-permute-start.8 = (f32[640,128]{1,0:T(8,128)S(1)}, f32[640,128]{1,0:T(8,128)S(1)}, u32[]{:S(2)}, u32[]{:S(2)}) collective-permute-start(f32[640,128]{1,0:T(8,128)S(1)} %get-tuple-element.28.refs_0_), channel_id=1, source_target_pairs={{0,1},{1,0},{2,3},{3,2},{4,5},{5,4},{6,7},{7,6},{8,9},{9,8},{10,11... | collective-permute-start | bytes 983048 | tf_op jit(solution)/shard_map/ppermute | solution.py:412
  18.0 14.4 %collective-permute-start.9 = (f32[640,128]{1,0:T(8,128)S(1)}, f32[640,128]{1,0:T(8,128)S(1)}, u32[]{:S(2)}, u32[]{:S(2)}) collective-permute-start(f32[640,128]{1,0:T(8,128)S(1)} %get-tuple-element.28.refs_0_), channel_id=1, source_target_pairs={{0,16},{1,2},{2,1},{3,4},{4,3},{5,6},{6,5},{7,23},{8,24},{9,10},{1... | collective-permute-start | bytes 983048 | tf_op jit(solution)/shard_map/ppermute | solution.py:412
  20.5 6.5 %collective-permute-start.4 = (f32[320,128]{1,0:T(8,128)S(1)}, f32[320,128]{1,0:T(8,128)S(1)}, u32[]{:S(2)}, u32[]{:S(2)}) collective-permute-start(f32[320,128]{1,0:T(8,128)S(1)} %collective-permute-done.2.refs_0_), channel_id=1, source_target_pairs={{0,16},{1,2},{2,1},{3,4},{4,3},{5,6},{6,5},{7,23},{8,24},{9,10},{1... | collective-permute-start | bytes 491528 | tf_op jit(solution)/shard_map/ppermute | solution.py:412
  20.6 6.8 %collective-permute-start.12 = (f32[320,128]{1,0:T(8,128)S(1)}, f32[320,128]{1,0:T(8,128)S(1)}, u32[]{:S(2)}, u32[]{:S(2)}) collective-permute-start(f32[320,128]{1,0:T(8,128)S(1)} %collective-permute-done.11.refs_0_), channel_id=1, source_target_pairs={{0,1},{1,0},{2,3},{3,2},{4,5},{5,4},{6,7},{7,6},{8,9},{9,8},{10,11... | collective-permute-start | bytes 491528 | tf_op jit(solution)/shard_map/ppermute | solution.py:412
  21.1 7.6 %collective-permute-start.13 = (f32[320,128]{1,0:T(8,128)S(1)}, f32[320,128]{1,0:T(8,128)S(1)}, u32[]{:S(2)}, u32[]{:S(2)}) collective-permute-start(f32[320,128]{1,0:T(8,128)S(1)} %collective-permute-done.11.refs_0_), channel_id=1, source_target_pairs={{0,16},{1,2},{2,1},{3,4},{4,3},{5,6},{6,5},{7,23},{8,24},{9,10},{1... | collective-permute-start | bytes 491528 | tf_op jit(solution)/shard_map/ppermute | solution.py:412
  28.7 4.7 %collective-permute-start.14 = (f32[320,128]{1,0:T(8,128)S(1)}, f32[320,128]{1,0:T(8,128)S(1)}, u32[]{:S(2)}, u32[]{:S(2)}) collective-permute-start(f32[320,128]{1,0:T(8,128)S(1)} %shard_map.99.refs_1_), channel_id=1, source_target_pairs={{0,1},{1,0},{2,3},{3,2},{4,5},{5,4},{6,7},{7,6},{8,16},{9,17},{10,... | collective-permute-start | bytes 491528 | tf_op jit(solution)/shard_map/ppermute | solution.py:412
  29.1 9.9 %collective-permute-start.6 = (f32[320,128]{1,0:T(8,128)S(1)}, f32[320,128]{1,0:T(8,128)S(1)}, u32[]{:S(2)}, u32[]{:S(2)}) collective-permute-start(f32[320,128]{1,0:T(8,128)S(1)} %collective-permute-done.5.refs_0_), channel_id=1, source_target_pairs={{0,1},{1,0},{2,3},{3,2},{4,5},{5,4},{6,7},{7,6},{8,9},{9,8},{10,11... | collective-permute-start | bytes 491528 | tf_op jit(solution)/shard_map/ppermute | solution.py:412
  30.9 8.1 %collective-permute-start.7 = (f32[320,128]{1,0:T(8,128)S(1)}, f32[320,128]{1,0:T(8,128)S(1)}, u32[]{:S(2)}, u32[]{:S(2)}) collective-permute-start(f32[320,128]{1,0:T(8,128)S(1)} %collective-permute-done.5.refs_0_), channel_id=1, source_target_pairs={{0,16},{1,2},{2,1},{3,4},{4,3},{5,6},{6,5},{7,23},{8,24},{9,10},{1... | collective-permute-start | bytes 491528 | tf_op jit(solution)/shard_map/ppermute | solution.py:412
  33.4 11.5 %collective-permute-start.15 = (f32[320,128]{1,0:T(8,128)S(1)}, f32[320,128]{1,0:T(8,128)S(1)}, u32[]{:S(2)}, u32[]{:S(2)}) collective-permute-start(f32[320,128]{1,0:T(8,128)S(1)} %collective-permute-done.14.refs_0_), channel_id=1, source_target_pairs={{0,1},{1,0},{2,3},{3,2},{4,5},{5,4},{6,7},{7,6},{8,9},{9,8},{10,11... | collective-permute-start | bytes 491528 | tf_op jit(solution)/shard_map/ppermute | solution.py:412
  39.0 5.8 %collective-permute-start.16 = (f32[320,128]{1,0:T(8,128)S(1)}, f32[320,128]{1,0:T(8,128)S(1)}, u32[]{:S(2)}, u32[]{:S(2)}) collective-permute-start(f32[320,128]{1,0:T(8,128)S(1)} %collective-permute-done.14.refs_0_), channel_id=1, source_target_pairs={{0,16},{1,2},{2,1},{3,4},{4,3},{5,6},{6,5},{7,23},{8,24},{9,10},{1... | collective-permute-start | bytes 491528 | tf_op jit(solution)/shard_map/ppermute | solution.py:412
  39.1 10.5 %collective-permute-start.10 = (f32[320,128]{1,0:T(8,128)S(1)}, f32[320,128]{1,0:T(8,128)S(1)}, u32[]{:S(2)}, u32[]{:S(2)}) collective-permute-start(f32[320,128]{1,0:T(8,128)S(1)} %shard_map.97.refs_2_), channel_id=1, source_target_pairs={{0,8},{1,9},{2,10},{3,11},{4,12},{5,13},{6,14},{7,15},{8,0},{9,1},... | collective-permute-start | bytes 491528 | tf_op jit(solution)/shard_map/ppermute | solution.py:412
  44.9 6.2 %collective-permute-start.18 = (f32[192,128]{1,0:T(8,128)S(1)}, f32[192,128]{1,0:T(8,128)S(1)}, u32[]{:S(2)}, u32[]{:S(2)}) collective-permute-start(f32[192,128]{1,0:T(8,128)S(1)} %get-tuple-element.33.refs_4_), channel_id=1, source_target_pairs={{0,8},{1,9},{2,10},{3,11},{4,12},{5,13},{6,14},{7,15},{8,0},{9,1},... | collective-permute-start | bytes 294920 | tf_op jit(solution)/shard_map/ppermute | solution.py:412
  49.6 8.8 %collective-permute-start.19 = (f32[320,128]{1,0:T(8,128)S(1)}, f32[320,128]{1,0:T(8,128)S(1)}, u32[]{:S(2)}, u32[]{:S(2)}) collective-permute-start(f32[320,128]{1,0:T(8,128)S(1)} %collective-permute-done.10.refs_0_), channel_id=1, source_target_pairs={{0,1},{1,0},{2,3},{3,2},{4,5},{5,4},{6,7},{7,6},{8,9},{9,8},{10,11... | collective-permute-start | bytes 491528 | tf_op jit(solution)/shard_map/ppermute | solution.py:412
  49.6 3.1 %collective-permute-start.17 = (f32[128,128]{1,0:T(8,128)S(1)}, f32[128,128]{1,0:T(8,128)S(1)}, u32[]{:S(2)}, u32[]{:S(2)}) collective-permute-start(f32[128,128]{1,0:T(8,128)S(1)} %get-tuple-element.32.refs_3_), channel_id=1, source_target_pairs={{0,8},{1,9},{2,10},{3,11},{4,12},{5,13},{6,14},{7,15},{8,0},{9,1},... | collective-permute-start | bytes 196616 | tf_op jit(solution)/shard_map/ppermute | solution.py:412
  51.1 7.3 %collective-permute-start.21 = (f32[192,128]{1,0:T(8,128)S(1)}, f32[192,128]{1,0:T(8,128)S(1)}, u32[]{:S(2)}, u32[]{:S(2)}) collective-permute-start(f32[192,128]{1,0:T(8,128)S(1)} %collective-permute-done.18.refs_2_), channel_id=1, source_target_pairs={{0,1},{1,0},{2,3},{3,2},{4,5},{5,4},{6,7},{7,6},{8,9},{9,8},{10,11... | collective-permute-start | bytes 294920 | tf_op jit(solution)/shard_map/ppermute | solution.py:412
  52.7 4.4 %collective-permute-start.20 = (f32[128,128]{1,0:T(8,128)S(1)}, f32[128,128]{1,0:T(8,128)S(1)}, u32[]{:S(2)}, u32[]{:S(2)}) collective-permute-start(f32[128,128]{1,0:T(8,128)S(1)} %collective-permute-done.17.refs_1_), channel_id=1, source_target_pairs={{0,1},{1,0},{2,3},{3,2},{4,5},{5,4},{6,7},{7,6},{8,9},{9,8},{10,11... | collective-permute-start | bytes 196616 | tf_op jit(solution)/shard_map/ppermute | solution.py:412
  54.4 7.3 %collective-permute-start.22 = (f32[320,128]{1,0:T(8,128)S(1)}, f32[320,128]{1,0:T(8,128)S(1)}, u32[]{:S(2)}, u32[]{:S(2)}) collective-permute-start(f32[320,128]{1,0:T(8,128)S(1)} %collective-permute-done.10.refs_0_), channel_id=1, source_target_pairs={{0,16},{1,2},{2,1},{3,4},{4,3},{5,6},{6,5},{7,23},{8,24},{9,10},{1... | collective-permute-start | bytes 491528 | tf_op jit(solution)/shard_map/ppermute | solution.py:412
  56.6 4.1 %collective-permute-start.23 = (f32[128,128]{1,0:T(8,128)S(1)}, f32[128,128]{1,0:T(8,128)S(1)}, u32[]{:S(2)}, u32[]{:S(2)}) collective-permute-start(f32[128,128]{1,0:T(8,128)S(1)} %collective-permute-done.17.refs_1_), channel_id=1, source_target_pairs={{0,16},{1,2},{2,1},{3,4},{4,3},{5,6},{6,5},{7,23},{8,24},{9,10},{1... | collective-permute-start | bytes 196616 | tf_op jit(solution)/shard_map/ppermute | solution.py:412
  57.1 4.6 %collective-permute-start.24 = (f32[192,128]{1,0:T(8,128)S(1)}, f32[192,128]{1,0:T(8,128)S(1)}, u32[]{:S(2)}, u32[]{:S(2)}) collective-permute-start(f32[192,128]{1,0:T(8,128)S(1)} %collective-permute-done.18.refs_2_), channel_id=1, source_target_pairs={{0,16},{1,2},{2,1},{3,4},{4,3},{5,6},{6,5},{7,23},{8,24},{9,10},{1... | collective-permute-start | bytes 294920 | tf_op jit(solution)/shard_map/ppermute | solution.py:412
  (1 other events, 2.2 us)

commit v12 on v11

--- a/solution.py
+++ b/solution.py
@@ -122,15 +122,20 @@
 
 
 def pack_kernel(tiles, band, shift_at, tiles_at, out, shift, held, sems):
-    loads = [pltpu.make_async_copy(shift_at, shift, sems.at[tiles])]
-    loads += [pltpu.make_async_copy(tiles_at.at[0, j], held.at[j], sems.at[j]) for j in range(tiles)]
+    loads = [pltpu.make_async_copy(shift_at, shift, sems.at[tiles * (band // 3)])]
+    loads += [
+        pltpu.make_async_copy(tiles_at.at[0, j, pl.ds(3 * k, 3)], held.at[j, pl.ds(3 * k, 3)], sems.at[j * (band // 3) + k])
+        for j in range(tiles)
+        for k in range(band // 3)
+    ]
     for load in loads:
         load.start()
     loads[0].wait()
     for j in range(tiles):
-        loads[1 + j].wait()
         move = shift[0, j]
         for k in range(band):
+            if k % 3 == 0:
+                loads[1 + j * (band // 3) + k // 3].wait()
             high, low = split(held[j, k])
             slot = k + 1 + move
             out[j, slot, :, :TILE] = high
@@ -459,7 +464,7 @@
         scratch_shapes=[
             pltpu.SMEM(band_shift.shape, jnp.int32),
             VMEM(operator.shape[1:], jnp.float32),
-            pltpu.SemaphoreType.DMA((tiles + 1,)),
+            pltpu.SemaphoreType.DMA((tiles * (band // 3) + 1,)),
         ],
         compiler_params=params(),
         cost_estimate=cost(10**7, 2 * operator.size * 4),

time: 64.2 us -> 64.2 us (level)
  no operation moved by 1% of the time
where the time goes in v12:
time: 64.2 us; the launch traced here: 63.6 us
  starting transfers between devices  33.8 us (53%)
  Pallas kernels  14.4 us (22%)
  waiting for transfers between devices  14.4 us (22%)
  between operations  0.95 us (1%)
    ppermute x25, starting transfers between devices, move(): return lax.ppermute(x, ('depth', 'lat'), pairs)  33.8 us
    ppermute x25, waiting for transfers between devices, move(): return lax.ppermute(x, ('depth', 'lat'), pairs)  14.4 us
    pallas_call x7, Pallas kernels, inner(): call(functools.partial(inner_kernel, step, sections, tiles, [len(part) fo...  5.1 us
    pallas_call x8, Pallas kernels, outer(): call(functools.partial(outer_kernel, step, sections, lats, tiles, shots,...  3.63 us
    pallas_call x1, Pallas kernels, shards(): call(functools.partial(pack_kernel, tiles, band), out_shape=jax.ShapeDtyp...  2.89 us
    pallas_call x1, Pallas kernels, shards(): call(functools.partial(prep_kernel, tiles, shots, sections), out_shape=[f...  1.53 us
  transfers between devices with their start and end apart: 25, of which 8 were waited for; matrix products, arithmetic and copies ran while one was open for 0% of the time, Pallas kernels for 16%

profile of v12, /device:TPU:1, one launch (start us, length us, event | category | flops | bytes accessed | tf_op | source)
XLA Modules:
  0.0 63.6 jit_solution(1810447470415208731)
XLA Ops:
  0.6 1.5 %shard_map.87 = (f32[648,128]{1,0:T(8,128)S(1)}, f32[640,128]{1,0:T(8,128)S(1)}) custom-call(s32[64]{0:T(128)} %assign_at.1, f32[1,640]{1,0:T(1,128)} %refl_at.1, f32[1,640,128]{2,1,0:T(8,128)} %up_at.1, f32[1,640,128]{2,1,0:T(8,128)} %down_at.1, f32[640,128]{1,0:T(8,128)} %src_at.1), custom_call_target="tpu_custom_call" | custom-call | flops 10000000 | bytes 1638400 | tf_op jit(solution)/shard_map/pallas_call | solution.py:441
  2.3 2.7 %collective-permute-start.1 = (f32[648,128]{1,0:T(8,128)S(1)}, f32[648,128]{1,0:T(8,128)S(1)}, u32[]{:S(2)}, u32[]{:S(2)}) collective-permute-start(f32[648,128]{1,0:T(8,128)S(1)} %get-tuple-element.20.refs_0_), channel_id=1, source_target_pairs={{0,16},{1,2},{2,1},{3,4},{4,3},{5,6},{6,5},{7,23},{8,24},{9,10},{1... | collective-permute-start | bytes 995336 | tf_op jit(solution)/shard_map/ppermute | solution.py:417
  5.0 2.9 %shard_map.86.packed = bf16[5,11,256,256]{3,2,1,0:T(8,128)(2,1)S(1)} custom-call(s32[1,5]{1,0:T(1,128)} %shift_at.1, f32[1,5,9,256,128]{4,3,2,1,0:T(8,128)} %tiles_at.1), custom_call_target="tpu_custom_call" | custom-call | flops 10000000 | bytes 11796480 | tf_op jit(solution)/shard_map/pallas_call | solution.py:459
  7.9 1.7 %shard_map.88.total = f32[5,256,128]{2,1,0:T(8,128)S(1)} custom-call(bf16[5,11,256,256]{3,2,1,0:T(8,128)(2,1)S(1)} %shard_map.86.packed, f32[648,128]{1,0:T(8,128)S(1)} %get-tuple-element.20.refs_0_, f32[648,128]{1,0:T(8,128)S(1)} %collective-permute-done.refs_1_), custom_call_target="tpu_custom_call" | custom-call | flops 1342177280 | bytes 8388608 | tf_op jit(solution)/shard_map/pallas_call | solution.py:482
  10.0 0.9 %shard_map.89 = (f32[320,128]{1,0:T(8,128)S(1)}, f32[320,128]{1,0:T(8,128)S(1)}) custom-call(bf16[5,11,256,256]{3,2,1,0:T(8,128)(2,1)S(1)} %shard_map.86.packed, f32[5,256,128]{2,1,0:T(8,128)S(1)} %shard_map.88.total, f32[648,128]{1,0:T(8,128)S(1)} %collective-permute-done.1.refs_0_.refs_2_), custom_call_target="tpu_custom_call" | custom-call | flops 503316480 | bytes 4194304 | tf_op jit(solution)/shard_map/pallas_call | solution.py:499
  12.5 4.3 %collective-permute-done.2.refs_0_ = f32[320,128]{1,0:T(8,128)S(1)} collective-permute-done((f32[320,128]{1,0:T(8,128)S(1)}, f32[320,128]{1,0:T(8,128)S(1)}, u32[]{:S(2)}, u32[]{:S(2)}) %collective-permute-start.2) | collective-permute-done | bytes 163872 | tf_op jit(solution)/shard_map/ppermute | solution.py:417
  16.8 1.2 %collective-permute-start.3 = (f32[320,128]{1,0:T(8,128)S(1)}, f32[320,128]{1,0:T(8,128)S(1)}, u32[]{:S(2)}, u32[]{:S(2)}) collective-permute-start(f32[320,128]{1,0:T(8,128)S(1)} %collective-permute-done.2.refs_0_), channel_id=1, source_target_pairs={{0,1},{1,0},{2,3},{3,2},{4,5},{5,4},{6,7},{7,6},{8,9},{9,8},{10,11... | collective-permute-start | bytes 491528 | tf_op jit(solution)/shard_map/ppermute | solution.py:417
  18.0 2.1 %collective-permute-start.9 = (f32[640,128]{1,0:T(8,128)S(1)}, f32[640,128]{1,0:T(8,128)S(1)}, u32[]{:S(2)}, u32[]{:S(2)}) collective-permute-start(f32[640,128]{1,0:T(8,128)S(1)} %get-tuple-element.28.refs_0_), channel_id=1, source_target_pairs={{0,16},{1,2},{2,1},{3,4},{4,3},{5,6},{6,5},{7,23},{8,24},{9,10},{1... | collective-permute-start | bytes 983048 | tf_op jit(solution)/shard_map/ppermute | solution.py:417
  21.1 1.5 %collective-permute-start.13 = (f32[320,128]{1,0:T(8,128)S(1)}, f32[320,128]{1,0:T(8,128)S(1)}, u32[]{:S(2)}, u32[]{:S(2)}) collective-permute-start(f32[320,128]{1,0:T(8,128)S(1)} %collective-permute-done.11.refs_0_), channel_id=1, source_target_pairs={{0,16},{1,2},{2,1},{3,4},{4,3},{5,6},{6,5},{7,23},{8,24},{9,10},{1... | collective-permute-start | bytes 491528 | tf_op jit(solution)/shard_map/ppermute | solution.py:417
  22.6 4.3 %collective-permute-done.4.refs_0_ = f32[320,128]{1,0:T(8,128)S(1)} collective-permute-done((f32[320,128]{1,0:T(8,128)S(1)}, f32[320,128]{1,0:T(8,128)S(1)}, u32[]{:S(2)}, u32[]{:S(2)}) %collective-permute-start.4) | collective-permute-done | bytes 163872 | tf_op jit(solution)/shard_map/ppermute | solution.py:417
  27.4 1.3 %collective-permute-done.13.refs_0_ = f32[320,128]{1,0:T(8,128)S(1)} collective-permute-done((f32[320,128]{1,0:T(8,128)S(1)}, f32[320,128]{1,0:T(8,128)S(1)}, u32[]{:S(2)}, u32[]{:S(2)}) %collective-permute-start.13) | collective-permute-done | bytes 163872 | tf_op jit(solution)/shard_map/ppermute | solution.py:417
  29.2 1.7 %shard_map.95.total = f32[5,256,128]{2,1,0:T(8,128)S(1)} custom-call(bf16[5,11,256,256]{3,2,1,0:T(8,128)(2,1)S(1)} %shard_map.86.packed, f32[640,128]{1,0:T(8,128)S(1)} %get-tuple-element.28.refs_0_, f32[640,128]{1,0:T(8,128)S(1)} %collective-permute-done.8.refs_1_), custom_call_target="tpu_custom_call" | custom-call | flops 1342177280 | bytes 8388608 | tf_op jit(solution)/shard_map/pallas_call | solution.py:482
  30.9 1.5 %collective-permute-start.7 = (f32[320,128]{1,0:T(8,128)S(1)}, f32[320,128]{1,0:T(8,128)S(1)}, u32[]{:S(2)}, u32[]{:S(2)}) collective-permute-start(f32[320,128]{1,0:T(8,128)S(1)} %collective-permute-done.5.refs_0_), channel_id=1, source_target_pairs={{0,16},{1,2},{2,1},{3,4},{4,3},{5,6},{6,5},{7,23},{8,24},{9,10},{1... | collective-permute-start | bytes 491528 | tf_op jit(solution)/shard_map/ppermute | solution.py:417
  33.4 5.7 %collective-permute-start.15 = (f32[320,128]{1,0:T(8,128)S(1)}, f32[320,128]{1,0:T(8,128)S(1)}, u32[]{:S(2)}, u32[]{:S(2)}) collective-permute-start(f32[320,128]{1,0:T(8,128)S(1)} %collective-permute-done.14.refs_0_), channel_id=1, source_target_pairs={{0,1},{1,0},{2,3},{3,2},{4,5},{5,4},{6,7},{7,6},{8,9},{9,8},{10,11... | collective-permute-start | bytes 491528 | tf_op jit(solution)/shard_map/ppermute | solution.py:417
  39.1 5.8 %collective-permute-start.10 = (f32[320,128]{1,0:T(8,128)S(1)}, f32[320,128]{1,0:T(8,128)S(1)}, u32[]{:S(2)}, u32[]{:S(2)}) collective-permute-start(f32[320,128]{1,0:T(8,128)S(1)} %shard_map.97.refs_2_), channel_id=1, source_target_pairs={{0,8},{1,9},{2,10},{3,11},{4,12},{5,13},{6,14},{7,15},{8,0},{9,1},... | collective-permute-start | bytes 491528 | tf_op jit(solution)/shard_map/ppermute | solution.py:417
  44.9 3.1 %collective-permute-start.18 = (f32[192,128]{1,0:T(8,128)S(1)}, f32[192,128]{1,0:T(8,128)S(1)}, u32[]{:S(2)}, u32[]{:S(2)}) collective-permute-start(f32[192,128]{1,0:T(8,128)S(1)} %get-tuple-element.33.refs_4_), channel_id=1, source_target_pairs={{0,8},{1,9},{2,10},{3,11},{4,12},{5,13},{6,14},{7,15},{8,0},{9,1},... | collective-permute-start | bytes 294920 | tf_op jit(solution)/shard_map/ppermute | solution.py:417
  48.0 1.6 %collective-permute-done.10.refs_0_ = f32[320,128]{1,0:T(8,128)S(1)} collective-permute-done((f32[320,128]{1,0:T(8,128)S(1)}, f32[320,128]{1,0:T(8,128)S(1)}, u32[]{:S(2)}, u32[]{:S(2)}) %collective-permute-start.10) | collective-permute-done | bytes 163872 | tf_op jit(solution)/shard_map/ppermute | solution.py:417
  49.6 1.5 %collective-permute-start.17 = (f32[128,128]{1,0:T(8,128)S(1)}, f32[128,128]{1,0:T(8,128)S(1)}, u32[]{:S(2)}, u32[]{:S(2)}) collective-permute-start(f32[128,128]{1,0:T(8,128)S(1)} %get-tuple-element.32.refs_3_), channel_id=1, source_target_pairs={{0,8},{1,9},{2,10},{3,11},{4,12},{5,13},{6,14},{7,15},{8,0},{9,1},... | collective-permute-start | bytes 196616 | tf_op jit(solution)/shard_map/ppermute | solution.py:417
  52.7 1.7 %collective-permute-start.20 = (f32[128,128]{1,0:T(8,128)S(1)}, f32[128,128]{1,0:T(8,128)S(1)}, u32[]{:S(2)}, u32[]{:S(2)}) collective-permute-start(f32[128,128]{1,0:T(8,128)S(1)} %collective-permute-done.17.refs_1_), channel_id=1, source_target_pairs={{0,1},{1,0},{2,3},{3,2},{4,5},{5,4},{6,7},{7,6},{8,9},{9,8},{10,11... | collective-permute-start | bytes 196616 | tf_op jit(solution)/shard_map/ppermute | solution.py:417
  54.4 1.3 %collective-permute-start.22 = (f32[320,128]{1,0:T(8,128)S(1)}, f32[320,128]{1,0:T(8,128)S(1)}, u32[]{:S(2)}, u32[]{:S(2)}) collective-permute-start(f32[320,128]{1,0:T(8,128)S(1)} %collective-permute-done.10.refs_0_), channel_id=1, source_target_pairs={{0,16},{1,2},{2,1},{3,4},{4,3},{5,6},{6,5},{7,23},{8,24},{9,10},{1... | collective-permute-start | bytes 491528 | tf_op jit(solution)/shard_map/ppermute | solution.py:417
  57.1 1.3 %collective-permute-start.24 = (f32[192,128]{1,0:T(8,128)S(1)}, f32[192,128]{1,0:T(8,128)S(1)}, u32[]{:S(2)}, u32[]{:S(2)}) collective-permute-start(f32[192,128]{1,0:T(8,128)S(1)} %collective-permute-done.18.refs_2_), channel_id=1, source_target_pairs={{0,16},{1,2},{2,1},{3,4},{4,3},{5,6},{6,5},{7,23},{8,24},{9,10},{1... | collective-permute-start | bytes 294920 | tf_op jit(solution)/shard_map/ppermute | solution.py:417
  58.4 1.8 %shard_map.104.total = f32[5,256,128]{2,1,0:T(8,128)S(1)} custom-call(bf16[5,11,256,256]{3,2,1,0:T(8,128)(2,1)S(1)} %shard_map.86.packed, f32[320,128]{1,0:T(8,128)S(1)} %collective-permute-done.10.refs_0_, f32[128,128]{1,0:T(8,128)S(1)} %collective-permute-done.17.refs_1_, f32[192,128]{1,0:T(8,128)S(1)} %collective-permute-done.18.refs_2_, ...), custom_call_target="tpu_custom_call" | custom-call | flops 1342177280 | bytes 8388608 | tf_op jit(solution)/shard_map/pallas_call | solution.py:482
  60.7 1.1 %collective-permute-done.24.refs_2_ = f32[192,128]{1,0:T(8,128)S(1)} collective-permute-done((f32[192,128]{1,0:T(8,128)S(1)}, f32[192,128]{1,0:T(8,128)S(1)}, u32[]{:S(2)}, u32[]{:S(2)}) %collective-permute-start.24) | collective-permute-done | bytes 98336 | tf_op jit(solution)/shard_map/ppermute | solution.py:417
  61.7 1.7 %shard_map.107 = (f32[1,640,128]{2,1,0:T(8,128)}, f32[1,640,128]{2,1,0:T(8,128)}) custom-call(bf16[5,11,256,256]{3,2,1,0:T(8,128)(2,1)S(1)} %shard_map.86.packed, f32[5,256,128]{2,1,0:T(8,128)S(1)} %shard_map.104.total, f32[320,128]{1,0:T(8,128)S(1)} %collective-permute-done.22.refs_0_, ...), custom_call_target="tpu_custom_call", output_to_operand_aliasing={{0}: (8, {}), {1}: (9, {})} | custom-call | flops 503316480 | bytes 4194304 | tf_op jit(solution)/shard_map/pallas_call | solution.py:499
  (48 shorter events, 8.5 us)
Async XLA Ops:
  2.2 5.7 %collective-permute-start = (f32[648,128]{1,0:T(8,128)S(1)}, f32[648,128]{1,0:T(8,128)S(1)}, u32[]{:S(2)}, u32[]{:S(2)}) collective-permute-start(f32[648,128]{1,0:T(8,128)S(1)} %get-tuple-element.20.refs_0_), channel_id=1, source_target_pairs={{0,1},{1,0},{2,3},{3,2},{4,5},{5,4},{6,7},{7,6},{8,9},{9,8},{10,11... | collective-permute-start | bytes 995336 | tf_op jit(solution)/shard_map/ppermute | solution.py:417
  2.3 7.7 %collective-permute-start.1 = (f32[648,128]{1,0:T(8,128)S(1)}, f32[648,128]{1,0:T(8,128)S(1)}, u32[]{:S(2)}, u32[]{:S(2)}) collective-permute-start(f32[648,128]{1,0:T(8,128)S(1)} %get-tuple-element.20.refs_0_), channel_id=1, source_target_pairs={{0,16},{1,2},{2,1},{3,4},{4,3},{5,6},{6,5},{7,23},{8,24},{9,10},{1... | collective-permute-start | bytes 995336 | tf_op jit(solution)/shard_map/ppermute | solution.py:417
  10.9 5.9 %collective-permute-start.2 = (f32[320,128]{1,0:T(8,128)S(1)}, f32[320,128]{1,0:T(8,128)S(1)}, u32[]{:S(2)}, u32[]{:S(2)}) collective-permute-start(f32[320,128]{1,0:T(8,128)S(1)} %get-tuple-element.21.refs_0_), channel_id=1, source_target_pairs={{0,8},{1,9},{2,10},{3,11},{4,12},{5,13},{6,14},{7,15},{8,0},{9,1},... | collective-permute-start | bytes 491528 | tf_op jit(solution)/shard_map/ppermute | solution.py:417
  11.7 8.9 %collective-permute-start.11 = (f32[320,128]{1,0:T(8,128)S(1)}, f32[320,128]{1,0:T(8,128)S(1)}, u32[]{:S(2)}, u32[]{:S(2)}) collective-permute-start(f32[320,128]{1,0:T(8,128)S(1)} %get-tuple-element.27.refs_1_), channel_id=1, source_target_pairs={{0,8},{1,9},{2,10},{3,11},{4,12},{5,13},{6,14},{7,15},{8,0},{9,1},... | collective-permute-start | bytes 491528 | tf_op jit(solution)/shard_map/ppermute | solution.py:417
  16.8 4.3 %collective-permute-start.3 = (f32[320,128]{1,0:T(8,128)S(1)}, f32[320,128]{1,0:T(8,128)S(1)}, u32[]{:S(2)}, u32[]{:S(2)}) collective-permute-start(f32[320,128]{1,0:T(8,128)S(1)} %collective-permute-done.2.refs_0_), channel_id=1, source_target_pairs={{0,1},{1,0},{2,3},{3,2},{4,5},{5,4},{6,7},{7,6},{8,9},{9,8},{10,11... | collective-permute-start | bytes 491528 | tf_op jit(solution)/shard_map/ppermute | solution.py:417
  18.0 11.2 %collective-permute-start.8 = (f32[640,128]{1,0:T(8,128)S(1)}, f32[640,128]{1,0:T(8,128)S(1)}, u32[]{:S(2)}, u32[]{:S(2)}) collective-permute-start(f32[640,128]{1,0:T(8,128)S(1)} %get-tuple-element.28.refs_0_), channel_id=1, source_target_pairs={{0,1},{1,0},{2,3},{3,2},{4,5},{5,4},{6,7},{7,6},{8,9},{9,8},{10,11... | collective-permute-start | bytes 983048 | tf_op jit(solution)/shard_map/ppermute | solution.py:417
  18.0 14.4 %collective-permute-start.9 = (f32[640,128]{1,0:T(8,128)S(1)}, f32[640,128]{1,0:T(8,128)S(1)}, u32[]{:S(2)}, u32[]{:S(2)}) collective-permute-start(f32[640,128]{1,0:T(8,128)S(1)} %get-tuple-element.28.refs_0_), channel_id=1, source_target_pairs={{0,16},{1,2},{2,1},{3,4},{4,3},{5,6},{6,5},{7,23},{8,24},{9,10},{1... | collective-permute-start | bytes 983048 | tf_op jit(solution)/shard_map/ppermute | solution.py:417
  20.5 6.5 %collective-permute-start.4 = (f32[320,128]{1,0:T(8,128)S(1)}, f32[320,128]{1,0:T(8,128)S(1)}, u32[]{:S(2)}, u32[]{:S(2)}) collective-permute-start(f32[320,128]{1,0:T(8,128)S(1)} %collective-permute-done.2.refs_0_), channel_id=1, source_target_pairs={{0,16},{1,2},{2,1},{3,4},{4,3},{5,6},{6,5},{7,23},{8,24},{9,10},{1... | collective-permute-start | bytes 491528 | tf_op jit(solution)/shard_map/ppermute | solution.py:417
  20.6 6.8 %collective-permute-start.12 = (f32[320,128]{1,0:T(8,128)S(1)}, f32[320,128]{1,0:T(8,128)S(1)}, u32[]{:S(2)}, u32[]{:S(2)}) collective-permute-start(f32[320,128]{1,0:T(8,128)S(1)} %collective-permute-done.11.refs_0_), channel_id=1, source_target_pairs={{0,1},{1,0},{2,3},{3,2},{4,5},{5,4},{6,7},{7,6},{8,9},{9,8},{10,11... | collective-permute-start | bytes 491528 | tf_op jit(solution)/shard_map/ppermute | solution.py:417
  21.1 7.6 %collective-permute-start.13 = (f32[320,128]{1,0:T(8,128)S(1)}, f32[320,128]{1,0:T(8,128)S(1)}, u32[]{:S(2)}, u32[]{:S(2)}) collective-permute-start(f32[320,128]{1,0:T(8,128)S(1)} %collective-permute-done.11.refs_0_), channel_id=1, source_target_pairs={{0,16},{1,2},{2,1},{3,4},{4,3},{5,6},{6,5},{7,23},{8,24},{9,10},{1... | collective-permute-start | bytes 491528 | tf_op jit(solution)/shard_map/ppermute | solution.py:417
  28.7 4.7 %collective-permute-start.14 = (f32[320,128]{1,0:T(8,128)S(1)}, f32[320,128]{1,0:T(8,128)S(1)}, u32[]{:S(2)}, u32[]{:S(2)}) collective-permute-start(f32[320,128]{1,0:T(8,128)S(1)} %shard_map.99.refs_1_), channel_id=1, source_target_pairs={{0,1},{1,0},{2,3},{3,2},{4,5},{5,4},{6,7},{7,6},{8,16},{9,17},{10,... | collective-permute-start | bytes 491528 | tf_op jit(solution)/shard_map/ppermute | solution.py:417
  29.1 9.9 %collective-permute-start.6 = (f32[320,128]{1,0:T(8,128)S(1)}, f32[320,128]{1,0:T(8,128)S(1)}, u32[]{:S(2)}, u32[]{:S(2)}) collective-permute-start(f32[320,128]{1,0:T(8,128)S(1)} %collective-permute-done.5.refs_0_), channel_id=1, source_target_pairs={{0,1},{1,0},{2,3},{3,2},{4,5},{5,4},{6,7},{7,6},{8,9},{9,8},{10,11... | collective-permute-start | bytes 491528 | tf_op jit(solution)/shard_map/ppermute | solution.py:417
  30.9 8.1 %collective-permute-start.7 = (f32[320,128]{1,0:T(8,128)S(1)}, f32[320,128]{1,0:T(8,128)S(1)}, u32[]{:S(2)}, u32[]{:S(2)}) collective-permute-start(f32[320,128]{1,0:T(8,128)S(1)} %collective-permute-done.5.refs_0_), channel_id=1, source_target_pairs={{0,16},{1,2},{2,1},{3,4},{4,3},{5,6},{6,5},{7,23},{8,24},{9,10},{1... | collective-permute-start | bytes 491528 | tf_op jit(solution)/shard_map/ppermute | solution.py:417
  33.4 11.5 %collective-permute-start.15 = (f32[320,128]{1,0:T(8,128)S(1)}, f32[320,128]{1,0:T(8,128)S(1)}, u32[]{:S(2)}, u32[]{:S(2)}) collective-permute-start(f32[320,128]{1,0:T(8,128)S(1)} %collective-permute-done.14.refs_0_), channel_id=1, source_target_pairs={{0,1},{1,0},{2,3},{3,2},{4,5},{5,4},{6,7},{7,6},{8,9},{9,8},{10,11... | collective-permute-start | bytes 491528 | tf_op jit(solution)/shard_map/ppermute | solution.py:417
  39.0 5.8 %collective-permute-start.16 = (f32[320,128]{1,0:T(8,128)S(1)}, f32[320,128]{1,0:T(8,128)S(1)}, u32[]{:S(2)}, u32[]{:S(2)}) collective-permute-start(f32[320,128]{1,0:T(8,128)S(1)} %collective-permute-done.14.refs_0_), channel_id=1, source_target_pairs={{0,16},{1,2},{2,1},{3,4},{4,3},{5,6},{6,5},{7,23},{8,24},{9,10},{1... | collective-permute-start | bytes 491528 | tf_op jit(solution)/shard_map/ppermute | solution.py:417
  39.1 10.5 %collective-permute-start.10 = (f32[320,128]{1,0:T(8,128)S(1)}, f32[320,128]{1,0:T(8,128)S(1)}, u32[]{:S(2)}, u32[]{:S(2)}) collective-permute-start(f32[320,128]{1,0:T(8,128)S(1)} %shard_map.97.refs_2_), channel_id=1, source_target_pairs={{0,8},{1,9},{2,10},{3,11},{4,12},{5,13},{6,14},{7,15},{8,0},{9,1},... | collective-permute-start | bytes 491528 | tf_op jit(solution)/shard_map/ppermute | solution.py:417
  44.9 6.2 %collective-permute-start.18 = (f32[192,128]{1,0:T(8,128)S(1)}, f32[192,128]{1,0:T(8,128)S(1)}, u32[]{:S(2)}, u32[]{:S(2)}) collective-permute-start(f32[192,128]{1,0:T(8,128)S(1)} %get-tuple-element.33.refs_4_), channel_id=1, source_target_pairs={{0,8},{1,9},{2,10},{3,11},{4,12},{5,13},{6,14},{7,15},{8,0},{9,1},... | collective-permute-start | bytes 294920 | tf_op jit(solution)/shard_map/ppermute | solution.py:417
  49.6 8.8 %collective-permute-start.19 = (f32[320,128]{1,0:T(8,128)S(1)}, f32[320,128]{1,0:T(8,128)S(1)}, u32[]{:S(2)}, u32[]{:S(2)}) collective-permute-start(f32[320,128]{1,0:T(8,128)S(1)} %collective-permute-done.10.refs_0_), channel_id=1, source_target_pairs={{0,1},{1,0},{2,3},{3,2},{4,5},{5,4},{6,7},{7,6},{8,9},{9,8},{10,11... | collective-permute-start | bytes 491528 | tf_op jit(solution)/shard_map/ppermute | solution.py:417
  49.6 3.1 %collective-permute-start.17 = (f32[128,128]{1,0:T(8,128)S(1)}, f32[128,128]{1,0:T(8,128)S(1)}, u32[]{:S(2)}, u32[]{:S(2)}) collective-permute-start(f32[128,128]{1,0:T(8,128)S(1)} %get-tuple-element.32.refs_3_), channel_id=1, source_target_pairs={{0,8},{1,9},{2,10},{3,11},{4,12},{5,13},{6,14},{7,15},{8,0},{9,1},... | collective-permute-start | bytes 196616 | tf_op jit(solution)/shard_map/ppermute | solution.py:417
  51.1 7.3 %collective-permute-start.21 = (f32[192,128]{1,0:T(8,128)S(1)}, f32[192,128]{1,0:T(8,128)S(1)}, u32[]{:S(2)}, u32[]{:S(2)}) collective-permute-start(f32[192,128]{1,0:T(8,128)S(1)} %collective-permute-done.18.refs_2_), channel_id=1, source_target_pairs={{0,1},{1,0},{2,3},{3,2},{4,5},{5,4},{6,7},{7,6},{8,9},{9,8},{10,11... | collective-permute-start | bytes 294920 | tf_op jit(solution)/shard_map/ppermute | solution.py:417
  52.7 4.4 %collective-permute-start.20 = (f32[128,128]{1,0:T(8,128)S(1)}, f32[128,128]{1,0:T(8,128)S(1)}, u32[]{:S(2)}, u32[]{:S(2)}) collective-permute-start(f32[128,128]{1,0:T(8,128)S(1)} %collective-permute-done.17.refs_1_), channel_id=1, source_target_pairs={{0,1},{1,0},{2,3},{3,2},{4,5},{5,4},{6,7},{7,6},{8,9},{9,8},{10,11... | collective-permute-start | bytes 196616 | tf_op jit(solution)/shard_map/ppermute | solution.py:417
  54.4 7.3 %collective-permute-start.22 = (f32[320,128]{1,0:T(8,128)S(1)}, f32[320,128]{1,0:T(8,128)S(1)}, u32[]{:S(2)}, u32[]{:S(2)}) collective-permute-start(f32[320,128]{1,0:T(8,128)S(1)} %collective-permute-done.10.refs_0_), channel_id=1, source_target_pairs={{0,16},{1,2},{2,1},{3,4},{4,3},{5,6},{6,5},{7,23},{8,24},{9,10},{1... | collective-permute-start | bytes 491528 | tf_op jit(solution)/shard_map/ppermute | solution.py:417
  56.6 4.1 %collective-permute-start.23 = (f32[128,128]{1,0:T(8,128)S(1)}, f32[128,128]{1,0:T(8,128)S(1)}, u32[]{:S(2)}, u32[]{:S(2)}) collective-permute-start(f32[128,128]{1,0:T(8,128)S(1)} %collective-permute-done.17.refs_1_), channel_id=1, source_target_pairs={{0,16},{1,2},{2,1},{3,4},{4,3},{5,6},{6,5},{7,23},{8,24},{9,10},{1... | collective-permute-start | bytes 196616 | tf_op jit(solution)/shard_map/ppermute | solution.py:417
  57.1 4.6 %collective-permute-start.24 = (f32[192,128]{1,0:T(8,128)S(1)}, f32[192,128]{1,0:T(8,128)S(1)}, u32[]{:S(2)}, u32[]{:S(2)}) collective-permute-start(f32[192,128]{1,0:T(8,128)S(1)} %collective-permute-done.18.refs_2_), channel_id=1, source_target_pairs={{0,16},{1,2},{2,1},{3,4},{4,3},{5,6},{6,5},{7,23},{8,24},{9,10},{1... | collective-permute-start | bytes 294920 | tf_op jit(solution)/shard_map/ppermute | solution.py:417
  (1 other events, 2.2 us)
